TPU v7x, 128 devices: a whole 4x4x4 slice. The times are simulated.
128 devices in a mesh: ctx: 8 (over y, core), tp: 16 (over z, x).
Axes of the slice: x: 4, y: 4, z: 4, core: 2. Of those that a mesh axis runs over, the one named last changes fastest.
Arguments:
- queries: bfloat16 [16384, 8192], P(('ctx', 'tp')), may hold values from -16 to 16
- key_tensor: bfloat16 [16384, 1024], P(('ctx', 'tp')), may hold values from -6 to 6
- value_tensor: bfloat16 [16384, 1024], P(('ctx', 'tp')), may hold values from -6 to 6
- output_gradient: bfloat16 [16384, 8192], P(('ctx', 'tp')), may hold values from -6 to 6
- key_blocks: int32 [128, 8], replicated, may hold values from 0 to 127, as said below
- slot_valid: int32 [128, 8], replicated, may hold values from 0 to 1, as said below
Outputs:
- d_q: bfloat16 [16384, 8192], P(('ctx', 'tp'))
- key_gradient: bfloat16 [16384, 1024], P(('ctx', 'tp'))
- value_gradient: bfloat16 [16384, 1024], P(('ctx', 'tp'))
Inputs may be any that keep to these rules, and one draw needn't show every extreme that they name: `key_blocks`: row b names blocks b - 1, b, b + 1 (clamped to the sequence), block 0, then 8 - 4 blocks that differ from one another and from b - 1, b and b + 1. Row 0 is not read. `slot_valid`: the slot of block b itself is 1 in every row; a window slot naming a block below 1 or above 127 is 0, the block 0 slot is 1, and among the random slots a ragged leading part is 1 except where it names block 0.
All inputs are finite; a program needn't handle non-finite values.
Results may differ from a plain program's by a relative error of at most 0.006.
Values may be sent and summed in bfloat16 or wider, within the bound.
No kernel may reach another device: no remote copies, remote signals or barrier semaphores. Data moves between devices by JAX's collectives and lax.ppermute only.
A program may use at most 256 MiB of HBM per device.

v0:
```python
import math

import jax
import jax.numpy as jnp
from jax import lax
from jax.sharding import PartitionSpec as P

QUERY_HEADS = 64
KEY_HEADS = 8
HEAD_SIZE = 128
BLOCK_TOKENS = 128
NB = 8
GROUP_SIZE = 8


def sparse_turn(packed):
    q_part, o_part, key_part, value_part, live_part = packed
    scaling = 1.0 / math.sqrt(HEAD_SIZE)
    scores = (
        jnp.einsum("pqhgd,pkhd->phgqk", q_part, key_part, preferred_element_type=jnp.float32)
        * scaling
    )
    scores = jnp.where(live_part[:, None, None, None, :], scores, -jnp.inf)
    row_max = jnp.max(scores, axis=-1, keepdims=True)
    raised = jnp.exp(scores - row_max)
    weights = raised / jnp.sum(raised, axis=-1, keepdims=True)
    prob_grad = jnp.einsum(
        "pqhgd,pkhd->phgqk", o_part, value_part, preferred_element_type=jnp.float32
    )
    row_dot = jnp.sum(weights * prob_grad, axis=-1, keepdims=True)
    score_grad = (weights * (prob_grad - row_dot)).astype(jnp.bfloat16)
    rounded_weights = weights.astype(jnp.bfloat16)
    value_grad = jnp.einsum(
        "phgqk,pqhgd->pkhd", rounded_weights, o_part, preferred_element_type=jnp.float32
    )
    key_grad = (
        jnp.einsum("phgqk,pqhgd->pkhd", score_grad, q_part, preferred_element_type=jnp.float32)
        * scaling
    )
    query_grad = (
        jnp.einsum("phgqk,pkhd->pqhgd", score_grad, key_part, preferred_element_type=jnp.float32)
        * scaling
    )
    return (query_grad, key_grad, value_grad)


def stretch_scores(q_rows, o_rows, key_part, value_part):
    scaling = 1.0 / math.sqrt(HEAD_SIZE)
    scores = (
        jnp.einsum("qhgd,khd->hgqk", q_rows, key_part, preferred_element_type=jnp.float32) * scaling
    )
    prob_grad = jnp.einsum("qhgd,khd->hgqk", o_rows, value_part, preferred_element_type=jnp.float32)
    return (scores, prob_grad)


def split_keys(key_span, value_span):
    key_total = key_span.shape[0]
    step_keys = math.gcd(key_total, 2048)
    steps_count = key_total // step_keys
    return (
        key_span.reshape((steps_count, step_keys) + key_span.shape[1:]),
        value_span.reshape((steps_count, step_keys) + value_span.shape[1:]),
    )


def stats_pass(q_rows, o_rows, key_span, value_span):
    key_steps, value_steps = split_keys(key_span, value_span)
    row_shape = (q_rows.shape[1], q_rows.shape[2], q_rows.shape[0])

    def stats_advance(running, packed):
        row_max, row_sum, row_dot = running
        scores, prob_grad = stretch_scores(q_rows, o_rows, packed[0], packed[1])
        new_max = jnp.maximum(row_max, jnp.max(scores, axis=-1))
        factor = jnp.exp(row_max - new_max)
        raised = jnp.exp(scores - new_max[..., None])
        return (
            (
                new_max,
                row_sum * factor + jnp.sum(raised, axis=-1),
                row_dot * factor + jnp.sum(raised * prob_grad, axis=-1),
            ),
            None,
        )

    initial = (
        jnp.full(row_shape, -jnp.inf, jnp.float32),
        jnp.zeros(row_shape, jnp.float32),
        jnp.zeros(row_shape, jnp.float32),
    )
    result, unused = lax.scan(stats_advance, initial, (key_steps, value_steps))
    return result


def grad_pass(q_rows, o_rows, key_span, value_span, row_max, row_sum, row_delta):
    key_steps, value_steps = split_keys(key_span, value_span)
    scaling = 1.0 / math.sqrt(HEAD_SIZE)

    def grad_advance(query_grad, packed):
        key_part, value_part = packed
        scores, prob_grad = stretch_scores(q_rows, o_rows, key_part, value_part)
        weights = jnp.exp(scores - row_max[..., None]) / row_sum[..., None]
        score_grad = (weights * (prob_grad - row_delta[..., None])).astype(jnp.bfloat16)
        rounded_weights = weights.astype(jnp.bfloat16)
        value_grad = jnp.einsum(
            "hgqk,qhgd->khd", rounded_weights, o_rows, preferred_element_type=jnp.float32
        )
        key_grad = (
            jnp.einsum("hgqk,qhgd->khd", score_grad, q_rows, preferred_element_type=jnp.float32)
            * scaling
        )
        query_grad = (
            query_grad
            + jnp.einsum("hgqk,khd->qhgd", score_grad, key_part, preferred_element_type=jnp.float32)
            * scaling
        )
        return (query_grad, (key_grad, value_grad))

    query_grad, grads_steps = lax.scan(
        grad_advance, jnp.zeros(q_rows.shape, jnp.float32), (key_steps, value_steps)
    )
    return (
        query_grad,
        grads_steps[0].reshape(key_span.shape),
        grads_steps[1].reshape(value_span.shape),
    )


def per_device(queries, key_tensor, value_tensor, output_gradient, key_blocks, slot_valid):
    context_length = lax.axis_size("ctx")
    tp_size = lax.axis_size("tp")
    token_count = queries.shape[0]
    local_key_value = KEY_HEADS // context_length
    per_piece = token_count // BLOCK_TOKENS
    length = context_length * tp_size * token_count
    blocks_total = length // BLOCK_TOKENS
    q_heads, o_heads, k_heads, v_heads = (
        lax.all_to_all(
            queries.reshape(token_count, KEY_HEADS, GROUP_SIZE * HEAD_SIZE),
            "ctx",
            split_axis=1,
            concat_axis=0,
            tiled=True,
        ),
        lax.all_to_all(
            output_gradient.reshape(token_count, KEY_HEADS, GROUP_SIZE * HEAD_SIZE),
            "ctx",
            split_axis=1,
            concat_axis=0,
            tiled=True,
        ),
        lax.all_to_all(
            key_tensor.reshape(token_count, KEY_HEADS, HEAD_SIZE),
            "ctx",
            split_axis=1,
            concat_axis=0,
            tiled=True,
        ),
        lax.all_to_all(
            value_tensor.reshape(token_count, KEY_HEADS, HEAD_SIZE),
            "ctx",
            split_axis=1,
            concat_axis=0,
            tiled=True,
        ),
    )
    key_full, value_full = (
        lax.all_gather(
            k_heads.reshape(context_length, token_count, local_key_value, HEAD_SIZE),
            "tp",
            axis=1,
            tiled=True,
        ),
        lax.all_gather(
            v_heads.reshape(context_length, token_count, local_key_value, HEAD_SIZE),
            "tp",
            axis=1,
            tiled=True,
        ),
    )
    key_by_block = key_full.reshape(blocks_total, BLOCK_TOKENS, local_key_value, HEAD_SIZE)
    value_by_block = value_full.reshape(blocks_total, BLOCK_TOKENS, local_key_value, HEAD_SIZE)
    tp_index = lax.axis_index("tp")
    slot_table = lax.dynamic_slice_in_dim(
        key_blocks.reshape(context_length, tp_size * per_piece, NB),
        tp_index * per_piece,
        per_piece,
        1,
    )
    live_table = lax.dynamic_slice_in_dim(
        slot_valid.reshape(context_length, tp_size * per_piece, NB),
        tp_index * per_piece,
        per_piece,
        1,
    )
    block_ids = (jnp.arange(context_length)[:, None] * tp_size + tp_index) * per_piece + jnp.arange(
        per_piece
    )[None, :]
    keep_rows = (block_ids != 0).astype(jnp.bfloat16)
    key_slots = key_by_block[slot_table].reshape(
        context_length, per_piece, NB * BLOCK_TOKENS, local_key_value, HEAD_SIZE
    )
    value_slots = value_by_block[slot_table].reshape(
        context_length, per_piece, NB * BLOCK_TOKENS, local_key_value, HEAD_SIZE
    )
    live_mask = jnp.broadcast_to(
        (live_table > 0)[..., None], (context_length, per_piece, NB, BLOCK_TOKENS)
    ).reshape(context_length, per_piece, NB * BLOCK_TOKENS)
    q_local = q_heads.reshape(
        context_length, per_piece, BLOCK_TOKENS, local_key_value, GROUP_SIZE, HEAD_SIZE
    )
    o_local = (
        o_heads.reshape(
            context_length, per_piece, BLOCK_TOKENS, local_key_value, GROUP_SIZE, HEAD_SIZE
        )
        * keep_rows[:, :, None, None, None, None]
    )
    dq_sparse, dk_slots, dv_slots = lax.map(
        sparse_turn, (q_local, o_local, key_slots, value_slots, live_mask)
    )
    flat_table = slot_table.reshape(context_length * per_piece, NB)
    dk_terms = dk_slots.reshape(
        context_length, per_piece, NB, BLOCK_TOKENS, local_key_value, HEAD_SIZE
    )
    dv_terms = dv_slots.reshape(
        context_length, per_piece, NB, BLOCK_TOKENS, local_key_value, HEAD_SIZE
    )
    dk_total = (
        jnp.zeros((blocks_total, BLOCK_TOKENS, local_key_value, HEAD_SIZE), jnp.float32)
        .at[flat_table]
        .add(
            dk_terms.reshape(
                context_length * per_piece, NB, BLOCK_TOKENS, local_key_value, HEAD_SIZE
            )
        )
        .reshape(length, local_key_value, HEAD_SIZE)
    )
    dv_total = (
        jnp.zeros((blocks_total, BLOCK_TOKENS, local_key_value, HEAD_SIZE), jnp.float32)
        .at[flat_table]
        .add(
            dv_terms.reshape(
                context_length * per_piece, NB, BLOCK_TOKENS, local_key_value, HEAD_SIZE
            )
        )
        .reshape(length, local_key_value, HEAD_SIZE)
    )
    q_first = q_heads[:BLOCK_TOKENS].reshape(BLOCK_TOKENS, local_key_value, GROUP_SIZE, HEAD_SIZE)
    o_first = o_heads[:BLOCK_TOKENS].reshape(BLOCK_TOKENS, local_key_value, GROUP_SIZE, HEAD_SIZE)
    key_line = key_full.reshape(length, local_key_value, HEAD_SIZE)
    value_line = value_full.reshape(length, local_key_value, HEAD_SIZE)

    def owner_pass(totals):
        row_max, row_sum, row_dot = stats_pass(q_first, o_first, key_line, value_line)
        dq_whole, dk_whole, dv_whole = grad_pass(
            q_first, o_first, key_line, value_line, row_max, row_sum, row_dot / row_sum
        )
        return (dq_whole, totals[0] + dk_whole, totals[1] + dv_whole)

    def other_pass(totals):
        return (
            jnp.zeros((BLOCK_TOKENS, local_key_value, GROUP_SIZE, HEAD_SIZE), jnp.float32),
            totals[0],
            totals[1],
        )

    dq_first, dk_total, dv_total = lax.cond(
        tp_index == 0, owner_pass, other_pass, (dk_total, dv_total)
    )
    dq_rows = dq_sparse.reshape(
        context_length * token_count, local_key_value, GROUP_SIZE * HEAD_SIZE
    )
    dq_rows = (
        dq_rows.at[:BLOCK_TOKENS]
        .add(dq_first.reshape(BLOCK_TOKENS, local_key_value, GROUP_SIZE * HEAD_SIZE))
        .astype(jnp.bfloat16)
    )
    dk_sum, dv_sum = (
        lax.psum_scatter(
            dk_total.reshape(context_length, tp_size * token_count, local_key_value, HEAD_SIZE),
            "tp",
            scatter_dimension=1,
            tiled=True,
        ),
        lax.psum_scatter(
            dv_total.reshape(context_length, tp_size * token_count, local_key_value, HEAD_SIZE),
            "tp",
            scatter_dimension=1,
            tiled=True,
        ),
    )
    dk_rows = dk_sum.reshape(context_length * token_count, local_key_value, HEAD_SIZE).astype(
        jnp.bfloat16
    )
    dv_rows = dv_sum.reshape(context_length * token_count, local_key_value, HEAD_SIZE).astype(
        jnp.bfloat16
    )
    dq_back, key_gradient_back, value_gradient_back = (
        lax.all_to_all(dq_rows, "ctx", split_axis=0, concat_axis=1, tiled=True),
        lax.all_to_all(dk_rows, "ctx", split_axis=0, concat_axis=1, tiled=True),
        lax.all_to_all(dv_rows, "ctx", split_axis=0, concat_axis=1, tiled=True),
    )
    return (
        dq_back.reshape(token_count, QUERY_HEADS * HEAD_SIZE),
        key_gradient_back.reshape(token_count, KEY_HEADS * HEAD_SIZE),
        value_gradient_back.reshape(token_count, KEY_HEADS * HEAD_SIZE),
    )


def solution(mesh):
    in_specs = (
        P(("ctx", "tp"), None),
        P(("ctx", "tp"), None),
        P(("ctx", "tp"), None),
        P(("ctx", "tp"), None),
        P(),
        P(),
    )
    out_specs = (P(("ctx", "tp"), None), P(("ctx", "tp"), None), P(("ctx", "tp"), None))
    return jax.shard_map(
        per_device, mesh=mesh, in_specs=in_specs, out_specs=out_specs, check_vma=False
    )
```

profile of v0, /device:TPU:0, one launch (start us, length us, event | category | flops | bytes accessed | tf_op | source)
XLA Modules:
  0.0 827.8 jit_solution(8880578688743592274)
XLA Ops:
  8.3 12.0 %all_to_all.105 = bf16[128,8,128]{0,2,1:T(8,128)(2,1)} all-to-all(bf16[128,8,128]{0,2,1:T(8,128)(2,1)S(1)} %bitcast.483), channel_id=1, replica_groups=mesh['ctx'=8,'tp'=16] {'ctx'}, dimensions={1} | all-to-all | bytes 524288 | tf_op jit(solution)/shard_map/all_to_all | solution.py:151
  21.5 10.6 %all_to_all.106 = bf16[128,8,128]{0,2,1:T(8,128)(2,1)} all-to-all(bf16[128,8,128]{0,2,1:T(8,128)(2,1)S(1)} %bitcast.484), channel_id=1, replica_groups=mesh['ctx'=8,'tp'=16] {'ctx'}, dimensions={1} | all-to-all | bytes 524288 | tf_op jit(solution)/shard_map/all_to_all | solution.py:158
  43.9 23.0 %all-to-all-done.3 = bf16[128,8,1024]{0,2,1:T(8,128)(2,1)S(1)} async-done(((bf16[128,8,1024]{0,2,1:T(8,128)(2,1)}), bf16[128,8,1024]{0,2,1:T(8,128)(2,1)S(1)}, u32[]{:S(2)}, u32[]{:S(2)}) %all-to-all-start.3) | async-done | bytes 2097184 | tf_op jit(solution)/shard_map/all_to_all | solution.py:144
  66.9 4.4 all-to-all-start.1
  78.6 19.8 %all-to-all-done.1 = bf16[128,8,1024]{0,2,1:T(8,128)(2,1)} async-done(((bf16[128,8,1024]{0,2,1:T(8,128)(2,1)}), bf16[128,8,1024]{0,2,1:T(8,128)(2,1)}, u32[]{:S(2)}, u32[]{:S(2)}) %all-to-all-start.1) | async-done | bytes 2097184 | tf_op jit(solution)/shard_map/all_to_all | solution.py:137
  102.7 4.3 copy.162
  108.6 6.5 copy.157
  115.0 4.3 gather_fusion
  119.4 16.8 %all-gather.5.cloned.1.call-done = bf16[8,2048,1,128]{1,3,0,2:T(8,128)(2,1)} async-done(((bf16[8,128,1,128]{1,3,0,2:T(8,128)(2,1)}), bf16[8,2048,1,128]{1,3,0,2:T(8,128)(2,1)}) %all-gather.5.cloned.1.call-update) | async-done | bytes 4194320 | tf_op jit(solution)/shard_map/all_gather | solution.py:173
  136.2 6.5 copy.164
  142.6 4.3 gather_fusion.1
  147.0 154.1 %while.45 = (s32[]{:T(128)}, f32[8,1,128,1,8,128]{2,5,4,3,1,0:T(8,128)}, f32[8,1,1024,1,128]{4,2,0,3,1:T(8,128)}, f32[8,1,1024,1,128]{4,2,0,3,1:T(8,128)}, bf16[...) while((s32[]{:T(128)}, ...), condition=%wide.region_4.5_spmd, body=%wide.region_0.4_spmd.sunk | while | flops 1368650752 | bytes 76865184 | solution.py:217
  301.1 4.3 broadcast.185.clone
  305.3 13.5 %scatter_fusion = f32[128,128,128]{2,1,0:T(8,128)} fusion(f32[128,128,128]{2,1,0:T(8,128)} %broadcast.185.clone, s32[64]{0:T(128)S(1)} %reshape.399, f32[64,128,128]{2,1,0:T(8,128)} %bitcast.467), kind=kCustom, calls=%fused_computation.2 | custom fusion | flops 1048576 | bytes 12583168 | tf_op jit(solution)/shard_map/scatter-add | solution.py:230
  318.9 4.3 broadcast.185.clone.1
  323.1 23.7 %scatter_fusion.1 = f32[128,128,128]{2,1,0:T(8,128)} fusion(f32[128,128,128]{2,1,0:T(8,128)} %broadcast.185.clone.1, s32[64]{0:T(128)S(1)} %reshape.399, f32[64,128,128]{2,1,0:T(8,128)} %bitcast.468), kind=kCustom, calls=%fused_computation.3 | custom fusion | flops 1048576 | bytes 12583168 | tf_op jit(solution)/shard_map/scatter-add | solution.py:240
  346.8 279.6 %conditional.1 = (f32[16384,1,128]{2,0,1:T(8,128)}, f32[16384,1,128]{2,0,1:T(8,128)}, f32[128,1,1024]{2,1,0:T(1,128)}) conditional(s32[]{:T(128)} %convert_element_type.56, (f32[16384,1,128]{2,0,1:T(8,128)}, f32[16384,1,128]{2,0,1:T(8,128)}) %tuple.127, (bf16[8,128,1,1024]{3,0,1,2:T(8,128)(2,1)}, bf16[8,128,1,1024]{3,0,1,2:T(8,128)(2,1)S(1)}, ...), branch_computations={%region_7.8_spmd, %region_8.16_spmd} | conditional | flops 3796508672 | bytes 291606656 | solution.py:266
  346.8 6.4 copy.180
  353.2 6.5 copy.181
  367.2 102.9 %while.43 = (s32[]{:T(128)}, f32[1,8,128]{2,1,0:T(8,128)S(1)}, f32[1,8,128]{2,1,0:T(8,128)S(1)}, f32[1,8,128]{2,1,0:T(8,128)S(1)}, bf16[8,2048,1,128]{3,1,2,0:T(...) while((s32[]{:T(128)}, f32[1,8,128]{2,1,0:T(8,128)S(1)}, ...), condition=%wide.region_13.13_spmd.clone, body=%wide.region_9.12_spmd.clone.sunk | while | flops 1092623360 | bytes 60368008 | solution.py:90
  367.2 5.5 bitcast_reduce_fusion.5
  372.7 5.4 fusion.151
  380.1 5.5 bitcast_reduce_fusion.5
  385.6 5.4 fusion.151
  392.9 5.5 bitcast_reduce_fusion.5
  398.5 5.4 fusion.151
  405.8 5.5 bitcast_reduce_fusion.5
  411.3 5.4 fusion.151
  418.7 5.5 bitcast_reduce_fusion.5
  424.2 5.4 fusion.151
  431.5 5.5 bitcast_reduce_fusion.5
  437.1 5.4 fusion.151
  444.4 5.5 bitcast_reduce_fusion.5
  449.9 5.4 fusion.151
  457.3 5.5 bitcast_reduce_fusion.5
  462.8 5.4 fusion.151
  470.2 137.9 %while.44 = (s32[]{:T(128)}, f32[128,1,8,128]{0,3,2,1:T(8,128)S(1)}, f32[8,2048,1,128]{3,1,2,0:T(8,128)}, f32[8,2048,1,128]{3,1,2,0:T(8,128)}, bf16[8,2048,1,128...) while((s32[]{:T(128)}, ...), condition=%wide.region_15.15_spmd.clone, body=%wide.region_14.14_spmd.clone.sunk | while | flops 2699689984 | bytes 127417048 | solution.py:118
  608.1 10.1 %add.62 = f32[16384,1,128]{2,0,1:T(8,128)} add(f32[16384,1,128]{2,0,1:T(8,128)} %get-tuple-element.178, f32[16384,1,128]{2,0,1:T(8,128)} %bitcast.27) | non-fusion elementwise | flops 2097152 | bytes 25165824 | tf_op jit(solution)/shard_map/cond/branch_1_fun/add | solution.py:257
  619.4 6.0 add.63
  627.0 5.3 copy.173
  636.0 7.0 convert_element_type.57
  643.6 12.8 %reduce.10 = bf16[1024,1024]{1,0:T(8,128)(2,1)S(1)} reduce(bf16[1024,1,1024]{2,1,0:T(2,128)(2,1)} %convert_element_type.57, bf16[]{:T(256)} %broadcast.260), dimensions={1}, to_apply=%convert_element_type.57.reduce_sub_computation | reduce | bytes 4194306 | tf_op jit(solution)/shard_map/convert_element_type | solution.py:275
  660.1 4.3 all-to-all-start.4
  664.4 44.5 %reduce-scatter.3.cloned.1.call-done = f32[8,128,1,128]{3,1,0,2:T(8,128)} async-done(((f32[8,2048,1,128]{3,1,0,2:T(8,128)}), f32[8,128,1,128]{3,1,0,2:T(8,128)}) %reduce-scatter.3.cloned.1.call-update) | async-done | bytes 524304 | tf_op jit(solution)/shard_map/reduce_scatter | solution.py:278
  711.6 4.3 all-to-all-start.5
  715.9 81.5 %reduce-scatter.5.cloned.1.call-done = f32[8,128,1,128]{3,1,0,2:T(8,128)} async-done(((f32[8,2048,1,128]{3,1,0,2:T(8,128)}), f32[8,128,1,128]{3,1,0,2:T(8,128)}) %reduce-scatter.5.cloned.1.call-update) | async-done | bytes 524304 | tf_op jit(solution)/shard_map/reduce_scatter | solution.py:284
  800.1 4.3 all-to-all-start.6
  804.4 4.4 reshape.459
  (347 shorter events, 368.9 us)
Async XLA Ops:
  7.2 101.4 %all-gather.3.cloned.1.call-start = ((), (), s32[]{:S(2)}) async-start(), calls=%async_computation.9 | async-start | bytes 4456448 | tf_op jit(solution)/shard_map/all_gather | solution.py:167
  20.4 115.8 %all-gather.5.cloned.1.call-start = ((), (), s32[]{:S(2)}) async-start(), calls=%async_computation.10 | async-start | bytes 4456448 | tf_op jit(solution)/shard_map/all_gather | solution.py:173
  36.2 30.7 %all-to-all-start.3 = ((bf16[128,8,1024]{0,2,1:T(8,128)(2,1)}), bf16[128,8,1024]{0,2,1:T(8,128)(2,1)S(1)}, u32[]{:S(2)}, u32[]{:S(2)}) async-start(bf16[128,8,1024]{0,2,1:T(8,128)(2,1)} %bitcast.465), calls=%async_computation.3 | async-start | bytes 4194304 | tf_op jit(solution)/shard_map/all_to_all | solution.py:144
  39.8 31.6 %copy-start.10 = (s32[128,8]{0,1:T(8,128)S(1)}, s32[128,8]{0,1:T(8,128)}, u32[]{:S(2)}) copy-start(s32[128,8]{0,1:T(8,128)} %param.20) | copy-start | bytes 12292
  39.8 31.9 %copy-start.11 = (s32[128,8]{0,1:T(8,128)S(1)}, s32[128,8]{0,1:T(8,128)}, u32[]{:S(2)}) copy-start(s32[128,8]{0,1:T(8,128)} %param.21) | copy-start | bytes 12292
  66.9 5.5 copy-start.8
  66.9 31.6 %all-to-all-start.1 = ((bf16[128,8,1024]{0,2,1:T(8,128)(2,1)}), bf16[128,8,1024]{0,2,1:T(8,128)(2,1)}, u32[]{:S(2)}, u32[]{:S(2)}) async-start(bf16[128,8,1024]{0,2,1:T(8,128)(2,1)} %bitcast.463), calls=%async_computation.1 | async-start | bytes 4194304 | tf_op jit(solution)/shard_map/all_to_all | solution.py:137
  71.3 637.7 %reduce-scatter.3.cloned.1.call-start = ((), (), s32[]{:S(2)}) async-start(), calls=%async_computation.11 | async-start | bytes 8912896 | tf_op jit(solution)/shard_map/reduce_scatter | solution.py:278
  75.8 26.9 %copy-start.6 = (bf16[128,8,1024]{2,1,0:T(8,128)(2,1)}, bf16[128,8,1024]{2,1,0:T(8,128)(2,1)S(1)}, u32[]{:S(2)}) copy-start(bf16[128,8,1024]{2,1,0:T(8,128)(2,1)S(1)} %copy.166) | copy-start | bytes 6291460
  102.7 4.3 copy-start.9
  153.3 3.9 copy-start.5
  172.6 3.9 copy-start.5
  191.9 3.9 copy-start.5
  211.2 3.9 copy-start.5
  230.4 3.9 copy-start.5
  249.7 3.9 copy-start.5
  268.9 3.9 copy-start.5
  288.1 3.9 copy-start.5
  323.1 23.7 %copy-start.7 = (bf16[128,8,1024]{2,1,0:T(8,128)(2,1)S(1)}, bf16[128,8,1024]{2,1,0:T(8,128)(2,1)}, u32[]{:S(2)}) copy-start(bf16[128,8,1024]{2,1,0:T(8,128)(2,1)} %copy-done.6) | copy-start | bytes 6291460
  372.7 5.9 copy-start.3
  385.6 5.9 copy-start.3
  398.5 5.9 copy-start.3
  411.3 5.9 copy-start.3
  424.2 5.9 copy-start.3
  437.1 5.9 copy-start.3
  449.9 5.9 copy-start.3
  462.8 5.9 copy-start.3
  472.9 3.2 copy-start
  480.4 4.8 copy-start.1
  490.1 3.2 copy-start
  497.6 4.8 copy-start.1
  507.4 3.2 copy-start
  514.8 4.8 copy-start.1
  524.6 3.2 copy-start
  532.0 4.8 copy-start.1
  549.3 4.8 copy-start.1
  559.0 3.2 copy-start
  566.5 4.8 copy-start.1
  576.3 3.2 copy-start
  583.7 4.8 copy-start.1
  593.5 3.2 copy-start
  600.9 4.8 copy-start.1
  608.0 10.1 %slice-start = ((s8[8388608]{0:T(1024)(128)(4,1)}), s8[4194304]{0:T(1024)(128)(4,1)S(1)}, s32[]{:S(2)}) async-start(s8[8388608]{0:T(1024)(128)(4,1)} %bitcast.459), calls=%async_computation.13 | async-start | bytes 8388608 | tf_op jit(solution)/shard_map/cond
  608.0 11.3 %slice-start.1 = ((s8[8388608]{0:T(1024)(128)(4,1)}), s8[4194304]{0:T(1024)(128)(4,1)S(1)}, s32[]{:S(2)}) async-start(s8[8388608]{0:T(1024)(128)(4,1)} %bitcast.459), calls=%async_computation.14 | async-start | bytes 8388608 | tf_op jit(solution)/shard_map/cond
  626.4 171.0 %reduce-scatter.5.cloned.1.call-start = ((), (), s32[]{:S(2)}) async-start(), calls=%async_computation.12 | async-start | bytes 8912896 | tf_op jit(solution)/shard_map/reduce_scatter | solution.py:284
  660.1 51.5 %all-to-all-start.4 = ((bf16[8,2,65536]{2,1,0:T(2,128)(2,1)}), bf16[8,2,65536]{2,1,0:T(2,128)(2,1)S(1)}, u32[]{:S(2)}, u32[]{:S(2)}) async-start(bf16[8,2,65536]{2,1,0:T(2,128)(2,1)} %reshape.458), calls=%async_computation.4 | async-start | bytes 4194304 | tf_op jit(solution)/shard_map/all_to_all | solution.py:298
  711.6 88.4 %all-to-all-start.5 = ((bf16[8,2,8192]{2,1,0:T(2,128)(2,1)}), bf16[8,2,8192]{2,1,0:T(2,128)(2,1)S(1)}, u32[]{:S(2)}, u32[]{:S(2)}) async-start(bf16[8,2,8192]{2,1,0:T(2,128)(2,1)} %reshape.460), calls=%async_computation.6 | async-start | bytes 524288 | tf_op jit(solution)/shard_map/all_to_all | solution.py:299
  800.1 19.5 %all-to-all-start.6 = ((bf16[8,2,8192]{2,1,0:T(2,128)(2,1)}), bf16[8,2,8192]{2,1,0:T(2,128)(2,1)S(1)}, u32[]{:S(2)}, u32[]{:S(2)}) async-start(bf16[8,2,8192]{2,1,0:T(2,128)(2,1)} %reshape.462), calls=%async_computation.8 | async-start | bytes 524288 | tf_op jit(solution)/shard_map/all_to_all | solution.py:300
  (17 other events, 34.5 us)
Sparse Core Ops, SparseCore 0:
  20.5 57.2 all-gather.2
  79.9 56.1 all-gather.4
  626.5 82.3 reduce-scatter.2
  712.2 85.1 reduce-scatter.4
where the time goes:
time: 843 us; the launch traced here: 828 us
  matrix products  297 us (35%)
  waiting for transfers between devices  186 us (22%)
  local copies, waits for them, and re-layouts  171 us (20%)
  other arithmetic  114 us (14%)
  blocking collectives  22.6 us (3%)
  starting transfers between devices  21 us (2%)
  between operations  14.4 us (2%)
    reduce_scatter x1, waiting for transfers between devices, per_device(): lax.psum_scatter(dv_total.reshape(context_length, tp_size * token_count,...  81.5 us
    dot_general x16, matrix products, stretch_scores(): jnp.einsum('qhgd,khd->hgqk', q_rows, key_part, preferred_element_type=jnp...  65.6 us
    dot_general x16, matrix products, stretch_scores(): jnp.einsum('qhgd,khd->hgqk', o_rows, value_part, preferred_element_type=j...  65.4 us
    reduce_scatter x1, waiting for transfers between devices, per_device(): lax.psum_scatter(dk_total.reshape(context_length, tp_size * token_count,...  44.5 us
    while x104, local copies, waits for them, and re-layouts  43.3 us
    dot_general x8, matrix products, sparse_turn(): jnp.einsum('pqhgd,pkhd->phgqk', o_part, value_part, preferred_element_typ...  31.4 us
    unnamed x28, local copies, waits for them, and re-layouts  29.5 us
    another operation x8, local copies, waits for them, and re-layouts  28.8 us
  transfers between devices with their start and end apart: 9, of which 5 were waited for; matrix products, arithmetic and copies ran while one was open for 11% of the time, Pallas kernels for 0%

commit v1 on v0

v1 whole, which is shorter than its diff:
```python
import functools
import math

import jax
import jax.numpy as jnp
from jax import lax
from jax.experimental import pallas as pl
from jax.experimental.pallas import tpu as pltpu
from jax.sharding import PartitionSpec as P

KEY_HEADS = 8
GROUP_SIZE = 8
HEAD_SIZE = 128
BLOCK = 128
NB = 8
GROUPS = 16
PIECE = 8
SENT = 5
FIRST_SENT = NB - SENT
BOTH = ("ctx", "tp")
SCALING = 1.0 / math.sqrt(HEAD_SIZE)
EXP_SCALE = SCALING * math.log2(math.e)
FAR = 1e30
F32 = jnp.float32
BF16 = jnp.bfloat16
VM = pltpu.VMEM


def dot(a, b, ca, cb):
    return lax.dot_general(a, b, (((ca,), (cb,)), ((), ())), preferred_element_type=F32)


def pack_body(k_ref, v_ref, out_ref):
    for h in range(KEY_HEADS):
        cols = pl.ds(h * HEAD_SIZE, HEAD_SIZE)
        out_ref[h, :, 0] = k_ref[:, cols].reshape(GROUPS, PIECE, HEAD_SIZE)
        out_ref[h, :, 1] = v_ref[:, cols].reshape(GROUPS, PIECE, HEAD_SIZE)


def pack_pieces(k, v):
    return pl.pallas_call(
        pack_body,
        out_shape=jax.ShapeDtypeStruct((KEY_HEADS, GROUPS, 2, PIECE, HEAD_SIZE), BF16),
        in_specs=[pl.BlockSpec(memory_space=VM)] * 2,
        out_specs=pl.BlockSpec(memory_space=VM),
        name="pack_pieces",
    )(k, v)


def gather_body(table_ref, held_ref, out_ref, *, rows):
    base = pl.program_id(0) * rows

    def one(d, carry):
        for s in range(SENT):
            block = table_ref[(base + d) * NB + FIRST_SENT + s]
            out_ref[d, s] = held_ref[block]
        return carry

    lax.fori_loop(0, rows, one, 0, unroll=4)


def gather_pieces(table, held, blocks):
    steps = 4
    rows = blocks // steps
    return pl.pallas_call(
        functools.partial(gather_body, rows=rows),
        out_shape=jax.ShapeDtypeStruct((blocks, SENT, 2, PIECE, HEAD_SIZE), BF16),
        grid_spec=pltpu.PrefetchScalarGridSpec(
            num_scalar_prefetch=1,
            grid=(steps,),
            in_specs=[pl.BlockSpec((blocks, 2, PIECE, HEAD_SIZE), lambda i, t: (0, 0, 0, 0))],
            out_specs=pl.BlockSpec(
                (rows, SENT, 2, PIECE, HEAD_SIZE), lambda i, t: (i, 0, 0, 0, 0)
            ),
        ),
        name="gather_pieces",
    )(table, held)


def scatter_body(table_ref, got_ref, dense_ref, out_ref, acc_ref, *, rows, blocks):
    step = pl.program_id(0)
    base = step * rows

    @pl.when(step == 0)
    def _():
        for kv in range(2):
            acc_ref[:, kv] = dense_ref[kv].reshape(blocks, PIECE, HEAD_SIZE)

    def one(d, carry):
        for s in range(SENT):
            block = table_ref[(base + d) * NB + FIRST_SENT + s]
            acc_ref[block] += got_ref[d, s].astype(F32)
        return carry

    lax.fori_loop(0, rows, one, 0, unroll=4)

    @pl.when(step == pl.num_programs(0) - 1)
    def _():
        out_ref[...] = acc_ref[...].astype(BF16)


def scatter_pieces(table, got, dense, blocks):
    steps = 4
    rows = blocks // steps
    return pl.pallas_call(
        functools.partial(scatter_body, rows=rows, blocks=blocks),
        out_shape=jax.ShapeDtypeStruct((blocks, 2, PIECE, HEAD_SIZE), BF16),
        grid_spec=pltpu.PrefetchScalarGridSpec(
            num_scalar_prefetch=1,
            grid=(steps,),
            in_specs=[
                pl.BlockSpec((rows, SENT, 2, PIECE, HEAD_SIZE), lambda i, t: (i, 0, 0, 0, 0)),
                pl.BlockSpec((2, blocks * PIECE, HEAD_SIZE), lambda i, t: (0, 0, 0)),
            ],
            out_specs=pl.BlockSpec((blocks, 2, PIECE, HEAD_SIZE), lambda i, t: (0, 0, 0, 0)),
            scratch_shapes=[VM((blocks, 2, PIECE, HEAD_SIZE), F32)],
        ),
        name="scatter_pieces",
    )(table, got, dense)


def two_heads(ref, p):
    first = ref[:, pl.ds(2 * p * HEAD_SIZE, HEAD_SIZE)]
    second = ref[:, pl.ds((2 * p + 1) * HEAD_SIZE, HEAD_SIZE)]
    return jnp.concatenate([first, second], axis=0)


def col_sum(x):
    return jnp.sum(x, axis=0, keepdims=True)


def sparse_body(
    meta_ref, valid_ref, q_ref, o_ref, k_ref, v_ref, kp_ref, vp_ref, kn_ref, vn_ref, g_ref,
    dq_ref, own_ref, prev_ref, next_ref, sent_ref,
    kc, vc, kt, st, dp, pb, ds, dk, dv,
):
    b = meta_ref[0]

    @pl.when(b == 0)
    def _():
        dq_ref[...] = jnp.zeros_like(dq_ref)
        own_ref[...] = jnp.zeros_like(own_ref)
        prev_ref[...] = jnp.zeros_like(prev_ref)
        next_ref[...] = jnp.zeros_like(next_ref)
        sent_ref[...] = jnp.zeros_like(sent_ref)

    @pl.when(b != 0)
    def _():
        for dst, parts, kv in ((kc, (kp_ref, k_ref, kn_ref), 0), (vc, (vp_ref, v_ref, vn_ref), 1)):
            for s, part in enumerate(parts):
                dst[s * BLOCK : (s + 1) * BLOCK] = part[...]
            for s in range(SENT):
                at = (FIRST_SENT + s) * BLOCK
                dst[at : at + BLOCK] = g_ref[0, :, s, kv].reshape(BLOCK, HEAD_SIZE)
        kt[...] = kc[...].T
        live = [valid_ref[b * NB + s] > 0 for s in range(NB)]
        for p in range(GROUP_SIZE // 2):
            w = p % 2
            qp = two_heads(q_ref, p)
            op = two_heads(o_ref, p)
            st[w] = dot(kc[...], qp, 1, 1)
            dp[w] = dot(vc[...], op, 1, 1)
            top = jnp.full((1, 2 * BLOCK), -FAR, F32)
            for s in range(NB):
                here = jnp.max(st[w, s * BLOCK : (s + 1) * BLOCK], axis=0, keepdims=True)
                top = jnp.maximum(top, jnp.where(live[s], here, -FAR))
            top = top * EXP_SCALE
            total = jnp.zeros((1, 2 * BLOCK), F32)
            cross = jnp.zeros((1, 2 * BLOCK), F32)
            for s in range(NB):
                rows = slice(s * BLOCK, (s + 1) * BLOCK)
                shift = jnp.where(live[s], top, FAR)
                raised = jnp.exp2(st[w, rows] * EXP_SCALE - shift)
                st[w, rows] = raised
                total = total + col_sum(raised)
                cross = cross + col_sum(raised * dp[w, rows])
            inverse = 1.0 / total
            delta = cross * inverse
            for s in range(NB):
                rows = slice(s * BLOCK, (s + 1) * BLOCK)
                weights = st[w, rows] * inverse
                pb[w, rows] = weights.astype(BF16)
                ds[w, rows] = (weights * (dp[w, rows] - delta)).astype(BF16)
            new_dv = dot(pb[w], op, 1, 0)
            new_dk = dot(ds[w], qp, 1, 0)
            dv[...] = new_dv if p == 0 else dv[...] + new_dv
            dk[...] = new_dk if p == 0 else dk[...] + new_dk
            dqt = dot(kt[...], ds[w], 1, 0) * SCALING
            for j in range(2):
                dq_ref[:, pl.ds((2 * p + j) * HEAD_SIZE, HEAD_SIZE)] = (
                    dqt[:, j * BLOCK : (j + 1) * BLOCK].T.astype(BF16)
                )
        for kv, acc, factor in ((0, dk, SCALING), (1, dv, 1.0)):
            prev_ref[kv] = (acc[0:BLOCK] * factor).astype(BF16)
            own_ref[kv] = acc[BLOCK : 2 * BLOCK] * factor
            next_ref[kv] = (acc[2 * BLOCK : 3 * BLOCK] * factor).astype(BF16)
            for s in range(SENT):
                at = (FIRST_SENT + s) * BLOCK
                sent_ref[0, :, s, kv] = (
                    (acc[at : at + BLOCK] * factor).astype(BF16).reshape(GROUPS, PIECE, HEAD_SIZE)
                )


def sparse_grads(meta, valid, q, o, k, v, kp, vp, kn, vn, got):
    wide = pl.BlockSpec((BLOCK, GROUP_SIZE * HEAD_SIZE), lambda h, m, t: (0, h))
    narrow = pl.BlockSpec((BLOCK, HEAD_SIZE), lambda h, m, t: (0, h))
    pair = pl.BlockSpec((2, BLOCK, HEAD_SIZE), lambda h, m, t: (0, 0, h))
    pieces = pl.BlockSpec(
        (1, GROUPS, SENT, 2, PIECE, HEAD_SIZE), lambda h, m, t: (h, 0, 0, 0, 0, 0)
    )
    keys = NB * BLOCK
    width = KEY_HEADS * HEAD_SIZE
    return pl.pallas_call(
        sparse_body,
        out_shape=(
            jax.ShapeDtypeStruct(q.shape, BF16),
            jax.ShapeDtypeStruct((2, BLOCK, width), F32),
            jax.ShapeDtypeStruct((2, BLOCK, width), BF16),
            jax.ShapeDtypeStruct((2, BLOCK, width), BF16),
            jax.ShapeDtypeStruct((KEY_HEADS, GROUPS, SENT, 2, PIECE, HEAD_SIZE), BF16),
        ),
        grid_spec=pltpu.PrefetchScalarGridSpec(
            num_scalar_prefetch=2,
            grid=(KEY_HEADS,),
            in_specs=[wide, wide] + [narrow] * 6 + [pieces],
            out_specs=[wide, pair, pair, pair, pieces],
            scratch_shapes=[
                VM((keys, HEAD_SIZE), BF16),
                VM((keys, HEAD_SIZE), BF16),
                VM((HEAD_SIZE, keys), BF16),
                VM((2, keys, 2 * BLOCK), F32),
                VM((2, keys, 2 * BLOCK), F32),
                VM((2, keys, 2 * BLOCK), BF16),
                VM((2, keys, 2 * BLOCK), BF16),
                VM((keys, HEAD_SIZE), F32),
                VM((keys, HEAD_SIZE), F32),
            ],
        ),
        name="sparse_grads",
    )(meta, valid, q, o, k, v, kp, vp, kn, vn, got)


def stats_body(q_ref, held_ref, out_ref, kc, vc):
    keys = kc.shape[0]
    kc[...] = held_ref[:, 0].reshape(keys, HEAD_SIZE)
    vc[...] = held_ref[:, 1].reshape(keys, HEAD_SIZE)
    for p in range(GROUP_SIZE // 2):
        cols = pl.ds(2 * p * BLOCK, 2 * BLOCK)
        scores = dot(kc[...], two_heads(q_ref.at[0], p), 1, 1)
        grads = dot(vc[...], two_heads(q_ref.at[1], p), 1, 1)
        top = jnp.max(scores, axis=0, keepdims=True) * EXP_SCALE
        raised = jnp.exp2(scores * EXP_SCALE - top)
        out_ref[0:1, cols] = top
        out_ref[1:2, cols] = col_sum(raised)
        out_ref[2:3, cols] = col_sum(raised * grads)
        out_ref[3:8, cols] = jnp.zeros((5, 2 * BLOCK), F32)


def dense_stats(qo, held):
    keys = held.shape[0] * PIECE
    return pl.pallas_call(
        stats_body,
        out_shape=jax.ShapeDtypeStruct((8, GROUP_SIZE * BLOCK), F32),
        in_specs=[pl.BlockSpec(memory_space=VM)] * 2,
        out_specs=pl.BlockSpec(memory_space=VM),
        scratch_shapes=[VM((keys, HEAD_SIZE), BF16), VM((keys, HEAD_SIZE), BF16)],
        name="dense_stats",
    )(qo, held)


def dense_body(q_ref, held_ref, stats_ref, dkv_ref, dq_ref, kc, vc, kt):
    keys = kc.shape[0]
    kc[...] = held_ref[:, 0].reshape(keys, HEAD_SIZE)
    vc[...] = held_ref[:, 1].reshape(keys, HEAD_SIZE)
    kt[...] = kc[...].T
    for p in range(GROUP_SIZE // 2):
        cols = pl.ds(2 * p * BLOCK, 2 * BLOCK)
        tops = stats_ref[:, 0, cols]
        top = jnp.max(tops, axis=0, keepdims=True)
        factors = jnp.exp2(tops - top)
        inverse = 1.0 / col_sum(stats_ref[:, 1, cols] * factors)
        delta = col_sum(stats_ref[:, 2, cols] * factors) * inverse
        qp = two_heads(q_ref.at[0], p)
        op = two_heads(q_ref.at[1], p)
        scores = dot(kc[...], qp, 1, 1)
        grads = dot(vc[...], op, 1, 1)
        weights = jnp.exp2(scores * EXP_SCALE - top) * inverse
        rounded = weights.astype(BF16)
        score_grad = (weights * (grads - delta)).astype(BF16)
        new_dk = dot(score_grad, qp, 1, 0) * SCALING
        new_dv = dot(rounded, op, 1, 0)
        dkv_ref[0] = new_dk if p == 0 else dkv_ref[0] + new_dk
        dkv_ref[1] = new_dv if p == 0 else dkv_ref[1] + new_dv
        dqt = dot(kt[...], score_grad, 1, 0) * SCALING
        for j in range(2):
            dq_ref[:, pl.ds((2 * p + j) * HEAD_SIZE, HEAD_SIZE)] = dqt[
                :, j * BLOCK : (j + 1) * BLOCK
            ].T


def dense_grads(qo, held, stats):
    keys = held.shape[0] * PIECE
    return pl.pallas_call(
        dense_body,
        out_shape=(
            jax.ShapeDtypeStruct((2, keys, HEAD_SIZE), F32),
            jax.ShapeDtypeStruct((BLOCK, GROUP_SIZE * HEAD_SIZE), F32),
        ),
        in_specs=[pl.BlockSpec(memory_space=VM)] * 3,
        out_specs=[pl.BlockSpec(memory_space=VM)] * 2,
        scratch_shapes=[
            VM((keys, HEAD_SIZE), BF16),
            VM((keys, HEAD_SIZE), BF16),
            VM((HEAD_SIZE, keys), BF16),
        ],
        name="dense_grads",
    )(qo, held, stats)


def combine_body(own_ref, prev_ref, next_ref, got_ref, dk_ref, dv_ref):
    for kv, out in ((0, dk_ref), (1, dv_ref)):
        for h in range(KEY_HEADS):
            cols = pl.ds(h * HEAD_SIZE, HEAD_SIZE)
            total = own_ref[kv, :, cols] + prev_ref[kv, :, cols].astype(F32)
            total = total + next_ref[kv, :, cols].astype(F32)
            total = total + got_ref[h, :, kv].reshape(BLOCK, HEAD_SIZE).astype(F32)
            out[:, cols] = total.astype(BF16)


def combine(own, from_prev, from_next, got):
    width = KEY_HEADS * HEAD_SIZE
    return pl.pallas_call(
        combine_body,
        out_shape=(jax.ShapeDtypeStruct((BLOCK, width), BF16),) * 2,
        in_specs=[pl.BlockSpec(memory_space=VM)] * 4,
        out_specs=[pl.BlockSpec(memory_space=VM)] * 2,
        name="combine",
    )(own, from_prev, from_next, got)


def spread_body(meta_ref, q_ref, o_ref, *rest):
    outs, sems = rest[:-1], rest[-1]

    @pl.when(meta_ref[0] == 0)
    def _():
        copies = []
        for h, out in enumerate(outs):
            cols = pl.ds(h * GROUP_SIZE * HEAD_SIZE, GROUP_SIZE * HEAD_SIZE)
            for j, ref in enumerate((q_ref, o_ref)):
                copies.append(pltpu.make_async_copy(ref.at[:, cols], out.at[j], sems.at[h, j]))
        for copy in copies:
            copy.start()
        for copy in copies:
            copy.wait()


def spread_heads(meta, q, o):
    hbm = pl.BlockSpec(memory_space=pl.ANY)
    return pl.pallas_call(
        spread_body,
        out_shape=(jax.ShapeDtypeStruct((2, BLOCK, GROUP_SIZE * HEAD_SIZE), BF16),) * KEY_HEADS,
        in_specs=[pl.BlockSpec(memory_space=pltpu.SMEM), hbm, hbm],
        out_specs=[hbm] * KEY_HEADS,
        scratch_shapes=[pltpu.SemaphoreType.DMA((KEY_HEADS, 2))],
        name="spread_heads",
    )(meta, q, o)


def first_body(meta_ref, dq_ref, *rest):
    parts, out, sems = rest[:KEY_HEADS], rest[KEY_HEADS], rest[KEY_HEADS + 1]

    @pl.when(meta_ref[0] == 0)
    def _():
        copies = []
        for h, part in enumerate(parts):
            cols = pl.ds(h * GROUP_SIZE * HEAD_SIZE, GROUP_SIZE * HEAD_SIZE)
            copies.append(pltpu.make_async_copy(part, out.at[:, cols], sems.at[h]))
        for copy in copies:
            copy.start()
        for copy in copies:
            copy.wait()


def put_first(meta, dq, parts):
    hbm = pl.BlockSpec(memory_space=pl.ANY)
    return pl.pallas_call(
        first_body,
        out_shape=jax.ShapeDtypeStruct(dq.shape, dq.dtype),
        in_specs=[pl.BlockSpec(memory_space=pltpu.SMEM)] + [hbm] * (KEY_HEADS + 1),
        out_specs=hbm,
        input_output_aliases={1: 0},
        scratch_shapes=[pltpu.SemaphoreType.DMA((KEY_HEADS,))],
        name="put_first",
    )(meta, dq, *parts)


def per_device(queries, key_tensor, value_tensor, output_gradient, key_blocks, slot_valid):
    tp_size = lax.axis_size("tp")
    blocks = lax.axis_size("ctx") * tp_size
    c_index = lax.axis_index("ctx")
    t_index = lax.axis_index("tp")
    b_index = c_index * tp_size + t_index
    meta = b_index.astype(jnp.int32).reshape(1)
    table = key_blocks.reshape(-1)
    valid = slot_valid.reshape(-1)
    up = [(i, (i + 1) % blocks) for i in range(blocks)]
    down = [(i, (i - 1) % blocks) for i in range(blocks)]

    def swap(x):
        return lax.all_to_all(x, BOTH, split_axis=0, concat_axis=0, tiled=True)

    pieces = pack_pieces(key_tensor, value_tensor)
    held = swap(pieces.reshape(blocks, 2, PIECE, HEAD_SIZE))
    kp, vp = lax.ppermute(key_tensor, BOTH, up), lax.ppermute(value_tensor, BOTH, up)
    kn, vn = lax.ppermute(key_tensor, BOTH, down), lax.ppermute(value_tensor, BOTH, down)
    listed = gather_pieces(table, held, blocks)
    got = swap(listed).reshape(KEY_HEADS, GROUPS, SENT, 2, PIECE, HEAD_SIZE)

    slices = spread_heads(meta, queries, output_gradient)
    qo = jnp.where(b_index == 0, slices[0], jnp.zeros_like(slices[0]))
    for h in range(1, KEY_HEADS):
        qo = qo + lax.ppermute(slices[h], BOTH, [(0, h * tp_size)])
    qo = lax.psum(qo, "tp")

    dq, own, to_prev, to_next, sent = sparse_grads(
        meta, valid, queries, output_gradient, key_tensor, value_tensor, kp, vp, kn, vn, got
    )
    back = swap(sent.reshape(blocks, SENT, 2, PIECE, HEAD_SIZE))
    from_next = lax.ppermute(to_prev, BOTH, down)
    from_prev = lax.ppermute(to_next, BOTH, up)

    stats = dense_stats(qo, held)
    stats = lax.all_gather(stats, "tp", axis=0)
    dense, dq_part = dense_grads(qo, held, stats)
    dq_first = lax.psum(dq_part, "tp").astype(BF16)
    parts = [dq_first] + [
        lax.ppermute(dq_first, BOTH, [(h * tp_size, 0)]) for h in range(1, KEY_HEADS)
    ]
    d_q = put_first(meta, dq, parts)

    summed = scatter_pieces(table, back, dense, blocks)
    home = swap(summed).reshape(KEY_HEADS, GROUPS, 2, PIECE, HEAD_SIZE)
    d_k, d_v = combine(own, from_prev, from_next, home)
    return d_q, d_k, d_v


def solution(mesh):
    spec = P(BOTH, None)
    return jax.shard_map(
        per_device,
        mesh=mesh,
        in_specs=(spec, spec, spec, spec, P(), P()),
        out_specs=(spec, spec, spec),
        check_vma=False,
    )
```

time: 843 us -> 612 us (0.73); the launches traced: 828 us -> 611 us
  matrix products: 297 us -> 0 us
  Pallas kernels: 0 us -> 227 us
  local copies, waits for them, and re-layouts: 171 us -> 8.52 us
  other arithmetic: 114 us -> 3.01 us
  blocking collectives: 22.6 us -> 103 us
  starting transfers between devices: 21 us -> 94.9 us
  waiting for transfers between devices: 186 us -> 160 us
    dot_general x96 -> x0, matrix products: 297 us -> none  [the longest x16 65.6 us: stretch_scores(): jnp.einsum('qhgd,khd->hgqk', q_rows, key_part, preferred_element_type=jnp...]
    pallas_call x0 -> x9, Pallas kernels: none -> 227 us  [the longest x1 128 us: spread_heads(): pl.pallas_call(spread_body, out_shape=(jax.ShapeDtypeStruct((2, BLOCK, GR...]
    reduce_scatter x2 -> x0, waiting for transfers between devices: 126 us -> none  [the longest x1 81.5 us: per_device(): lax.psum_scatter(dv_total.reshape(context_length, tp_size * token_count,...]
    psum x0 -> x1, waiting for transfers between devices: none -> 82.5 us  [per_device(): qo = lax.psum(qo, 'tp')]
    psum x0 -> x1, blocking collectives: none -> 78.1 us  [per_device(): dq_first = lax.psum(dq_part, 'tp').astype(BF16)]
    ppermute x0 -> x20, waiting for transfers between devices: none -> 65.4 us  [the longest x1 31.2 us: per_device(): lax.ppermute(key_tensor, BOTH, up)]
    while x105 -> x0, local copies, waits for them, and re-layouts: 48.6 us -> none
    scatter-add x3 -> x0, other arithmetic: 39.6 us -> none  [the longest x1 23.7 us: per_device(): dv_total = jnp.zeros((blocks_total, BLOCK_TOKENS, local_key_value, HEAD_S...]
  transfers between devices with their start and end apart: 9 -> 25, of which waited for: 5 -> 9; matrix products, arithmetic and copies ran while one was open for 11% -> 1% of each run, Pallas kernels for 0% -> 34%
where the time goes in v1:
time: 612 us; the launch traced here: 611 us
  Pallas kernels  227 us (37%)
  waiting for transfers between devices  160 us (26%)
  blocking collectives  103 us (17%)
  starting transfers between devices  94.9 us (16%)
  between operations  14.3 us (2%)
  local copies, waits for them, and re-layouts  8.52 us (1%)
    pallas_call x1, Pallas kernels, spread_heads(): pl.pallas_call(spread_body, out_shape=(jax.ShapeDtypeStruct((2, BLOCK, GR...  128 us
    psum x1, waiting for transfers between devices, per_device(): qo = lax.psum(qo, 'tp')  82.5 us
    psum x1, blocking collectives, per_device(): dq_first = lax.psum(dq_part, 'tp').astype(BF16)  78.1 us
    pallas_call x1, Pallas kernels, put_first(): pl.pallas_call(first_body, out_shape=jax.ShapeDtypeStruct(dq.shape, dq.dt...  64.7 us
    all_to_all x4, starting transfers between devices, swap(): return lax.all_to_all(x, BOTH, split_axis=0, concat_axis=0, tiled=True)  56 us
    ppermute x1, waiting for transfers between devices, per_device(): lax.ppermute(key_tensor, BOTH, up)  31.2 us
    all_gather x1, blocking collectives, per_device(): stats = lax.all_gather(stats, 'tp', axis=0)  25.4 us
    ppermute x7, waiting for transfers between devices, per_device(): qo = qo + lax.ppermute(slices[h], BOTH, [(0, h * tp_size)])  14.7 us
  transfers between devices with their start and end apart: 25, of which 9 were waited for; matrix products, arithmetic and copies ran while one was open for 1% of the time, Pallas kernels for 34%

profile of v1, /device:TPU:0, one launch (start us, length us, event | category | flops | bytes accessed | tf_op | source)
XLA Modules:
  0.0 610.9 jit_solution(9306434536831200943)
XLA Ops:
  7.2 1.9 pack_pieces.1
  9.1 11.2 %all-to-all-start = ((bf16[128,2,8,128]{3,2,1,0:T(8,128)(2,1)}), bf16[128,2,8,128]{3,2,1,0:T(8,128)(2,1)S(1)}, u32[]{:S(2)}, u32[]{:S(2)}) async-start(bf16[128,2,8,128]{3,2,1,0:T(8,128)(2,1)} %bitcast.10), calls=%async_computation | async-start | bytes 1048576 | tf_op jit(solution)/shard_map/all_to_all | solution.py:410
  20.3 0.8 copy.11
  21.7 12.1 %all-to-all-done.held_ref = bf16[128,2,8,128]{3,2,1,0:T(8,128)(2,1)S(1)} async-done(((bf16[128,2,8,128]{3,2,1,0:T(8,128)(2,1)}), bf16[128,2,8,128]{3,2,1,0:T(8,128)(2,1)S(1)}, u32[]{:S(2)}, u32[]{:S(2)}) %all-to-all-start) | async-done | bytes 524320 | tf_op jit(solution)/shard_map/all_to_all | solution.py:410
  33.8 0.8 copy-done.2
  34.7 4.2 gather_pieces.1
  38.9 4.8 all-to-all-start.1
  43.7 0.9 collective-permute-start
  44.6 1.5 collective-permute-start.1
  46.1 5.7 collective-permute-start.2
  53.2 31.2 %collective-permute-done.kp_ref = bf16[128,1024]{1,0:T(8,128)(2,1)S(1)} collective-permute-done((bf16[128,1024]{1,0:T(8,128)(2,1)S(1)}, bf16[128,1024]{1,0:T(8,128)(2,1)S(1)}, u32[]{:S(2)}, u32[]{:S(2)}) %collective-permute-start) | collective-permute-done | bytes 262176 | tf_op jit(solution)/shard_map/ppermute | solution.py:414
  84.5 5.7 collective-permute-done.1.vp_ref
  90.2 1.5 copy-done.1
  91.7 9.3 %sparse_grads.1 = (bf16[128,8192]{1,0:T(8,128)(2,1)}, f32[2,128,1024]{2,1,0:T(8,128)}, bf16[2,128,1024]{2,1,0:T(8,128)(2,1)}, bf16[2,128,1024]{2,1,0:T(8,128)(2,1)}, bf16[8,16,5,2,8,128]{5,4,3,2,1,0:T(8,128)(2,1)}) custom-call(s32[1]{0:T(128)} %bitcast.meta_ref, s32[1024]{0:T(1024)} %reshape.28.valid_ref, bf16[128,8192]{1,0:T(8,128)(2,1)} %q_ref.3, ...), custom_call_target="tpu_custom_call" | custom-call | tf_op jit(solution)/shard_map/sparse_grads/pallas_call | solution.py:213
  101.0 34.5 %all-to-all-start.2 = ((bf16[128,5,2,8,128]{4,3,2,1,0:T(8,128)(2,1)}), bf16[128,5,2,8,128]{4,3,2,1,0:T(8,128)(2,1)S(1)}, u32[]{:S(2)}, u32[]{:S(2)}) async-start(bf16[128,5,2,8,128]{4,3,2,1,0:T(8,128)(2,1)} %bitcast.7), calls=%async_computation.2 | async-start | bytes 5242880 | tf_op jit(solution)/shard_map/all_to_all | solution.py:410
  135.6 128.3 %spread_heads.1 = (bf16[2,128,1024]{2,1,0:T(8,128)(2,1)}, bf16[2,128,1024]{2,1,0:T(8,128)(2,1)}, bf16[2,128,1024]{2,1,0:T(8,128)(2,1)}, bf16[2,128,1024]{2,1,0:T...) custom-call(s32[1]{0:T(128)} %bitcast.meta_ref, ...), custom_call_target="tpu_custom_call" | custom-call | tf_op jit(solution)/shard_map/spread_heads/pallas_call | solution.py:359
  263.9 1.3 collective-permute-start.10
  265.2 2.1 collective-permute-start.4
  267.4 2.1 collective-permute-start.5
  269.4 2.1 collective-permute-start.6
  271.5 2.1 collective-permute-start.7
  273.6 2.1 collective-permute-start.8
  275.7 2.1 collective-permute-start.9
  277.8 3.5 collective-permute-done.6
  281.3 5.6 collective-permute-done.7
  286.9 5.6 collective-permute-done.8
  292.5 3.0 add_add_fusion
  295.5 82.5 %all-reduce.3.cloned.1.call-done.q_ref = bf16[2,128,1024]{2,1,0:T(8,128)(2,1)} async-done(((bf16[2,128,1024]{2,1,0:T(8,128)(2,1)}), bf16[2,128,1024]{2,1,0:T(8,128)(2,1)}) %all-reduce.3.cloned.1.call-update) | async-done | bytes 524304 | tf_op jit(solution)/shard_map/psum | solution.py:423
  378.0 4.0 dense_stats.1
  382.1 25.4 %all-gather = f32[128,1024]{1,0:T(8,128)} all-gather(f32[8,1024]{1,0:T(8,128)} %dense_stats.1), channel_id=2, replica_groups=mesh['ctx'=8,'tp'=16] {'tp'}, dimensions={0}, use_global_device_ids=true | all-gather | bytes 557056 | tf_op jit(solution)/shard_map/all_gather | solution.py:433
  407.4 5.3 dense_grads.1
  412.7 78.1 %all-reduce.4.rest_0_ = bf16[128,1024]{1,0:T(8,128)(2,1)S(1)} all-reduce(f32[128,1024]{1,0:T(8,128)} %get-tuple-element.29), channel_id=1, replica_groups=mesh['ctx'=8,'tp'=16] {'tp'}, use_global_device_ids=true, to_apply=%region_1.2 | all-reduce | flops 131072 | bytes 786432 | tf_op jit(solution)/shard_map/psum | solution.py:435
  490.9 1.3 collective-permute-start.11
  492.2 1.3 collective-permute-start.12
  493.5 1.3 collective-permute-start.13
  494.8 1.3 collective-permute-start.14
  496.9 7.2 %collective-permute-start.19 = (bf16[2,128,1024]{2,1,0:T(8,128)(2,1)}, bf16[2,128,1024]{2,1,0:T(8,128)(2,1)}, u32[]{:S(2)}, u32[]{:S(2)}) collective-permute-start(bf16[2,128,1024]{2,1,0:T(8,128)(2,1)} %get-tuple-element.32), channel_id=1, source_target_pairs={{0,127},{1,0},{2,1},{3,2},{4,3},{5,4},{6,5},{7,6},{8,7},{9,8},{10,... | collective-permute-start | bytes 1572872 | tf_op jit(solution)/shard_map/ppermute | solution.py:429
  504.0 1.5 copy-done
  505.5 6.3 %scatter_pieces.1 = bf16[128,2,8,128]{3,2,1,0:T(8,128)(2,1)} custom-call(s32[1024]{0:T(1024)} %reshape.29.table_ref, bf16[128,5,2,8,128]{4,3,2,1,0:T(8,128)(2,1)} %copy-done, f32[2,1024,128]{2,1,0:T(8,128)} %get-tuple-element.34.dense_ref), custom_call_target="tpu_custom_call" | custom-call | tf_op jit(solution)/shard_map/scatter_pieces/pallas_call | solution.py:105
  511.8 5.5 all-to-all-start.3
  517.3 1.3 collective-permute-start.15
  518.7 1.3 collective-permute-start.16
  520.0 1.3 collective-permute-start.17
  521.3 8.1 %collective-permute-done.15.rest_5_ = bf16[128,1024]{1,0:T(8,128)(2,1)S(1)} collective-permute-done((bf16[128,1024]{1,0:T(8,128)(2,1)S(1)}, bf16[128,1024]{1,0:T(8,128)(2,1)S(1)}, u32[]{:S(2)}, u32[]{:S(2)}) %collective-permute-start.15) | collective-permute-done | bytes 262176 | tf_op jit(solution)/shard_map/ppermute | solution.py:437
  529.4 5.5 collective-permute-done.16.rest_6_
  535.7 64.7 %put_first.1 = bf16[128,8192]{1,0:T(8,128)(2,1)} custom-call(s32[1]{0:T(128)} %bitcast.meta_ref, bf16[128,8192]{1,0:T(8,128)(2,1)} %get-tuple-element.20.dq_ref, bf16[128,1024]{1,0:T(8,128)(2,1)} %copy-done.4, bf16[128,1024]{1,0:T(8,128)(2,1)} %copy-done.8, bf16[128,1024]{1,0:T(8,128)(2,1)} %collective-permute-done.12.rest_2_, ...), custom_call_target="tpu_custom_call", output_to_operand_aliasing={{}: (1, {})} | custom-call | tf_op jit(solution)/shard_map/put_first/pallas_call | solution.py:386
  600.5 0.8 copy-done.7
  601.4 2.6 combine.1
  (47 shorter events, 4.0 us)
Async XLA Ops:
  9.1 24.8 %all-to-all-start = ((bf16[128,2,8,128]{3,2,1,0:T(8,128)(2,1)}), bf16[128,2,8,128]{3,2,1,0:T(8,128)(2,1)S(1)}, u32[]{:S(2)}, u32[]{:S(2)}) async-start(bf16[128,2,8,128]{3,2,1,0:T(8,128)(2,1)} %bitcast.10), calls=%async_computation | async-start | bytes 1048576 | tf_op jit(solution)/shard_map/all_to_all | solution.py:410
  33.8 0.8 copy-start.2
  38.9 4.8 copy-start.5
  38.9 5.7 copy-start.6
  38.9 13.5 %copy-start.13 = (s32[128,8]{0,1:T(8,128)S(1)}, s32[128,8]{0,1:T(8,128)}, u32[]{:S(2)}) copy-start(s32[128,8]{0,1:T(8,128)} %param.11) | copy-start | bytes 12292
  38.9 51.3 %all-to-all-start.1 = ((bf16[128,5,2,8,128]{4,3,2,1,0:T(8,128)(2,1)}), bf16[128,5,2,8,128]{4,3,2,1,0:T(8,128)(2,1)S(1)}, u32[]{:S(2)}, u32[]{:S(2)}) async-start(bf16[128,5,2,8,128]{4,3,2,1,0:T(8,128)(2,1)} %gather_pieces.1), calls=%async_computation.1 | async-start | bytes 5242880 | tf_op jit(solution)/shard_map/all_to_all | solution.py:410
  43.7 40.8 %collective-permute-start = (bf16[128,1024]{1,0:T(8,128)(2,1)S(1)}, bf16[128,1024]{1,0:T(8,128)(2,1)S(1)}, u32[]{:S(2)}, u32[]{:S(2)}) collective-permute-start(bf16[128,1024]{1,0:T(8,128)(2,1)S(1)} %copy-done.5), channel_id=1, source_target_pairs={{0,1},{1,2},{2,3},{3,4},{4,5},{5,6},{6,7},{7,8},{8,9},{9,10},{10,1... | collective-permute-start | bytes 786440 | tf_op jit(solution)/shard_map/ppermute | solution.py:414
  44.6 45.6 %collective-permute-start.1 = (bf16[128,1024]{1,0:T(8,128)(2,1)S(1)}, bf16[128,1024]{1,0:T(8,128)(2,1)}, u32[]{:S(2)}, u32[]{:S(2)}) collective-permute-start(bf16[128,1024]{1,0:T(8,128)(2,1)S(1)} %copy-done.6), channel_id=1, source_target_pairs={{0,1},{1,2},{2,3},{3,4},{4,5},{5,6},{6,7},{7,8},{8,9},{9,10},{10,1... | collective-permute-start | bytes 786440 | tf_op jit(solution)/shard_map/ppermute | solution.py:414
  46.1 44.1 %collective-permute-start.2 = (bf16[128,1024]{1,0:T(8,128)(2,1)S(1)}, bf16[128,1024]{1,0:T(8,128)(2,1)}, u32[]{:S(2)}, u32[]{:S(2)}) collective-permute-start(bf16[128,1024]{1,0:T(8,128)(2,1)S(1)} %copy-done.5), channel_id=1, source_target_pairs={{0,127},{1,0},{2,1},{3,2},{4,3},{5,4},{6,5},{7,6},{8,7},{9,8},{10,... | collective-permute-start | bytes 786440 | tf_op jit(solution)/shard_map/ppermute | solution.py:415
  51.8 38.4 %collective-permute-start.3 = (bf16[128,1024]{1,0:T(8,128)(2,1)S(1)}, bf16[128,1024]{1,0:T(8,128)(2,1)}, u32[]{:S(2)}, u32[]{:S(2)}) collective-permute-start(bf16[128,1024]{1,0:T(8,128)(2,1)S(1)} %copy-done.6), channel_id=1, source_target_pairs={{0,127},{1,0},{2,1},{3,2},{4,3},{5,4},{6,5},{7,6},{8,7},{9,8},{10,... | collective-permute-start | bytes 786440 | tf_op jit(solution)/shard_map/ppermute | solution.py:415
  84.5 5.7 copy-start.9
  90.2 1.5 copy-start.1
  101.0 403.0 %all-to-all-start.2 = ((bf16[128,5,2,8,128]{4,3,2,1,0:T(8,128)(2,1)}), bf16[128,5,2,8,128]{4,3,2,1,0:T(8,128)(2,1)S(1)}, u32[]{:S(2)}, u32[]{:S(2)}) async-start(bf16[128,5,2,8,128]{4,3,2,1,0:T(8,128)(2,1)} %bitcast.7), calls=%async_computation.2 | async-start | bytes 5242880 | tf_op jit(solution)/shard_map/all_to_all | solution.py:410
  135.5 242.5 %all-reduce.3.cloned.1.call-start = ((), (), s32[]{:S(2)}) async-start(), calls=%async_computation.4 | async-start | bytes 1048576 | tf_op jit(solution)/shard_map/psum | solution.py:423
  263.9 9.7 %collective-permute-start.10 = (bf16[2,128,1024]{2,1,0:T(8,128)(2,1)}, bf16[2,128,1024]{2,1,0:T(8,128)(2,1)S(1)}, u32[]{:S(2)}, u32[]{:S(2)}) collective-permute-start(bf16[2,128,1024]{2,1,0:T(8,128)(2,1)} %get-tuple-element.28), channel_id=1, source_target_pairs={{0,112}} | collective-permute-start | bytes 1572872 | tf_op jit(solution)/shard_map/ppermute | solution.py:422
  265.2 10.5 %collective-permute-start.4 = (bf16[2,128,1024]{2,1,0:T(8,128)(2,1)}, bf16[2,128,1024]{2,1,0:T(8,128)(2,1)}, u32[]{:S(2)}, u32[]{:S(2)}) collective-permute-start(bf16[2,128,1024]{2,1,0:T(8,128)(2,1)} %get-tuple-element.22), channel_id=1, source_target_pairs={{0,16}} | collective-permute-start | bytes 1572872 | tf_op jit(solution)/shard_map/ppermute | solution.py:422
  267.4 10.4 %collective-permute-start.5 = (bf16[2,128,1024]{2,1,0:T(8,128)(2,1)}, bf16[2,128,1024]{2,1,0:T(8,128)(2,1)}, u32[]{:S(2)}, u32[]{:S(2)}) collective-permute-start(bf16[2,128,1024]{2,1,0:T(8,128)(2,1)} %get-tuple-element.23), channel_id=1, source_target_pairs={{0,32}} | collective-permute-start | bytes 1572872 | tf_op jit(solution)/shard_map/ppermute | solution.py:422
  269.4 11.8 %collective-permute-start.6 = (bf16[2,128,1024]{2,1,0:T(8,128)(2,1)}, bf16[2,128,1024]{2,1,0:T(8,128)(2,1)}, u32[]{:S(2)}, u32[]{:S(2)}) collective-permute-start(bf16[2,128,1024]{2,1,0:T(8,128)(2,1)} %get-tuple-element.24), channel_id=1, source_target_pairs={{0,48}} | collective-permute-start | bytes 1572872 | tf_op jit(solution)/shard_map/ppermute | solution.py:422
  271.5 15.3 %collective-permute-start.7 = (bf16[2,128,1024]{2,1,0:T(8,128)(2,1)}, bf16[2,128,1024]{2,1,0:T(8,128)(2,1)}, u32[]{:S(2)}, u32[]{:S(2)}) collective-permute-start(bf16[2,128,1024]{2,1,0:T(8,128)(2,1)} %get-tuple-element.25), channel_id=1, source_target_pairs={{0,64}} | collective-permute-start | bytes 1572872 | tf_op jit(solution)/shard_map/ppermute | solution.py:422
  273.6 18.9 %collective-permute-start.8 = (bf16[2,128,1024]{2,1,0:T(8,128)(2,1)}, bf16[2,128,1024]{2,1,0:T(8,128)(2,1)}, u32[]{:S(2)}, u32[]{:S(2)}) collective-permute-start(bf16[2,128,1024]{2,1,0:T(8,128)(2,1)} %get-tuple-element.26), channel_id=1, source_target_pairs={{0,80}} | collective-permute-start | bytes 1572872 | tf_op jit(solution)/shard_map/ppermute | solution.py:422
  275.7 16.8 %collective-permute-start.9 = (bf16[2,128,1024]{2,1,0:T(8,128)(2,1)}, bf16[2,128,1024]{2,1,0:T(8,128)(2,1)}, u32[]{:S(2)}, u32[]{:S(2)}) collective-permute-start(bf16[2,128,1024]{2,1,0:T(8,128)(2,1)} %get-tuple-element.27), channel_id=1, source_target_pairs={{0,96}} | collective-permute-start | bytes 1572872 | tf_op jit(solution)/shard_map/ppermute | solution.py:422
  490.9 44.1 %copy-start.4 = (bf16[128,1024]{1,0:T(8,128)(2,1)}, bf16[128,1024]{1,0:T(8,128)(2,1)S(1)}, u32[]{:S(2)}) copy-start(bf16[128,1024]{1,0:T(8,128)(2,1)S(1)} %all-reduce.4.rest_0_) | copy-start | bytes 786436
  490.9 5.3 collective-permute-start.11
  492.2 25.2 %collective-permute-start.12 = (bf16[128,1024]{1,0:T(8,128)(2,1)S(1)}, bf16[128,1024]{1,0:T(8,128)(2,1)}, u32[]{:S(2)}, u32[]{:S(2)}) collective-permute-start(bf16[128,1024]{1,0:T(8,128)(2,1)S(1)} %all-reduce.4.rest_0_), channel_id=1, source_target_pairs={{32,0}} | collective-permute-start | bytes 786440 | tf_op jit(solution)/shard_map/ppermute | solution.py:437
  493.5 25.2 %collective-permute-start.13 = (bf16[128,1024]{1,0:T(8,128)(2,1)S(1)}, bf16[128,1024]{1,0:T(8,128)(2,1)}, u32[]{:S(2)}, u32[]{:S(2)}) collective-permute-start(bf16[128,1024]{1,0:T(8,128)(2,1)S(1)} %all-reduce.4.rest_0_), channel_id=1, source_target_pairs={{48,0}} | collective-permute-start | bytes 786440 | tf_op jit(solution)/shard_map/ppermute | solution.py:437
  494.8 25.2 %collective-permute-start.14 = (bf16[128,1024]{1,0:T(8,128)(2,1)S(1)}, bf16[128,1024]{1,0:T(8,128)(2,1)}, u32[]{:S(2)}, u32[]{:S(2)}) collective-permute-start(bf16[128,1024]{1,0:T(8,128)(2,1)S(1)} %all-reduce.4.rest_0_), channel_id=1, source_target_pairs={{64,0}} | collective-permute-start | bytes 786440 | tf_op jit(solution)/shard_map/ppermute | solution.py:437
  496.1 104.3 %collective-permute-start.18 = (bf16[2,128,1024]{2,1,0:T(8,128)(2,1)}, bf16[2,128,1024]{2,1,0:T(8,128)(2,1)S(1)}, u32[]{:S(2)}, u32[]{:S(2)}) collective-permute-start(bf16[2,128,1024]{2,1,0:T(8,128)(2,1)} %get-tuple-element.31), channel_id=1, source_target_pairs={{0,1},{1,2},{2,3},{3,4},{4,5},{5,6},{6,7},{7,8},{8,9},{9,10},{10,1... | collective-permute-start | bytes 1572872 | tf_op jit(solution)/shard_map/ppermute | solution.py:430
  496.2 0.7 copy-start.8
  496.9 103.6 %collective-permute-start.19 = (bf16[2,128,1024]{2,1,0:T(8,128)(2,1)}, bf16[2,128,1024]{2,1,0:T(8,128)(2,1)}, u32[]{:S(2)}, u32[]{:S(2)}) collective-permute-start(bf16[2,128,1024]{2,1,0:T(8,128)(2,1)} %get-tuple-element.32), channel_id=1, source_target_pairs={{0,127},{1,0},{2,1},{3,2},{4,3},{5,4},{6,5},{7,6},{8,7},{9,8},{10,... | collective-permute-start | bytes 1572872 | tf_op jit(solution)/shard_map/ppermute | solution.py:429
  504.0 1.5 copy-start
  511.8 88.6 %all-to-all-start.3 = ((bf16[128,2,8,128]{3,2,1,0:T(8,128)(2,1)}), bf16[128,2,8,128]{3,2,1,0:T(8,128)(2,1)S(1)}, u32[]{:S(2)}, u32[]{:S(2)}) async-start(bf16[128,2,8,128]{3,2,1,0:T(8,128)(2,1)} %scatter_pieces.1), calls=%async_computation.3 | async-start | bytes 1048576 | tf_op jit(solution)/shard_map/all_to_all | solution.py:410
  517.3 12.0 %collective-permute-start.15 = (bf16[128,1024]{1,0:T(8,128)(2,1)S(1)}, bf16[128,1024]{1,0:T(8,128)(2,1)S(1)}, u32[]{:S(2)}, u32[]{:S(2)}) collective-permute-start(bf16[128,1024]{1,0:T(8,128)(2,1)S(1)} %all-reduce.4.rest_0_), channel_id=1, source_target_pairs={{80,0}} | collective-permute-start | bytes 786440 | tf_op jit(solution)/shard_map/ppermute | solution.py:437
  518.7 16.3 %collective-permute-start.16 = (bf16[128,1024]{1,0:T(8,128)(2,1)S(1)}, bf16[128,1024]{1,0:T(8,128)(2,1)S(1)}, u32[]{:S(2)}, u32[]{:S(2)}) collective-permute-start(bf16[128,1024]{1,0:T(8,128)(2,1)S(1)} %all-reduce.4.rest_0_), channel_id=1, source_target_pairs={{96,0}} | collective-permute-start | bytes 786440 | tf_op jit(solution)/shard_map/ppermute | solution.py:437
  520.0 15.0 %collective-permute-start.17 = (bf16[128,1024]{1,0:T(8,128)(2,1)S(1)}, bf16[128,1024]{1,0:T(8,128)(2,1)S(1)}, u32[]{:S(2)}, u32[]{:S(2)}) collective-permute-start(bf16[128,1024]{1,0:T(8,128)(2,1)S(1)} %all-reduce.4.rest_0_), channel_id=1, source_target_pairs={{112,0}} | collective-permute-start | bytes 786440 | tf_op jit(solution)/shard_map/ppermute | solution.py:437
  529.4 5.6 copy-start.10
  534.9 0.7 copy-start.11
  535.0 0.8 copy-start.12
  600.4 0.8 copy-start.7
  600.5 1.0 copy-start.3
Sparse Core Ops, SparseCore 0:
  295.7 82.3 all-reduce.2

commit v2 on v1

v2 whole, which is shorter than its diff:
```python
import functools
import math

import jax
import jax.numpy as jnp
from jax import lax
from jax.experimental import pallas as pl
from jax.experimental.pallas import tpu as pltpu
from jax.sharding import PartitionSpec as P

KEY_HEADS = 8
GROUP_SIZE = 8
HEAD_SIZE = 128
BLOCK = 128
NB = 8
GROUPS = 16
PIECE = 8
SENT = 5
FIRST_SENT = NB - SENT
CHUNKS = 2
HALF = KEY_HEADS // CHUNKS
BOTH = ("ctx", "tp")
SCALING = 1.0 / math.sqrt(HEAD_SIZE)
EXP_SCALE = SCALING * math.log2(math.e)
FAR = 1e30
F32 = jnp.float32
BF16 = jnp.bfloat16
VM = pltpu.VMEM


def dot(a, b, ca, cb):
    return lax.dot_general(a, b, (((ca,), (cb,)), ((), ())), preferred_element_type=F32)


def pack_body(k_ref, v_ref, out_ref, both_ref):
    for kv, ref in enumerate((k_ref, v_ref)):
        both_ref[kv] = ref[...]
        for j in range(CHUNKS):
            for y in range(HALF):
                cols = pl.ds((j * HALF + y) * HEAD_SIZE, HEAD_SIZE)
                out_ref[y, kv, :, j] = ref[:, cols].reshape(GROUPS, PIECE, HEAD_SIZE)


def pack_pieces(k, v):
    return pl.pallas_call(
        pack_body,
        out_shape=(
            jax.ShapeDtypeStruct((HALF, 2, GROUPS, CHUNKS, PIECE, HEAD_SIZE), BF16),
            jax.ShapeDtypeStruct((2,) + k.shape, BF16),
        ),
        in_specs=[pl.BlockSpec(memory_space=VM)] * 2,
        out_specs=[pl.BlockSpec(memory_space=VM)] * 2,
        name="pack_pieces",
    )(k, v)


def gather_body(table_ref, held_ref, out_ref, *, rows, chunk):
    base = pl.program_id(0) * rows

    def one(d, carry):
        for s in range(SENT):
            block = table_ref[(base + d) * NB + FIRST_SENT + s]
            out_ref[d, s] = held_ref[block, chunk]
        return carry

    lax.fori_loop(0, rows, one, 0, unroll=4)


def gather_pieces(table, held, blocks, chunk):
    steps = 4
    rows = blocks // steps
    return pl.pallas_call(
        functools.partial(gather_body, rows=rows, chunk=chunk),
        out_shape=jax.ShapeDtypeStruct((blocks, SENT, PIECE, HEAD_SIZE), BF16),
        grid_spec=pltpu.PrefetchScalarGridSpec(
            num_scalar_prefetch=1,
            grid=(steps,),
            in_specs=[
                pl.BlockSpec((blocks, CHUNKS, PIECE, HEAD_SIZE), lambda i, t: (0, 0, 0, 0))
            ],
            out_specs=pl.BlockSpec((rows, SENT, PIECE, HEAD_SIZE), lambda i, t: (i, 0, 0, 0)),
        ),
        name="gather_pieces",
    )(table, held)


def give_body(meta_ref, held_ref, out_ref):
    out_ref[...] = held_ref[:, 1 - meta_ref[1]]


def give_pieces(meta, held):
    return pl.pallas_call(
        give_body,
        out_shape=jax.ShapeDtypeStruct(held.shape[:1] + held.shape[2:], BF16),
        in_specs=[pl.BlockSpec(memory_space=pltpu.SMEM), pl.BlockSpec(memory_space=VM)],
        out_specs=pl.BlockSpec(memory_space=VM),
        name="give_pieces",
    )(meta, held)


def add_listed(table_ref, got_ref, acc_ref, rows):
    base = pl.program_id(0) * rows

    def one(d, carry):
        for s in range(SENT):
            block = table_ref[(base + d) * NB + FIRST_SENT + s]
            acc_ref[block] += got_ref[d, s].astype(F32)
        return carry

    lax.fori_loop(0, rows, one, 0, unroll=4)


def scatter_body(table_ref, got_ref, out_ref, *, rows):
    @pl.when(pl.program_id(0) == 0)
    def _():
        out_ref[...] = jnp.zeros_like(out_ref)

    add_listed(table_ref, got_ref, out_ref, rows)


def scatter_last_body(
    table_ref, meta_ref, got_ref, first_ref, dense_ref, other_ref, out_ref, acc_ref, *, rows
):
    @pl.when(pl.program_id(0) == 0)
    def _():
        acc_ref[...] = jnp.zeros_like(acc_ref)

    add_listed(table_ref, got_ref, acc_ref, rows)

    @pl.when(pl.program_id(0) == pl.num_programs(0) - 1)
    def _():
        core = meta_ref[1]
        mine = dense_ref[0].reshape(acc_ref.shape)
        other = other_ref[...].reshape(acc_ref.shape)
        out_ref[:, core] = (jnp.where(core == 0, first_ref[...], acc_ref[...]) + mine).astype(BF16)
        out_ref[:, 1 - core] = (
            jnp.where(core == 0, acc_ref[...], first_ref[...]) + other
        ).astype(BF16)


def scatter_pieces(table, got, blocks):
    steps = 4
    rows = blocks // steps
    return pl.pallas_call(
        functools.partial(scatter_body, rows=rows),
        out_shape=jax.ShapeDtypeStruct((blocks, PIECE, HEAD_SIZE), F32),
        grid_spec=pltpu.PrefetchScalarGridSpec(
            num_scalar_prefetch=1,
            grid=(steps,),
            in_specs=[pl.BlockSpec((rows, SENT, PIECE, HEAD_SIZE), lambda i, t: (i, 0, 0, 0))],
            out_specs=pl.BlockSpec((blocks, PIECE, HEAD_SIZE), lambda i, t: (0, 0, 0)),
        ),
        name="scatter_pieces",
    )(table, got)


def scatter_last(table, meta, got, first, dense, other, blocks):
    steps = 4
    rows = blocks // steps
    whole = pl.BlockSpec((blocks, PIECE, HEAD_SIZE), lambda i, t, m: (0, 0, 0))
    return pl.pallas_call(
        functools.partial(scatter_last_body, rows=rows),
        out_shape=jax.ShapeDtypeStruct((blocks, CHUNKS, PIECE, HEAD_SIZE), BF16),
        grid_spec=pltpu.PrefetchScalarGridSpec(
            num_scalar_prefetch=2,
            grid=(steps,),
            in_specs=[
                pl.BlockSpec((rows, SENT, PIECE, HEAD_SIZE), lambda i, t, m: (i, 0, 0, 0)),
                whole,
                pl.BlockSpec((1, blocks * PIECE, HEAD_SIZE), lambda i, t, m: (0, 0, 0)),
                pl.BlockSpec((blocks * PIECE, HEAD_SIZE), lambda i, t, m: (0, 0)),
            ],
            out_specs=pl.BlockSpec(
                (blocks, CHUNKS, PIECE, HEAD_SIZE), lambda i, t, m: (0, 0, 0, 0)
            ),
            scratch_shapes=[VM((blocks, PIECE, HEAD_SIZE), F32)],
        ),
        name="scatter_last",
    )(table, meta, got, first, dense, other)


def two_heads(ref, p):
    first = ref[:, pl.ds(2 * p * HEAD_SIZE, HEAD_SIZE)]
    second = ref[:, pl.ds((2 * p + 1) * HEAD_SIZE, HEAD_SIZE)]
    return jnp.concatenate([first, second], axis=0)


def col_sum(x):
    return jnp.sum(x, axis=0, keepdims=True)


def sparse_body(
    meta_ref, valid_ref, q_ref, o_ref, self_ref, before_ref, after_ref, g_ref, *rest
):
    dq_ref, own_ref, prev_ref, next_ref, sent_ref = rest[-14:-9]
    kc, vc, kt, st, dp, pb, ds, dk, dv = rest[-9:]
    b = meta_ref[0]

    @pl.when(b == 0)
    def _():
        dq_ref[...] = jnp.zeros_like(dq_ref)
        own_ref[...] = jnp.zeros_like(own_ref)
        prev_ref[...] = jnp.zeros_like(prev_ref)
        next_ref[...] = jnp.zeros_like(next_ref)
        sent_ref[...] = jnp.zeros_like(sent_ref)

    @pl.when(b != 0)
    def _():
        for kv, dst in ((0, kc), (1, vc)):
            for s, part in enumerate((before_ref, self_ref, after_ref)):
                dst[s * BLOCK : (s + 1) * BLOCK] = part[kv]
            for s in range(SENT):
                at = (FIRST_SENT + s) * BLOCK
                dst[at : at + BLOCK] = g_ref[0, kv, :, s].reshape(BLOCK, HEAD_SIZE)
        kt[...] = kc[...].T
        live = [valid_ref[b * NB + s] > 0 for s in range(NB)]
        for p in range(GROUP_SIZE // 2):
            w = p % 2
            qp = two_heads(q_ref, p)
            op = two_heads(o_ref, p)
            st[w] = dot(kc[...], qp, 1, 1)
            dp[w] = dot(vc[...], op, 1, 1)
            top = jnp.full((1, 2 * BLOCK), -FAR, F32)
            for s in range(NB):
                here = jnp.max(st[w, s * BLOCK : (s + 1) * BLOCK], axis=0, keepdims=True)
                top = jnp.maximum(top, jnp.where(live[s], here, -FAR))
            top = top * EXP_SCALE
            total = jnp.zeros((1, 2 * BLOCK), F32)
            cross = jnp.zeros((1, 2 * BLOCK), F32)
            for s in range(NB):
                rows = slice(s * BLOCK, (s + 1) * BLOCK)
                shift = jnp.where(live[s], top, FAR)
                raised = jnp.exp2(st[w, rows] * EXP_SCALE - shift)
                st[w, rows] = raised
                total = total + col_sum(raised)
                cross = cross + col_sum(raised * dp[w, rows])
            inverse = 1.0 / total
            delta = cross * inverse
            for s in range(NB):
                rows = slice(s * BLOCK, (s + 1) * BLOCK)
                weights = st[w, rows] * inverse
                pb[w, rows] = weights.astype(BF16)
                ds[w, rows] = (weights * (dp[w, rows] - delta)).astype(BF16)
            new_dv = dot(pb[w], op, 1, 0)
            new_dk = dot(ds[w], qp, 1, 0)
            dv[...] = new_dv if p == 0 else dv[...] + new_dv
            dk[...] = new_dk if p == 0 else dk[...] + new_dk
            dqt = dot(kt[...], ds[w], 1, 0) * SCALING
            for j in range(2):
                dq_ref[:, pl.ds((2 * p + j) * HEAD_SIZE, HEAD_SIZE)] = (
                    dqt[:, j * BLOCK : (j + 1) * BLOCK].T.astype(BF16)
                )
        for kv, acc, factor in ((0, dk, SCALING), (1, dv, 1.0)):
            prev_ref[kv] = (acc[0:BLOCK] * factor).astype(BF16)
            own_ref[kv] = acc[BLOCK : 2 * BLOCK] * factor
            next_ref[kv] = (acc[2 * BLOCK : 3 * BLOCK] * factor).astype(BF16)
            for s in range(SENT):
                at = (FIRST_SENT + s) * BLOCK
                sent_ref[0, kv, :, s] = (
                    (acc[at : at + BLOCK] * factor).astype(BF16).reshape(GROUPS, PIECE, HEAD_SIZE)
                )


def sparse_grads(chunk, meta, valid, q, o, own, before, after, got, earlier=()):
    def at(h):
        return chunk * HALF + h

    wide = pl.BlockSpec((BLOCK, GROUP_SIZE * HEAD_SIZE), lambda h, m, t: (0, at(h)))
    pair = pl.BlockSpec((2, BLOCK, HEAD_SIZE), lambda h, m, t: (0, 0, at(h)))
    pieces = pl.BlockSpec(
        (1, 2, GROUPS, SENT, PIECE, HEAD_SIZE), lambda h, m, t: (h, 0, 0, 0, 0, 0)
    )
    keys = NB * BLOCK
    width = KEY_HEADS * HEAD_SIZE
    return pl.pallas_call(
        sparse_body,
        out_shape=(
            jax.ShapeDtypeStruct(q.shape, BF16),
            jax.ShapeDtypeStruct((2, BLOCK, width), F32),
            jax.ShapeDtypeStruct((2, BLOCK, width), BF16),
            jax.ShapeDtypeStruct((2, BLOCK, width), BF16),
            jax.ShapeDtypeStruct((HALF, 2, GROUPS, SENT, PIECE, HEAD_SIZE), BF16),
        ),
        grid_spec=pltpu.PrefetchScalarGridSpec(
            num_scalar_prefetch=2,
            grid=(HALF,),
            in_specs=[wide, wide, pair, pair, pair, pieces]
            + [pl.BlockSpec(memory_space=pl.ANY)] * len(earlier),
            out_specs=[wide, pair, pair, pair, pieces],
            scratch_shapes=[
                VM((keys, HEAD_SIZE), BF16),
                VM((keys, HEAD_SIZE), BF16),
                VM((HEAD_SIZE, keys), BF16),
                VM((2, keys, 2 * BLOCK), F32),
                VM((2, keys, 2 * BLOCK), F32),
                VM((2, keys, 2 * BLOCK), BF16),
                VM((2, keys, 2 * BLOCK), BF16),
                VM((keys, HEAD_SIZE), F32),
                VM((keys, HEAD_SIZE), F32),
            ],
        ),
        input_output_aliases={8 + n: n for n in range(len(earlier))},
        name="sparse_grads",
    )(meta, valid, q, o, own, before, after, got, *earlier)


def load_held(meta_ref, held_ref, other_ref, kc, vc):
    core = meta_ref[1]
    mine = held_ref[:, core].reshape(kc.shape)
    other = other_ref[...].reshape(kc.shape)

    @pl.when(core == 0)
    def _():
        kc[...] = mine
        vc[...] = other

    @pl.when(core != 0)
    def _():
        kc[...] = other
        vc[...] = mine


def stats_body(meta_ref, q_ref, held_ref, other_ref, out_ref, kc, vc):
    load_held(meta_ref, held_ref, other_ref, kc, vc)
    for p in range(GROUP_SIZE // 2):
        scores = dot(kc[...], two_heads(q_ref.at[0], p), 1, 1)
        grads = dot(vc[...], two_heads(q_ref.at[1], p), 1, 1)
        top = jnp.max(scores, axis=0, keepdims=True) * EXP_SCALE
        raised = jnp.exp2(scores * EXP_SCALE - top)
        for n, row in enumerate((top, col_sum(raised), col_sum(raised * grads))):
            for j in range(2):
                at = n * GROUP_SIZE + 2 * p + j
                out_ref[at : at + 1] = row[:, j * BLOCK : (j + 1) * BLOCK]


def dense_stats(meta, qo, held, other):
    keys = held.shape[0] * PIECE
    return pl.pallas_call(
        stats_body,
        out_shape=jax.ShapeDtypeStruct((3 * GROUP_SIZE, BLOCK), F32),
        in_specs=[pl.BlockSpec(memory_space=pltpu.SMEM)] + [pl.BlockSpec(memory_space=VM)] * 3,
        out_specs=pl.BlockSpec(memory_space=VM),
        scratch_shapes=[VM((keys, HEAD_SIZE), BF16), VM((keys, HEAD_SIZE), BF16)],
        name="dense_stats",
    )(meta, qo, held, other)


def merge_stats(parts):
    n = GROUP_SIZE
    top = functools.reduce(jnp.maximum, [x[:n] for x in parts])
    factors = [jnp.exp2(x[:n] - top) for x in parts]
    total = sum(x[n : 2 * n] * f for x, f in zip(parts, factors))
    cross = sum(x[2 * n :] * f for x, f in zip(parts, factors))
    return jnp.concatenate([top, total, cross], axis=0)


def dense_body(
    meta_ref, q_ref, held_ref, other_ref, s0, s1, s2, s3, dkv_ref, dq_ref, kc, vc, kt, stats
):
    load_held(meta_ref, held_ref, other_ref, kc, vc)
    kt[...] = kc[...].T
    stats[...] = merge_stats([s0[...], s1[...], s2[...], s3[...]])
    core = meta_ref[1]

    def row(n, p):
        at = n * GROUP_SIZE + 2 * p
        return jnp.concatenate([stats[at : at + 1], stats[at + 1 : at + 2]], axis=1)

    for p in range(GROUP_SIZE // 2):
        top = row(0, p)
        inverse = 1.0 / row(1, p)
        delta = row(2, p) * inverse
        qp = two_heads(q_ref.at[0], p)
        op = two_heads(q_ref.at[1], p)
        scores = dot(kc[...], qp, 1, 1)
        grads = dot(vc[...], op, 1, 1)
        weights = jnp.exp2(scores * EXP_SCALE - top) * inverse
        rounded = weights.astype(BF16)
        score_grad = (weights * (grads - delta)).astype(BF16)
        new_dk = dot(score_grad, qp, 1, 0) * SCALING
        new_dv = dot(rounded, op, 1, 0)
        dkv_ref[core] = new_dk if p == 0 else dkv_ref[core] + new_dk
        dkv_ref[1 - core] = new_dv if p == 0 else dkv_ref[1 - core] + new_dv
        dqt = dot(kt[...], score_grad, 1, 0) * SCALING
        for j in range(2):
            dq_ref[:, pl.ds((2 * p + j) * HEAD_SIZE, HEAD_SIZE)] = (
                dqt[:, j * BLOCK : (j + 1) * BLOCK].T.astype(BF16)
            )


def dense_grads(meta, qo, held, other, stats):
    keys = held.shape[0] * PIECE
    return pl.pallas_call(
        dense_body,
        out_shape=(
            jax.ShapeDtypeStruct((2, keys, HEAD_SIZE), F32),
            jax.ShapeDtypeStruct((BLOCK, GROUP_SIZE * HEAD_SIZE), BF16),
        ),
        in_specs=[pl.BlockSpec(memory_space=pltpu.SMEM)] + [pl.BlockSpec(memory_space=VM)] * 7,
        out_specs=[pl.BlockSpec(memory_space=VM)] * 2,
        scratch_shapes=[
            VM((keys, HEAD_SIZE), BF16),
            VM((keys, HEAD_SIZE), BF16),
            VM((HEAD_SIZE, keys), BF16),
            VM((3 * GROUP_SIZE, BLOCK), F32),
        ],
        name="dense_grads",
    )(meta, qo, held, other, *stats)


def combine_body(own_ref, prev_ref, next_ref, got_ref, dk_ref, dv_ref):
    for kv, out in ((0, dk_ref), (1, dv_ref)):
        for h in range(KEY_HEADS):
            cols = pl.ds(h * HEAD_SIZE, HEAD_SIZE)
            total = own_ref[kv, :, cols] + prev_ref[kv, :, cols].astype(F32)
            total = total + next_ref[kv, :, cols].astype(F32)
            pieces = got_ref[h % HALF, kv, :, h // HALF].reshape(BLOCK, HEAD_SIZE)
            out[:, cols] = (total + pieces.astype(F32)).astype(BF16)


def combine(own, from_prev, from_next, got):
    width = KEY_HEADS * HEAD_SIZE
    return pl.pallas_call(
        combine_body,
        out_shape=(jax.ShapeDtypeStruct((BLOCK, width), BF16),) * 2,
        in_specs=[pl.BlockSpec(memory_space=VM)] * 4,
        out_specs=[pl.BlockSpec(memory_space=VM)] * 2,
        name="combine",
    )(own, from_prev, from_next, got)


def spread_body(meta_ref, q_ref, o_ref, *rest):
    outs, stage, sems = rest[:-2], rest[-2], rest[-1]

    @pl.when(meta_ref[0] == 0)
    def _():
        loads, stores = [], []
        for h, out in enumerate(outs):
            cols = pl.ds(h * GROUP_SIZE * HEAD_SIZE, GROUP_SIZE * HEAD_SIZE)
            for j, ref in enumerate((q_ref, o_ref)):
                loads.append(
                    pltpu.make_async_copy(ref.at[:, cols], stage.at[h, j], sems.at[0, h, j])
                )
                stores.append(pltpu.make_async_copy(stage.at[h, j], out.at[j], sems.at[1, h, j]))
        for copy in loads:
            copy.start()
        for load, store in zip(loads, stores):
            load.wait()
            store.start()
        for copy in stores:
            copy.wait()


def spread_heads(meta, q, o):
    hbm = pl.BlockSpec(memory_space=pl.ANY)
    shape = (2, BLOCK, GROUP_SIZE * HEAD_SIZE)
    return pl.pallas_call(
        spread_body,
        out_shape=(jax.ShapeDtypeStruct(shape, BF16),) * KEY_HEADS,
        in_specs=[pl.BlockSpec(memory_space=pltpu.SMEM), hbm, hbm],
        out_specs=[hbm] * KEY_HEADS,
        scratch_shapes=[
            VM((KEY_HEADS,) + shape, BF16),
            pltpu.SemaphoreType.DMA((2, KEY_HEADS, 2)),
        ],
        name="spread_heads",
    )(meta, q, o)


def first_body(meta_ref, dq_ref, *rest):
    parts, out, stage, sems = rest[:KEY_HEADS], rest[KEY_HEADS], rest[-2], rest[-1]

    @pl.when(meta_ref[0] == 0)
    def _():
        loads, stores = [], []
        for h, part in enumerate(parts):
            cols = pl.ds(h * GROUP_SIZE * HEAD_SIZE, GROUP_SIZE * HEAD_SIZE)
            loads.append(pltpu.make_async_copy(part, stage.at[h], sems.at[0, h]))
            stores.append(pltpu.make_async_copy(stage.at[h], out.at[:, cols], sems.at[1, h]))
        for copy in loads:
            copy.start()
        for load, store in zip(loads, stores):
            load.wait()
            store.start()
        for copy in stores:
            copy.wait()


def put_first(meta, dq, parts):
    hbm = pl.BlockSpec(memory_space=pl.ANY)
    return pl.pallas_call(
        first_body,
        out_shape=jax.ShapeDtypeStruct(dq.shape, dq.dtype),
        in_specs=[pl.BlockSpec(memory_space=pltpu.SMEM)] + [hbm] * (KEY_HEADS + 1),
        out_specs=hbm,
        input_output_aliases={1: 0},
        scratch_shapes=[
            VM((KEY_HEADS, BLOCK, GROUP_SIZE * HEAD_SIZE), BF16),
            pltpu.SemaphoreType.DMA((2, KEY_HEADS)),
        ],
        name="put_first",
    )(meta, dq, *parts)


def tp_pairs(pairs, ctx_size, tp_size):
    return [(c * tp_size + a, c * tp_size + b) for c in range(ctx_size) for a, b in pairs]


def per_device(queries, key_tensor, value_tensor, output_gradient, key_blocks, slot_valid):
    tp_size, ctx_size = lax.axis_size("tp"), lax.axis_size("ctx")
    blocks = ctx_size * tp_size
    b_index = lax.axis_index("ctx") * tp_size + lax.axis_index("tp")
    core = lax.axis_index("ctx") % 2
    meta = jnp.stack([b_index, core]).astype(jnp.int32)
    table = key_blocks.reshape(-1)
    valid = slot_valid.reshape(-1)
    up = [(i, (i + 1) % blocks) for i in range(blocks)]
    down = [(i, (i - 1) % blocks) for i in range(blocks)]
    partner = [(i, (i // tp_size ^ 1) * tp_size + i % tp_size) for i in range(blocks)]
    rows = range(4)

    def swap(x):
        return lax.all_to_all(x, BOTH, split_axis=0, concat_axis=0, tiled=True)

    def send(x, pairs):
        return lax.ppermute(x, BOTH, pairs)

    def send_tp(x, pairs):
        return send(x, tp_pairs(pairs, ctx_size, tp_size))

    pieces, both = pack_pieces(key_tensor, value_tensor)
    held = swap(pieces.reshape(blocks, CHUNKS, PIECE, HEAD_SIZE))
    before, after = send(both, up), send(both, down)
    slices = spread_heads(meta, queries, output_gradient)
    qo = jnp.where(b_index == 0, slices[0], jnp.zeros_like(slices[0]))
    for c in range(1, ctx_size):
        qo = qo + send(slices[c // 2 + HALF * (c % 2)], [(0, c * tp_size)])

    listed = [gather_pieces(table, held, blocks, j) for j in range(CHUNKS)]
    given = send(give_pieces(meta, held), partner)

    one = send_tp(qo, [(0, 1)])
    qo = qo + one + send_tp(qo, [(0, 3)]) + send_tp(one, [(1, 2)])
    one = send_tp(qo, [(x, 4 + x) for x in rows])
    three = send_tp(qo, [(x, 12 + x) for x in rows])
    qo = qo + one + three + send_tp(one, [(4 + x, 8 + x) for x in rows])

    shape = (HALF, 2, GROUPS, SENT, PIECE, HEAD_SIZE)
    got = [swap(x).reshape(shape) for x in listed]
    *earlier, sent0 = sparse_grads(
        0, meta, valid, queries, output_gradient, both, before, after, got[0]
    )
    back0 = swap(sent0.reshape(blocks, SENT, PIECE, HEAD_SIZE))

    stats = dense_stats(meta, qo, held, given)
    others = [
        send_tp(stats, [(4 * z + x, 4 * z + (x + n) % 4) for z in rows for x in rows])
        for n in range(1, 4)
    ]
    stats = merge_stats([stats] + others)
    others = [
        send_tp(stats, [(4 * z + x, 4 * ((z + n) % 4) + x) for z in rows for x in rows])
        for n in range(1, 4)
    ]

    *grads, sent1 = sparse_grads(
        1, meta, valid, queries, output_gradient, both, before, after, got[1], earlier
    )
    dq, own, to_prev, to_next = grads
    back1 = swap(sent1.reshape(blocks, SENT, PIECE, HEAD_SIZE))
    from_next, from_prev = send(to_prev, down), send(to_next, up)

    dense, part = dense_grads(meta, qo, held, given, [stats] + others)
    dense_other = send(dense[1], partner)

    def add(*xs):
        return sum(x.astype(F32) for x in xs).astype(BF16)

    near = add(part, send_tp(part, [(4 * z + 2, 4 * z + 1) for z in rows]))
    part = add(
        part,
        send_tp(part, [(4 * z + 3, 4 * z) for z in rows]),
        send_tp(near, [(4 * z + 1, 4 * z) for z in rows]),
    )
    near = add(part, send_tp(part, [(8, 4)]))
    part = add(part, send_tp(part, [(12, 0)]), send_tp(near, [(4, 0)]))
    parts = [part] * KEY_HEADS
    for c in range(1, ctx_size):
        parts[c // 2 + HALF * (c % 2)] = send(part, [(c * tp_size, 0)])
    d_q = put_first(meta, dq, parts)

    first = scatter_pieces(table, back0, blocks)
    summed = scatter_last(table, meta, back1, first, dense, dense_other, blocks)
    home = swap(summed).reshape(HALF, 2, GROUPS, CHUNKS, PIECE, HEAD_SIZE)
    d_k, d_v = combine(own, from_prev, from_next, home)
    return d_q, d_k, d_v


def solution(mesh):
    spec = P(BOTH, None)
    return jax.shard_map(
        per_device,
        mesh=mesh,
        in_specs=(spec, spec, spec, spec, P(), P()),
        out_specs=(spec, spec, spec),
        check_vma=False,
    )
```

time: 612 us -> 319 us (0.52)
  Pallas kernels: 227 us -> 53.4 us
  blocking collectives: 103 us -> 0 us
  waiting for transfers between devices: 160 us -> 81.4 us
  starting transfers between devices: 94.9 us -> 162 us
  between operations: 14.3 us -> 1.48 us
    pallas_call x5 -> x8, Pallas kernels: 145 us -> 31.9 us  [the longest x2 7.9 us: gather_pieces(): pl.pallas_call(functools.partial(gather_body, rows=rows, chunk=chunk), ou...]
    psum x1 -> x0, waiting for transfers between devices: 82.5 us -> none  [per_device(): qo = lax.psum(qo, 'tp')]
    psum x1 -> x0, blocking collectives: 78.1 us -> none  [per_device(): dq_first = lax.psum(dq_part, 'tp').astype(BF16)]
    pallas_call x1, Pallas kernels: 64.7 us -> 3.06 us  [put_first(): pl.pallas_call(first_body, out_shape=jax.ShapeDtypeStruct(dq.shape, dq.dt...]
    ppermute x20 -> x38, starting transfers between devices: 38.8 us -> 77.3 us  [send(): return lax.ppermute(x, BOTH, pairs)]
    all_to_all x4 -> x6, starting transfers between devices: 56 us -> 84.8 us  [swap(): return lax.all_to_all(x, BOTH, split_axis=0, concat_axis=0, tiled=True)]
    all_gather x1 -> x0, blocking collectives: 25.4 us -> none  [per_device(): stats = lax.all_gather(stats, 'tp', axis=0)]
    ppermute x20 -> x38, waiting for transfers between devices: 65.4 us -> 74.4 us  [send(): return lax.ppermute(x, BOTH, pairs)]
  transfers between devices with their start and end apart: 25 -> 44, of which waited for: 9 -> 10; matrix products, arithmetic and copies ran while one was open for 1% -> 3% of each run, Pallas kernels for 34% -> 14%
where the time goes in v2:
time: 319 us; the launch traced here: 318 us
  starting transfers between devices  162 us (51%)
  waiting for transfers between devices  81.4 us (26%)
  Pallas kernels  53.4 us (17%)
  local copies, waits for them, and re-layouts  12.1 us (4%)
  other arithmetic  7.16 us (2%)
    all_to_all x6, starting transfers between devices, swap(): return lax.all_to_all(x, BOTH, split_axis=0, concat_axis=0, tiled=True)  84.8 us
    ppermute x38, starting transfers between devices, send(): return lax.ppermute(x, BOTH, pairs)  77.3 us
    ppermute x38, waiting for transfers between devices, send(): return lax.ppermute(x, BOTH, pairs)  74.4 us
    pallas_call x2, Pallas kernels, sparse_grads(): pl.pallas_call(sparse_body, out_shape=(jax.ShapeDtypeStruct(q.shape, BF16...  10.5 us
    unnamed x62, local copies, waits for them, and re-layouts  9.93 us
    pallas_call x2, Pallas kernels, gather_pieces(): pl.pallas_call(functools.partial(gather_body, rows=rows, chunk=chunk), ou...  7.9 us
    all_to_all x6, waiting for transfers between devices, swap(): return lax.all_to_all(x, BOTH, split_axis=0, concat_axis=0, tiled=True)  7.01 us
  transfers between devices with their start and end apart: 44, of which 10 were waited for; matrix products, arithmetic and copies ran while one was open for 3% of the time, Pallas kernels for 14%

profile of v2, /device:TPU:0, one launch (start us, length us, event | category | flops | bytes accessed | tf_op | source)
XLA Modules:
  0.0 317.6 jit_solution(14974240465421651193)
XLA Ops:
  1.3 4.6 %spread_heads.1 = (bf16[2,128,1024]{2,1,0:T(8,128)(2,1)}, bf16[2,128,1024]{2,1,0:T(8,128)(2,1)}, bf16[2,128,1024]{2,1,0:T(8,128)(2,1)}, bf16[2,128,1024]{2,1,0:T...) custom-call(s32[2]{0:T(128)} %pad_add_fusion.meta_ref, ...), custom_call_target="tpu_custom_call" | custom-call | tf_op jit(solution)/shard_map/spread_heads/pallas_call | solution.py:457
  5.9 1.5 collective-permute-start.8
  7.3 1.3 collective-permute-start.7
  8.7 1.3 collective-permute-start.6
  10.0 1.3 collective-permute-start.5
  11.3 2.1 collective-permute-start.4
  14.3 2.1 collective-permute-start.3
  16.4 3.5 %collective-permute-done.7 = bf16[2,128,1024]{2,1,0:T(8,128)(2,1)S(1)} collective-permute-done((bf16[2,128,1024]{2,1,0:T(8,128)(2,1)}, bf16[2,128,1024]{2,1,0:T(8,128)(2,1)S(1)}, u32[]{:S(2)}, u32[]{:S(2)}) %collective-permute-start.7) | collective-permute-done | bytes 524320 | tf_op jit(solution)/shard_map/ppermute | solution.py:526
  19.9 2.1 collective-permute-start.2
  22.0 2.1 pack_pieces.1
  24.1 4.9 %all-to-all-start = ((bf16[128,2,8,128]{3,2,1,0:T(8,128)(2,1)}), bf16[128,2,8,128]{3,2,1,0:T(8,128)(2,1)S(1)}, u32[]{:S(2)}, u32[]{:S(2)}) async-start(bf16[128,2,8,128]{3,2,1,0:T(8,128)(2,1)} %bitcast.15), calls=%async_computation | async-start | bytes 1048576 | tf_op jit(solution)/shard_map/all_to_all | solution.py:523
  29.1 9.7 %collective-permute-done.3 = bf16[2,128,1024]{2,1,0:T(8,128)(2,1)} collective-permute-done((bf16[2,128,1024]{2,1,0:T(8,128)(2,1)}, bf16[2,128,1024]{2,1,0:T(8,128)(2,1)}, u32[]{:S(2)}, u32[]{:S(2)}) %collective-permute-start.3) | collective-permute-done | bytes 524320 | tf_op jit(solution)/shard_map/ppermute | solution.py:526
  38.7 1.7 add_add_fusion.2
  40.5 1.3 collective-permute-start.9
  43.4 3.9 %gather_pieces.3 = bf16[128,5,8,128]{3,2,1,0:T(8,128)(2,1)} custom-call(s32[1024]{0:T(1024)} %reshape.31.table_ref, bf16[128,2,8,128]{3,2,1,0:T(8,128)(2,1)} %copy-done), custom_call_target="tpu_custom_call" | custom-call | tf_op jit(solution)/shard_map/gather_pieces/pallas_call | solution.py:72
  47.3 4.6 %all-to-all-start.2 = ((bf16[128,5,8,128]{3,2,1,0:T(8,128)(2,1)}), bf16[128,5,8,128]{3,2,1,0:T(8,128)(2,1)S(1)}, u32[]{:S(2)}, u32[]{:S(2)}) async-start(bf16[128,5,8,128]{3,2,1,0:T(8,128)(2,1)} %gather_pieces.3), calls=%async_computation.2 | async-start | bytes 2621440 | tf_op jit(solution)/shard_map/all_to_all | solution.py:523
  52.0 4.1 %collective-permute-start.10 = (bf16[2,128,1024]{2,1,0:T(8,128)(2,1)S(1)}, bf16[2,128,1024]{2,1,0:T(8,128)(2,1)S(1)}, u32[]{:S(2)}, u32[]{:S(2)}) collective-permute-start(bf16[2,128,1024]{2,1,0:T(8,128)(2,1)S(1)} %add_add_fusion.2), channel_id=1, source_target_pairs={{0,3},{16,19},{32,35},{48,51},{64,67},{80,83},{96,99},{112,115}} | collective-permute-start | bytes 1572872 | tf_op jit(solution)/shard_map/ppermute | solution.py:526
  56.8 19.6 %collective-permute-done.10 = bf16[2,128,1024]{2,1,0:T(8,128)(2,1)S(1)} collective-permute-done((bf16[2,128,1024]{2,1,0:T(8,128)(2,1)S(1)}, bf16[2,128,1024]{2,1,0:T(8,128)(2,1)S(1)}, u32[]{:S(2)}, u32[]{:S(2)}) %collective-permute-start.10) | collective-permute-done | bytes 524320 | tf_op jit(solution)/shard_map/ppermute | solution.py:526
  76.5 2.1 collective-permute-start.12
  78.6 4.0 %gather_pieces.2 = bf16[128,5,8,128]{3,2,1,0:T(8,128)(2,1)} custom-call(s32[1024]{0:T(1024)} %reshape.31.table_ref, bf16[128,2,8,128]{3,2,1,0:T(8,128)(2,1)} %copy-done), custom_call_target="tpu_custom_call" | custom-call | tf_op jit(solution)/shard_map/gather_pieces/pallas_call | solution.py:72
  83.6 8.5 %all-to-all-start.1 = ((bf16[128,5,8,128]{3,2,1,0:T(8,128)(2,1)}), bf16[128,5,8,128]{3,2,1,0:T(8,128)(2,1)S(1)}, u32[]{:S(2)}, u32[]{:S(2)}) async-start(bf16[128,5,8,128]{3,2,1,0:T(8,128)(2,1)} %gather_pieces.2), calls=%async_computation.1 | async-start | bytes 2621440 | tf_op jit(solution)/shard_map/all_to_all | solution.py:523
  92.1 5.5 %collective-permute-start.13 = (bf16[2,128,1024]{2,1,0:T(8,128)(2,1)S(1)}, bf16[2,128,1024]{2,1,0:T(8,128)(2,1)}, u32[]{:S(2)}, u32[]{:S(2)}) collective-permute-start(bf16[2,128,1024]{2,1,0:T(8,128)(2,1)S(1)} %add_add_fusion.1), channel_id=1, source_target_pairs={{0,12},{1,13},{2,14},{3,15},{16,28},{17,29},{18,30},{19,31},{32,44... | collective-permute-start | bytes 1572872 | tf_op jit(solution)/shard_map/ppermute | solution.py:526
  97.7 1.5 collective-permute-start.14
  99.2 1.5 collective-permute-start
  100.6 5.7 %collective-permute-start.1 = (bf16[2,128,1024]{2,1,0:T(8,128)(2,1)}, bf16[2,128,1024]{2,1,0:T(8,128)(2,1)S(1)}, u32[]{:S(2)}, u32[]{:S(2)}) collective-permute-start(bf16[2,128,1024]{2,1,0:T(8,128)(2,1)} %get-tuple-element.27.self_ref), channel_id=1, source_target_pairs={{0,127},{1,0},{2,1},{3,2},{4,3},{5,4},{6,5},{7,6},{8,7},{9,8},{10,... | collective-permute-start | bytes 1572872 | tf_op jit(solution)/shard_map/ppermute | solution.py:526
  106.3 1.8 give_pieces.1
  108.1 10.3 %collective-permute-done.13 = bf16[2,128,1024]{2,1,0:T(8,128)(2,1)} collective-permute-done((bf16[2,128,1024]{2,1,0:T(8,128)(2,1)S(1)}, bf16[2,128,1024]{2,1,0:T(8,128)(2,1)}, u32[]{:S(2)}, u32[]{:S(2)}) %collective-permute-start.13) | collective-permute-done | bytes 524320 | tf_op jit(solution)/shard_map/ppermute | solution.py:526
  118.4 2.3 add_add_fusion.q_ref
  121.4 4.2 %dense_stats.1 = f32[24,128]{1,0:T(8,128)} custom-call(s32[2]{0:T(128)} %pad_add_fusion.meta_ref, bf16[2,128,1024]{2,1,0:T(8,128)(2,1)} %add_add_fusion.q_ref, bf16[128,2,8,128]{3,2,1,0:T(8,128)(2,1)} %copy-done, bf16[128,8,128]{2,1,0:T(8,128)(2,1)} %copy-done.9), custom_call_target="tpu_custom_call" | custom-call | tf_op jit(solution)/shard_map/dense_stats/pallas_call | solution.py:338
  125.6 13.8 %collective-permute-start.18 = (f32[24,128]{1,0:T(8,128)}, f32[24,128]{1,0:T(8,128)S(1)}, u32[]{:S(2)}, u32[]{:S(2)}) collective-permute-start(f32[24,128]{1,0:T(8,128)} %dense_stats.1), channel_id=1, source_target_pairs={{0,3},{1,0},{2,1},{3,2},{4,7},{5,4},{6,5},{7,6},{8,11},{9,8},{10,9... | collective-permute-start | bytes 36872 | tf_op jit(solution)/shard_map/ppermute | solution.py:526
  142.1 5.2 %sparse_grads.2 = (bf16[128,8192]{1,0:T(8,128)(2,1)}, f32[2,128,1024]{2,1,0:T(8,128)}, bf16[2,128,1024]{2,1,0:T(8,128)(2,1)}, bf16[2,128,1024]{2,1,0:T(8,128)(2,1)}, bf16[4,2,16,5,8,128]{5,4,3,2,1,0:T(8,128)(2,1)}) custom-call(s32[2]{0:T(128)} %pad_add_fusion.meta_ref, s32[1024]{0:T(1024)} %reshape.30.valid_ref, bf16[128,8192]{1,0:T(8,128)(2,1)} %q_ref.5, ...), custom_call_target="tpu_custom_call" | custom-call | tf_op jit(solution)/shard_map/sparse_grads/pallas_call | solution.py:275
  148.4 25.2 %all-to-all-start.4 = ((bf16[128,5,8,128]{3,2,1,0:T(8,128)(2,1)}), bf16[128,5,8,128]{3,2,1,0:T(8,128)(2,1)S(1)}, u32[]{:S(2)}, u32[]{:S(2)}) async-start(bf16[128,5,8,128]{3,2,1,0:T(8,128)(2,1)} %bitcast.13), calls=%async_computation.4 | async-start | bytes 2621440 | tf_op jit(solution)/shard_map/all_to_all | solution.py:523
  174.9 3.2 %collective-permute-start.20 = (f32[24,128]{1,0:T(8,128)S(1)}, f32[24,128]{1,0:T(8,128)S(1)}, u32[]{:S(2)}, u32[]{:S(2)}) collective-permute-start(f32[24,128]{1,0:T(8,128)S(1)} %pad_maximum_fusion.s0), channel_id=1, source_target_pairs={{0,8},{1,9},{2,10},{3,11},{4,12},{5,13},{6,14},{7,15},{8,0},{9,1},... | collective-permute-start | bytes 36872 | tf_op jit(solution)/shard_map/ppermute | solution.py:526
  179.3 5.5 %collective-permute-done.20.s2 = f32[24,128]{1,0:T(8,128)S(1)} collective-permute-done((f32[24,128]{1,0:T(8,128)S(1)}, f32[24,128]{1,0:T(8,128)S(1)}, u32[]{:S(2)}, u32[]{:S(2)}) %collective-permute-start.20) | collective-permute-done | bytes 12320 | tf_op jit(solution)/shard_map/ppermute | solution.py:526
  184.8 1.4 collective-permute-done.21.s3
  186.9 5.3 %dense_grads.1 = (f32[2,1024,128]{2,1,0:T(8,128)}, bf16[128,1024]{1,0:T(8,128)(2,1)}) custom-call(s32[2]{0:T(128)} %pad_add_fusion.meta_ref, bf16[2,128,1024]{2,1,0:T(8,128)(2,1)} %add_add_fusion.q_ref, bf16[128,2,8,128]{3,2,1,0:T(8,128)(2,1)} %copy-done, bf16[128,8,128]{2,1,0:T(8,128)(2,1)} %copy-done.9, f32[24,128]{1,0:T(8,128)} %copy-done.24, ...), custom_call_target="tpu_custom_call" | custom-call | tf_op jit(solution)/shard_map/dense_grads/pallas_call | solution.py:393
  195.2 1.5 collective-permute-start.24
  196.7 5.3 %sparse_grads.3 = (bf16[128,8192]{1,0:T(8,128)(2,1)}, f32[2,128,1024]{2,1,0:T(8,128)}, bf16[2,128,1024]{2,1,0:T(8,128)(2,1)}, bf16[2,128,1024]{2,1,0:T(8,128)(2,1)}, bf16[4,2,16,5,8,128]{5,4,3,2,1,0:T(8,128)(2,1)}) custom-call(s32[2]{0:T(128)} %pad_add_fusion.meta_ref, ...), custom_call_target="tpu_custom_call", output_to_operand_aliasing={{0}: (8, {}), {1}: (9, {}), {2}: (10, {}), {3}: (11, {})} | custom-call | tf_op jit(solution)/shard_map/sparse_grads/pallas_call | solution.py:275
  203.0 35.5 %all-to-all-start.3 = ((bf16[128,5,8,128]{3,2,1,0:T(8,128)(2,1)}), bf16[128,5,8,128]{3,2,1,0:T(8,128)(2,1)S(1)}, u32[]{:S(2)}, u32[]{:S(2)}) async-start(bf16[128,5,8,128]{3,2,1,0:T(8,128)(2,1)} %bitcast.14), calls=%async_computation.3 | async-start | bytes 2621440 | tf_op jit(solution)/shard_map/all_to_all | solution.py:523
  244.0 7.2 %collective-permute-start.36 = (bf16[2,128,1024]{2,1,0:T(8,128)(2,1)}, bf16[2,128,1024]{2,1,0:T(8,128)(2,1)}, u32[]{:S(2)}, u32[]{:S(2)}) collective-permute-start(bf16[2,128,1024]{2,1,0:T(8,128)(2,1)} %get-tuple-element.45), channel_id=1, source_target_pairs={{0,127},{1,0},{2,1},{3,2},{4,3},{5,4},{6,5},{7,6},{8,7},{9,8},{10,... | collective-permute-start | bytes 1572872 | tf_op jit(solution)/shard_map/ppermute | solution.py:526
  251.1 22.9 %collective-permute-done.25 = bf16[128,1024]{1,0:T(8,128)(2,1)S(1)} collective-permute-done((bf16[128,1024]{1,0:T(8,128)(2,1)S(1)}, bf16[128,1024]{1,0:T(8,128)(2,1)S(1)}, u32[]{:S(2)}, u32[]{:S(2)}) %collective-permute-start.25) | collective-permute-done | bytes 262176 | tf_op jit(solution)/shard_map/ppermute | solution.py:526
  276.8 5.0 %scatter_pieces.1.first_ref = f32[128,8,128]{2,1,0:T(8,128)} custom-call(s32[1024]{0:T(1024)} %reshape.31.table_ref, bf16[128,5,8,128]{3,2,1,0:T(8,128)(2,1)} %copy-done.3), custom_call_target="tpu_custom_call" | custom-call | tf_op jit(solution)/shard_map/scatter_pieces/pallas_call | solution.py:144
  283.7 6.2 %scatter_last.1 = bf16[128,2,8,128]{3,2,1,0:T(8,128)(2,1)} custom-call(s32[1024]{0:T(1024)} %reshape.31.table_ref, s32[2]{0:T(128)} %pad_add_fusion.meta_ref, bf16[128,5,8,128]{3,2,1,0:T(8,128)(2,1)} %copy-done.2, f32[128,8,128]{2,1,0:T(8,128)} %scatter_pieces.1.first_ref, f32[2,1024,128]{2,1,0:T(8,128)} %get-tuple-element.48.dense_ref, f32[1024,128]{1,0:T(8,128)} %copy-done.15), custom_call_target="tpu_custom_call" | custom-call | tf_op jit(solution)/shard_map/scatter_last/pallas_call | solution.py:161
  290.0 6.1 %all-to-all-start.5 = ((bf16[128,2,8,128]{3,2,1,0:T(8,128)(2,1)}), bf16[128,2,8,128]{3,2,1,0:T(8,128)(2,1)S(1)}, u32[]{:S(2)}, u32[]{:S(2)}) async-start(bf16[128,2,8,128]{3,2,1,0:T(8,128)(2,1)} %scatter_last.1), calls=%async_computation.5 | async-start | bytes 1048576 | tf_op jit(solution)/shard_map/all_to_all | solution.py:523
  296.1 1.3 collective-permute-start.30
  302.7 7.0 %all-to-all-done.5 = bf16[128,2,8,128]{3,2,1,0:T(8,128)(2,1)S(1)} async-done(((bf16[128,2,8,128]{3,2,1,0:T(8,128)(2,1)}), bf16[128,2,8,128]{3,2,1,0:T(8,128)(2,1)S(1)}, u32[]{:S(2)}, u32[]{:S(2)}) %all-to-all-start.5) | async-done | bytes 524320 | tf_op jit(solution)/shard_map/all_to_all | solution.py:523
  310.4 2.6 combine.1
  314.4 3.1 put_first.1
  (129 shorter events, 33.7 us)
Async XLA Ops:
  5.9 32.9 %copy-start.13 = (bf16[2,128,1024]{2,1,0:T(8,128)(2,1)S(1)}, bf16[2,128,1024]{2,1,0:T(8,128)(2,1)}, u32[]{:S(2)}) copy-start(bf16[2,128,1024]{2,1,0:T(8,128)(2,1)} %get-tuple-element.34) | copy-start | bytes 1572868
  5.9 8.4 %collective-permute-start.8 = (bf16[2,128,1024]{2,1,0:T(8,128)(2,1)}, bf16[2,128,1024]{2,1,0:T(8,128)(2,1)S(1)}, u32[]{:S(2)}, u32[]{:S(2)}) collective-permute-start(bf16[2,128,1024]{2,1,0:T(8,128)(2,1)} %get-tuple-element.41), channel_id=1, source_target_pairs={{0,112}} | collective-permute-start | bytes 1572872 | tf_op jit(solution)/shard_map/ppermute | solution.py:526
  7.3 12.6 %collective-permute-start.7 = (bf16[2,128,1024]{2,1,0:T(8,128)(2,1)}, bf16[2,128,1024]{2,1,0:T(8,128)(2,1)S(1)}, u32[]{:S(2)}, u32[]{:S(2)}) collective-permute-start(bf16[2,128,1024]{2,1,0:T(8,128)(2,1)} %get-tuple-element.40), channel_id=1, source_target_pairs={{0,96}} | collective-permute-start | bytes 1572872 | tf_op jit(solution)/shard_map/ppermute | solution.py:526
  8.7 20.4 %collective-permute-start.6 = (bf16[2,128,1024]{2,1,0:T(8,128)(2,1)}, bf16[2,128,1024]{2,1,0:T(8,128)(2,1)S(1)}, u32[]{:S(2)}, u32[]{:S(2)}) collective-permute-start(bf16[2,128,1024]{2,1,0:T(8,128)(2,1)} %get-tuple-element.39), channel_id=1, source_target_pairs={{0,80}} | collective-permute-start | bytes 1572872 | tf_op jit(solution)/shard_map/ppermute | solution.py:526
  10.0 19.0 %collective-permute-start.5 = (bf16[2,128,1024]{2,1,0:T(8,128)(2,1)}, bf16[2,128,1024]{2,1,0:T(8,128)(2,1)S(1)}, u32[]{:S(2)}, u32[]{:S(2)}) collective-permute-start(bf16[2,128,1024]{2,1,0:T(8,128)(2,1)} %get-tuple-element.38), channel_id=1, source_target_pairs={{0,64}} | collective-permute-start | bytes 1572872 | tf_op jit(solution)/shard_map/ppermute | solution.py:526
  11.3 17.7 %collective-permute-start.4 = (bf16[2,128,1024]{2,1,0:T(8,128)(2,1)}, bf16[2,128,1024]{2,1,0:T(8,128)(2,1)}, u32[]{:S(2)}, u32[]{:S(2)}) collective-permute-start(bf16[2,128,1024]{2,1,0:T(8,128)(2,1)} %get-tuple-element.37), channel_id=1, source_target_pairs={{0,48}} | collective-permute-start | bytes 1572872 | tf_op jit(solution)/shard_map/ppermute | solution.py:526
  14.3 24.4 %collective-permute-start.3 = (bf16[2,128,1024]{2,1,0:T(8,128)(2,1)}, bf16[2,128,1024]{2,1,0:T(8,128)(2,1)}, u32[]{:S(2)}, u32[]{:S(2)}) collective-permute-start(bf16[2,128,1024]{2,1,0:T(8,128)(2,1)} %get-tuple-element.36), channel_id=1, source_target_pairs={{0,32}} | collective-permute-start | bytes 1572872 | tf_op jit(solution)/shard_map/ppermute | solution.py:526
  19.9 18.8 %collective-permute-start.2 = (bf16[2,128,1024]{2,1,0:T(8,128)(2,1)}, bf16[2,128,1024]{2,1,0:T(8,128)(2,1)}, u32[]{:S(2)}, u32[]{:S(2)}) collective-permute-start(bf16[2,128,1024]{2,1,0:T(8,128)(2,1)} %get-tuple-element.35), channel_id=1, source_target_pairs={{0,16}} | collective-permute-start | bytes 1572872 | tf_op jit(solution)/shard_map/ppermute | solution.py:526
  24.1 18.5 %all-to-all-start = ((bf16[128,2,8,128]{3,2,1,0:T(8,128)(2,1)}), bf16[128,2,8,128]{3,2,1,0:T(8,128)(2,1)S(1)}, u32[]{:S(2)}, u32[]{:S(2)}) async-start(bf16[128,2,8,128]{3,2,1,0:T(8,128)(2,1)} %bitcast.15), calls=%async_computation | async-start | bytes 1048576 | tf_op jit(solution)/shard_map/all_to_all | solution.py:523
  40.5 15.6 %collective-permute-start.9 = (bf16[2,128,1024]{2,1,0:T(8,128)(2,1)S(1)}, bf16[2,128,1024]{2,1,0:T(8,128)(2,1)S(1)}, u32[]{:S(2)}, u32[]{:S(2)}) collective-permute-start(bf16[2,128,1024]{2,1,0:T(8,128)(2,1)S(1)} %add_add_fusion.2), channel_id=1, source_target_pairs={{0,1},{16,17},{32,33},{48,49},{64,65},{80,81},{96,97},{112,113}} | collective-permute-start | bytes 1572872 | tf_op jit(solution)/shard_map/ppermute | solution.py:526
  47.3 35.2 %all-to-all-start.2 = ((bf16[128,5,8,128]{3,2,1,0:T(8,128)(2,1)}), bf16[128,5,8,128]{3,2,1,0:T(8,128)(2,1)S(1)}, u32[]{:S(2)}, u32[]{:S(2)}) async-start(bf16[128,5,8,128]{3,2,1,0:T(8,128)(2,1)} %gather_pieces.3), calls=%async_computation.2 | async-start | bytes 2621440 | tf_op jit(solution)/shard_map/all_to_all | solution.py:523
  52.0 24.4 %collective-permute-start.10 = (bf16[2,128,1024]{2,1,0:T(8,128)(2,1)S(1)}, bf16[2,128,1024]{2,1,0:T(8,128)(2,1)S(1)}, u32[]{:S(2)}, u32[]{:S(2)}) collective-permute-start(bf16[2,128,1024]{2,1,0:T(8,128)(2,1)S(1)} %add_add_fusion.2), channel_id=1, source_target_pairs={{0,3},{16,19},{32,35},{48,51},{64,67},{80,83},{96,99},{112,115}} | collective-permute-start | bytes 1572872 | tf_op jit(solution)/shard_map/ppermute | solution.py:526
  56.1 20.3 %collective-permute-start.11 = (bf16[2,128,1024]{2,1,0:T(8,128)(2,1)S(1)}, bf16[2,128,1024]{2,1,0:T(8,128)(2,1)S(1)}, u32[]{:S(2)}, u32[]{:S(2)}) collective-permute-start(bf16[2,128,1024]{2,1,0:T(8,128)(2,1)S(1)} %collective-permute-done.9), channel_id=1, source_target_pairs={{1,2},{17,18},{33,34},{49,50},{65,66},{81,82},{97,98},{113,114}} | collective-permute-start | bytes 1572872 | tf_op jit(solution)/shard_map/ppermute | solution.py:526
  76.5 21.2 %collective-permute-start.12 = (bf16[2,128,1024]{2,1,0:T(8,128)(2,1)S(1)}, bf16[2,128,1024]{2,1,0:T(8,128)(2,1)}, u32[]{:S(2)}, u32[]{:S(2)}) collective-permute-start(bf16[2,128,1024]{2,1,0:T(8,128)(2,1)S(1)} %add_add_fusion.1), channel_id=1, source_target_pairs={{0,4},{1,5},{2,6},{3,7},{16,20},{17,21},{18,22},{19,23},{32,36},{3... | collective-permute-start | bytes 1572872 | tf_op jit(solution)/shard_map/ppermute | solution.py:526
  83.6 63.8 %all-to-all-start.1 = ((bf16[128,5,8,128]{3,2,1,0:T(8,128)(2,1)}), bf16[128,5,8,128]{3,2,1,0:T(8,128)(2,1)S(1)}, u32[]{:S(2)}, u32[]{:S(2)}) async-start(bf16[128,5,8,128]{3,2,1,0:T(8,128)(2,1)} %gather_pieces.2), calls=%async_computation.1 | async-start | bytes 2621440 | tf_op jit(solution)/shard_map/all_to_all | solution.py:523
  92.1 26.3 %collective-permute-start.13 = (bf16[2,128,1024]{2,1,0:T(8,128)(2,1)S(1)}, bf16[2,128,1024]{2,1,0:T(8,128)(2,1)}, u32[]{:S(2)}, u32[]{:S(2)}) collective-permute-start(bf16[2,128,1024]{2,1,0:T(8,128)(2,1)S(1)} %add_add_fusion.1), channel_id=1, source_target_pairs={{0,12},{1,13},{2,14},{3,15},{16,28},{17,29},{18,30},{19,31},{32,44... | collective-permute-start | bytes 1572872 | tf_op jit(solution)/shard_map/ppermute | solution.py:526
  97.7 20.7 %collective-permute-start.14 = (bf16[2,128,1024]{2,1,0:T(8,128)(2,1)}, bf16[2,128,1024]{2,1,0:T(8,128)(2,1)}, u32[]{:S(2)}, u32[]{:S(2)}) collective-permute-start(bf16[2,128,1024]{2,1,0:T(8,128)(2,1)} %collective-permute-done.12), channel_id=1, source_target_pairs={{4,8},{5,9},{6,10},{7,11},{20,24},{21,25},{22,26},{23,27},{36,40},... | collective-permute-start | bytes 1572872 | tf_op jit(solution)/shard_map/ppermute | solution.py:526
  99.2 41.9 %collective-permute-start = (bf16[2,128,1024]{2,1,0:T(8,128)(2,1)}, bf16[2,128,1024]{2,1,0:T(8,128)(2,1)S(1)}, u32[]{:S(2)}, u32[]{:S(2)}) collective-permute-start(bf16[2,128,1024]{2,1,0:T(8,128)(2,1)} %get-tuple-element.27.self_ref), channel_id=1, source_target_pairs={{0,1},{1,2},{2,3},{3,4},{4,5},{5,6},{6,7},{7,8},{8,9},{9,10},{10,1... | collective-permute-start | bytes 1572872 | tf_op jit(solution)/shard_map/ppermute | solution.py:526
  100.6 40.4 %collective-permute-start.1 = (bf16[2,128,1024]{2,1,0:T(8,128)(2,1)}, bf16[2,128,1024]{2,1,0:T(8,128)(2,1)S(1)}, u32[]{:S(2)}, u32[]{:S(2)}) collective-permute-start(bf16[2,128,1024]{2,1,0:T(8,128)(2,1)} %get-tuple-element.27.self_ref), channel_id=1, source_target_pairs={{0,127},{1,0},{2,1},{3,2},{4,3},{5,4},{6,5},{7,6},{8,7},{9,8},{10,... | collective-permute-start | bytes 1572872 | tf_op jit(solution)/shard_map/ppermute | solution.py:526
  108.1 12.6 %collective-permute-start.15 = (bf16[128,8,128]{2,1,0:T(8,128)(2,1)}, bf16[128,8,128]{2,1,0:T(8,128)(2,1)S(1)}, u32[]{:S(2)}, u32[]{:S(2)}) collective-permute-start(bf16[128,8,128]{2,1,0:T(8,128)(2,1)} %give_pieces.1), channel_id=1, source_target_pairs={{0,16},{1,17},{2,18},{3,19},{4,20},{5,21},{6,22},{7,23},{8,24},{9,... | collective-permute-start | bytes 786440 | tf_op jit(solution)/shard_map/ppermute | solution.py:526
  125.6 48.0 %collective-permute-start.18 = (f32[24,128]{1,0:T(8,128)}, f32[24,128]{1,0:T(8,128)S(1)}, u32[]{:S(2)}, u32[]{:S(2)}) collective-permute-start(f32[24,128]{1,0:T(8,128)} %dense_stats.1), channel_id=1, source_target_pairs={{0,3},{1,0},{2,1},{3,2},{4,7},{5,4},{6,5},{7,6},{8,11},{9,8},{10,9... | collective-permute-start | bytes 36872 | tf_op jit(solution)/shard_map/ppermute | solution.py:526
  139.4 34.3 %collective-permute-start.17 = (f32[24,128]{1,0:T(8,128)}, f32[24,128]{1,0:T(8,128)S(1)}, u32[]{:S(2)}, u32[]{:S(2)}) collective-permute-start(f32[24,128]{1,0:T(8,128)} %dense_stats.1), channel_id=1, source_target_pairs={{0,2},{1,3},{2,0},{3,1},{4,6},{5,7},{6,4},{7,5},{8,10},{9,11},{10,... | collective-permute-start | bytes 36872 | tf_op jit(solution)/shard_map/ppermute | solution.py:526
  139.4 34.3 %collective-permute-start.16 = (f32[24,128]{1,0:T(8,128)}, f32[24,128]{1,0:T(8,128)S(1)}, u32[]{:S(2)}, u32[]{:S(2)}) collective-permute-start(f32[24,128]{1,0:T(8,128)} %dense_stats.1), channel_id=1, source_target_pairs={{0,1},{1,2},{2,3},{3,0},{4,5},{5,6},{6,7},{7,4},{8,9},{9,10},{10,1... | collective-permute-start | bytes 36872 | tf_op jit(solution)/shard_map/ppermute | solution.py:526
  147.4 26.3 %copy-start.23 = (f32[24,128]{1,0:T(8,128)S(1)}, f32[24,128]{1,0:T(8,128)}, u32[]{:S(2)}) copy-start(f32[24,128]{1,0:T(8,128)} %dense_stats.1) | copy-start | bytes 36868
  148.4 53.5 %all-to-all-start.4 = ((bf16[128,5,8,128]{3,2,1,0:T(8,128)(2,1)}), bf16[128,5,8,128]{3,2,1,0:T(8,128)(2,1)S(1)}, u32[]{:S(2)}, u32[]{:S(2)}) async-start(bf16[128,5,8,128]{3,2,1,0:T(8,128)(2,1)} %bitcast.13), calls=%async_computation.4 | async-start | bytes 2621440 | tf_op jit(solution)/shard_map/all_to_all | solution.py:523
  173.8 5.6 %collective-permute-start.19 = (f32[24,128]{1,0:T(8,128)S(1)}, f32[24,128]{1,0:T(8,128)S(1)}, u32[]{:S(2)}, u32[]{:S(2)}) collective-permute-start(f32[24,128]{1,0:T(8,128)S(1)} %pad_maximum_fusion.s0), channel_id=1, source_target_pairs={{0,4},{1,5},{2,6},{3,7},{4,8},{5,9},{6,10},{7,11},{8,12},{9,13},{1... | collective-permute-start | bytes 36872 | tf_op jit(solution)/shard_map/ppermute | solution.py:526
  174.9 9.9 %collective-permute-start.20 = (f32[24,128]{1,0:T(8,128)S(1)}, f32[24,128]{1,0:T(8,128)S(1)}, u32[]{:S(2)}, u32[]{:S(2)}) collective-permute-start(f32[24,128]{1,0:T(8,128)S(1)} %pad_maximum_fusion.s0), channel_id=1, source_target_pairs={{0,8},{1,9},{2,10},{3,11},{4,12},{5,13},{6,14},{7,15},{8,0},{9,1},... | collective-permute-start | bytes 36872 | tf_op jit(solution)/shard_map/ppermute | solution.py:526
  178.1 8.1 %collective-permute-start.21 = (f32[24,128]{1,0:T(8,128)S(1)}, f32[24,128]{1,0:T(8,128)S(1)}, u32[]{:S(2)}, u32[]{:S(2)}) collective-permute-start(f32[24,128]{1,0:T(8,128)S(1)} %pad_maximum_fusion.s0), channel_id=1, source_target_pairs={{0,12},{1,13},{2,14},{3,15},{4,0},{5,1},{6,2},{7,3},{8,4},{9,5},{1... | collective-permute-start | bytes 36872 | tf_op jit(solution)/shard_map/ppermute | solution.py:526
  192.1 2.0 collective-permute-start.23
  192.8 45.7 %collective-permute-start.22 = (bf16[128,1024]{1,0:T(8,128)(2,1)}, bf16[128,1024]{1,0:T(8,128)(2,1)S(1)}, u32[]{:S(2)}, u32[]{:S(2)}) collective-permute-start(bf16[128,1024]{1,0:T(8,128)(2,1)} %get-tuple-element.42), channel_id=1, source_target_pairs={{3,0},{7,4},{11,8},{15,12},{19,16},{23,20},{27,24},{31,28},{35,32}... | collective-permute-start | bytes 786440 | tf_op jit(solution)/shard_map/ppermute | solution.py:526
  195.2 43.4 %collective-permute-start.24 = (bf16[128,1024]{1,0:T(8,128)(2,1)S(1)}, bf16[128,1024]{1,0:T(8,128)(2,1)}, u32[]{:S(2)}, u32[]{:S(2)}) collective-permute-start(bf16[128,1024]{1,0:T(8,128)(2,1)S(1)} %fusion.2), channel_id=1, source_target_pairs={{1,0},{5,4},{9,8},{13,12},{17,16},{21,20},{25,24},{29,28},{33,32},... | collective-permute-start | bytes 786440 | tf_op jit(solution)/shard_map/ppermute | solution.py:526
  201.9 36.6 %copy-start.11 = (bf16[128,1024]{1,0:T(8,128)(2,1)S(1)}, bf16[128,1024]{1,0:T(8,128)(2,1)}, u32[]{:S(2)}) copy-start(bf16[128,1024]{1,0:T(8,128)(2,1)} %get-tuple-element.42) | copy-start | bytes 786436
  203.0 78.8 %all-to-all-start.3 = ((bf16[128,5,8,128]{3,2,1,0:T(8,128)(2,1)}), bf16[128,5,8,128]{3,2,1,0:T(8,128)(2,1)S(1)}, u32[]{:S(2)}, u32[]{:S(2)}) async-start(bf16[128,5,8,128]{3,2,1,0:T(8,128)(2,1)} %bitcast.14), calls=%async_computation.3 | async-start | bytes 2621440 | tf_op jit(solution)/shard_map/all_to_all | solution.py:523
  239.7 2.8 collective-permute-start.26
  241.2 40.6 %collective-permute-start.37 = (f32[1024,128]{1,0:T(8,128)}, f32[1024,128]{1,0:T(8,128)S(1)}, u32[]{:S(2)}, u32[]{:S(2)}) collective-permute-start(f32[1024,128]{1,0:T(8,128)} %slice_bitcast_fusion), channel_id=1, source_target_pairs={{0,16},{1,17},{2,18},{3,19},{4,20},{5,21},{6,22},{7,23},{8,24},{9,... | collective-permute-start | bytes 1572872 | tf_op jit(solution)/shard_map/ppermute | solution.py:526
  241.2 32.8 %collective-permute-start.25 = (bf16[128,1024]{1,0:T(8,128)(2,1)S(1)}, bf16[128,1024]{1,0:T(8,128)(2,1)S(1)}, u32[]{:S(2)}, u32[]{:S(2)}) collective-permute-start(bf16[128,1024]{1,0:T(8,128)(2,1)S(1)} %fusion.1), channel_id=1, source_target_pairs={{12,0},{28,16},{44,32},{60,48},{76,64},{92,80},{108,96},{124,112}} | collective-permute-start | bytes 786440 | tf_op jit(solution)/shard_map/ppermute | solution.py:526
  242.6 31.4 %collective-permute-start.27 = (bf16[128,1024]{1,0:T(8,128)(2,1)S(1)}, bf16[128,1024]{1,0:T(8,128)(2,1)S(1)}, u32[]{:S(2)}, u32[]{:S(2)}) collective-permute-start(bf16[128,1024]{1,0:T(8,128)(2,1)S(1)} %fusion.5), channel_id=1, source_target_pairs={{4,0},{20,16},{36,32},{52,48},{68,64},{84,80},{100,96},{116,112}} | collective-permute-start | bytes 786440 | tf_op jit(solution)/shard_map/ppermute | solution.py:526
  243.9 53.5 %collective-permute-start.35 = (bf16[2,128,1024]{2,1,0:T(8,128)(2,1)}, bf16[2,128,1024]{2,1,0:T(8,128)(2,1)S(1)}, u32[]{:S(2)}, u32[]{:S(2)}) collective-permute-start(bf16[2,128,1024]{2,1,0:T(8,128)(2,1)} %get-tuple-element.44), channel_id=1, source_target_pairs={{0,1},{1,2},{2,3},{3,4},{4,5},{5,6},{6,7},{7,8},{8,9},{9,10},{10,1... | collective-permute-start | bytes 1572872 | tf_op jit(solution)/shard_map/ppermute | solution.py:526
  244.0 54.7 %collective-permute-start.36 = (bf16[2,128,1024]{2,1,0:T(8,128)(2,1)}, bf16[2,128,1024]{2,1,0:T(8,128)(2,1)}, u32[]{:S(2)}, u32[]{:S(2)}) collective-permute-start(bf16[2,128,1024]{2,1,0:T(8,128)(2,1)} %get-tuple-element.45), channel_id=1, source_target_pairs={{0,127},{1,0},{2,1},{3,2},{4,3},{5,4},{6,5},{7,6},{8,7},{9,8},{10,... | collective-permute-start | bytes 1572872 | tf_op jit(solution)/shard_map/ppermute | solution.py:526
  274.2 27.2 %copy-start.10 = (bf16[128,1024]{1,0:T(8,128)(2,1)}, bf16[128,1024]{1,0:T(8,128)(2,1)S(1)}, u32[]{:S(2)}) copy-start(bf16[128,1024]{1,0:T(8,128)(2,1)S(1)} %fusion.4.rest_0_) | copy-start | bytes 786436
  274.2 25.8 %collective-permute-start.28 = (bf16[128,1024]{1,0:T(8,128)(2,1)S(1)}, bf16[128,1024]{1,0:T(8,128)(2,1)S(1)}, u32[]{:S(2)}, u32[]{:S(2)}) collective-permute-start(bf16[128,1024]{1,0:T(8,128)(2,1)S(1)} %fusion.4.rest_0_), channel_id=1, source_target_pairs={{32,0}} | collective-permute-start | bytes 786440 | tf_op jit(solution)/shard_map/ppermute | solution.py:526
  275.5 25.8 %collective-permute-start.29 = (bf16[128,1024]{1,0:T(8,128)(2,1)S(1)}, bf16[128,1024]{1,0:T(8,128)(2,1)S(1)}, u32[]{:S(2)}, u32[]{:S(2)}) collective-permute-start(bf16[128,1024]{1,0:T(8,128)(2,1)S(1)} %fusion.4.rest_0_), channel_id=1, source_target_pairs={{64,0}} | collective-permute-start | bytes 786440 | tf_op jit(solution)/shard_map/ppermute | solution.py:526
  290.0 19.7 %all-to-all-start.5 = ((bf16[128,2,8,128]{3,2,1,0:T(8,128)(2,1)}), bf16[128,2,8,128]{3,2,1,0:T(8,128)(2,1)S(1)}, u32[]{:S(2)}, u32[]{:S(2)}) async-start(bf16[128,2,8,128]{3,2,1,0:T(8,128)(2,1)} %scatter_last.1), calls=%async_computation.5 | async-start | bytes 1048576 | tf_op jit(solution)/shard_map/all_to_all | solution.py:523
  296.1 17.0 %collective-permute-start.30 = (bf16[128,1024]{1,0:T(8,128)(2,1)S(1)}, bf16[128,1024]{1,0:T(8,128)(2,1)S(1)}, u32[]{:S(2)}, u32[]{:S(2)}) collective-permute-start(bf16[128,1024]{1,0:T(8,128)(2,1)S(1)} %fusion.4.rest_0_), channel_id=1, source_target_pairs={{96,0}} | collective-permute-start | bytes 786440 | tf_op jit(solution)/shard_map/ppermute | solution.py:526
  297.4 15.7 %collective-permute-start.31 = (bf16[128,1024]{1,0:T(8,128)(2,1)S(1)}, bf16[128,1024]{1,0:T(8,128)(2,1)S(1)}, u32[]{:S(2)}, u32[]{:S(2)}) collective-permute-start(bf16[128,1024]{1,0:T(8,128)(2,1)S(1)} %fusion.4.rest_0_), channel_id=1, source_target_pairs={{16,0}} | collective-permute-start | bytes 786440 | tf_op jit(solution)/shard_map/ppermute | solution.py:526
  298.7 14.4 %collective-permute-start.32 = (bf16[128,1024]{1,0:T(8,128)(2,1)S(1)}, bf16[128,1024]{1,0:T(8,128)(2,1)S(1)}, u32[]{:S(2)}, u32[]{:S(2)}) collective-permute-start(bf16[128,1024]{1,0:T(8,128)(2,1)S(1)} %fusion.4.rest_0_), channel_id=1, source_target_pairs={{48,0}} | collective-permute-start | bytes 786440 | tf_op jit(solution)/shard_map/ppermute | solution.py:526
  300.0 13.1 %collective-permute-start.33 = (bf16[128,1024]{1,0:T(8,128)(2,1)S(1)}, bf16[128,1024]{1,0:T(8,128)(2,1)S(1)}, u32[]{:S(2)}, u32[]{:S(2)}) collective-permute-start(bf16[128,1024]{1,0:T(8,128)(2,1)S(1)} %fusion.4.rest_0_), channel_id=1, source_target_pairs={{80,0}} | collective-permute-start | bytes 786440 | tf_op jit(solution)/shard_map/ppermute | solution.py:526
  301.4 12.3 %collective-permute-start.34 = (bf16[128,1024]{1,0:T(8,128)(2,1)S(1)}, bf16[128,1024]{1,0:T(8,128)(2,1)S(1)}, u32[]{:S(2)}, u32[]{:S(2)}) collective-permute-start(bf16[128,1024]{1,0:T(8,128)(2,1)S(1)} %fusion.4.rest_0_), channel_id=1, source_target_pairs={{112,0}} | collective-permute-start | bytes 786440 | tf_op jit(solution)/shard_map/ppermute | solution.py:526
  (26 other events, 107.2 us)

commit v3 on v2

--- a/solution.py
+++ b/solution.py
@@ -7,6 +7,7 @@
 from jax.experimental import pallas as pl
 from jax.experimental.pallas import tpu as pltpu
 from jax.sharding import PartitionSpec as P
+
 
 KEY_HEADS = 8
 GROUP_SIZE = 8
@@ -19,6 +20,7 @@
 FIRST_SENT = NB - SENT
 CHUNKS = 2
 HALF = KEY_HEADS // CHUNKS
+CALL_HEADS = 2
 BOTH = ("ctx", "tp")
 SCALING = 1.0 / math.sqrt(HEAD_SIZE)
 EXP_SCALE = SCALING * math.log2(math.e)
@@ -214,10 +216,17 @@
                 dst[at : at + BLOCK] = g_ref[0, kv, :, s].reshape(BLOCK, HEAD_SIZE)
         kt[...] = kc[...].T
         live = [valid_ref[b * NB + s] > 0 for s in range(NB)]
-        for p in range(GROUP_SIZE // 2):
-            w = p % 2
-            qp = two_heads(q_ref, p)
-            op = two_heads(o_ref, p)
+        dk[...] = jnp.zeros_like(dk)
+        dv[...] = jnp.zeros_like(dv)
+
+        def heads(ref, p):
+            at = pl.multiple_of(2 * p * HEAD_SIZE, 2 * HEAD_SIZE)
+            both = ref[:, pl.ds(at, 2 * HEAD_SIZE)]
+            return jnp.concatenate([both[:, :HEAD_SIZE], both[:, HEAD_SIZE:]], axis=0)
+
+        def pair(p, w):
+            qp = heads(q_ref, p)
+            op = heads(o_ref, p)
             st[w] = dot(kc[...], qp, 1, 1)
             dp[w] = dot(vc[...], op, 1, 1)
             top = jnp.full((1, 2 * BLOCK), -FAR, F32)
@@ -243,13 +252,18 @@
                 ds[w, rows] = (weights * (dp[w, rows] - delta)).astype(BF16)
             new_dv = dot(pb[w], op, 1, 0)
             new_dk = dot(ds[w], qp, 1, 0)
-            dv[...] = new_dv if p == 0 else dv[...] + new_dv
-            dk[...] = new_dk if p == 0 else dk[...] + new_dk
+            dv[...] += new_dv
+            dk[...] += new_dk
             dqt = dot(kt[...], ds[w], 1, 0) * SCALING
-            for j in range(2):
-                dq_ref[:, pl.ds((2 * p + j) * HEAD_SIZE, HEAD_SIZE)] = (
-                    dqt[:, j * BLOCK : (j + 1) * BLOCK].T.astype(BF16)
-                )
+            out = jnp.concatenate([dqt[:, :BLOCK].T, dqt[:, BLOCK:].T], axis=1).astype(BF16)
+            dq_ref[:, pl.ds(pl.multiple_of(2 * p * HEAD_SIZE, 2 * HEAD_SIZE), 2 * HEAD_SIZE)] = out
+
+        def two_pairs(i, carry):
+            for w in range(2):
+                pair(2 * i + w, w)
+            return carry
+
+        lax.fori_loop(0, GROUP_SIZE // 4, two_pairs, 0)
         for kv, acc, factor in ((0, dk, SCALING), (1, dv, 1.0)):
             prev_ref[kv] = (acc[0:BLOCK] * factor).astype(BF16)
             own_ref[kv] = acc[BLOCK : 2 * BLOCK] * factor
@@ -261,14 +275,14 @@
                 )
 
 
-def sparse_grads(chunk, meta, valid, q, o, own, before, after, got, earlier=()):
-    def at(h):
-        return chunk * HALF + h
-
-    wide = pl.BlockSpec((BLOCK, GROUP_SIZE * HEAD_SIZE), lambda h, m, t: (0, at(h)))
-    pair = pl.BlockSpec((2, BLOCK, HEAD_SIZE), lambda h, m, t: (0, 0, at(h)))
+def sparse_grads(call, meta, valid, q, o, own, before, after, got, earlier=()):
+    first = call * CALL_HEADS
+    inside = first % HALF
+
+    wide = pl.BlockSpec((BLOCK, GROUP_SIZE * HEAD_SIZE), lambda h, m, t: (0, first + h))
+    pair = pl.BlockSpec((2, BLOCK, HEAD_SIZE), lambda h, m, t: (0, 0, first + h))
     pieces = pl.BlockSpec(
-        (1, 2, GROUPS, SENT, PIECE, HEAD_SIZE), lambda h, m, t: (h, 0, 0, 0, 0, 0)
+        (1, 2, GROUPS, SENT, PIECE, HEAD_SIZE), lambda h, m, t: (inside + h, 0, 0, 0, 0, 0)
     )
     keys = NB * BLOCK
     width = KEY_HEADS * HEAD_SIZE
@@ -283,7 +297,7 @@
         ),
         grid_spec=pltpu.PrefetchScalarGridSpec(
             num_scalar_prefetch=2,
-            grid=(HALF,),
+            grid=(CALL_HEADS,),
             in_specs=[wide, wide, pair, pair, pair, pieces]
             + [pl.BlockSpec(memory_space=pl.ANY)] * len(earlier),
             out_specs=[wide, pair, pair, pair, pieces],
@@ -355,23 +369,31 @@
 
 
 def dense_body(
-    meta_ref, q_ref, held_ref, other_ref, s0, s1, s2, s3, dkv_ref, dq_ref, kc, vc, kt, stats
+    meta_ref, q_ref, held_ref, other_ref, s0, s1, s2, s3, dkv_ref, d0, d1, d2, d3,
+    kc, vc, kt, stats,
 ):
     load_held(meta_ref, held_ref, other_ref, kc, vc)
     kt[...] = kc[...].T
     stats[...] = merge_stats([s0[...], s1[...], s2[...], s3[...]])
     core = meta_ref[1]
 
-    def row(n, p):
-        at = n * GROUP_SIZE + 2 * p
-        return jnp.concatenate([stats[at : at + 1], stats[at + 1 : at + 2]], axis=1)
-
-    for p in range(GROUP_SIZE // 2):
-        top = row(0, p)
-        inverse = 1.0 / row(1, p)
-        delta = row(2, p) * inverse
-        qp = two_heads(q_ref.at[0], p)
-        op = two_heads(q_ref.at[1], p)
+    for m, dq_ref in enumerate((d0, d1, d2, d3)):
+        p = lax.rem(meta_ref[2] + m, 4)
+
+        def row(n):
+            at = n * GROUP_SIZE + 2 * p
+            return jnp.concatenate([stats[pl.ds(at, 1)], stats[pl.ds(at + 1, 1)]], axis=1)
+
+        def heads(ref):
+            at = pl.multiple_of(2 * p * HEAD_SIZE, 2 * HEAD_SIZE)
+            both = ref[:, pl.ds(at, 2 * HEAD_SIZE)]
+            return jnp.concatenate([both[:, :HEAD_SIZE], both[:, HEAD_SIZE:]], axis=0)
+
+        top = row(0)
+        inverse = 1.0 / row(1)
+        delta = row(2) * inverse
+        qp = heads(q_ref.at[0])
+        op = heads(q_ref.at[1])
         scores = dot(kc[...], qp, 1, 1)
         grads = dot(vc[...], op, 1, 1)
         weights = jnp.exp2(scores * EXP_SCALE - top) * inverse
@@ -379,25 +401,23 @@
         score_grad = (weights * (grads - delta)).astype(BF16)
         new_dk = dot(score_grad, qp, 1, 0) * SCALING
         new_dv = dot(rounded, op, 1, 0)
-        dkv_ref[core] = new_dk if p == 0 else dkv_ref[core] + new_dk
-        dkv_ref[1 - core] = new_dv if p == 0 else dkv_ref[1 - core] + new_dv
+        dkv_ref[core] = new_dk if m == 0 else dkv_ref[core] + new_dk
+        dkv_ref[1 - core] = new_dv if m == 0 else dkv_ref[1 - core] + new_dv
         dqt = dot(kt[...], score_grad, 1, 0) * SCALING
         for j in range(2):
-            dq_ref[:, pl.ds((2 * p + j) * HEAD_SIZE, HEAD_SIZE)] = (
+            dq_ref[:, j * HEAD_SIZE : (j + 1) * HEAD_SIZE] = (
                 dqt[:, j * BLOCK : (j + 1) * BLOCK].T.astype(BF16)
             )
 
 
 def dense_grads(meta, qo, held, other, stats):
     keys = held.shape[0] * PIECE
+    quarter = jax.ShapeDtypeStruct((BLOCK, 2 * HEAD_SIZE), BF16)
     return pl.pallas_call(
         dense_body,
-        out_shape=(
-            jax.ShapeDtypeStruct((2, keys, HEAD_SIZE), F32),
-            jax.ShapeDtypeStruct((BLOCK, GROUP_SIZE * HEAD_SIZE), BF16),
-        ),
+        out_shape=(jax.ShapeDtypeStruct((2, keys, HEAD_SIZE), F32),) + (quarter,) * 4,
         in_specs=[pl.BlockSpec(memory_space=pltpu.SMEM)] + [pl.BlockSpec(memory_space=VM)] * 7,
-        out_specs=[pl.BlockSpec(memory_space=VM)] * 2,
+        out_specs=[pl.BlockSpec(memory_space=VM)] * 5,
         scratch_shapes=[
             VM((keys, HEAD_SIZE), BF16),
             VM((keys, HEAD_SIZE), BF16),
@@ -506,18 +526,22 @@
     return [(c * tp_size + a, c * tp_size + b) for c in range(ctx_size) for a, b in pairs]
 
 
+def add(*xs):
+    return sum(x.astype(F32) for x in xs).astype(BF16)
+
+
 def per_device(queries, key_tensor, value_tensor, output_gradient, key_blocks, slot_valid):
     tp_size, ctx_size = lax.axis_size("tp"), lax.axis_size("ctx")
     blocks = ctx_size * tp_size
     b_index = lax.axis_index("ctx") * tp_size + lax.axis_index("tp")
     core = lax.axis_index("ctx") % 2
-    meta = jnp.stack([b_index, core]).astype(jnp.int32)
+    meta = jnp.stack([b_index, core, lax.axis_index("tp") % 4]).astype(jnp.int32)
     table = key_blocks.reshape(-1)
     valid = slot_valid.reshape(-1)
     up = [(i, (i + 1) % blocks) for i in range(blocks)]
     down = [(i, (i - 1) % blocks) for i in range(blocks)]
     partner = [(i, (i // tp_size ^ 1) * tp_size + i % tp_size) for i in range(blocks)]
-    rows = range(4)
+    four = range(4)
 
     def swap(x):
         return lax.all_to_all(x, BOTH, split_axis=0, concat_axis=0, tiled=True)
@@ -527,6 +551,12 @@
 
     def send_tp(x, pairs):
         return send(x, tp_pairs(pairs, ctx_size, tp_size))
+
+    def along_x(n):
+        return [(4 * z + x, 4 * z + (x + n) % 4) for z in four for x in four]
+
+    def along_z(n):
+        return [(4 * z + x, 4 * ((z + n) % 4) + x) for z in four for x in four]
 
     pieces, both = pack_pieces(key_tensor, value_tensor)
     held = swap(pieces.reshape(blocks, CHUNKS, PIECE, HEAD_SIZE))
@@ -536,61 +566,53 @@
     for c in range(1, ctx_size):
         qo = qo + send(slices[c // 2 + HALF * (c % 2)], [(0, c * tp_size)])
 
-    listed = [gather_pieces(table, held, blocks, j) for j in range(CHUNKS)]
-    given = send(give_pieces(meta, held), partner)
-
-    one = send_tp(qo, [(0, 1)])
-    qo = qo + one + send_tp(qo, [(0, 3)]) + send_tp(one, [(1, 2)])
-    one = send_tp(qo, [(x, 4 + x) for x in rows])
-    three = send_tp(qo, [(x, 12 + x) for x in rows])
-    qo = qo + one + three + send_tp(one, [(4 + x, 8 + x) for x in rows])
-
+    listed = []
+    for j in range(CHUNKS):
+        listed.append(gather_pieces(table, held, blocks, j))
+    given = give_pieces(meta, held)
+    given = send(given, partner)
     shape = (HALF, 2, GROUPS, SENT, PIECE, HEAD_SIZE)
-    got = [swap(x).reshape(shape) for x in listed]
-    *earlier, sent0 = sparse_grads(
-        0, meta, valid, queries, output_gradient, both, before, after, got[0]
-    )
-    back0 = swap(sent0.reshape(blocks, SENT, PIECE, HEAD_SIZE))
+    got = []
+    for j in range(CHUNKS):
+        got.append(swap(listed[j]).reshape(shape))
+
+    qo = qo + send_tp(qo, [(0, 1)])
+    qo = qo + send_tp(qo, [(0, 3), (1, 2)])
+    qo = qo + send_tp(qo, [(x, 4 + x) for x in four])
+    qo = qo + send_tp(qo, [(x, 12 + x) for x in four] + [(4 + x, 8 + x) for x in four])
+
+    grads, back = (), []
+    calls = HALF // CALL_HEADS
+    for j in range(CHUNKS):
+        for n in range(calls):
+            call = calls * j + n
+            grads = sparse_grads(
+                call, meta, valid, queries, output_gradient, both, before, after, got[j],
+                grads if n > 0 else grads[:4],
+            )
+        back.append(swap(grads[4].reshape(blocks, SENT, PIECE, HEAD_SIZE)))
+    dq, own, to_prev, to_next = grads[:4]
+    from_next, from_prev = send(to_prev, down), send(to_next, up)
 
     stats = dense_stats(meta, qo, held, given)
-    others = [
-        send_tp(stats, [(4 * z + x, 4 * z + (x + n) % 4) for z in rows for x in rows])
-        for n in range(1, 4)
-    ]
+    others = [send_tp(stats, along_x(n)) for n in range(1, 4)]
     stats = merge_stats([stats] + others)
-    others = [
-        send_tp(stats, [(4 * z + x, 4 * ((z + n) % 4) + x) for z in rows for x in rows])
-        for n in range(1, 4)
-    ]
-
-    *grads, sent1 = sparse_grads(
-        1, meta, valid, queries, output_gradient, both, before, after, got[1], earlier
-    )
-    dq, own, to_prev, to_next = grads
-    back1 = swap(sent1.reshape(blocks, SENT, PIECE, HEAD_SIZE))
-    from_next, from_prev = send(to_prev, down), send(to_next, up)
-
-    dense, part = dense_grads(meta, qo, held, given, [stats] + others)
+    others = [send_tp(stats, along_z(n)) for n in range(1, 4)]
+    dense, *part = dense_grads(meta, qo, held, given, [stats] + others)
     dense_other = send(dense[1], partner)
-
-    def add(*xs):
-        return sum(x.astype(F32) for x in xs).astype(BF16)
-
-    near = add(part, send_tp(part, [(4 * z + 2, 4 * z + 1) for z in rows]))
-    part = add(
-        part,
-        send_tp(part, [(4 * z + 3, 4 * z) for z in rows]),
-        send_tp(near, [(4 * z + 1, 4 * z) for z in rows]),
-    )
-    near = add(part, send_tp(part, [(8, 4)]))
-    part = add(part, send_tp(part, [(12, 0)]), send_tp(near, [(4, 0)]))
-    parts = [part] * KEY_HEADS
+    others = [send_tp(part[n], along_x(n)) for n in range(1, 4)]
+    total = add(part[0], *others)
+    others = [send_tp(total, [(4 * n + x, x) for x in four]) for n in range(1, 4)]
+    total = add(total, *others)
+    others = [send_tp(total, [(n, 0)]) for n in range(1, 4)]
+    total = jnp.concatenate([total] + others, axis=1)
+    parts = [total] * KEY_HEADS
     for c in range(1, ctx_size):
-        parts[c // 2 + HALF * (c % 2)] = send(part, [(c * tp_size, 0)])
+        parts[c // 2 + HALF * (c % 2)] = send(total, [(c * tp_size, 0)])
     d_q = put_first(meta, dq, parts)
 
-    first = scatter_pieces(table, back0, blocks)
-    summed = scatter_last(table, meta, back1, first, dense, dense_other, blocks)
+    first = scatter_pieces(table, back[0], blocks)
+    summed = scatter_last(table, meta, back[1], first, dense, dense_other, blocks)
     home = swap(summed).reshape(HALF, 2, GROUPS, CHUNKS, PIECE, HEAD_SIZE)
     d_k, d_v = combine(own, from_prev, from_next, home)
     return d_q, d_k, d_v
@@ -598,6 +620,7 @@
 
 def solution(mesh):
     spec = P(BOTH, None)
+
     return jax.shard_map(
         per_device,
         mesh=mesh,

time: 319 us -> 342 us (1.072)
  waiting for transfers between devices: 81.4 us -> 106 us
  starting transfers between devices: 162 us -> 158 us
    ppermute x38 -> x39, waiting for transfers between devices: 74.4 us -> 92.7 us  [send(): return lax.ppermute(x, BOTH, pairs)]
    all_to_all x6, waiting for transfers between devices: 7.01 us -> 12.8 us  [swap(): return lax.all_to_all(x, BOTH, split_axis=0, concat_axis=0, tiled=True)]
    ppermute x38 -> x39, starting transfers between devices: 77.3 us -> 73 us  [send(): return lax.ppermute(x, BOTH, pairs)]
    pallas_call x2 -> x4, Pallas kernels: 10.5 us -> 13.2 us  [sparse_grads(): pl.pallas_call(sparse_body, out_shape=(jax.ShapeDtypeStruct(q.shape, BF16...]
    unnamed x62 -> x56, local copies, waits for them, and re-layouts: 9.93 us -> 9.94 us
  transfers between devices with their start and end apart: 44 -> 45, of which waited for: 10 -> 22; matrix products, arithmetic and copies ran while one was open for 3% -> 3% of each run, Pallas kernels for 14% -> 14%
where the time goes in v3:
time: 342 us; the launch traced here: 341 us
  starting transfers between devices  158 us (46%)
  waiting for transfers between devices  106 us (31%)
  Pallas kernels  56.2 us (16%)
  local copies, waits for them, and re-layouts  12.4 us (4%)
  other arithmetic  7.4 us (2%)
    ppermute x39, waiting for transfers between devices, send(): return lax.ppermute(x, BOTH, pairs)  92.7 us
    all_to_all x6, starting transfers between devices, swap(): return lax.all_to_all(x, BOTH, split_axis=0, concat_axis=0, tiled=True)  84.9 us
    ppermute x39, starting transfers between devices, send(): return lax.ppermute(x, BOTH, pairs)  73 us
    pallas_call x4, Pallas kernels, sparse_grads(): pl.pallas_call(sparse_body, out_shape=(jax.ShapeDtypeStruct(q.shape, BF16...  13.2 us
    all_to_all x6, waiting for transfers between devices, swap(): return lax.all_to_all(x, BOTH, split_axis=0, concat_axis=0, tiled=True)  12.8 us
    unnamed x56, local copies, waits for them, and re-layouts  9.94 us
    pallas_call x2, Pallas kernels, gather_pieces(): pl.pallas_call(functools.partial(gather_body, rows=rows, chunk=chunk), ou...  7.91 us
  transfers between devices with their start and end apart: 45, of which 22 were waited for; matrix products, arithmetic and copies ran while one was open for 3% of the time, Pallas kernels for 14%

profile of v3, /device:TPU:0, one launch (start us, length us, event | category | flops | bytes accessed | tf_op | source)
XLA Modules:
  0.0 340.6 jit_solution(3259142642286918377)
XLA Ops:
  0.6 2.1 pack_pieces.1
  2.8 11.2 %all-to-all-start = ((bf16[128,2,8,128]{3,2,1,0:T(8,128)(2,1)}), bf16[128,2,8,128]{3,2,1,0:T(8,128)(2,1)S(1)}, u32[]{:S(2)}, u32[]{:S(2)}) async-start(bf16[128,2,8,128]{3,2,1,0:T(8,128)(2,1)} %bitcast.18), calls=%async_computation | async-start | bytes 1048576 | tf_op jit(solution)/shard_map/all_to_all | solution.py:547
  14.7 12.8 %all-to-all-done.held_ref = bf16[128,2,8,128]{3,2,1,0:T(8,128)(2,1)S(1)} async-done(((bf16[128,2,8,128]{3,2,1,0:T(8,128)(2,1)}), bf16[128,2,8,128]{3,2,1,0:T(8,128)(2,1)S(1)}, u32[]{:S(2)}, u32[]{:S(2)}) %all-to-all-start) | async-done | bytes 524320 | tf_op jit(solution)/shard_map/all_to_all | solution.py:547
  28.3 3.9 %gather_pieces.3 = bf16[128,5,8,128]{3,2,1,0:T(8,128)(2,1)} custom-call(s32[1024]{0:T(1024)} %reshape.31.table_ref, bf16[128,2,8,128]{3,2,1,0:T(8,128)(2,1)} %copy-done), custom_call_target="tpu_custom_call" | custom-call | tf_op jit(solution)/shard_map/gather_pieces/pallas_call | solution.py:74
  32.3 4.6 %all-to-all-start.2 = ((bf16[128,5,8,128]{3,2,1,0:T(8,128)(2,1)}), bf16[128,5,8,128]{3,2,1,0:T(8,128)(2,1)S(1)}, u32[]{:S(2)}, u32[]{:S(2)}) async-start(bf16[128,5,8,128]{3,2,1,0:T(8,128)(2,1)} %gather_pieces.3), calls=%async_computation.2 | async-start | bytes 2621440 | tf_op jit(solution)/shard_map/all_to_all | solution.py:547
  37.5 4.6 %spread_heads.1 = (bf16[2,128,1024]{2,1,0:T(8,128)(2,1)}, bf16[2,128,1024]{2,1,0:T(8,128)(2,1)}, bf16[2,128,1024]{2,1,0:T(8,128)(2,1)}, bf16[2,128,1024]{2,1,0:T...) custom-call(s32[3]{0:T(128)} %pad_add_fusion.meta_ref, ...), custom_call_target="tpu_custom_call" | custom-call | tf_op jit(solution)/shard_map/spread_heads/pallas_call | solution.py:477
  42.1 2.1 collective-permute-start.8
  44.2 2.1 collective-permute-start.7
  50.5 2.1 collective-permute-start.4
  52.6 3.5 %collective-permute-done.8 = bf16[2,128,1024]{2,1,0:T(8,128)(2,1)} collective-permute-done((bf16[2,128,1024]{2,1,0:T(8,128)(2,1)}, bf16[2,128,1024]{2,1,0:T(8,128)(2,1)}, u32[]{:S(2)}, u32[]{:S(2)}) %collective-permute-start.8) | collective-permute-done | bytes 524320 | tf_op jit(solution)/shard_map/ppermute | solution.py:550
  58.2 3.5 %collective-permute-done.7 = bf16[2,128,1024]{2,1,0:T(8,128)(2,1)} collective-permute-done((bf16[2,128,1024]{2,1,0:T(8,128)(2,1)}, bf16[2,128,1024]{2,1,0:T(8,128)(2,1)}, u32[]{:S(2)}, u32[]{:S(2)}) %collective-permute-start.7) | collective-permute-done | bytes 524320 | tf_op jit(solution)/shard_map/ppermute | solution.py:550
  63.8 4.0 %gather_pieces.2 = bf16[128,5,8,128]{3,2,1,0:T(8,128)(2,1)} custom-call(s32[1024]{0:T(1024)} %reshape.31.table_ref, bf16[128,2,8,128]{3,2,1,0:T(8,128)(2,1)} %copy-done), custom_call_target="tpu_custom_call" | custom-call | tf_op jit(solution)/shard_map/gather_pieces/pallas_call | solution.py:74
  68.9 5.0 %all-to-all-start.1 = ((bf16[128,5,8,128]{3,2,1,0:T(8,128)(2,1)}), bf16[128,5,8,128]{3,2,1,0:T(8,128)(2,1)S(1)}, u32[]{:S(2)}, u32[]{:S(2)}) async-start(bf16[128,5,8,128]{3,2,1,0:T(8,128)(2,1)} %gather_pieces.2), calls=%async_computation.1 | async-start | bytes 2621440 | tf_op jit(solution)/shard_map/all_to_all | solution.py:547
  74.4 2.2 add_add_fusion
  76.6 2.5 collective-permute-start.9
  79.2 19.1 %collective-permute-done.9 = bf16[2,128,1024]{2,1,0:T(8,128)(2,1)S(1)} collective-permute-done((bf16[2,128,1024]{2,1,0:T(8,128)(2,1)S(1)}, bf16[2,128,1024]{2,1,0:T(8,128)(2,1)S(1)}, u32[]{:S(2)}, u32[]{:S(2)}) %collective-permute-start.9) | collective-permute-done | bytes 524320 | tf_op jit(solution)/shard_map/ppermute | solution.py:550
  99.9 2.6 collective-permute-start
  102.4 4.7 %collective-permute-start.1 = (bf16[2,128,1024]{2,1,0:T(8,128)(2,1)S(1)}, bf16[2,128,1024]{2,1,0:T(8,128)(2,1)S(1)}, u32[]{:S(2)}, u32[]{:S(2)}) collective-permute-start(bf16[2,128,1024]{2,1,0:T(8,128)(2,1)S(1)} %copy-done.3), channel_id=1, source_target_pairs={{0,127},{1,0},{2,1},{3,2},{4,3},{5,4},{6,5},{7,6},{8,7},{9,8},{10,... | collective-permute-start | bytes 1572872 | tf_op jit(solution)/shard_map/ppermute | solution.py:550
  107.1 5.0 %collective-permute-done.10 = bf16[2,128,1024]{2,1,0:T(8,128)(2,1)S(1)} collective-permute-done((bf16[2,128,1024]{2,1,0:T(8,128)(2,1)S(1)}, bf16[2,128,1024]{2,1,0:T(8,128)(2,1)S(1)}, u32[]{:S(2)}, u32[]{:S(2)}) %collective-permute-start.10) | collective-permute-done | bytes 524320 | tf_op jit(solution)/shard_map/ppermute | solution.py:550
  113.1 2.1 collective-permute-start.11
  116.1 3.5 %collective-permute-done.before_ref = bf16[2,128,1024]{2,1,0:T(8,128)(2,1)S(1)} collective-permute-done((bf16[2,128,1024]{2,1,0:T(8,128)(2,1)S(1)}, bf16[2,128,1024]{2,1,0:T(8,128)(2,1)S(1)}, u32[]{:S(2)}, u32[]{:S(2)}) %collective-permute-start) | collective-permute-done | bytes 524320 | tf_op jit(solution)/shard_map/ppermute | solution.py:550
  119.5 2.1 collective-permute-done.1.after_ref
  122.5 3.3 sparse_grads.4
  125.8 3.3 sparse_grads.5
  130.2 30.7 %all-to-all-start.4 = ((bf16[128,5,8,128]{3,2,1,0:T(8,128)(2,1)}), bf16[128,5,8,128]{3,2,1,0:T(8,128)(2,1)S(1)}, u32[]{:S(2)}, u32[]{:S(2)}) async-start(bf16[128,5,8,128]{3,2,1,0:T(8,128)(2,1)} %bitcast.16), calls=%async_computation.4 | async-start | bytes 2621440 | tf_op jit(solution)/shard_map/all_to_all | solution.py:547
  162.2 4.8 %collective-permute-start.12 = (bf16[2,128,1024]{2,1,0:T(8,128)(2,1)S(1)}, bf16[2,128,1024]{2,1,0:T(8,128)(2,1)S(1)}, u32[]{:S(2)}, u32[]{:S(2)}) collective-permute-start(bf16[2,128,1024]{2,1,0:T(8,128)(2,1)S(1)} %add.91), channel_id=1, source_target_pairs={{0,12},{1,13},{2,14},{3,15},{4,8},{5,9},{6,10},{7,11},{16,28},{17,... | collective-permute-start | bytes 1572872 | tf_op jit(solution)/shard_map/ppermute | solution.py:550
  168.8 18.3 %collective-permute-done.12 = bf16[2,128,1024]{2,1,0:T(8,128)(2,1)S(1)} collective-permute-done((bf16[2,128,1024]{2,1,0:T(8,128)(2,1)S(1)}, bf16[2,128,1024]{2,1,0:T(8,128)(2,1)S(1)}, u32[]{:S(2)}, u32[]{:S(2)}) %collective-permute-start.12) | collective-permute-done | bytes 524320 | tf_op jit(solution)/shard_map/ppermute | solution.py:550
  188.9 4.2 %dense_stats.1 = f32[24,128]{1,0:T(8,128)} custom-call(s32[3]{0:T(128)} %pad_add_fusion.meta_ref, bf16[2,128,1024]{2,1,0:T(8,128)(2,1)} %add.92.q_ref, bf16[128,2,8,128]{3,2,1,0:T(8,128)(2,1)} %copy-done, bf16[128,8,128]{2,1,0:T(8,128)(2,1)} %copy-done.11), custom_call_target="tpu_custom_call" | custom-call | tf_op jit(solution)/shard_map/dense_stats/pallas_call | solution.py:352
  193.1 2.5 collective-permute-start.16
  197.2 3.3 sparse_grads.6
  200.5 3.3 sparse_grads.7
  205.0 28.8 %all-to-all-start.3 = ((bf16[128,5,8,128]{3,2,1,0:T(8,128)(2,1)}), bf16[128,5,8,128]{3,2,1,0:T(8,128)(2,1)S(1)}, u32[]{:S(2)}, u32[]{:S(2)}) async-start(bf16[128,5,8,128]{3,2,1,0:T(8,128)(2,1)} %bitcast.15), calls=%async_computation.3 | async-start | bytes 2621440 | tf_op jit(solution)/shard_map/all_to_all | solution.py:547
  234.9 3.2 collective-permute-start.18
  239.3 5.6 %collective-permute-done.18.s2 = f32[24,128]{1,0:T(8,128)S(1)} collective-permute-done((f32[24,128]{1,0:T(8,128)S(1)}, f32[24,128]{1,0:T(8,128)S(1)}, u32[]{:S(2)}, u32[]{:S(2)}) %collective-permute-start.18) | collective-permute-done | bytes 12320 | tf_op jit(solution)/shard_map/ppermute | solution.py:550
  246.9 5.5 %dense_grads.1 = (f32[2,1024,128]{2,1,0:T(8,128)}, bf16[128,256]{1,0:T(8,128)(2,1)}, bf16[128,256]{1,0:T(8,128)(2,1)}, bf16[128,256]{1,0:T(8,128)(2,1)}, bf16[128,256]{1,0:T(8,128)(2,1)}) custom-call(s32[3]{0:T(128)} %pad_add_fusion.meta_ref, bf16[2,128,1024]{2,1,0:T(8,128)(2,1)} %add.92.q_ref, bf16[128,2,8,128]{3,2,1,0:T(8,128)(2,1)} %copy-done, ...), custom_call_target="tpu_custom_call" | custom-call | tf_op jit(solution)/shard_map/dense_grads/pallas_call | solution.py:416
  252.4 5.4 %collective-permute-start.22 = (bf16[128,256]{1,0:T(8,128)(2,1)}, bf16[128,256]{1,0:T(8,128)(2,1)S(1)}, u32[]{:S(2)}, u32[]{:S(2)}) collective-permute-start(bf16[128,256]{1,0:T(8,128)(2,1)} %get-tuple-element.68), channel_id=1, source_target_pairs={{0,3},{1,0},{2,1},{3,2},{4,7},{5,4},{6,5},{7,6},{8,11},{9,8},{10,9... | collective-permute-start | bytes 196616 | tf_op jit(solution)/shard_map/ppermute | solution.py:550
  260.9 3.0 collective-permute-done.21
  270.2 2.3 collective-permute-done.25
  278.0 3.5 %collective-permute-done.28 = bf16[128,256]{1,0:T(8,128)(2,1)S(1)} collective-permute-done((bf16[128,256]{1,0:T(8,128)(2,1)S(1)}, bf16[128,256]{1,0:T(8,128)(2,1)S(1)}, u32[]{:S(2)}, u32[]{:S(2)}) %collective-permute-start.28) | collective-permute-done | bytes 65568 | tf_op jit(solution)/shard_map/ppermute | solution.py:550
  288.3 4.8 %collective-permute-done.29.rest_1_ = bf16[128,1024]{1,0:T(8,128)(2,1)S(1)} collective-permute-done((bf16[128,1024]{1,0:T(8,128)(2,1)S(1)}, bf16[128,1024]{1,0:T(8,128)(2,1)S(1)}, u32[]{:S(2)}, u32[]{:S(2)}) %collective-permute-start.29) | collective-permute-done | bytes 262176 | tf_op jit(solution)/shard_map/ppermute | solution.py:550
  294.0 7.1 %collective-permute-start.37 = (bf16[2,128,1024]{2,1,0:T(8,128)(2,1)S(1)}, bf16[2,128,1024]{2,1,0:T(8,128)(2,1)}, u32[]{:S(2)}, u32[]{:S(2)}) collective-permute-start(bf16[2,128,1024]{2,1,0:T(8,128)(2,1)S(1)} %copy-done.8), channel_id=1, source_target_pairs={{0,127},{1,0},{2,1},{3,2},{4,3},{5,4},{6,5},{7,6},{8,7},{9,8},{10,... | collective-permute-start | bytes 1572872 | tf_op jit(solution)/shard_map/ppermute | solution.py:550
  301.1 5.0 %scatter_pieces.1.first_ref = f32[128,8,128]{2,1,0:T(8,128)} custom-call(s32[1024]{0:T(1024)} %reshape.31.table_ref, bf16[128,5,8,128]{3,2,1,0:T(8,128)(2,1)} %copy-done.7), custom_call_target="tpu_custom_call" | custom-call | tf_op jit(solution)/shard_map/scatter_pieces/pallas_call | solution.py:146
  307.2 6.3 %scatter_last.1 = bf16[128,2,8,128]{3,2,1,0:T(8,128)(2,1)} custom-call(s32[1024]{0:T(1024)} %reshape.31.table_ref, s32[3]{0:T(128)} %pad_add_fusion.meta_ref, bf16[128,5,8,128]{3,2,1,0:T(8,128)(2,1)} %copy-done.6, f32[128,8,128]{2,1,0:T(8,128)} %scatter_pieces.1.first_ref, f32[2,1024,128]{2,1,0:T(8,128)} %get-tuple-element.74.dense_ref, f32[1024,128]{1,0:T(8,128)} %copy-done.14), custom_call_target="tpu_custom_call" | custom-call | tf_op jit(solution)/shard_map/scatter_last/pallas_call | solution.py:163
  313.5 4.6 %all-to-all-start.5 = ((bf16[128,2,8,128]{3,2,1,0:T(8,128)(2,1)}), bf16[128,2,8,128]{3,2,1,0:T(8,128)(2,1)S(1)}, u32[]{:S(2)}, u32[]{:S(2)}) async-start(bf16[128,2,8,128]{3,2,1,0:T(8,128)(2,1)} %scatter_last.1), calls=%async_computation.5 | async-start | bytes 1048576 | tf_op jit(solution)/shard_map/all_to_all | solution.py:547
  322.0 6.4 %collective-permute-done.33.rest_5_ = bf16[128,1024]{1,0:T(8,128)(2,1)S(1)} collective-permute-done((bf16[128,1024]{1,0:T(8,128)(2,1)S(1)}, bf16[128,1024]{1,0:T(8,128)(2,1)S(1)}, u32[]{:S(2)}, u32[]{:S(2)}) %collective-permute-start.33) | collective-permute-done | bytes 262176 | tf_op jit(solution)/shard_map/ppermute | solution.py:550
  330.5 2.8 collective-permute-done.35.rest_7_
  334.0 3.1 put_first.1
  338.0 2.6 combine.1
  (128 shorter events, 60.5 us)
Async XLA Ops:
  2.8 24.8 %all-to-all-start = ((bf16[128,2,8,128]{3,2,1,0:T(8,128)(2,1)}), bf16[128,2,8,128]{3,2,1,0:T(8,128)(2,1)S(1)}, u32[]{:S(2)}, u32[]{:S(2)}) async-start(bf16[128,2,8,128]{3,2,1,0:T(8,128)(2,1)} %bitcast.18), calls=%async_computation | async-start | bytes 1048576 | tf_op jit(solution)/shard_map/all_to_all | solution.py:547
  32.3 35.5 %all-to-all-start.2 = ((bf16[128,5,8,128]{3,2,1,0:T(8,128)(2,1)}), bf16[128,5,8,128]{3,2,1,0:T(8,128)(2,1)S(1)}, u32[]{:S(2)}, u32[]{:S(2)}) async-start(bf16[128,5,8,128]{3,2,1,0:T(8,128)(2,1)} %gather_pieces.3), calls=%async_computation.2 | async-start | bytes 2621440 | tf_op jit(solution)/shard_map/all_to_all | solution.py:547
  42.1 14.0 %collective-permute-start.8 = (bf16[2,128,1024]{2,1,0:T(8,128)(2,1)}, bf16[2,128,1024]{2,1,0:T(8,128)(2,1)}, u32[]{:S(2)}, u32[]{:S(2)}) collective-permute-start(bf16[2,128,1024]{2,1,0:T(8,128)(2,1)} %get-tuple-element.64), channel_id=1, source_target_pairs={{0,112}} | collective-permute-start | bytes 1572872 | tf_op jit(solution)/shard_map/ppermute | solution.py:550
  44.2 17.5 %collective-permute-start.7 = (bf16[2,128,1024]{2,1,0:T(8,128)(2,1)}, bf16[2,128,1024]{2,1,0:T(8,128)(2,1)}, u32[]{:S(2)}, u32[]{:S(2)}) collective-permute-start(bf16[2,128,1024]{2,1,0:T(8,128)(2,1)} %get-tuple-element.63), channel_id=1, source_target_pairs={{0,96}} | collective-permute-start | bytes 1572872 | tf_op jit(solution)/shard_map/ppermute | solution.py:550
  46.4 27.5 %collective-permute-start.6 = (bf16[2,128,1024]{2,1,0:T(8,128)(2,1)}, bf16[2,128,1024]{2,1,0:T(8,128)(2,1)}, u32[]{:S(2)}, u32[]{:S(2)}) collective-permute-start(bf16[2,128,1024]{2,1,0:T(8,128)(2,1)} %get-tuple-element.62), channel_id=1, source_target_pairs={{0,80}} | collective-permute-start | bytes 1572872 | tf_op jit(solution)/shard_map/ppermute | solution.py:550
  48.4 25.4 %collective-permute-start.5 = (bf16[2,128,1024]{2,1,0:T(8,128)(2,1)}, bf16[2,128,1024]{2,1,0:T(8,128)(2,1)}, u32[]{:S(2)}, u32[]{:S(2)}) collective-permute-start(bf16[2,128,1024]{2,1,0:T(8,128)(2,1)} %get-tuple-element.61), channel_id=1, source_target_pairs={{0,64}} | collective-permute-start | bytes 1572872 | tf_op jit(solution)/shard_map/ppermute | solution.py:550
  50.5 23.4 %collective-permute-start.4 = (bf16[2,128,1024]{2,1,0:T(8,128)(2,1)}, bf16[2,128,1024]{2,1,0:T(8,128)(2,1)}, u32[]{:S(2)}, u32[]{:S(2)}) collective-permute-start(bf16[2,128,1024]{2,1,0:T(8,128)(2,1)} %get-tuple-element.60), channel_id=1, source_target_pairs={{0,48}} | collective-permute-start | bytes 1572872 | tf_op jit(solution)/shard_map/ppermute | solution.py:550
  56.2 18.3 %collective-permute-start.3 = (bf16[2,128,1024]{2,1,0:T(8,128)(2,1)}, bf16[2,128,1024]{2,1,0:T(8,128)(2,1)}, u32[]{:S(2)}, u32[]{:S(2)}) collective-permute-start(bf16[2,128,1024]{2,1,0:T(8,128)(2,1)} %get-tuple-element.59), channel_id=1, source_target_pairs={{0,32}} | collective-permute-start | bytes 1572872 | tf_op jit(solution)/shard_map/ppermute | solution.py:550
  61.8 12.7 %collective-permute-start.2 = (bf16[2,128,1024]{2,1,0:T(8,128)(2,1)}, bf16[2,128,1024]{2,1,0:T(8,128)(2,1)}, u32[]{:S(2)}, u32[]{:S(2)}) collective-permute-start(bf16[2,128,1024]{2,1,0:T(8,128)(2,1)} %get-tuple-element.58), channel_id=1, source_target_pairs={{0,16}} | collective-permute-start | bytes 1572872 | tf_op jit(solution)/shard_map/ppermute | solution.py:550
  68.9 60.2 %all-to-all-start.1 = ((bf16[128,5,8,128]{3,2,1,0:T(8,128)(2,1)}), bf16[128,5,8,128]{3,2,1,0:T(8,128)(2,1)S(1)}, u32[]{:S(2)}, u32[]{:S(2)}) async-start(bf16[128,5,8,128]{3,2,1,0:T(8,128)(2,1)} %gather_pieces.2), calls=%async_computation.1 | async-start | bytes 2621440 | tf_op jit(solution)/shard_map/all_to_all | solution.py:547
  76.6 21.7 %collective-permute-start.9 = (bf16[2,128,1024]{2,1,0:T(8,128)(2,1)S(1)}, bf16[2,128,1024]{2,1,0:T(8,128)(2,1)S(1)}, u32[]{:S(2)}, u32[]{:S(2)}) collective-permute-start(bf16[2,128,1024]{2,1,0:T(8,128)(2,1)S(1)} %add_add_fusion), channel_id=1, source_target_pairs={{0,1},{16,17},{32,33},{48,49},{64,65},{80,81},{96,97},{112,113}} | collective-permute-start | bytes 1572872 | tf_op jit(solution)/shard_map/ppermute | solution.py:550
  98.5 13.6 %collective-permute-start.10 = (bf16[2,128,1024]{2,1,0:T(8,128)(2,1)S(1)}, bf16[2,128,1024]{2,1,0:T(8,128)(2,1)S(1)}, u32[]{:S(2)}, u32[]{:S(2)}) collective-permute-start(bf16[2,128,1024]{2,1,0:T(8,128)(2,1)S(1)} %add.89), channel_id=1, source_target_pairs={{0,3},{1,2},{16,19},{17,18},{32,35},{33,34},{48,51},{49,50},{64,67... | collective-permute-start | bytes 1572872 | tf_op jit(solution)/shard_map/ppermute | solution.py:550
  99.9 19.7 %collective-permute-start = (bf16[2,128,1024]{2,1,0:T(8,128)(2,1)S(1)}, bf16[2,128,1024]{2,1,0:T(8,128)(2,1)S(1)}, u32[]{:S(2)}, u32[]{:S(2)}) collective-permute-start(bf16[2,128,1024]{2,1,0:T(8,128)(2,1)S(1)} %copy-done.3), channel_id=1, source_target_pairs={{0,1},{1,2},{2,3},{3,4},{4,5},{5,6},{6,7},{7,8},{8,9},{9,10},{10,1... | collective-permute-start | bytes 1572872 | tf_op jit(solution)/shard_map/ppermute | solution.py:550
  102.4 19.2 %collective-permute-start.1 = (bf16[2,128,1024]{2,1,0:T(8,128)(2,1)S(1)}, bf16[2,128,1024]{2,1,0:T(8,128)(2,1)S(1)}, u32[]{:S(2)}, u32[]{:S(2)}) collective-permute-start(bf16[2,128,1024]{2,1,0:T(8,128)(2,1)S(1)} %copy-done.3), channel_id=1, source_target_pairs={{0,127},{1,0},{2,1},{3,2},{4,3},{5,4},{6,5},{7,6},{8,7},{9,8},{10,... | collective-permute-start | bytes 1572872 | tf_op jit(solution)/shard_map/ppermute | solution.py:550
  113.1 47.7 %collective-permute-start.11 = (bf16[2,128,1024]{2,1,0:T(8,128)(2,1)}, bf16[2,128,1024]{2,1,0:T(8,128)(2,1)}, u32[]{:S(2)}, u32[]{:S(2)}) collective-permute-start(bf16[2,128,1024]{2,1,0:T(8,128)(2,1)} %add.90), channel_id=1, source_target_pairs={{0,4},{1,5},{2,6},{3,7},{16,20},{17,21},{18,22},{19,23},{32,36},{3... | collective-permute-start | bytes 1572872 | tf_op jit(solution)/shard_map/ppermute | solution.py:550
  130.2 73.7 %all-to-all-start.4 = ((bf16[128,5,8,128]{3,2,1,0:T(8,128)(2,1)}), bf16[128,5,8,128]{3,2,1,0:T(8,128)(2,1)S(1)}, u32[]{:S(2)}, u32[]{:S(2)}) async-start(bf16[128,5,8,128]{3,2,1,0:T(8,128)(2,1)} %bitcast.16), calls=%async_computation.4 | async-start | bytes 2621440 | tf_op jit(solution)/shard_map/all_to_all | solution.py:547
  162.2 24.9 %collective-permute-start.12 = (bf16[2,128,1024]{2,1,0:T(8,128)(2,1)S(1)}, bf16[2,128,1024]{2,1,0:T(8,128)(2,1)S(1)}, u32[]{:S(2)}, u32[]{:S(2)}) collective-permute-start(bf16[2,128,1024]{2,1,0:T(8,128)(2,1)S(1)} %add.91), channel_id=1, source_target_pairs={{0,12},{1,13},{2,14},{3,15},{4,8},{5,9},{6,10},{7,11},{16,28},{17,... | collective-permute-start | bytes 1572872 | tf_op jit(solution)/shard_map/ppermute | solution.py:550
  168.8 19.3 %collective-permute-start.13 = (bf16[128,8,128]{2,1,0:T(8,128)(2,1)}, bf16[128,8,128]{2,1,0:T(8,128)(2,1)S(1)}, u32[]{:S(2)}, u32[]{:S(2)}) collective-permute-start(bf16[128,8,128]{2,1,0:T(8,128)(2,1)} %give_pieces.1), channel_id=1, source_target_pairs={{0,16},{1,17},{2,18},{3,19},{4,20},{5,21},{6,22},{7,23},{8,24},{9,... | collective-permute-start | bytes 786440 | tf_op jit(solution)/shard_map/ppermute | solution.py:550
  193.1 10.7 %collective-permute-start.16 = (f32[24,128]{1,0:T(8,128)}, f32[24,128]{1,0:T(8,128)S(1)}, u32[]{:S(2)}, u32[]{:S(2)}) collective-permute-start(f32[24,128]{1,0:T(8,128)} %dense_stats.1), channel_id=1, source_target_pairs={{0,3},{1,0},{2,1},{3,2},{4,7},{5,4},{6,5},{7,6},{8,11},{9,8},{10,9... | collective-permute-start | bytes 36872 | tf_op jit(solution)/shard_map/ppermute | solution.py:550
  195.6 8.2 %collective-permute-start.15 = (f32[24,128]{1,0:T(8,128)}, f32[24,128]{1,0:T(8,128)S(1)}, u32[]{:S(2)}, u32[]{:S(2)}) collective-permute-start(f32[24,128]{1,0:T(8,128)} %dense_stats.1), channel_id=1, source_target_pairs={{0,2},{1,3},{2,0},{3,1},{4,6},{5,7},{6,4},{7,5},{8,10},{9,11},{10,... | collective-permute-start | bytes 36872 | tf_op jit(solution)/shard_map/ppermute | solution.py:550
  196.5 7.3 %collective-permute-start.14 = (f32[24,128]{1,0:T(8,128)}, f32[24,128]{1,0:T(8,128)S(1)}, u32[]{:S(2)}, u32[]{:S(2)}) collective-permute-start(f32[24,128]{1,0:T(8,128)} %dense_stats.1), channel_id=1, source_target_pairs={{0,1},{1,2},{2,3},{3,0},{4,5},{5,6},{6,7},{7,4},{8,9},{9,10},{10,1... | collective-permute-start | bytes 36872 | tf_op jit(solution)/shard_map/ppermute | solution.py:550
  205.0 101.2 %all-to-all-start.3 = ((bf16[128,5,8,128]{3,2,1,0:T(8,128)(2,1)}), bf16[128,5,8,128]{3,2,1,0:T(8,128)(2,1)S(1)}, u32[]{:S(2)}, u32[]{:S(2)}) async-start(bf16[128,5,8,128]{3,2,1,0:T(8,128)(2,1)} %bitcast.15), calls=%async_computation.3 | async-start | bytes 2621440 | tf_op jit(solution)/shard_map/all_to_all | solution.py:547
  233.8 5.6 %collective-permute-start.17 = (f32[24,128]{1,0:T(8,128)S(1)}, f32[24,128]{1,0:T(8,128)S(1)}, u32[]{:S(2)}, u32[]{:S(2)}) collective-permute-start(f32[24,128]{1,0:T(8,128)S(1)} %pad_maximum_fusion.1.s0), channel_id=1, source_target_pairs={{0,4},{1,5},{2,6},{3,7},{4,8},{5,9},{6,10},{7,11},{8,12},{9,13},{1... | collective-permute-start | bytes 36872 | tf_op jit(solution)/shard_map/ppermute | solution.py:550
  234.9 10.0 %collective-permute-start.18 = (f32[24,128]{1,0:T(8,128)S(1)}, f32[24,128]{1,0:T(8,128)S(1)}, u32[]{:S(2)}, u32[]{:S(2)}) collective-permute-start(f32[24,128]{1,0:T(8,128)S(1)} %pad_maximum_fusion.1.s0), channel_id=1, source_target_pairs={{0,8},{1,9},{2,10},{3,11},{4,12},{5,13},{6,14},{7,15},{8,0},{9,1},... | collective-permute-start | bytes 36872 | tf_op jit(solution)/shard_map/ppermute | solution.py:550
  238.2 8.2 %collective-permute-start.19 = (f32[24,128]{1,0:T(8,128)S(1)}, f32[24,128]{1,0:T(8,128)S(1)}, u32[]{:S(2)}, u32[]{:S(2)}) collective-permute-start(f32[24,128]{1,0:T(8,128)S(1)} %pad_maximum_fusion.1.s0), channel_id=1, source_target_pairs={{0,12},{1,13},{2,14},{3,15},{4,0},{5,1},{6,2},{7,3},{8,4},{9,5},{1... | collective-permute-start | bytes 36872 | tf_op jit(solution)/shard_map/ppermute | solution.py:550
  252.4 40.7 %copy-start.9 = (bf16[2,128,1024]{2,1,0:T(8,128)(2,1)S(1)}, bf16[2,128,1024]{2,1,0:T(8,128)(2,1)}, u32[]{:S(2)}) copy-start(bf16[2,128,1024]{2,1,0:T(8,128)(2,1)} %get-tuple-element.70) | copy-start | bytes 1572868
  252.4 41.6 %copy-start.8 = (bf16[2,128,1024]{2,1,0:T(8,128)(2,1)S(1)}, bf16[2,128,1024]{2,1,0:T(8,128)(2,1)}, u32[]{:S(2)}) copy-start(bf16[2,128,1024]{2,1,0:T(8,128)(2,1)} %get-tuple-element.71) | copy-start | bytes 1572868
  252.4 8.5 %collective-permute-start.22 = (bf16[128,256]{1,0:T(8,128)(2,1)}, bf16[128,256]{1,0:T(8,128)(2,1)S(1)}, u32[]{:S(2)}, u32[]{:S(2)}) collective-permute-start(bf16[128,256]{1,0:T(8,128)(2,1)} %get-tuple-element.68), channel_id=1, source_target_pairs={{0,3},{1,0},{2,1},{3,2},{4,7},{5,4},{6,5},{7,6},{8,11},{9,8},{10,9... | collective-permute-start | bytes 196616 | tf_op jit(solution)/shard_map/ppermute | solution.py:550
  257.8 6.1 %collective-permute-start.21 = (bf16[128,256]{1,0:T(8,128)(2,1)}, bf16[128,256]{1,0:T(8,128)(2,1)S(1)}, u32[]{:S(2)}, u32[]{:S(2)}) collective-permute-start(bf16[128,256]{1,0:T(8,128)(2,1)} %get-tuple-element.67), channel_id=1, source_target_pairs={{0,2},{1,3},{2,0},{3,1},{4,6},{5,7},{6,4},{7,5},{8,10},{9,11},{10,... | collective-permute-start | bytes 196616 | tf_op jit(solution)/shard_map/ppermute | solution.py:550
  257.8 6.4 %collective-permute-start.20 = (bf16[128,256]{1,0:T(8,128)(2,1)}, bf16[128,256]{1,0:T(8,128)(2,1)S(1)}, u32[]{:S(2)}, u32[]{:S(2)}) collective-permute-start(bf16[128,256]{1,0:T(8,128)(2,1)} %get-tuple-element.66), channel_id=1, source_target_pairs={{0,1},{1,2},{2,3},{3,0},{4,5},{5,6},{6,7},{7,4},{8,9},{9,10},{10,1... | collective-permute-start | bytes 196616 | tf_op jit(solution)/shard_map/ppermute | solution.py:550
  265.1 7.4 %collective-permute-start.25 = (bf16[128,256]{1,0:T(8,128)(2,1)S(1)}, bf16[128,256]{1,0:T(8,128)(2,1)S(1)}, u32[]{:S(2)}, u32[]{:S(2)}) collective-permute-start(bf16[128,256]{1,0:T(8,128)(2,1)S(1)} %add_convert_fusion.1), channel_id=1, source_target_pairs={{12,0},{13,1},{14,2},{15,3},{28,16},{29,17},{30,18},{31,19},{44,32... | collective-permute-start | bytes 196616 | tf_op jit(solution)/shard_map/ppermute | solution.py:550
  266.4 7.7 %collective-permute-start.24 = (bf16[128,256]{1,0:T(8,128)(2,1)S(1)}, bf16[128,256]{1,0:T(8,128)(2,1)S(1)}, u32[]{:S(2)}, u32[]{:S(2)}) collective-permute-start(bf16[128,256]{1,0:T(8,128)(2,1)S(1)} %add_convert_fusion.1), channel_id=1, source_target_pairs={{8,0},{9,1},{10,2},{11,3},{24,16},{25,17},{26,18},{27,19},{40,32},... | collective-permute-start | bytes 196616 | tf_op jit(solution)/shard_map/ppermute | solution.py:550
  267.7 6.4 %collective-permute-start.23 = (bf16[128,256]{1,0:T(8,128)(2,1)S(1)}, bf16[128,256]{1,0:T(8,128)(2,1)S(1)}, u32[]{:S(2)}, u32[]{:S(2)}) collective-permute-start(bf16[128,256]{1,0:T(8,128)(2,1)S(1)} %add_convert_fusion.1), channel_id=1, source_target_pairs={{4,0},{5,1},{6,2},{7,3},{20,16},{21,17},{22,18},{23,19},{36,32},{3... | collective-permute-start | bytes 196616 | tf_op jit(solution)/shard_map/ppermute | solution.py:550
  270.1 23.0 %collective-permute-start.38 = (f32[1024,128]{1,0:T(8,128)S(1)}, f32[1024,128]{1,0:T(8,128)S(1)}, u32[]{:S(2)}, u32[]{:S(2)}) collective-permute-start(f32[1024,128]{1,0:T(8,128)S(1)} %slice_bitcast_fusion), channel_id=1, source_target_pairs={{0,16},{1,17},{2,18},{3,19},{4,20},{5,21},{6,22},{7,23},{8,24},{9,... | collective-permute-start | bytes 1572872 | tf_op jit(solution)/shard_map/ppermute | solution.py:550
  274.1 7.4 %collective-permute-start.28 = (bf16[128,256]{1,0:T(8,128)(2,1)S(1)}, bf16[128,256]{1,0:T(8,128)(2,1)S(1)}, u32[]{:S(2)}, u32[]{:S(2)}) collective-permute-start(bf16[128,256]{1,0:T(8,128)(2,1)S(1)} %add_convert_fusion), channel_id=1, source_target_pairs={{3,0},{19,16},{35,32},{51,48},{67,64},{83,80},{99,96},{115,112}} | collective-permute-start | bytes 196616 | tf_op jit(solution)/shard_map/ppermute | solution.py:550
  275.4 7.7 %collective-permute-start.27 = (bf16[128,256]{1,0:T(8,128)(2,1)S(1)}, bf16[128,256]{1,0:T(8,128)(2,1)S(1)}, u32[]{:S(2)}, u32[]{:S(2)}) collective-permute-start(bf16[128,256]{1,0:T(8,128)(2,1)S(1)} %add_convert_fusion), channel_id=1, source_target_pairs={{2,0},{18,16},{34,32},{50,48},{66,64},{82,80},{98,96},{114,112}} | collective-permute-start | bytes 196616 | tf_op jit(solution)/shard_map/ppermute | solution.py:550
  276.7 6.4 %collective-permute-start.26 = (bf16[128,256]{1,0:T(8,128)(2,1)S(1)}, bf16[128,256]{1,0:T(8,128)(2,1)S(1)}, u32[]{:S(2)}, u32[]{:S(2)}) collective-permute-start(bf16[128,256]{1,0:T(8,128)(2,1)S(1)} %add_convert_fusion), channel_id=1, source_target_pairs={{1,0},{17,16},{33,32},{49,48},{65,64},{81,80},{97,96},{113,112}} | collective-permute-start | bytes 196616 | tf_op jit(solution)/shard_map/ppermute | solution.py:550
  283.1 10.0 %collective-permute-start.29 = (bf16[128,1024]{1,0:T(8,128)(2,1)S(1)}, bf16[128,1024]{1,0:T(8,128)(2,1)S(1)}, u32[]{:S(2)}, u32[]{:S(2)}) collective-permute-start(bf16[128,1024]{1,0:T(8,128)(2,1)S(1)} %pad_maximum_fusion.rest_0_), channel_id=1, source_target_pairs={{32,0}} | collective-permute-start | bytes 786440 | tf_op jit(solution)/shard_map/ppermute | solution.py:550
  284.4 33.7 %collective-permute-start.30 = (bf16[128,1024]{1,0:T(8,128)(2,1)S(1)}, bf16[128,1024]{1,0:T(8,128)(2,1)}, u32[]{:S(2)}, u32[]{:S(2)}) collective-permute-start(bf16[128,1024]{1,0:T(8,128)(2,1)S(1)} %pad_maximum_fusion.rest_0_), channel_id=1, source_target_pairs={{64,0}} | collective-permute-start | bytes 786440 | tf_op jit(solution)/shard_map/ppermute | solution.py:550
  285.7 33.7 %collective-permute-start.31 = (bf16[128,1024]{1,0:T(8,128)(2,1)S(1)}, bf16[128,1024]{1,0:T(8,128)(2,1)}, u32[]{:S(2)}, u32[]{:S(2)}) collective-permute-start(bf16[128,1024]{1,0:T(8,128)(2,1)S(1)} %pad_maximum_fusion.rest_0_), channel_id=1, source_target_pairs={{96,0}} | collective-permute-start | bytes 786440 | tf_op jit(solution)/shard_map/ppermute | solution.py:550
  287.0 33.7 %collective-permute-start.32 = (bf16[128,1024]{1,0:T(8,128)(2,1)S(1)}, bf16[128,1024]{1,0:T(8,128)(2,1)}, u32[]{:S(2)}, u32[]{:S(2)}) collective-permute-start(bf16[128,1024]{1,0:T(8,128)(2,1)S(1)} %pad_maximum_fusion.rest_0_), channel_id=1, source_target_pairs={{16,0}} | collective-permute-start | bytes 786440 | tf_op jit(solution)/shard_map/ppermute | solution.py:550
  293.1 40.2 %copy-start.16 = (bf16[128,1024]{1,0:T(8,128)(2,1)}, bf16[128,1024]{1,0:T(8,128)(2,1)S(1)}, u32[]{:S(2)}) copy-start(bf16[128,1024]{1,0:T(8,128)(2,1)S(1)} %collective-permute-done.29.rest_1_) | copy-start | bytes 786436
  293.1 43.9 %collective-permute-start.36 = (bf16[2,128,1024]{2,1,0:T(8,128)(2,1)S(1)}, bf16[2,128,1024]{2,1,0:T(8,128)(2,1)S(1)}, u32[]{:S(2)}, u32[]{:S(2)}) collective-permute-start(bf16[2,128,1024]{2,1,0:T(8,128)(2,1)S(1)} %copy-done.9), channel_id=1, source_target_pairs={{0,1},{1,2},{2,3},{3,4},{4,5},{5,6},{6,7},{7,8},{8,9},{9,10},{10,1... | collective-permute-start | bytes 1572872 | tf_op jit(solution)/shard_map/ppermute | solution.py:550
  294.0 43.1 %collective-permute-start.37 = (bf16[2,128,1024]{2,1,0:T(8,128)(2,1)S(1)}, bf16[2,128,1024]{2,1,0:T(8,128)(2,1)}, u32[]{:S(2)}, u32[]{:S(2)}) collective-permute-start(bf16[2,128,1024]{2,1,0:T(8,128)(2,1)S(1)} %copy-done.8), channel_id=1, source_target_pairs={{0,127},{1,0},{2,1},{3,2},{4,3},{5,4},{6,5},{7,6},{8,7},{9,8},{10,... | collective-permute-start | bytes 1572872 | tf_op jit(solution)/shard_map/ppermute | solution.py:550
  313.5 23.6 %all-to-all-start.5 = ((bf16[128,2,8,128]{3,2,1,0:T(8,128)(2,1)}), bf16[128,2,8,128]{3,2,1,0:T(8,128)(2,1)S(1)}, u32[]{:S(2)}, u32[]{:S(2)}) async-start(bf16[128,2,8,128]{3,2,1,0:T(8,128)(2,1)} %scatter_last.1), calls=%async_computation.5 | async-start | bytes 1048576 | tf_op jit(solution)/shard_map/all_to_all | solution.py:547
  318.1 10.3 %collective-permute-start.33 = (bf16[128,1024]{1,0:T(8,128)(2,1)S(1)}, bf16[128,1024]{1,0:T(8,128)(2,1)S(1)}, u32[]{:S(2)}, u32[]{:S(2)}) collective-permute-start(bf16[128,1024]{1,0:T(8,128)(2,1)S(1)} %pad_maximum_fusion.rest_0_), channel_id=1, source_target_pairs={{48,0}} | collective-permute-start | bytes 786440 | tf_op jit(solution)/shard_map/ppermute | solution.py:550
  319.4 11.1 %collective-permute-start.34 = (bf16[128,1024]{1,0:T(8,128)(2,1)S(1)}, bf16[128,1024]{1,0:T(8,128)(2,1)S(1)}, u32[]{:S(2)}, u32[]{:S(2)}) collective-permute-start(bf16[128,1024]{1,0:T(8,128)(2,1)S(1)} %pad_maximum_fusion.rest_0_), channel_id=1, source_target_pairs={{80,0}} | collective-permute-start | bytes 786440 | tf_op jit(solution)/shard_map/ppermute | solution.py:550
  320.7 12.5 %collective-permute-start.35 = (bf16[128,1024]{1,0:T(8,128)(2,1)S(1)}, bf16[128,1024]{1,0:T(8,128)(2,1)S(1)}, u32[]{:S(2)}, u32[]{:S(2)}) collective-permute-start(bf16[128,1024]{1,0:T(8,128)(2,1)S(1)} %pad_maximum_fusion.rest_0_), channel_id=1, source_target_pairs={{112,0}} | collective-permute-start | bytes 786440 | tf_op jit(solution)/shard_map/ppermute | solution.py:550
  (24 other events, 164.0 us)

commit v4 on v3

--- a/solution.py
+++ b/solution.py
@@ -187,6 +187,12 @@
     return jnp.concatenate([first, second], axis=0)
 
 
+def dynamic_heads(ref, p):
+    at = pl.multiple_of(2 * p * HEAD_SIZE, 2 * HEAD_SIZE)
+    both = ref[:, pl.ds(at, 2 * HEAD_SIZE)]
+    return jnp.concatenate([both[:, :HEAD_SIZE], both[:, HEAD_SIZE:]], axis=0)
+
+
 def col_sum(x):
     return jnp.sum(x, axis=0, keepdims=True)
 
@@ -216,13 +222,9 @@
                 dst[at : at + BLOCK] = g_ref[0, kv, :, s].reshape(BLOCK, HEAD_SIZE)
         kt[...] = kc[...].T
         live = [valid_ref[b * NB + s] > 0 for s in range(NB)]
-        dk[...] = jnp.zeros_like(dk)
-        dv[...] = jnp.zeros_like(dv)
 
         def heads(ref, p):
-            at = pl.multiple_of(2 * p * HEAD_SIZE, 2 * HEAD_SIZE)
-            both = ref[:, pl.ds(at, 2 * HEAD_SIZE)]
-            return jnp.concatenate([both[:, :HEAD_SIZE], both[:, HEAD_SIZE:]], axis=0)
+            return two_heads(ref, p)
 
         def pair(p, w):
             qp = heads(q_ref, p)
@@ -252,18 +254,19 @@
                 ds[w, rows] = (weights * (dp[w, rows] - delta)).astype(BF16)
             new_dv = dot(pb[w], op, 1, 0)
             new_dk = dot(ds[w], qp, 1, 0)
-            dv[...] += new_dv
-            dk[...] += new_dk
+            dv[...] = new_dv if p == 0 else dv[...] + new_dv
+            dk[...] = new_dk if p == 0 else dk[...] + new_dk
             dqt = dot(kt[...], ds[w], 1, 0) * SCALING
             out = jnp.concatenate([dqt[:, :BLOCK].T, dqt[:, BLOCK:].T], axis=1).astype(BF16)
-            dq_ref[:, pl.ds(pl.multiple_of(2 * p * HEAD_SIZE, 2 * HEAD_SIZE), 2 * HEAD_SIZE)] = out
+            dq_ref[:, pl.ds(2 * p * HEAD_SIZE, 2 * HEAD_SIZE)] = out
 
         def two_pairs(i, carry):
             for w in range(2):
                 pair(2 * i + w, w)
             return carry
 
-        lax.fori_loop(0, GROUP_SIZE // 4, two_pairs, 0)
+        for i in range(GROUP_SIZE // 4):
+            two_pairs(i, 0)
         for kv, acc, factor in ((0, dk, SCALING), (1, dv, 1.0)):
             prev_ref[kv] = (acc[0:BLOCK] * factor).astype(BF16)
             own_ref[kv] = acc[BLOCK : 2 * BLOCK] * factor
@@ -336,15 +339,19 @@
 
 def stats_body(meta_ref, q_ref, held_ref, other_ref, out_ref, kc, vc):
     load_held(meta_ref, held_ref, other_ref, kc, vc)
-    for p in range(GROUP_SIZE // 2):
-        scores = dot(kc[...], two_heads(q_ref.at[0], p), 1, 1)
-        grads = dot(vc[...], two_heads(q_ref.at[1], p), 1, 1)
+
+    def pair(p, carry):
+        scores = dot(kc[...], dynamic_heads(q_ref.at[0], p), 1, 1)
+        grads = dot(vc[...], dynamic_heads(q_ref.at[1], p), 1, 1)
         top = jnp.max(scores, axis=0, keepdims=True) * EXP_SCALE
         raised = jnp.exp2(scores * EXP_SCALE - top)
         for n, row in enumerate((top, col_sum(raised), col_sum(raised * grads))):
             for j in range(2):
                 at = n * GROUP_SIZE + 2 * p + j
-                out_ref[at : at + 1] = row[:, j * BLOCK : (j + 1) * BLOCK]
+                out_ref[pl.ds(at, 1)] = row[:, j * BLOCK : (j + 1) * BLOCK]
+        return carry
+
+    lax.fori_loop(0, GROUP_SIZE // 2, pair, 0)
 
 
 def dense_stats(meta, qo, held, other):
@@ -377,37 +384,38 @@
     stats[...] = merge_stats([s0[...], s1[...], s2[...], s3[...]])
     core = meta_ref[1]
 
-    for m, dq_ref in enumerate((d0, d1, d2, d3)):
+    dkv_ref[...] = jnp.zeros_like(dkv_ref)
+
+    def pair(m, carry):
         p = lax.rem(meta_ref[2] + m, 4)
 
         def row(n):
             at = n * GROUP_SIZE + 2 * p
             return jnp.concatenate([stats[pl.ds(at, 1)], stats[pl.ds(at + 1, 1)]], axis=1)
 
-        def heads(ref):
-            at = pl.multiple_of(2 * p * HEAD_SIZE, 2 * HEAD_SIZE)
-            both = ref[:, pl.ds(at, 2 * HEAD_SIZE)]
-            return jnp.concatenate([both[:, :HEAD_SIZE], both[:, HEAD_SIZE:]], axis=0)
-
         top = row(0)
         inverse = 1.0 / row(1)
         delta = row(2) * inverse
-        qp = heads(q_ref.at[0])
-        op = heads(q_ref.at[1])
+        qp = dynamic_heads(q_ref.at[0], p)
+        op = dynamic_heads(q_ref.at[1], p)
         scores = dot(kc[...], qp, 1, 1)
         grads = dot(vc[...], op, 1, 1)
         weights = jnp.exp2(scores * EXP_SCALE - top) * inverse
         rounded = weights.astype(BF16)
         score_grad = (weights * (grads - delta)).astype(BF16)
-        new_dk = dot(score_grad, qp, 1, 0) * SCALING
-        new_dv = dot(rounded, op, 1, 0)
-        dkv_ref[core] = new_dk if m == 0 else dkv_ref[core] + new_dk
-        dkv_ref[1 - core] = new_dv if m == 0 else dkv_ref[1 - core] + new_dv
+        dkv_ref[core] += dot(score_grad, qp, 1, 0) * SCALING
+        dkv_ref[1 - core] += dot(rounded, op, 1, 0)
         dqt = dot(kt[...], score_grad, 1, 0) * SCALING
-        for j in range(2):
-            dq_ref[:, j * HEAD_SIZE : (j + 1) * HEAD_SIZE] = (
-                dqt[:, j * BLOCK : (j + 1) * BLOCK].T.astype(BF16)
-            )
+        out = jnp.concatenate([dqt[:, :BLOCK].T, dqt[:, BLOCK:].T], axis=1).astype(BF16)
+        for n, dq_ref in enumerate((d0, d1, d2, d3)):
+
+            @pl.when(m == n)
+            def _():
+                dq_ref[...] = out
+
+        return carry
+
+    lax.fori_loop(0, 4, pair, 0)
 
 
 def dense_grads(meta, qo, held, other, stats):
@@ -563,8 +571,9 @@
     before, after = send(both, up), send(both, down)
     slices = spread_heads(meta, queries, output_gradient)
     qo = jnp.where(b_index == 0, slices[0], jnp.zeros_like(slices[0]))
-    for c in range(1, ctx_size):
-        qo = qo + send(slices[c // 2 + HALF * (c % 2)], [(0, c * tp_size)])
+    for c in (4, 2, 6, 3, 5, 7, 1):
+        moved = send(slices[c // 2 + HALF * (c % 2)], [(0, c * tp_size)])
+        qo = qo + moved
 
     listed = []
     for j in range(CHUNKS):
@@ -576,10 +585,14 @@
     for j in range(CHUNKS):
         got.append(swap(listed[j]).reshape(shape))
 
-    qo = qo + send_tp(qo, [(0, 1)])
-    qo = qo + send_tp(qo, [(0, 3), (1, 2)])
-    qo = qo + send_tp(qo, [(x, 4 + x) for x in four])
-    qo = qo + send_tp(qo, [(x, 12 + x) for x in four] + [(4 + x, 8 + x) for x in four])
+    moved = send_tp(qo, [(0, 1)])
+    qo = qo + moved
+    moved = send_tp(qo, [(0, 3), (1, 2)])
+    qo = qo + moved
+    moved = send_tp(qo, [(x, 4 + x) for x in four])
+    qo = qo + moved
+    moved = send_tp(qo, [(x, 12 + x) for x in four] + [(4 + x, 8 + x) for x in four])
+    qo = qo + moved
 
     grads, back = (), []
     calls = HALF // CALL_HEADS

time: 342 us -> 336 us (0.982)
  starting transfers between devices: 158 us -> 152 us
    all_to_all x6, starting transfers between devices: 84.9 us -> 80 us  [swap(): return lax.all_to_all(x, BOTH, split_axis=0, concat_axis=0, tiled=True)]
  transfers between devices with their start and end apart: 45 -> 45, of which waited for: 22 -> 21; matrix products, arithmetic and copies ran while one was open for 3% -> 3% of each run, Pallas kernels for 14% -> 15%
where the time goes in v4:
time: 336 us; the launch traced here: 334 us
  starting transfers between devices  152 us (45%)
  waiting for transfers between devices  103 us (31%)
  Pallas kernels  57.9 us (17%)
  local copies, waits for them, and re-layouts  12.4 us (4%)
  other arithmetic  7.4 us (2%)
    ppermute x39, waiting for transfers between devices, send(): return lax.ppermute(x, BOTH, pairs)  89.9 us
    all_to_all x6, starting transfers between devices, swap(): return lax.all_to_all(x, BOTH, split_axis=0, concat_axis=0, tiled=True)  80 us
    ppermute x39, starting transfers between devices, send(): return lax.ppermute(x, BOTH, pairs)  72.2 us
    pallas_call x4, Pallas kernels, sparse_grads(): pl.pallas_call(sparse_body, out_shape=(jax.ShapeDtypeStruct(q.shape, BF16...  13.2 us
    all_to_all x6, waiting for transfers between devices, swap(): return lax.all_to_all(x, BOTH, split_axis=0, concat_axis=0, tiled=True)  12.8 us
    unnamed x56, local copies, waits for them, and re-layouts  9.92 us
    pallas_call x2, Pallas kernels, gather_pieces(): pl.pallas_call(functools.partial(gather_body, rows=rows, chunk=chunk), ou...  7.91 us
  transfers between devices with their start and end apart: 45, of which 21 were waited for; matrix products, arithmetic and copies ran while one was open for 3% of the time, Pallas kernels for 15%

profile of v4, /device:TPU:0, one launch (start us, length us, event | category | flops | bytes accessed | tf_op | source)
XLA Modules:
  0.0 333.7 jit_solution(3195133074044877337)
XLA Ops:
  0.6 2.1 pack_pieces.1
  2.8 11.2 %all-to-all-start = ((bf16[128,2,8,128]{3,2,1,0:T(8,128)(2,1)}), bf16[128,2,8,128]{3,2,1,0:T(8,128)(2,1)S(1)}, u32[]{:S(2)}, u32[]{:S(2)}) async-start(bf16[128,2,8,128]{3,2,1,0:T(8,128)(2,1)} %bitcast.18), calls=%async_computation | async-start | bytes 1048576 | tf_op jit(solution)/shard_map/all_to_all | solution.py:555
  14.7 12.8 %all-to-all-done.held_ref = bf16[128,2,8,128]{3,2,1,0:T(8,128)(2,1)S(1)} async-done(((bf16[128,2,8,128]{3,2,1,0:T(8,128)(2,1)}), bf16[128,2,8,128]{3,2,1,0:T(8,128)(2,1)S(1)}, u32[]{:S(2)}, u32[]{:S(2)}) %all-to-all-start) | async-done | bytes 524320 | tf_op jit(solution)/shard_map/all_to_all | solution.py:555
  28.3 3.9 %gather_pieces.3 = bf16[128,5,8,128]{3,2,1,0:T(8,128)(2,1)} custom-call(s32[1024]{0:T(1024)} %reshape.31.table_ref, bf16[128,2,8,128]{3,2,1,0:T(8,128)(2,1)} %copy-done), custom_call_target="tpu_custom_call" | custom-call | tf_op jit(solution)/shard_map/gather_pieces/pallas_call | solution.py:74
  32.3 4.6 %all-to-all-start.2 = ((bf16[128,5,8,128]{3,2,1,0:T(8,128)(2,1)}), bf16[128,5,8,128]{3,2,1,0:T(8,128)(2,1)S(1)}, u32[]{:S(2)}, u32[]{:S(2)}) async-start(bf16[128,5,8,128]{3,2,1,0:T(8,128)(2,1)} %gather_pieces.3), calls=%async_computation.2 | async-start | bytes 2621440 | tf_op jit(solution)/shard_map/all_to_all | solution.py:555
  37.5 4.5 %spread_heads.1 = (bf16[2,128,1024]{2,1,0:T(8,128)(2,1)}, bf16[2,128,1024]{2,1,0:T(8,128)(2,1)}, bf16[2,128,1024]{2,1,0:T(8,128)(2,1)}, bf16[2,128,1024]{2,1,0:T...) custom-call(s32[3]{0:T(128)} %pad_add_fusion.meta_ref, ...), custom_call_target="tpu_custom_call" | custom-call | tf_op jit(solution)/shard_map/spread_heads/pallas_call | solution.py:485
  42.1 2.1 collective-permute-start.8
  44.2 2.1 collective-permute-start.7
  46.4 2.1 collective-permute-start.6
  48.4 2.1 collective-permute-start.5
  50.5 2.1 collective-permute-start.4
  52.6 2.1 collective-permute-start.3
  54.7 2.1 collective-permute-done.7
  58.8 4.0 %gather_pieces.2 = bf16[128,5,8,128]{3,2,1,0:T(8,128)(2,1)} custom-call(s32[1024]{0:T(1024)} %reshape.31.table_ref, bf16[128,2,8,128]{3,2,1,0:T(8,128)(2,1)} %copy-done), custom_call_target="tpu_custom_call" | custom-call | tf_op jit(solution)/shard_map/gather_pieces/pallas_call | solution.py:74
  63.9 4.6 %all-to-all-start.1 = ((bf16[128,5,8,128]{3,2,1,0:T(8,128)(2,1)}), bf16[128,5,8,128]{3,2,1,0:T(8,128)(2,1)S(1)}, u32[]{:S(2)}, u32[]{:S(2)}) async-start(bf16[128,5,8,128]{3,2,1,0:T(8,128)(2,1)} %gather_pieces.2), calls=%async_computation.1 | async-start | bytes 2621440 | tf_op jit(solution)/shard_map/all_to_all | solution.py:555
  68.9 17.2 %collective-permute-done.2 = bf16[2,128,1024]{2,1,0:T(8,128)(2,1)} collective-permute-done((bf16[2,128,1024]{2,1,0:T(8,128)(2,1)}, bf16[2,128,1024]{2,1,0:T(8,128)(2,1)}, u32[]{:S(2)}, u32[]{:S(2)}) %collective-permute-start.2) | collective-permute-done | bytes 524320 | tf_op jit(solution)/shard_map/ppermute | solution.py:558
  86.1 2.2 add_add_fusion
  89.8 11.6 %collective-permute-done.9 = bf16[2,128,1024]{2,1,0:T(8,128)(2,1)S(1)} collective-permute-done((bf16[2,128,1024]{2,1,0:T(8,128)(2,1)S(1)}, bf16[2,128,1024]{2,1,0:T(8,128)(2,1)S(1)}, u32[]{:S(2)}, u32[]{:S(2)}) %collective-permute-start.9) | collective-permute-done | bytes 524320 | tf_op jit(solution)/shard_map/ppermute | solution.py:558
  102.9 2.6 collective-permute-start
  105.5 4.7 %collective-permute-start.1 = (bf16[2,128,1024]{2,1,0:T(8,128)(2,1)S(1)}, bf16[2,128,1024]{2,1,0:T(8,128)(2,1)S(1)}, u32[]{:S(2)}, u32[]{:S(2)}) collective-permute-start(bf16[2,128,1024]{2,1,0:T(8,128)(2,1)S(1)} %copy-done.3), channel_id=1, source_target_pairs={{0,127},{1,0},{2,1},{3,2},{4,3},{5,4},{6,5},{7,6},{8,7},{9,8},{10,... | collective-permute-start | bytes 1572872 | tf_op jit(solution)/shard_map/ppermute | solution.py:558
  111.2 2.1 collective-permute-start.11
  114.1 2.9 collective-permute-done.before_ref
  118.2 3.3 sparse_grads.4
  121.5 3.3 sparse_grads.5
  125.9 28.5 %all-to-all-start.4 = ((bf16[128,5,8,128]{3,2,1,0:T(8,128)(2,1)}), bf16[128,5,8,128]{3,2,1,0:T(8,128)(2,1)S(1)}, u32[]{:S(2)}, u32[]{:S(2)}) async-start(bf16[128,5,8,128]{3,2,1,0:T(8,128)(2,1)} %bitcast.16), calls=%async_computation.4 | async-start | bytes 2621440 | tf_op jit(solution)/shard_map/all_to_all | solution.py:555
  155.8 4.8 %collective-permute-start.12 = (bf16[2,128,1024]{2,1,0:T(8,128)(2,1)S(1)}, bf16[2,128,1024]{2,1,0:T(8,128)(2,1)S(1)}, u32[]{:S(2)}, u32[]{:S(2)}) collective-permute-start(bf16[2,128,1024]{2,1,0:T(8,128)(2,1)S(1)} %add.91), channel_id=1, source_target_pairs={{0,12},{1,13},{2,14},{3,15},{4,8},{5,9},{6,10},{7,11},{16,28},{17,... | collective-permute-start | bytes 1572872 | tf_op jit(solution)/shard_map/ppermute | solution.py:558
  162.4 18.3 %collective-permute-done.12 = bf16[2,128,1024]{2,1,0:T(8,128)(2,1)S(1)} collective-permute-done((bf16[2,128,1024]{2,1,0:T(8,128)(2,1)S(1)}, bf16[2,128,1024]{2,1,0:T(8,128)(2,1)S(1)}, u32[]{:S(2)}, u32[]{:S(2)}) %collective-permute-start.12) | collective-permute-done | bytes 524320 | tf_op jit(solution)/shard_map/ppermute | solution.py:558
  182.4 5.1 %dense_stats.1 = f32[24,128]{1,0:T(8,128)} custom-call(s32[3]{0:T(128)} %pad_add_fusion.meta_ref, bf16[2,128,1024]{2,1,0:T(8,128)(2,1)} %add.92.q_ref, bf16[128,2,8,128]{3,2,1,0:T(8,128)(2,1)} %copy-done, bf16[128,8,128]{2,1,0:T(8,128)(2,1)} %copy-done.11), custom_call_target="tpu_custom_call" | custom-call | tf_op jit(solution)/shard_map/dense_stats/pallas_call | solution.py:359
  187.5 2.5 collective-permute-start.16
  191.6 3.3 sparse_grads.6
  194.9 3.3 sparse_grads.7
  199.4 26.5 %all-to-all-start.3 = ((bf16[128,5,8,128]{3,2,1,0:T(8,128)(2,1)}), bf16[128,5,8,128]{3,2,1,0:T(8,128)(2,1)S(1)}, u32[]{:S(2)}, u32[]{:S(2)}) async-start(bf16[128,5,8,128]{3,2,1,0:T(8,128)(2,1)} %bitcast.15), calls=%async_computation.3 | async-start | bytes 2621440 | tf_op jit(solution)/shard_map/all_to_all | solution.py:555
  227.0 3.2 collective-permute-start.18
  231.4 5.6 %collective-permute-done.18.s2 = f32[24,128]{1,0:T(8,128)S(1)} collective-permute-done((f32[24,128]{1,0:T(8,128)S(1)}, f32[24,128]{1,0:T(8,128)S(1)}, u32[]{:S(2)}, u32[]{:S(2)}) %collective-permute-start.18) | collective-permute-done | bytes 12320 | tf_op jit(solution)/shard_map/ppermute | solution.py:558
  239.0 6.2 %dense_grads.1 = (f32[2,1024,128]{2,1,0:T(8,128)}, bf16[128,256]{1,0:T(8,128)(2,1)}, bf16[128,256]{1,0:T(8,128)(2,1)}, bf16[128,256]{1,0:T(8,128)(2,1)}, bf16[128,256]{1,0:T(8,128)(2,1)}) custom-call(s32[3]{0:T(128)} %pad_add_fusion.meta_ref, bf16[2,128,1024]{2,1,0:T(8,128)(2,1)} %add.92.q_ref, bf16[128,2,8,128]{3,2,1,0:T(8,128)(2,1)} %copy-done, ...), custom_call_target="tpu_custom_call" | custom-call | tf_op jit(solution)/shard_map/dense_grads/pallas_call | solution.py:424
  245.2 5.7 %collective-permute-start.22 = (bf16[128,256]{1,0:T(8,128)(2,1)}, bf16[128,256]{1,0:T(8,128)(2,1)S(1)}, u32[]{:S(2)}, u32[]{:S(2)}) collective-permute-start(bf16[128,256]{1,0:T(8,128)(2,1)} %get-tuple-element.68), channel_id=1, source_target_pairs={{0,3},{1,0},{2,1},{3,2},{4,7},{5,4},{6,5},{7,6},{8,11},{9,8},{10,9... | collective-permute-start | bytes 196616 | tf_op jit(solution)/shard_map/ppermute | solution.py:558
  254.0 3.0 collective-permute-done.21
  263.3 2.3 collective-permute-done.25
  271.1 3.5 %collective-permute-done.28 = bf16[128,256]{1,0:T(8,128)(2,1)S(1)} collective-permute-done((bf16[128,256]{1,0:T(8,128)(2,1)S(1)}, bf16[128,256]{1,0:T(8,128)(2,1)S(1)}, u32[]{:S(2)}, u32[]{:S(2)}) %collective-permute-start.28) | collective-permute-done | bytes 65568 | tf_op jit(solution)/shard_map/ppermute | solution.py:558
  281.4 4.8 %collective-permute-done.29.rest_1_ = bf16[128,1024]{1,0:T(8,128)(2,1)S(1)} collective-permute-done((bf16[128,1024]{1,0:T(8,128)(2,1)S(1)}, bf16[128,1024]{1,0:T(8,128)(2,1)S(1)}, u32[]{:S(2)}, u32[]{:S(2)}) %collective-permute-start.29) | collective-permute-done | bytes 262176 | tf_op jit(solution)/shard_map/ppermute | solution.py:558
  287.0 7.1 %collective-permute-start.37 = (bf16[2,128,1024]{2,1,0:T(8,128)(2,1)S(1)}, bf16[2,128,1024]{2,1,0:T(8,128)(2,1)}, u32[]{:S(2)}, u32[]{:S(2)}) collective-permute-start(bf16[2,128,1024]{2,1,0:T(8,128)(2,1)S(1)} %copy-done.8), channel_id=1, source_target_pairs={{0,127},{1,0},{2,1},{3,2},{4,3},{5,4},{6,5},{7,6},{8,7},{9,8},{10,... | collective-permute-start | bytes 1572872 | tf_op jit(solution)/shard_map/ppermute | solution.py:558
  294.2 5.0 %scatter_pieces.1.first_ref = f32[128,8,128]{2,1,0:T(8,128)} custom-call(s32[1024]{0:T(1024)} %reshape.31.table_ref, bf16[128,5,8,128]{3,2,1,0:T(8,128)(2,1)} %copy-done.7), custom_call_target="tpu_custom_call" | custom-call | tf_op jit(solution)/shard_map/scatter_pieces/pallas_call | solution.py:146
  300.3 6.3 %scatter_last.1 = bf16[128,2,8,128]{3,2,1,0:T(8,128)(2,1)} custom-call(s32[1024]{0:T(1024)} %reshape.31.table_ref, s32[3]{0:T(128)} %pad_add_fusion.meta_ref, bf16[128,5,8,128]{3,2,1,0:T(8,128)(2,1)} %copy-done.6, f32[128,8,128]{2,1,0:T(8,128)} %scatter_pieces.1.first_ref, f32[2,1024,128]{2,1,0:T(8,128)} %get-tuple-element.74.dense_ref, f32[1024,128]{1,0:T(8,128)} %copy-done.14), custom_call_target="tpu_custom_call" | custom-call | tf_op jit(solution)/shard_map/scatter_last/pallas_call | solution.py:163
  306.6 4.6 %all-to-all-start.5 = ((bf16[128,2,8,128]{3,2,1,0:T(8,128)(2,1)}), bf16[128,2,8,128]{3,2,1,0:T(8,128)(2,1)S(1)}, u32[]{:S(2)}, u32[]{:S(2)}) async-start(bf16[128,2,8,128]{3,2,1,0:T(8,128)(2,1)} %scatter_last.1), calls=%async_computation.5 | async-start | bytes 1048576 | tf_op jit(solution)/shard_map/all_to_all | solution.py:555
  315.1 6.4 %collective-permute-done.33.rest_5_ = bf16[128,1024]{1,0:T(8,128)(2,1)S(1)} collective-permute-done((bf16[128,1024]{1,0:T(8,128)(2,1)S(1)}, bf16[128,1024]{1,0:T(8,128)(2,1)S(1)}, u32[]{:S(2)}, u32[]{:S(2)}) %collective-permute-start.33) | collective-permute-done | bytes 262176 | tf_op jit(solution)/shard_map/ppermute | solution.py:558
  323.6 2.8 collective-permute-done.35.rest_7_
  327.0 3.1 put_first.1
  331.1 2.6 combine.1
  (128 shorter events, 55.9 us)
Async XLA Ops:
  2.8 24.8 %all-to-all-start = ((bf16[128,2,8,128]{3,2,1,0:T(8,128)(2,1)}), bf16[128,2,8,128]{3,2,1,0:T(8,128)(2,1)S(1)}, u32[]{:S(2)}, u32[]{:S(2)}) async-start(bf16[128,2,8,128]{3,2,1,0:T(8,128)(2,1)} %bitcast.18), calls=%async_computation | async-start | bytes 1048576 | tf_op jit(solution)/shard_map/all_to_all | solution.py:555
  32.3 30.5 %all-to-all-start.2 = ((bf16[128,5,8,128]{3,2,1,0:T(8,128)(2,1)}), bf16[128,5,8,128]{3,2,1,0:T(8,128)(2,1)S(1)}, u32[]{:S(2)}, u32[]{:S(2)}) async-start(bf16[128,5,8,128]{3,2,1,0:T(8,128)(2,1)} %gather_pieces.3), calls=%async_computation.2 | async-start | bytes 2621440 | tf_op jit(solution)/shard_map/all_to_all | solution.py:555
  42.1 10.5 %collective-permute-start.8 = (bf16[2,128,1024]{2,1,0:T(8,128)(2,1)}, bf16[2,128,1024]{2,1,0:T(8,128)(2,1)}, u32[]{:S(2)}, u32[]{:S(2)}) collective-permute-start(bf16[2,128,1024]{2,1,0:T(8,128)(2,1)} %get-tuple-element.64), channel_id=1, source_target_pairs={{0,16}} | collective-permute-start | bytes 1572872 | tf_op jit(solution)/shard_map/ppermute | solution.py:558
  44.2 12.5 %collective-permute-start.7 = (bf16[2,128,1024]{2,1,0:T(8,128)(2,1)}, bf16[2,128,1024]{2,1,0:T(8,128)(2,1)}, u32[]{:S(2)}, u32[]{:S(2)}) collective-permute-start(bf16[2,128,1024]{2,1,0:T(8,128)(2,1)} %get-tuple-element.63), channel_id=1, source_target_pairs={{0,112}} | collective-permute-start | bytes 1572872 | tf_op jit(solution)/shard_map/ppermute | solution.py:558
  46.4 22.2 %collective-permute-start.6 = (bf16[2,128,1024]{2,1,0:T(8,128)(2,1)}, bf16[2,128,1024]{2,1,0:T(8,128)(2,1)}, u32[]{:S(2)}, u32[]{:S(2)}) collective-permute-start(bf16[2,128,1024]{2,1,0:T(8,128)(2,1)} %get-tuple-element.62), channel_id=1, source_target_pairs={{0,80}} | collective-permute-start | bytes 1572872 | tf_op jit(solution)/shard_map/ppermute | solution.py:558
  48.4 20.1 %collective-permute-start.5 = (bf16[2,128,1024]{2,1,0:T(8,128)(2,1)}, bf16[2,128,1024]{2,1,0:T(8,128)(2,1)}, u32[]{:S(2)}, u32[]{:S(2)}) collective-permute-start(bf16[2,128,1024]{2,1,0:T(8,128)(2,1)} %get-tuple-element.61), channel_id=1, source_target_pairs={{0,48}} | collective-permute-start | bytes 1572872 | tf_op jit(solution)/shard_map/ppermute | solution.py:558
  50.5 18.0 %collective-permute-start.4 = (bf16[2,128,1024]{2,1,0:T(8,128)(2,1)}, bf16[2,128,1024]{2,1,0:T(8,128)(2,1)}, u32[]{:S(2)}, u32[]{:S(2)}) collective-permute-start(bf16[2,128,1024]{2,1,0:T(8,128)(2,1)} %get-tuple-element.60), channel_id=1, source_target_pairs={{0,96}} | collective-permute-start | bytes 1572872 | tf_op jit(solution)/shard_map/ppermute | solution.py:558
  52.6 16.3 %collective-permute-start.3 = (bf16[2,128,1024]{2,1,0:T(8,128)(2,1)}, bf16[2,128,1024]{2,1,0:T(8,128)(2,1)}, u32[]{:S(2)}, u32[]{:S(2)}) collective-permute-start(bf16[2,128,1024]{2,1,0:T(8,128)(2,1)} %get-tuple-element.59), channel_id=1, source_target_pairs={{0,32}} | collective-permute-start | bytes 1572872 | tf_op jit(solution)/shard_map/ppermute | solution.py:558
  56.8 29.3 %collective-permute-start.2 = (bf16[2,128,1024]{2,1,0:T(8,128)(2,1)}, bf16[2,128,1024]{2,1,0:T(8,128)(2,1)}, u32[]{:S(2)}, u32[]{:S(2)}) collective-permute-start(bf16[2,128,1024]{2,1,0:T(8,128)(2,1)} %get-tuple-element.58), channel_id=1, source_target_pairs={{0,64}} | collective-permute-start | bytes 1572872 | tf_op jit(solution)/shard_map/ppermute | solution.py:558
  63.9 60.9 %all-to-all-start.1 = ((bf16[128,5,8,128]{3,2,1,0:T(8,128)(2,1)}), bf16[128,5,8,128]{3,2,1,0:T(8,128)(2,1)S(1)}, u32[]{:S(2)}, u32[]{:S(2)}) async-start(bf16[128,5,8,128]{3,2,1,0:T(8,128)(2,1)} %gather_pieces.2), calls=%async_computation.1 | async-start | bytes 2621440 | tf_op jit(solution)/shard_map/all_to_all | solution.py:555
  88.3 13.0 %collective-permute-start.9 = (bf16[2,128,1024]{2,1,0:T(8,128)(2,1)S(1)}, bf16[2,128,1024]{2,1,0:T(8,128)(2,1)S(1)}, u32[]{:S(2)}, u32[]{:S(2)}) collective-permute-start(bf16[2,128,1024]{2,1,0:T(8,128)(2,1)S(1)} %add_add_fusion), channel_id=1, source_target_pairs={{0,1},{16,17},{32,33},{48,49},{64,65},{80,81},{96,97},{112,113}} | collective-permute-start | bytes 1572872 | tf_op jit(solution)/shard_map/ppermute | solution.py:558
  101.6 8.6 %collective-permute-start.10 = (bf16[2,128,1024]{2,1,0:T(8,128)(2,1)S(1)}, bf16[2,128,1024]{2,1,0:T(8,128)(2,1)S(1)}, u32[]{:S(2)}, u32[]{:S(2)}) collective-permute-start(bf16[2,128,1024]{2,1,0:T(8,128)(2,1)S(1)} %add.89), channel_id=1, source_target_pairs={{0,3},{1,2},{16,19},{17,18},{32,35},{33,34},{48,51},{49,50},{64,67... | collective-permute-start | bytes 1572872 | tf_op jit(solution)/shard_map/ppermute | solution.py:558
  102.9 14.1 %collective-permute-start = (bf16[2,128,1024]{2,1,0:T(8,128)(2,1)S(1)}, bf16[2,128,1024]{2,1,0:T(8,128)(2,1)S(1)}, u32[]{:S(2)}, u32[]{:S(2)}) collective-permute-start(bf16[2,128,1024]{2,1,0:T(8,128)(2,1)S(1)} %copy-done.3), channel_id=1, source_target_pairs={{0,1},{1,2},{2,3},{3,4},{4,5},{5,6},{6,7},{7,8},{8,9},{9,10},{10,1... | collective-permute-start | bytes 1572872 | tf_op jit(solution)/shard_map/ppermute | solution.py:558
  105.5 11.9 %collective-permute-start.1 = (bf16[2,128,1024]{2,1,0:T(8,128)(2,1)S(1)}, bf16[2,128,1024]{2,1,0:T(8,128)(2,1)S(1)}, u32[]{:S(2)}, u32[]{:S(2)}) collective-permute-start(bf16[2,128,1024]{2,1,0:T(8,128)(2,1)S(1)} %copy-done.3), channel_id=1, source_target_pairs={{0,127},{1,0},{2,1},{3,2},{4,3},{5,4},{6,5},{7,6},{8,7},{9,8},{10,... | collective-permute-start | bytes 1572872 | tf_op jit(solution)/shard_map/ppermute | solution.py:558
  111.2 43.2 %collective-permute-start.11 = (bf16[2,128,1024]{2,1,0:T(8,128)(2,1)}, bf16[2,128,1024]{2,1,0:T(8,128)(2,1)}, u32[]{:S(2)}, u32[]{:S(2)}) collective-permute-start(bf16[2,128,1024]{2,1,0:T(8,128)(2,1)} %add.90), channel_id=1, source_target_pairs={{0,4},{1,5},{2,6},{3,7},{16,20},{17,21},{18,22},{19,23},{32,36},{3... | collective-permute-start | bytes 1572872 | tf_op jit(solution)/shard_map/ppermute | solution.py:558
  125.9 72.4 %all-to-all-start.4 = ((bf16[128,5,8,128]{3,2,1,0:T(8,128)(2,1)}), bf16[128,5,8,128]{3,2,1,0:T(8,128)(2,1)S(1)}, u32[]{:S(2)}, u32[]{:S(2)}) async-start(bf16[128,5,8,128]{3,2,1,0:T(8,128)(2,1)} %bitcast.16), calls=%async_computation.4 | async-start | bytes 2621440 | tf_op jit(solution)/shard_map/all_to_all | solution.py:555
  155.8 24.9 %collective-permute-start.12 = (bf16[2,128,1024]{2,1,0:T(8,128)(2,1)S(1)}, bf16[2,128,1024]{2,1,0:T(8,128)(2,1)S(1)}, u32[]{:S(2)}, u32[]{:S(2)}) collective-permute-start(bf16[2,128,1024]{2,1,0:T(8,128)(2,1)S(1)} %add.91), channel_id=1, source_target_pairs={{0,12},{1,13},{2,14},{3,15},{4,8},{5,9},{6,10},{7,11},{16,28},{17,... | collective-permute-start | bytes 1572872 | tf_op jit(solution)/shard_map/ppermute | solution.py:558
  162.4 19.3 %collective-permute-start.13 = (bf16[128,8,128]{2,1,0:T(8,128)(2,1)}, bf16[128,8,128]{2,1,0:T(8,128)(2,1)S(1)}, u32[]{:S(2)}, u32[]{:S(2)}) collective-permute-start(bf16[128,8,128]{2,1,0:T(8,128)(2,1)} %give_pieces.1), channel_id=1, source_target_pairs={{0,16},{1,17},{2,18},{3,19},{4,20},{5,21},{6,22},{7,23},{8,24},{9,... | collective-permute-start | bytes 786440 | tf_op jit(solution)/shard_map/ppermute | solution.py:558
  187.5 10.7 %collective-permute-start.16 = (f32[24,128]{1,0:T(8,128)}, f32[24,128]{1,0:T(8,128)S(1)}, u32[]{:S(2)}, u32[]{:S(2)}) collective-permute-start(f32[24,128]{1,0:T(8,128)} %dense_stats.1), channel_id=1, source_target_pairs={{0,3},{1,0},{2,1},{3,2},{4,7},{5,4},{6,5},{7,6},{8,11},{9,8},{10,9... | collective-permute-start | bytes 36872 | tf_op jit(solution)/shard_map/ppermute | solution.py:558
  190.0 8.2 %collective-permute-start.15 = (f32[24,128]{1,0:T(8,128)}, f32[24,128]{1,0:T(8,128)S(1)}, u32[]{:S(2)}, u32[]{:S(2)}) collective-permute-start(f32[24,128]{1,0:T(8,128)} %dense_stats.1), channel_id=1, source_target_pairs={{0,2},{1,3},{2,0},{3,1},{4,6},{5,7},{6,4},{7,5},{8,10},{9,11},{10,... | collective-permute-start | bytes 36872 | tf_op jit(solution)/shard_map/ppermute | solution.py:558
  190.9 7.3 %collective-permute-start.14 = (f32[24,128]{1,0:T(8,128)}, f32[24,128]{1,0:T(8,128)S(1)}, u32[]{:S(2)}, u32[]{:S(2)}) collective-permute-start(f32[24,128]{1,0:T(8,128)} %dense_stats.1), channel_id=1, source_target_pairs={{0,1},{1,2},{2,3},{3,0},{4,5},{5,6},{6,7},{7,4},{8,9},{9,10},{10,1... | collective-permute-start | bytes 36872 | tf_op jit(solution)/shard_map/ppermute | solution.py:558
  199.4 99.8 %all-to-all-start.3 = ((bf16[128,5,8,128]{3,2,1,0:T(8,128)(2,1)}), bf16[128,5,8,128]{3,2,1,0:T(8,128)(2,1)S(1)}, u32[]{:S(2)}, u32[]{:S(2)}) async-start(bf16[128,5,8,128]{3,2,1,0:T(8,128)(2,1)} %bitcast.15), calls=%async_computation.3 | async-start | bytes 2621440 | tf_op jit(solution)/shard_map/all_to_all | solution.py:555
  225.9 5.6 %collective-permute-start.17 = (f32[24,128]{1,0:T(8,128)S(1)}, f32[24,128]{1,0:T(8,128)S(1)}, u32[]{:S(2)}, u32[]{:S(2)}) collective-permute-start(f32[24,128]{1,0:T(8,128)S(1)} %pad_maximum_fusion.1.s0), channel_id=1, source_target_pairs={{0,4},{1,5},{2,6},{3,7},{4,8},{5,9},{6,10},{7,11},{8,12},{9,13},{1... | collective-permute-start | bytes 36872 | tf_op jit(solution)/shard_map/ppermute | solution.py:558
  227.0 10.0 %collective-permute-start.18 = (f32[24,128]{1,0:T(8,128)S(1)}, f32[24,128]{1,0:T(8,128)S(1)}, u32[]{:S(2)}, u32[]{:S(2)}) collective-permute-start(f32[24,128]{1,0:T(8,128)S(1)} %pad_maximum_fusion.1.s0), channel_id=1, source_target_pairs={{0,8},{1,9},{2,10},{3,11},{4,12},{5,13},{6,14},{7,15},{8,0},{9,1},... | collective-permute-start | bytes 36872 | tf_op jit(solution)/shard_map/ppermute | solution.py:558
  230.2 8.2 %collective-permute-start.19 = (f32[24,128]{1,0:T(8,128)S(1)}, f32[24,128]{1,0:T(8,128)S(1)}, u32[]{:S(2)}, u32[]{:S(2)}) collective-permute-start(f32[24,128]{1,0:T(8,128)S(1)} %pad_maximum_fusion.1.s0), channel_id=1, source_target_pairs={{0,12},{1,13},{2,14},{3,15},{4,0},{5,1},{6,2},{7,3},{8,4},{9,5},{1... | collective-permute-start | bytes 36872 | tf_op jit(solution)/shard_map/ppermute | solution.py:558
  245.2 41.0 %copy-start.9 = (bf16[2,128,1024]{2,1,0:T(8,128)(2,1)S(1)}, bf16[2,128,1024]{2,1,0:T(8,128)(2,1)}, u32[]{:S(2)}) copy-start(bf16[2,128,1024]{2,1,0:T(8,128)(2,1)} %get-tuple-element.70) | copy-start | bytes 1572868
  245.2 41.8 %copy-start.8 = (bf16[2,128,1024]{2,1,0:T(8,128)(2,1)S(1)}, bf16[2,128,1024]{2,1,0:T(8,128)(2,1)}, u32[]{:S(2)}) copy-start(bf16[2,128,1024]{2,1,0:T(8,128)(2,1)} %get-tuple-element.71) | copy-start | bytes 1572868
  245.2 8.8 %collective-permute-start.22 = (bf16[128,256]{1,0:T(8,128)(2,1)}, bf16[128,256]{1,0:T(8,128)(2,1)S(1)}, u32[]{:S(2)}, u32[]{:S(2)}) collective-permute-start(bf16[128,256]{1,0:T(8,128)(2,1)} %get-tuple-element.68), channel_id=1, source_target_pairs={{0,3},{1,0},{2,1},{3,2},{4,7},{5,4},{6,5},{7,6},{8,11},{9,8},{10,9... | collective-permute-start | bytes 196616 | tf_op jit(solution)/shard_map/ppermute | solution.py:558
  250.9 6.1 %collective-permute-start.21 = (bf16[128,256]{1,0:T(8,128)(2,1)}, bf16[128,256]{1,0:T(8,128)(2,1)S(1)}, u32[]{:S(2)}, u32[]{:S(2)}) collective-permute-start(bf16[128,256]{1,0:T(8,128)(2,1)} %get-tuple-element.67), channel_id=1, source_target_pairs={{0,2},{1,3},{2,0},{3,1},{4,6},{5,7},{6,4},{7,5},{8,10},{9,11},{10,... | collective-permute-start | bytes 196616 | tf_op jit(solution)/shard_map/ppermute | solution.py:558
  250.9 6.4 %collective-permute-start.20 = (bf16[128,256]{1,0:T(8,128)(2,1)}, bf16[128,256]{1,0:T(8,128)(2,1)S(1)}, u32[]{:S(2)}, u32[]{:S(2)}) collective-permute-start(bf16[128,256]{1,0:T(8,128)(2,1)} %get-tuple-element.66), channel_id=1, source_target_pairs={{0,1},{1,2},{2,3},{3,0},{4,5},{5,6},{6,7},{7,4},{8,9},{9,10},{10,1... | collective-permute-start | bytes 196616 | tf_op jit(solution)/shard_map/ppermute | solution.py:558
  258.2 7.4 %collective-permute-start.25 = (bf16[128,256]{1,0:T(8,128)(2,1)S(1)}, bf16[128,256]{1,0:T(8,128)(2,1)S(1)}, u32[]{:S(2)}, u32[]{:S(2)}) collective-permute-start(bf16[128,256]{1,0:T(8,128)(2,1)S(1)} %add_convert_fusion.1), channel_id=1, source_target_pairs={{12,0},{13,1},{14,2},{15,3},{28,16},{29,17},{30,18},{31,19},{44,32... | collective-permute-start | bytes 196616 | tf_op jit(solution)/shard_map/ppermute | solution.py:558
  259.5 7.7 %collective-permute-start.24 = (bf16[128,256]{1,0:T(8,128)(2,1)S(1)}, bf16[128,256]{1,0:T(8,128)(2,1)S(1)}, u32[]{:S(2)}, u32[]{:S(2)}) collective-permute-start(bf16[128,256]{1,0:T(8,128)(2,1)S(1)} %add_convert_fusion.1), channel_id=1, source_target_pairs={{8,0},{9,1},{10,2},{11,3},{24,16},{25,17},{26,18},{27,19},{40,32},... | collective-permute-start | bytes 196616 | tf_op jit(solution)/shard_map/ppermute | solution.py:558
  260.8 6.4 %collective-permute-start.23 = (bf16[128,256]{1,0:T(8,128)(2,1)S(1)}, bf16[128,256]{1,0:T(8,128)(2,1)S(1)}, u32[]{:S(2)}, u32[]{:S(2)}) collective-permute-start(bf16[128,256]{1,0:T(8,128)(2,1)S(1)} %add_convert_fusion.1), channel_id=1, source_target_pairs={{4,0},{5,1},{6,2},{7,3},{20,16},{21,17},{22,18},{23,19},{36,32},{3... | collective-permute-start | bytes 196616 | tf_op jit(solution)/shard_map/ppermute | solution.py:558
  263.2 23.0 %collective-permute-start.38 = (f32[1024,128]{1,0:T(8,128)S(1)}, f32[1024,128]{1,0:T(8,128)S(1)}, u32[]{:S(2)}, u32[]{:S(2)}) collective-permute-start(f32[1024,128]{1,0:T(8,128)S(1)} %slice_bitcast_fusion), channel_id=1, source_target_pairs={{0,16},{1,17},{2,18},{3,19},{4,20},{5,21},{6,22},{7,23},{8,24},{9,... | collective-permute-start | bytes 1572872 | tf_op jit(solution)/shard_map/ppermute | solution.py:558
  267.2 7.4 %collective-permute-start.28 = (bf16[128,256]{1,0:T(8,128)(2,1)S(1)}, bf16[128,256]{1,0:T(8,128)(2,1)S(1)}, u32[]{:S(2)}, u32[]{:S(2)}) collective-permute-start(bf16[128,256]{1,0:T(8,128)(2,1)S(1)} %add_convert_fusion), channel_id=1, source_target_pairs={{3,0},{19,16},{35,32},{51,48},{67,64},{83,80},{99,96},{115,112}} | collective-permute-start | bytes 196616 | tf_op jit(solution)/shard_map/ppermute | solution.py:558
  268.5 7.7 %collective-permute-start.27 = (bf16[128,256]{1,0:T(8,128)(2,1)S(1)}, bf16[128,256]{1,0:T(8,128)(2,1)S(1)}, u32[]{:S(2)}, u32[]{:S(2)}) collective-permute-start(bf16[128,256]{1,0:T(8,128)(2,1)S(1)} %add_convert_fusion), channel_id=1, source_target_pairs={{2,0},{18,16},{34,32},{50,48},{66,64},{82,80},{98,96},{114,112}} | collective-permute-start | bytes 196616 | tf_op jit(solution)/shard_map/ppermute | solution.py:558
  269.8 6.4 %collective-permute-start.26 = (bf16[128,256]{1,0:T(8,128)(2,1)S(1)}, bf16[128,256]{1,0:T(8,128)(2,1)S(1)}, u32[]{:S(2)}, u32[]{:S(2)}) collective-permute-start(bf16[128,256]{1,0:T(8,128)(2,1)S(1)} %add_convert_fusion), channel_id=1, source_target_pairs={{1,0},{17,16},{33,32},{49,48},{65,64},{81,80},{97,96},{113,112}} | collective-permute-start | bytes 196616 | tf_op jit(solution)/shard_map/ppermute | solution.py:558
  276.2 10.0 %collective-permute-start.29 = (bf16[128,1024]{1,0:T(8,128)(2,1)S(1)}, bf16[128,1024]{1,0:T(8,128)(2,1)S(1)}, u32[]{:S(2)}, u32[]{:S(2)}) collective-permute-start(bf16[128,1024]{1,0:T(8,128)(2,1)S(1)} %pad_maximum_fusion.rest_0_), channel_id=1, source_target_pairs={{32,0}} | collective-permute-start | bytes 786440 | tf_op jit(solution)/shard_map/ppermute | solution.py:558
  277.5 33.7 %collective-permute-start.30 = (bf16[128,1024]{1,0:T(8,128)(2,1)S(1)}, bf16[128,1024]{1,0:T(8,128)(2,1)}, u32[]{:S(2)}, u32[]{:S(2)}) collective-permute-start(bf16[128,1024]{1,0:T(8,128)(2,1)S(1)} %pad_maximum_fusion.rest_0_), channel_id=1, source_target_pairs={{64,0}} | collective-permute-start | bytes 786440 | tf_op jit(solution)/shard_map/ppermute | solution.py:558
  278.8 33.7 %collective-permute-start.31 = (bf16[128,1024]{1,0:T(8,128)(2,1)S(1)}, bf16[128,1024]{1,0:T(8,128)(2,1)}, u32[]{:S(2)}, u32[]{:S(2)}) collective-permute-start(bf16[128,1024]{1,0:T(8,128)(2,1)S(1)} %pad_maximum_fusion.rest_0_), channel_id=1, source_target_pairs={{96,0}} | collective-permute-start | bytes 786440 | tf_op jit(solution)/shard_map/ppermute | solution.py:558
  280.1 33.7 %collective-permute-start.32 = (bf16[128,1024]{1,0:T(8,128)(2,1)S(1)}, bf16[128,1024]{1,0:T(8,128)(2,1)}, u32[]{:S(2)}, u32[]{:S(2)}) collective-permute-start(bf16[128,1024]{1,0:T(8,128)(2,1)S(1)} %pad_maximum_fusion.rest_0_), channel_id=1, source_target_pairs={{16,0}} | collective-permute-start | bytes 786440 | tf_op jit(solution)/shard_map/ppermute | solution.py:558
  286.2 40.2 %copy-start.16 = (bf16[128,1024]{1,0:T(8,128)(2,1)}, bf16[128,1024]{1,0:T(8,128)(2,1)S(1)}, u32[]{:S(2)}) copy-start(bf16[128,1024]{1,0:T(8,128)(2,1)S(1)} %collective-permute-done.29.rest_1_) | copy-start | bytes 786436
  286.2 43.9 %collective-permute-start.36 = (bf16[2,128,1024]{2,1,0:T(8,128)(2,1)S(1)}, bf16[2,128,1024]{2,1,0:T(8,128)(2,1)S(1)}, u32[]{:S(2)}, u32[]{:S(2)}) collective-permute-start(bf16[2,128,1024]{2,1,0:T(8,128)(2,1)S(1)} %copy-done.9), channel_id=1, source_target_pairs={{0,1},{1,2},{2,3},{3,4},{4,5},{5,6},{6,7},{7,8},{8,9},{9,10},{10,1... | collective-permute-start | bytes 1572872 | tf_op jit(solution)/shard_map/ppermute | solution.py:558
  287.0 43.1 %collective-permute-start.37 = (bf16[2,128,1024]{2,1,0:T(8,128)(2,1)S(1)}, bf16[2,128,1024]{2,1,0:T(8,128)(2,1)}, u32[]{:S(2)}, u32[]{:S(2)}) collective-permute-start(bf16[2,128,1024]{2,1,0:T(8,128)(2,1)S(1)} %copy-done.8), channel_id=1, source_target_pairs={{0,127},{1,0},{2,1},{3,2},{4,3},{5,4},{6,5},{7,6},{8,7},{9,8},{10,... | collective-permute-start | bytes 1572872 | tf_op jit(solution)/shard_map/ppermute | solution.py:558
  306.6 23.6 %all-to-all-start.5 = ((bf16[128,2,8,128]{3,2,1,0:T(8,128)(2,1)}), bf16[128,2,8,128]{3,2,1,0:T(8,128)(2,1)S(1)}, u32[]{:S(2)}, u32[]{:S(2)}) async-start(bf16[128,2,8,128]{3,2,1,0:T(8,128)(2,1)} %scatter_last.1), calls=%async_computation.5 | async-start | bytes 1048576 | tf_op jit(solution)/shard_map/all_to_all | solution.py:555
  311.2 10.3 %collective-permute-start.33 = (bf16[128,1024]{1,0:T(8,128)(2,1)S(1)}, bf16[128,1024]{1,0:T(8,128)(2,1)S(1)}, u32[]{:S(2)}, u32[]{:S(2)}) collective-permute-start(bf16[128,1024]{1,0:T(8,128)(2,1)S(1)} %pad_maximum_fusion.rest_0_), channel_id=1, source_target_pairs={{48,0}} | collective-permute-start | bytes 786440 | tf_op jit(solution)/shard_map/ppermute | solution.py:558
  312.5 11.1 %collective-permute-start.34 = (bf16[128,1024]{1,0:T(8,128)(2,1)S(1)}, bf16[128,1024]{1,0:T(8,128)(2,1)S(1)}, u32[]{:S(2)}, u32[]{:S(2)}) collective-permute-start(bf16[128,1024]{1,0:T(8,128)(2,1)S(1)} %pad_maximum_fusion.rest_0_), channel_id=1, source_target_pairs={{80,0}} | collective-permute-start | bytes 786440 | tf_op jit(solution)/shard_map/ppermute | solution.py:558
  313.8 12.5 %collective-permute-start.35 = (bf16[128,1024]{1,0:T(8,128)(2,1)S(1)}, bf16[128,1024]{1,0:T(8,128)(2,1)S(1)}, u32[]{:S(2)}, u32[]{:S(2)}) collective-permute-start(bf16[128,1024]{1,0:T(8,128)(2,1)S(1)} %pad_maximum_fusion.rest_0_), channel_id=1, source_target_pairs={{112,0}} | collective-permute-start | bytes 786440 | tf_op jit(solution)/shard_map/ppermute | solution.py:558
  (24 other events, 157.0 us)

commit v5 on v3

--- a/solution.py
+++ b/solution.py
@@ -20,7 +20,7 @@
 FIRST_SENT = NB - SENT
 CHUNKS = 2
 HALF = KEY_HEADS // CHUNKS
-CALL_HEADS = 2
+CALL_HEADS = 4
 BOTH = ("ctx", "tp")
 SCALING = 1.0 / math.sqrt(HEAD_SIZE)
 EXP_SCALE = SCALING * math.log2(math.e)
@@ -65,11 +65,11 @@
             out_ref[d, s] = held_ref[block, chunk]
         return carry
 
-    lax.fori_loop(0, rows, one, 0, unroll=4)
+    lax.fori_loop(0, rows, one, 0, unroll=8)
 
 
 def gather_pieces(table, held, blocks, chunk):
-    steps = 4
+    steps = 2
     rows = blocks // steps
     return pl.pallas_call(
         functools.partial(gather_body, rows=rows, chunk=chunk),
@@ -100,48 +100,59 @@
     )(meta, held)
 
 
-def add_listed(table_ref, got_ref, acc_ref, rows):
+def add_listed(table_ref, got_ref, accs, rows):
     base = pl.program_id(0) * rows
 
-    def one(d, carry):
-        for s in range(SENT):
+    @pl.when(pl.program_id(0) == 0)
+    def _():
+        for acc in accs:
+            acc[...] = jnp.zeros_like(acc)
+
+    def one(d, total):
+        for s in range(1, SENT):
             block = table_ref[(base + d) * NB + FIRST_SENT + s]
-            acc_ref[block] += got_ref[d, s].astype(F32)
-        return carry
-
-    lax.fori_loop(0, rows, one, 0, unroll=4)
-
-
-def scatter_body(table_ref, got_ref, out_ref, *, rows):
-    @pl.when(pl.program_id(0) == 0)
-    def _():
-        out_ref[...] = jnp.zeros_like(out_ref)
-
-    add_listed(table_ref, got_ref, out_ref, rows)
+            accs[s][block] += got_ref[d, s].astype(F32)
+        return total + got_ref[d, 0].astype(F32)
+
+    zero = jnp.zeros((PIECE, HEAD_SIZE), F32)
+    accs[0][...] += lax.fori_loop(0, rows, one, zero, unroll=8)
+
+
+def listed_total(accs):
+    accs[1][0] += accs[0][...]
+    return (accs[1][...] + accs[2][...]) + (accs[3][...] + accs[4][...])
+
+
+def scatter_body(table_ref, got_ref, out_ref, *accs, rows):
+    add_listed(table_ref, got_ref, accs, rows)
+
+    @pl.when(pl.program_id(0) == pl.num_programs(0) - 1)
+    def _():
+        out_ref[...] = listed_total(accs)
 
 
 def scatter_last_body(
-    table_ref, meta_ref, got_ref, first_ref, dense_ref, other_ref, out_ref, acc_ref, *, rows
+    table_ref, meta_ref, got_ref, first_ref, dense_ref, other_ref, out_ref, *accs, rows
 ):
-    @pl.when(pl.program_id(0) == 0)
-    def _():
-        acc_ref[...] = jnp.zeros_like(acc_ref)
-
-    add_listed(table_ref, got_ref, acc_ref, rows)
+    add_listed(table_ref, got_ref, accs, rows)
 
     @pl.when(pl.program_id(0) == pl.num_programs(0) - 1)
     def _():
         core = meta_ref[1]
-        mine = dense_ref[0].reshape(acc_ref.shape)
-        other = other_ref[...].reshape(acc_ref.shape)
-        out_ref[:, core] = (jnp.where(core == 0, first_ref[...], acc_ref[...]) + mine).astype(BF16)
-        out_ref[:, 1 - core] = (
-            jnp.where(core == 0, acc_ref[...], first_ref[...]) + other
-        ).astype(BF16)
+        second = listed_total(accs)
+        mine = dense_ref[0].reshape(second.shape)
+        other = other_ref[...].reshape(second.shape)
+        out_ref[:, core] = (jnp.where(core == 0, first_ref[...], second) + mine).astype(BF16)
+        out_ref[:, 1 - core] = (jnp.where(core == 0, second, first_ref[...]) + other).astype(BF16)
+
+
+def slot_sums(blocks):
+    whole = VM((blocks, PIECE, HEAD_SIZE), F32)
+    return [VM((PIECE, HEAD_SIZE), F32)] + [whole] * (SENT - 1)
 
 
 def scatter_pieces(table, got, blocks):
-    steps = 4
+    steps = 2
     rows = blocks // steps
     return pl.pallas_call(
         functools.partial(scatter_body, rows=rows),
@@ -151,13 +162,14 @@
             grid=(steps,),
             in_specs=[pl.BlockSpec((rows, SENT, PIECE, HEAD_SIZE), lambda i, t: (i, 0, 0, 0))],
             out_specs=pl.BlockSpec((blocks, PIECE, HEAD_SIZE), lambda i, t: (0, 0, 0)),
+            scratch_shapes=slot_sums(blocks),
         ),
         name="scatter_pieces",
     )(table, got)
 
 
 def scatter_last(table, meta, got, first, dense, other, blocks):
-    steps = 4
+    steps = 2
     rows = blocks // steps
     whole = pl.BlockSpec((blocks, PIECE, HEAD_SIZE), lambda i, t, m: (0, 0, 0))
     return pl.pallas_call(
@@ -175,7 +187,7 @@
             out_specs=pl.BlockSpec(
                 (blocks, CHUNKS, PIECE, HEAD_SIZE), lambda i, t, m: (0, 0, 0, 0)
             ),
-            scratch_shapes=[VM((blocks, PIECE, HEAD_SIZE), F32)],
+            scratch_shapes=slot_sums(blocks),
         ),
         name="scatter_last",
     )(table, meta, got, first, dense, other)
@@ -216,13 +228,9 @@
                 dst[at : at + BLOCK] = g_ref[0, kv, :, s].reshape(BLOCK, HEAD_SIZE)
         kt[...] = kc[...].T
         live = [valid_ref[b * NB + s] > 0 for s in range(NB)]
-        dk[...] = jnp.zeros_like(dk)
-        dv[...] = jnp.zeros_like(dv)
 
         def heads(ref, p):
-            at = pl.multiple_of(2 * p * HEAD_SIZE, 2 * HEAD_SIZE)
-            both = ref[:, pl.ds(at, 2 * HEAD_SIZE)]
-            return jnp.concatenate([both[:, :HEAD_SIZE], both[:, HEAD_SIZE:]], axis=0)
+            return two_heads(ref, p)
 
         def pair(p, w):
             qp = heads(q_ref, p)
@@ -252,18 +260,19 @@
                 ds[w, rows] = (weights * (dp[w, rows] - delta)).astype(BF16)
             new_dv = dot(pb[w], op, 1, 0)
             new_dk = dot(ds[w], qp, 1, 0)
-            dv[...] += new_dv
-            dk[...] += new_dk
+            dv[...] = new_dv if p == 0 else dv[...] + new_dv
+            dk[...] = new_dk if p == 0 else dk[...] + new_dk
             dqt = dot(kt[...], ds[w], 1, 0) * SCALING
             out = jnp.concatenate([dqt[:, :BLOCK].T, dqt[:, BLOCK:].T], axis=1).astype(BF16)
-            dq_ref[:, pl.ds(pl.multiple_of(2 * p * HEAD_SIZE, 2 * HEAD_SIZE), 2 * HEAD_SIZE)] = out
+            dq_ref[:, pl.ds(2 * p * HEAD_SIZE, 2 * HEAD_SIZE)] = out
 
         def two_pairs(i, carry):
             for w in range(2):
                 pair(2 * i + w, w)
             return carry
 
-        lax.fori_loop(0, GROUP_SIZE // 4, two_pairs, 0)
+        for i in range(GROUP_SIZE // 4):
+            two_pairs(i, 0)
         for kv, acc, factor in ((0, dk, SCALING), (1, dv, 1.0)):
             prev_ref[kv] = (acc[0:BLOCK] * factor).astype(BF16)
             own_ref[kv] = acc[BLOCK : 2 * BLOCK] * factor
@@ -369,31 +378,23 @@
 
 
 def dense_body(
-    meta_ref, q_ref, held_ref, other_ref, s0, s1, s2, s3, dkv_ref, d0, d1, d2, d3,
-    kc, vc, kt, stats,
+    meta_ref, q_ref, held_ref, other_ref, s0, s1, s2, s3, dkv_ref, dq_ref, kc, vc, kt, stats
 ):
     load_held(meta_ref, held_ref, other_ref, kc, vc)
     kt[...] = kc[...].T
     stats[...] = merge_stats([s0[...], s1[...], s2[...], s3[...]])
     core = meta_ref[1]
 
-    for m, dq_ref in enumerate((d0, d1, d2, d3)):
-        p = lax.rem(meta_ref[2] + m, 4)
-
-        def row(n):
-            at = n * GROUP_SIZE + 2 * p
-            return jnp.concatenate([stats[pl.ds(at, 1)], stats[pl.ds(at + 1, 1)]], axis=1)
-
-        def heads(ref):
-            at = pl.multiple_of(2 * p * HEAD_SIZE, 2 * HEAD_SIZE)
-            both = ref[:, pl.ds(at, 2 * HEAD_SIZE)]
-            return jnp.concatenate([both[:, :HEAD_SIZE], both[:, HEAD_SIZE:]], axis=0)
-
-        top = row(0)
-        inverse = 1.0 / row(1)
-        delta = row(2) * inverse
-        qp = heads(q_ref.at[0])
-        op = heads(q_ref.at[1])
+    def row(n, p):
+        at = n * GROUP_SIZE + 2 * p
+        return jnp.concatenate([stats[at : at + 1], stats[at + 1 : at + 2]], axis=1)
+
+    for p in range(GROUP_SIZE // 2):
+        top = row(0, p)
+        inverse = 1.0 / row(1, p)
+        delta = row(2, p) * inverse
+        qp = two_heads(q_ref.at[0], p)
+        op = two_heads(q_ref.at[1], p)
         scores = dot(kc[...], qp, 1, 1)
         grads = dot(vc[...], op, 1, 1)
         weights = jnp.exp2(scores * EXP_SCALE - top) * inverse
@@ -401,23 +402,25 @@
         score_grad = (weights * (grads - delta)).astype(BF16)
         new_dk = dot(score_grad, qp, 1, 0) * SCALING
         new_dv = dot(rounded, op, 1, 0)
-        dkv_ref[core] = new_dk if m == 0 else dkv_ref[core] + new_dk
-        dkv_ref[1 - core] = new_dv if m == 0 else dkv_ref[1 - core] + new_dv
+        dkv_ref[core] = new_dk if p == 0 else dkv_ref[core] + new_dk
+        dkv_ref[1 - core] = new_dv if p == 0 else dkv_ref[1 - core] + new_dv
         dqt = dot(kt[...], score_grad, 1, 0) * SCALING
         for j in range(2):
-            dq_ref[:, j * HEAD_SIZE : (j + 1) * HEAD_SIZE] = (
+            dq_ref[:, pl.ds((2 * p + j) * HEAD_SIZE, HEAD_SIZE)] = (
                 dqt[:, j * BLOCK : (j + 1) * BLOCK].T.astype(BF16)
             )
 
 
 def dense_grads(meta, qo, held, other, stats):
     keys = held.shape[0] * PIECE
-    quarter = jax.ShapeDtypeStruct((BLOCK, 2 * HEAD_SIZE), BF16)
     return pl.pallas_call(
         dense_body,
-        out_shape=(jax.ShapeDtypeStruct((2, keys, HEAD_SIZE), F32),) + (quarter,) * 4,
+        out_shape=(
+            jax.ShapeDtypeStruct((2, keys, HEAD_SIZE), F32),
+            jax.ShapeDtypeStruct((BLOCK, GROUP_SIZE * HEAD_SIZE), BF16),
+        ),
         in_specs=[pl.BlockSpec(memory_space=pltpu.SMEM)] + [pl.BlockSpec(memory_space=VM)] * 7,
-        out_specs=[pl.BlockSpec(memory_space=VM)] * 5,
+        out_specs=[pl.BlockSpec(memory_space=VM)] * 2,
         scratch_shapes=[
             VM((keys, HEAD_SIZE), BF16),
             VM((keys, HEAD_SIZE), BF16),
@@ -522,6 +525,29 @@
     )(meta, dq, *parts)
 
 
+def pick_body(meta_ref, *rest, at):
+    parts, out_ref, sem = rest[:-2], rest[-2], rest[-1]
+    for n, part in enumerate(parts):
+
+        @pl.when(meta_ref[at] == n)
+        def _():
+            copy = pltpu.make_async_copy(part, out_ref, sem)
+            copy.start()
+            copy.wait()
+
+
+def pick(meta, at, parts):
+    return pl.pallas_call(
+        functools.partial(pick_body, at=at),
+        out_shape=jax.ShapeDtypeStruct(parts[0].shape, parts[0].dtype),
+        in_specs=[pl.BlockSpec(memory_space=pltpu.SMEM)]
+        + [pl.BlockSpec(memory_space=pl.ANY)] * len(parts),
+        out_specs=pl.BlockSpec(memory_space=VM),
+        scratch_shapes=[pltpu.SemaphoreType.DMA(())],
+        name="pick",
+    )(meta, *parts)
+
+
 def tp_pairs(pairs, ctx_size, tp_size):
     return [(c * tp_size + a, c * tp_size + b) for c in range(ctx_size) for a, b in pairs]
 
@@ -535,7 +561,9 @@
     blocks = ctx_size * tp_size
     b_index = lax.axis_index("ctx") * tp_size + lax.axis_index("tp")
     core = lax.axis_index("ctx") % 2
-    meta = jnp.stack([b_index, core, lax.axis_index("tp") % 4]).astype(jnp.int32)
+    t_index = lax.axis_index("tp")
+    meta = jnp.stack([b_index, core, t_index % 4, t_index // 4, lax.axis_index("ctx")])
+    meta = meta.astype(jnp.int32)
     table = key_blocks.reshape(-1)
     valid = slot_valid.reshape(-1)
     up = [(i, (i + 1) % blocks) for i in range(blocks)]
@@ -562,9 +590,9 @@
     held = swap(pieces.reshape(blocks, CHUNKS, PIECE, HEAD_SIZE))
     before, after = send(both, up), send(both, down)
     slices = spread_heads(meta, queries, output_gradient)
-    qo = jnp.where(b_index == 0, slices[0], jnp.zeros_like(slices[0]))
-    for c in range(1, ctx_size):
-        qo = qo + send(slices[c // 2 + HALF * (c % 2)], [(0, c * tp_size)])
+    moved = [slices[0]] * ctx_size
+    for c in (4, 2, 6, 3, 5, 7, 1):
+        moved[c] = send(slices[c // 2 + HALF * (c % 2)], [(0, c * tp_size)])
 
     listed = []
     for j in range(CHUNKS):
@@ -576,10 +604,11 @@
     for j in range(CHUNKS):
         got.append(swap(listed[j]).reshape(shape))
 
-    qo = qo + send_tp(qo, [(0, 1)])
-    qo = qo + send_tp(qo, [(0, 3), (1, 2)])
-    qo = qo + send_tp(qo, [(x, 4 + x) for x in four])
-    qo = qo + send_tp(qo, [(x, 12 + x) for x in four] + [(4 + x, 8 + x) for x in four])
+    qo = pick(meta, 4, moved)
+    moved = [qo] + [send_tp(qo, [(0, n)]) for n in range(1, 4)]
+    qo = pick(meta, 2, moved)
+    moved = [qo] + [send_tp(qo, [(x, 4 * n + x) for x in four]) for n in range(1, 4)]
+    qo = pick(meta, 3, moved)
 
     grads, back = (), []
     calls = HALF // CALL_HEADS
@@ -598,14 +627,12 @@
     others = [send_tp(stats, along_x(n)) for n in range(1, 4)]
     stats = merge_stats([stats] + others)
     others = [send_tp(stats, along_z(n)) for n in range(1, 4)]
-    dense, *part = dense_grads(meta, qo, held, given, [stats] + others)
+    dense, part = dense_grads(meta, qo, held, given, [stats] + others)
     dense_other = send(dense[1], partner)
-    others = [send_tp(part[n], along_x(n)) for n in range(1, 4)]
-    total = add(part[0], *others)
-    others = [send_tp(total, [(4 * n + x, x) for x in four]) for n in range(1, 4)]
+    others = [send_tp(part, [(4 * n + x, x) for x in four]) for n in range(1, 4)]
+    total = add(part, *others)
+    others = [send_tp(total, [(n, 0)]) for n in range(1, 4)]
     total = add(total, *others)
-    others = [send_tp(total, [(n, 0)]) for n in range(1, 4)]
-    total = jnp.concatenate([total] + others, axis=1)
     parts = [total] * KEY_HEADS
     for c in range(1, ctx_size):
         parts[c // 2 + HALF * (c % 2)] = send(total, [(c * tp_size, 0)])

time: 342 us -> 319 us (0.933)
  starting transfers between devices: 158 us -> 132 us
  other arithmetic: 7.4 us -> 2.81 us
    all_to_all x6, starting transfers between devices: 84.9 us -> 71.4 us  [swap(): return lax.all_to_all(x, BOTH, split_axis=0, concat_axis=0, tiled=True)]
    ppermute x39 -> x38, starting transfers between devices: 73 us -> 60.5 us  [send(): return lax.ppermute(x, BOTH, pairs)]
    all_to_all x6, waiting for transfers between devices: 12.8 us -> 21.6 us  [swap(): return lax.all_to_all(x, BOTH, split_axis=0, concat_axis=0, tiled=True)]
    pallas_call x0 -> x3, Pallas kernels: none -> 7.68 us  [pick(): pl.pallas_call(functools.partial(pick_body, at=at), out_shape=jax.ShapeDt...]
    add x5 -> x0, other arithmetic: 5.83 us -> none  [the longest x1 2.19 us: per_device(): qo = qo + send(slices[c // 2 + HALF * (c % 2)], [(0, c * tp_size)])]
    ppermute x39 -> x38, waiting for transfers between devices: 92.7 us -> 87.2 us  [send(): return lax.ppermute(x, BOTH, pairs)]
    unnamed x56 -> x68, local copies, waits for them, and re-layouts: 9.94 us -> 13.5 us
    pallas_call x4 -> x2, Pallas kernels: 13.2 us -> 10.5 us  [sparse_grads(): pl.pallas_call(sparse_body, out_shape=(jax.ShapeDtypeStruct(q.shape, BF16...]
  transfers between devices with their start and end apart: 45 -> 44, of which waited for: 22 -> 15; matrix products, arithmetic and copies ran while one was open for 3% -> 2% of each run, Pallas kernels for 14% -> 15%
where the time goes in v5:
time: 319 us; the launch traced here: 317 us
  starting transfers between devices  132 us (41%)
  waiting for transfers between devices  109 us (34%)
  Pallas kernels  57.1 us (18%)
  local copies, waits for them, and re-layouts  15.6 us (5%)
    ppermute x38, waiting for transfers between devices, send(): return lax.ppermute(x, BOTH, pairs)  87.2 us
    all_to_all x6, starting transfers between devices, swap(): return lax.all_to_all(x, BOTH, split_axis=0, concat_axis=0, tiled=True)  71.4 us
    ppermute x38, starting transfers between devices, send(): return lax.ppermute(x, BOTH, pairs)  60.5 us
    all_to_all x6, waiting for transfers between devices, swap(): return lax.all_to_all(x, BOTH, split_axis=0, concat_axis=0, tiled=True)  21.6 us
    unnamed x68, local copies, waits for them, and re-layouts  13.5 us
    pallas_call x2, Pallas kernels, sparse_grads(): pl.pallas_call(sparse_body, out_shape=(jax.ShapeDtypeStruct(q.shape, BF16...  10.5 us
    pallas_call x3, Pallas kernels, pick(): pl.pallas_call(functools.partial(pick_body, at=at), out_shape=jax.ShapeDt...  7.68 us
    pallas_call x2, Pallas kernels, gather_pieces(): pl.pallas_call(functools.partial(gather_body, rows=rows, chunk=chunk), ou...  7 us
  transfers between devices with their start and end apart: 44, of which 15 were waited for; matrix products, arithmetic and copies ran while one was open for 2% of the time, Pallas kernels for 15%

profile of v5, /device:TPU:0, one launch (start us, length us, event | category | flops | bytes accessed | tf_op | source)
XLA Modules:
  0.0 317.4 jit_solution(15293257715665457137)
XLA Ops:
  0.6 2.1 pack_pieces.1
  2.8 11.2 %all-to-all-start = ((bf16[128,2,8,128]{3,2,1,0:T(8,128)(2,1)}), bf16[128,2,8,128]{3,2,1,0:T(8,128)(2,1)S(1)}, u32[]{:S(2)}, u32[]{:S(2)}) async-start(bf16[128,2,8,128]{3,2,1,0:T(8,128)(2,1)} %bitcast.18), calls=%async_computation | async-start | bytes 1048576 | tf_op jit(solution)/shard_map/all_to_all | solution.py:575
  14.7 12.8 %all-to-all-done.held_ref = bf16[128,2,8,128]{3,2,1,0:T(8,128)(2,1)S(1)} async-done(((bf16[128,2,8,128]{3,2,1,0:T(8,128)(2,1)}), bf16[128,2,8,128]{3,2,1,0:T(8,128)(2,1)S(1)}, u32[]{:S(2)}, u32[]{:S(2)}) %all-to-all-start) | async-done | bytes 524320 | tf_op jit(solution)/shard_map/all_to_all | solution.py:575
  28.4 3.5 %gather_pieces.3 = bf16[128,5,8,128]{3,2,1,0:T(8,128)(2,1)} custom-call(s32[1024]{0:T(1024)} %reshape.31.table_ref, bf16[128,2,8,128]{3,2,1,0:T(8,128)(2,1)} %copy-done), custom_call_target="tpu_custom_call" | custom-call | tf_op jit(solution)/shard_map/gather_pieces/pallas_call | solution.py:74
  31.9 4.6 %all-to-all-start.2 = ((bf16[128,5,8,128]{3,2,1,0:T(8,128)(2,1)}), bf16[128,5,8,128]{3,2,1,0:T(8,128)(2,1)S(1)}, u32[]{:S(2)}, u32[]{:S(2)}) async-start(bf16[128,5,8,128]{3,2,1,0:T(8,128)(2,1)} %gather_pieces.3), calls=%async_computation.2 | async-start | bytes 2621440 | tf_op jit(solution)/shard_map/all_to_all | solution.py:575
  37.2 4.6 %spread_heads.1 = (bf16[2,128,1024]{2,1,0:T(8,128)(2,1)}, bf16[2,128,1024]{2,1,0:T(8,128)(2,1)}, bf16[2,128,1024]{2,1,0:T(8,128)(2,1)}, bf16[2,128,1024]{2,1,0:T...) custom-call(s32[5]{0:T(128)} %stack.23.meta_ref, ...), custom_call_target="tpu_custom_call" | custom-call | tf_op jit(solution)/shard_map/spread_heads/pallas_call | solution.py:480
  41.8 2.1 collective-permute-start.2
  43.9 2.1 collective-permute-start.3
  46.0 3.5 %gather_pieces.2 = bf16[128,5,8,128]{3,2,1,0:T(8,128)(2,1)} custom-call(s32[1024]{0:T(1024)} %reshape.31.table_ref, bf16[128,2,8,128]{3,2,1,0:T(8,128)(2,1)} %copy-done), custom_call_target="tpu_custom_call" | custom-call | tf_op jit(solution)/shard_map/gather_pieces/pallas_call | solution.py:74
  49.5 8.8 %all-to-all-done.2 = bf16[128,5,8,128]{3,2,1,0:T(8,128)(2,1)S(1)} async-done(((bf16[128,5,8,128]{3,2,1,0:T(8,128)(2,1)}), bf16[128,5,8,128]{3,2,1,0:T(8,128)(2,1)S(1)}, u32[]{:S(2)}, u32[]{:S(2)}) %all-to-all-start.2) | async-done | bytes 1310752 | tf_op jit(solution)/shard_map/all_to_all | solution.py:575
  59.3 4.6 %all-to-all-start.1 = ((bf16[128,5,8,128]{3,2,1,0:T(8,128)(2,1)}), bf16[128,5,8,128]{3,2,1,0:T(8,128)(2,1)S(1)}, u32[]{:S(2)}, u32[]{:S(2)}) async-start(bf16[128,5,8,128]{3,2,1,0:T(8,128)(2,1)} %gather_pieces.2), calls=%async_computation.1 | async-start | bytes 2621440 | tf_op jit(solution)/shard_map/all_to_all | solution.py:575
  63.9 2.5 collective-permute-start.4
  66.5 3.3 %collective-permute-start.5 = (bf16[2,128,1024]{2,1,0:T(8,128)(2,1)}, bf16[2,128,1024]{2,1,0:T(8,128)(2,1)}, u32[]{:S(2)}, u32[]{:S(2)}) collective-permute-start(bf16[2,128,1024]{2,1,0:T(8,128)(2,1)} %get-tuple-element.38), channel_id=1, source_target_pairs={{0,64}} | collective-permute-start | bytes 1572872 | tf_op jit(solution)/shard_map/ppermute | solution.py:578
  73.8 8.9 %collective-permute-done.4.rest_3_ = bf16[2,128,1024]{2,1,0:T(8,128)(2,1)S(1)} collective-permute-done((bf16[2,128,1024]{2,1,0:T(8,128)(2,1)}, bf16[2,128,1024]{2,1,0:T(8,128)(2,1)S(1)}, u32[]{:S(2)}, u32[]{:S(2)}) %collective-permute-start.4) | collective-permute-done | bytes 524320 | tf_op jit(solution)/shard_map/ppermute | solution.py:578
  82.7 5.6 %collective-permute-done.5.rest_4_ = bf16[2,128,1024]{2,1,0:T(8,128)(2,1)} collective-permute-done((bf16[2,128,1024]{2,1,0:T(8,128)(2,1)}, bf16[2,128,1024]{2,1,0:T(8,128)(2,1)}, u32[]{:S(2)}, u32[]{:S(2)}) %collective-permute-start.5) | collective-permute-done | bytes 524320 | tf_op jit(solution)/shard_map/ppermute | solution.py:578
  89.9 4.0 %collective-permute-done.6.rest_5_ = bf16[2,128,1024]{2,1,0:T(8,128)(2,1)S(1)} collective-permute-done((bf16[2,128,1024]{2,1,0:T(8,128)(2,1)}, bf16[2,128,1024]{2,1,0:T(8,128)(2,1)S(1)}, u32[]{:S(2)}, u32[]{:S(2)}) %collective-permute-start.6) | collective-permute-done | bytes 524320 | tf_op jit(solution)/shard_map/ppermute | solution.py:578
  96.5 2.7 pick.3.rest_0_
  99.1 2.1 collective-permute-start.9
  101.2 2.1 collective-permute-start.10
  103.3 2.1 collective-permute-start.11
  107.2 5.2 %sparse_grads.2 = (bf16[128,8192]{1,0:T(8,128)(2,1)}, f32[2,128,1024]{2,1,0:T(8,128)}, bf16[2,128,1024]{2,1,0:T(8,128)(2,1)}, bf16[2,128,1024]{2,1,0:T(8,128)(2,1)}, bf16[4,2,16,5,8,128]{5,4,3,2,1,0:T(8,128)(2,1)}) custom-call(s32[5]{0:T(128)} %stack.23.meta_ref, s32[1024]{0:T(1024)} %reshape.30.valid_ref, bf16[128,8192]{1,0:T(8,128)(2,1)} %q_ref.5, ...), custom_call_target="tpu_custom_call" | custom-call | tf_op jit(solution)/shard_map/sparse_grads/pallas_call | solution.py:298
  113.5 21.2 %all-to-all-start.4 = ((bf16[128,5,8,128]{3,2,1,0:T(8,128)(2,1)}), bf16[128,5,8,128]{3,2,1,0:T(8,128)(2,1)S(1)}, u32[]{:S(2)}, u32[]{:S(2)}) async-start(bf16[128,5,8,128]{3,2,1,0:T(8,128)(2,1)} %bitcast.16), calls=%async_computation.4 | async-start | bytes 2621440 | tf_op jit(solution)/shard_map/all_to_all | solution.py:575
  134.8 2.5 pick.4.rest_0_
  137.3 3.0 collective-permute-start.12
  140.3 2.5 collective-permute-start.13
  144.1 1.8 give_pieces.1
  145.9 14.8 %collective-permute-done.12.rest_1_ = bf16[2,128,1024]{2,1,0:T(8,128)(2,1)S(1)} collective-permute-done((bf16[2,128,1024]{2,1,0:T(8,128)(2,1)}, bf16[2,128,1024]{2,1,0:T(8,128)(2,1)S(1)}, u32[]{:S(2)}, u32[]{:S(2)}) %collective-permute-start.12) | collective-permute-done | bytes 524320 | tf_op jit(solution)/shard_map/ppermute | solution.py:578
  160.8 11.2 %collective-permute-done.13.rest_2_ = bf16[2,128,1024]{2,1,0:T(8,128)(2,1)S(1)} collective-permute-done((bf16[2,128,1024]{2,1,0:T(8,128)(2,1)}, bf16[2,128,1024]{2,1,0:T(8,128)(2,1)S(1)}, u32[]{:S(2)}, u32[]{:S(2)}) %collective-permute-start.13) | collective-permute-done | bytes 524320 | tf_op jit(solution)/shard_map/ppermute | solution.py:578
  173.6 2.5 pick.5.q_ref
  176.8 4.4 %dense_stats.1 = f32[24,128]{1,0:T(8,128)} custom-call(s32[5]{0:T(128)} %stack.23.meta_ref, bf16[2,128,1024]{2,1,0:T(8,128)(2,1)} %pick.5.q_ref, bf16[128,2,8,128]{3,2,1,0:T(8,128)(2,1)} %copy-done, bf16[128,8,128]{2,1,0:T(8,128)(2,1)} %copy-done.11), custom_call_target="tpu_custom_call" | custom-call | tf_op jit(solution)/shard_map/dense_stats/pallas_call | solution.py:361
  181.2 2.2 collective-permute-start.18
  185.4 3.5 %collective-permute-done.17 = f32[24,128]{1,0:T(8,128)S(1)} collective-permute-done((f32[24,128]{1,0:T(8,128)}, f32[24,128]{1,0:T(8,128)S(1)}, u32[]{:S(2)}, u32[]{:S(2)}) %collective-permute-start.17) | collective-permute-done | bytes 12320 | tf_op jit(solution)/shard_map/ppermute | solution.py:578
  191.4 4.0 %collective-permute-start.20 = (f32[24,128]{1,0:T(8,128)S(1)}, f32[24,128]{1,0:T(8,128)S(1)}, u32[]{:S(2)}, u32[]{:S(2)}) collective-permute-start(f32[24,128]{1,0:T(8,128)S(1)} %pad_maximum_fusion.s0), channel_id=1, source_target_pairs={{0,8},{1,9},{2,10},{3,11},{4,12},{5,13},{6,14},{7,15},{8,0},{9,1},... | collective-permute-start | bytes 36872 | tf_op jit(solution)/shard_map/ppermute | solution.py:578
  195.3 2.5 collective-permute-start.21
  199.9 5.3 %dense_grads.1 = (f32[2,1024,128]{2,1,0:T(8,128)}, bf16[128,1024]{1,0:T(8,128)(2,1)}) custom-call(s32[5]{0:T(128)} %stack.23.meta_ref, bf16[2,128,1024]{2,1,0:T(8,128)(2,1)} %pick.5.q_ref, bf16[128,2,8,128]{3,2,1,0:T(8,128)(2,1)} %copy-done, bf16[128,8,128]{2,1,0:T(8,128)(2,1)} %copy-done.11, f32[24,128]{1,0:T(8,128)} %copy-done.27, f32[24,128]{1,0:T(8,128)} %copy-done.28, ...), custom_call_target="tpu_custom_call" | custom-call | tf_op jit(solution)/shard_map/dense_grads/pallas_call | solution.py:416
  209.1 5.2 %sparse_grads.3 = (bf16[128,8192]{1,0:T(8,128)(2,1)}, f32[2,128,1024]{2,1,0:T(8,128)}, bf16[2,128,1024]{2,1,0:T(8,128)(2,1)}, bf16[2,128,1024]{2,1,0:T(8,128)(2,1)}, bf16[4,2,16,5,8,128]{5,4,3,2,1,0:T(8,128)(2,1)}) custom-call(s32[5]{0:T(128)} %stack.23.meta_ref, ...), custom_call_target="tpu_custom_call", output_to_operand_aliasing={{0}: (8, {}), {1}: (9, {}), {2}: (10, {}), {3}: (11, {})} | custom-call | tf_op jit(solution)/shard_map/sparse_grads/pallas_call | solution.py:298
  215.4 24.1 %all-to-all-start.3 = ((bf16[128,5,8,128]{3,2,1,0:T(8,128)(2,1)}), bf16[128,5,8,128]{3,2,1,0:T(8,128)(2,1)S(1)}, u32[]{:S(2)}, u32[]{:S(2)}) async-start(bf16[128,5,8,128]{3,2,1,0:T(8,128)(2,1)} %bitcast.17), calls=%async_computation.3 | async-start | bytes 2621440 | tf_op jit(solution)/shard_map/all_to_all | solution.py:575
  244.8 22.5 %collective-permute-done.27 = bf16[128,1024]{1,0:T(8,128)(2,1)S(1)} collective-permute-done((bf16[128,1024]{1,0:T(8,128)(2,1)S(1)}, bf16[128,1024]{1,0:T(8,128)(2,1)S(1)}, u32[]{:S(2)}, u32[]{:S(2)}) %collective-permute-start.27) | collective-permute-done | bytes 262176 | tf_op jit(solution)/shard_map/ppermute | solution.py:578
  272.7 3.0 collective-permute-done.28.rest_1_
  275.7 4.2 %collective-permute-start.36 = (bf16[2,128,1024]{2,1,0:T(8,128)(2,1)}, bf16[2,128,1024]{2,1,0:T(8,128)(2,1)S(1)}, u32[]{:S(2)}, u32[]{:S(2)}) collective-permute-start(bf16[2,128,1024]{2,1,0:T(8,128)(2,1)} %get-tuple-element.45), channel_id=1, source_target_pairs={{0,127},{1,0},{2,1},{3,2},{4,3},{5,4},{6,5},{7,6},{8,7},{9,8},{10,... | collective-permute-start | bytes 1572872 | tf_op jit(solution)/shard_map/ppermute | solution.py:578
  279.9 3.6 %scatter_pieces.1.first_ref = f32[128,8,128]{2,1,0:T(8,128)} custom-call(s32[1024]{0:T(1024)} %reshape.31.table_ref, bf16[128,5,8,128]{3,2,1,0:T(8,128)(2,1)} %copy-done.3), custom_call_target="tpu_custom_call" | custom-call | tf_op jit(solution)/shard_map/scatter_pieces/pallas_call | solution.py:157
  284.6 4.4 %scatter_last.1 = bf16[128,2,8,128]{3,2,1,0:T(8,128)(2,1)} custom-call(s32[1024]{0:T(1024)} %reshape.31.table_ref, s32[5]{0:T(128)} %stack.23.meta_ref, bf16[128,5,8,128]{3,2,1,0:T(8,128)(2,1)} %copy-done.2, f32[128,8,128]{2,1,0:T(8,128)} %scatter_pieces.1.first_ref, f32[2,1024,128]{2,1,0:T(8,128)} %get-tuple-element.48.dense_ref, f32[1024,128]{1,0:T(8,128)} %copy-done.15), custom_call_target="tpu_custom_call" | custom-call | tf_op jit(solution)/shard_map/scatter_last/pallas_call | solution.py:175
  289.0 5.6 %all-to-all-start.5 = ((bf16[128,2,8,128]{3,2,1,0:T(8,128)(2,1)}), bf16[128,2,8,128]{3,2,1,0:T(8,128)(2,1)S(1)}, u32[]{:S(2)}, u32[]{:S(2)}) async-start(bf16[128,2,8,128]{3,2,1,0:T(8,128)(2,1)} %scatter_last.1), calls=%async_computation.5 | async-start | bytes 1048576 | tf_op jit(solution)/shard_map/all_to_all | solution.py:575
  298.6 6.5 %collective-permute-done.32.rest_5_ = bf16[128,1024]{1,0:T(8,128)(2,1)S(1)} collective-permute-done((bf16[128,1024]{1,0:T(8,128)(2,1)S(1)}, bf16[128,1024]{1,0:T(8,128)(2,1)S(1)}, u32[]{:S(2)}, u32[]{:S(2)}) %collective-permute-start.32) | collective-permute-done | bytes 262176 | tf_op jit(solution)/shard_map/ppermute | solution.py:578
  305.0 2.0 collective-permute-done.33.rest_6_
  307.0 2.8 collective-permute-done.34.rest_7_
  310.5 3.1 put_first.1
  314.7 2.6 combine.1
  (133 shorter events, 46.6 us)
Async XLA Ops:
  0.6 13.3 %copy-start.31 = (s32[128,8]{0,1:T(8,128)S(1)}, s32[128,8]{0,1:T(8,128)}, u32[]{:S(2)}) copy-start(s32[128,8]{0,1:T(8,128)} %param.10) | copy-start | bytes 12292
  2.8 24.8 %all-to-all-start = ((bf16[128,2,8,128]{3,2,1,0:T(8,128)(2,1)}), bf16[128,2,8,128]{3,2,1,0:T(8,128)(2,1)S(1)}, u32[]{:S(2)}, u32[]{:S(2)}) async-start(bf16[128,2,8,128]{3,2,1,0:T(8,128)(2,1)} %bitcast.18), calls=%async_computation | async-start | bytes 1048576 | tf_op jit(solution)/shard_map/all_to_all | solution.py:575
  31.9 26.4 %all-to-all-start.2 = ((bf16[128,5,8,128]{3,2,1,0:T(8,128)(2,1)}), bf16[128,5,8,128]{3,2,1,0:T(8,128)(2,1)S(1)}, u32[]{:S(2)}, u32[]{:S(2)}) async-start(bf16[128,5,8,128]{3,2,1,0:T(8,128)(2,1)} %gather_pieces.3), calls=%async_computation.2 | async-start | bytes 2621440 | tf_op jit(solution)/shard_map/all_to_all | solution.py:575
  41.8 29.3 %collective-permute-start.2 = (bf16[2,128,1024]{2,1,0:T(8,128)(2,1)}, bf16[2,128,1024]{2,1,0:T(8,128)(2,1)}, u32[]{:S(2)}, u32[]{:S(2)}) collective-permute-start(bf16[2,128,1024]{2,1,0:T(8,128)(2,1)} %get-tuple-element.35), channel_id=1, source_target_pairs={{0,16}} | collective-permute-start | bytes 1572872 | tf_op jit(solution)/shard_map/ppermute | solution.py:578
  43.9 28.5 %collective-permute-start.3 = (bf16[2,128,1024]{2,1,0:T(8,128)(2,1)}, bf16[2,128,1024]{2,1,0:T(8,128)(2,1)}, u32[]{:S(2)}, u32[]{:S(2)}) collective-permute-start(bf16[2,128,1024]{2,1,0:T(8,128)(2,1)} %get-tuple-element.36), channel_id=1, source_target_pairs={{0,32}} | collective-permute-start | bytes 1572872 | tf_op jit(solution)/shard_map/ppermute | solution.py:578
  49.5 33.3 %copy-start.7 = (bf16[2,128,1024]{2,1,0:T(8,128)(2,1)S(1)}, bf16[2,128,1024]{2,1,0:T(8,128)(2,1)}, u32[]{:S(2)}) copy-start(bf16[2,128,1024]{2,1,0:T(8,128)(2,1)} %get-tuple-element.27.self_ref) | copy-start | bytes 1572868
  59.3 53.2 %all-to-all-start.1 = ((bf16[128,5,8,128]{3,2,1,0:T(8,128)(2,1)}), bf16[128,5,8,128]{3,2,1,0:T(8,128)(2,1)S(1)}, u32[]{:S(2)}, u32[]{:S(2)}) async-start(bf16[128,5,8,128]{3,2,1,0:T(8,128)(2,1)} %gather_pieces.2), calls=%async_computation.1 | async-start | bytes 2621440 | tf_op jit(solution)/shard_map/all_to_all | solution.py:575
  63.9 18.8 %collective-permute-start.4 = (bf16[2,128,1024]{2,1,0:T(8,128)(2,1)}, bf16[2,128,1024]{2,1,0:T(8,128)(2,1)S(1)}, u32[]{:S(2)}, u32[]{:S(2)}) collective-permute-start(bf16[2,128,1024]{2,1,0:T(8,128)(2,1)} %get-tuple-element.37), channel_id=1, source_target_pairs={{0,48}} | collective-permute-start | bytes 1572872 | tf_op jit(solution)/shard_map/ppermute | solution.py:578
  66.5 21.9 %collective-permute-start.5 = (bf16[2,128,1024]{2,1,0:T(8,128)(2,1)}, bf16[2,128,1024]{2,1,0:T(8,128)(2,1)}, u32[]{:S(2)}, u32[]{:S(2)}) collective-permute-start(bf16[2,128,1024]{2,1,0:T(8,128)(2,1)} %get-tuple-element.38), channel_id=1, source_target_pairs={{0,64}} | collective-permute-start | bytes 1572872 | tf_op jit(solution)/shard_map/ppermute | solution.py:578
  69.8 24.2 %collective-permute-start.6 = (bf16[2,128,1024]{2,1,0:T(8,128)(2,1)}, bf16[2,128,1024]{2,1,0:T(8,128)(2,1)S(1)}, u32[]{:S(2)}, u32[]{:S(2)}) collective-permute-start(bf16[2,128,1024]{2,1,0:T(8,128)(2,1)} %get-tuple-element.39), channel_id=1, source_target_pairs={{0,80}} | collective-permute-start | bytes 1572872 | tf_op jit(solution)/shard_map/ppermute | solution.py:578
  71.1 23.7 %collective-permute-start.7 = (bf16[2,128,1024]{2,1,0:T(8,128)(2,1)}, bf16[2,128,1024]{2,1,0:T(8,128)(2,1)S(1)}, u32[]{:S(2)}, u32[]{:S(2)}) collective-permute-start(bf16[2,128,1024]{2,1,0:T(8,128)(2,1)} %get-tuple-element.40), channel_id=1, source_target_pairs={{0,96}} | collective-permute-start | bytes 1572872 | tf_op jit(solution)/shard_map/ppermute | solution.py:578
  72.5 23.2 %collective-permute-start.8 = (bf16[2,128,1024]{2,1,0:T(8,128)(2,1)}, bf16[2,128,1024]{2,1,0:T(8,128)(2,1)S(1)}, u32[]{:S(2)}, u32[]{:S(2)}) collective-permute-start(bf16[2,128,1024]{2,1,0:T(8,128)(2,1)} %get-tuple-element.41), channel_id=1, source_target_pairs={{0,112}} | collective-permute-start | bytes 1572872 | tf_op jit(solution)/shard_map/ppermute | solution.py:578
  82.7 23.5 %collective-permute-start = (bf16[2,128,1024]{2,1,0:T(8,128)(2,1)S(1)}, bf16[2,128,1024]{2,1,0:T(8,128)(2,1)S(1)}, u32[]{:S(2)}, u32[]{:S(2)}) collective-permute-start(bf16[2,128,1024]{2,1,0:T(8,128)(2,1)S(1)} %copy-done.7), channel_id=1, source_target_pairs={{0,1},{1,2},{2,3},{3,4},{4,5},{5,6},{6,7},{7,8},{8,9},{9,10},{10,1... | collective-permute-start | bytes 1572872 | tf_op jit(solution)/shard_map/ppermute | solution.py:578
  88.3 17.8 %collective-permute-start.1 = (bf16[2,128,1024]{2,1,0:T(8,128)(2,1)S(1)}, bf16[2,128,1024]{2,1,0:T(8,128)(2,1)S(1)}, u32[]{:S(2)}, u32[]{:S(2)}) collective-permute-start(bf16[2,128,1024]{2,1,0:T(8,128)(2,1)S(1)} %copy-done.7), channel_id=1, source_target_pairs={{0,127},{1,0},{2,1},{3,2},{4,3},{5,4},{6,5},{7,6},{8,7},{9,8},{10,... | collective-permute-start | bytes 1572872 | tf_op jit(solution)/shard_map/ppermute | solution.py:578
  99.1 35.6 %collective-permute-start.9 = (bf16[2,128,1024]{2,1,0:T(8,128)(2,1)}, bf16[2,128,1024]{2,1,0:T(8,128)(2,1)}, u32[]{:S(2)}, u32[]{:S(2)}) collective-permute-start(bf16[2,128,1024]{2,1,0:T(8,128)(2,1)} %pick.3.rest_0_), channel_id=1, source_target_pairs={{0,1},{16,17},{32,33},{48,49},{64,65},{80,81},{96,97},{112,113}} | collective-permute-start | bytes 1572872 | tf_op jit(solution)/shard_map/ppermute | solution.py:578
  101.2 33.5 %collective-permute-start.10 = (bf16[2,128,1024]{2,1,0:T(8,128)(2,1)}, bf16[2,128,1024]{2,1,0:T(8,128)(2,1)}, u32[]{:S(2)}, u32[]{:S(2)}) collective-permute-start(bf16[2,128,1024]{2,1,0:T(8,128)(2,1)} %pick.3.rest_0_), channel_id=1, source_target_pairs={{0,2},{16,18},{32,34},{48,50},{64,66},{80,82},{96,98},{112,114}} | collective-permute-start | bytes 1572872 | tf_op jit(solution)/shard_map/ppermute | solution.py:578
  103.3 31.4 %collective-permute-start.11 = (bf16[2,128,1024]{2,1,0:T(8,128)(2,1)}, bf16[2,128,1024]{2,1,0:T(8,128)(2,1)}, u32[]{:S(2)}, u32[]{:S(2)}) collective-permute-start(bf16[2,128,1024]{2,1,0:T(8,128)(2,1)} %pick.3.rest_0_), channel_id=1, source_target_pairs={{0,3},{16,19},{32,35},{48,51},{64,67},{80,83},{96,99},{112,115}} | collective-permute-start | bytes 1572872 | tf_op jit(solution)/shard_map/ppermute | solution.py:578
  113.5 100.8 %all-to-all-start.4 = ((bf16[128,5,8,128]{3,2,1,0:T(8,128)(2,1)}), bf16[128,5,8,128]{3,2,1,0:T(8,128)(2,1)S(1)}, u32[]{:S(2)}, u32[]{:S(2)}) async-start(bf16[128,5,8,128]{3,2,1,0:T(8,128)(2,1)} %bitcast.16), calls=%async_computation.4 | async-start | bytes 2621440 | tf_op jit(solution)/shard_map/all_to_all | solution.py:575
  137.3 23.5 %collective-permute-start.12 = (bf16[2,128,1024]{2,1,0:T(8,128)(2,1)}, bf16[2,128,1024]{2,1,0:T(8,128)(2,1)S(1)}, u32[]{:S(2)}, u32[]{:S(2)}) collective-permute-start(bf16[2,128,1024]{2,1,0:T(8,128)(2,1)} %pick.4.rest_0_), channel_id=1, source_target_pairs={{0,4},{1,5},{2,6},{3,7},{16,20},{17,21},{18,22},{19,23},{32,36},{3... | collective-permute-start | bytes 1572872 | tf_op jit(solution)/shard_map/ppermute | solution.py:578
  140.3 31.7 %collective-permute-start.13 = (bf16[2,128,1024]{2,1,0:T(8,128)(2,1)}, bf16[2,128,1024]{2,1,0:T(8,128)(2,1)S(1)}, u32[]{:S(2)}, u32[]{:S(2)}) collective-permute-start(bf16[2,128,1024]{2,1,0:T(8,128)(2,1)} %pick.4.rest_0_), channel_id=1, source_target_pairs={{0,8},{1,9},{2,10},{3,11},{16,24},{17,25},{18,26},{19,27},{32,40},... | collective-permute-start | bytes 1572872 | tf_op jit(solution)/shard_map/ppermute | solution.py:578
  142.8 29.2 %collective-permute-start.14 = (bf16[2,128,1024]{2,1,0:T(8,128)(2,1)}, bf16[2,128,1024]{2,1,0:T(8,128)(2,1)S(1)}, u32[]{:S(2)}, u32[]{:S(2)}) collective-permute-start(bf16[2,128,1024]{2,1,0:T(8,128)(2,1)} %pick.4.rest_0_), channel_id=1, source_target_pairs={{0,12},{1,13},{2,14},{3,15},{16,28},{17,29},{18,30},{19,31},{32,44... | collective-permute-start | bytes 1572872 | tf_op jit(solution)/shard_map/ppermute | solution.py:578
  145.9 30.2 %collective-permute-start.15 = (bf16[128,8,128]{2,1,0:T(8,128)(2,1)}, bf16[128,8,128]{2,1,0:T(8,128)(2,1)S(1)}, u32[]{:S(2)}, u32[]{:S(2)}) collective-permute-start(bf16[128,8,128]{2,1,0:T(8,128)(2,1)} %give_pieces.1), channel_id=1, source_target_pairs={{0,16},{1,17},{2,18},{3,19},{4,20},{5,21},{6,22},{7,23},{8,24},{9,... | collective-permute-start | bytes 786440 | tf_op jit(solution)/shard_map/ppermute | solution.py:578
  181.2 4.1 %collective-permute-start.18 = (f32[24,128]{1,0:T(8,128)}, f32[24,128]{1,0:T(8,128)S(1)}, u32[]{:S(2)}, u32[]{:S(2)}) collective-permute-start(f32[24,128]{1,0:T(8,128)} %dense_stats.1), channel_id=1, source_target_pairs={{0,3},{1,0},{2,1},{3,2},{4,7},{5,4},{6,5},{7,6},{8,11},{9,8},{10,9... | collective-permute-start | bytes 36872 | tf_op jit(solution)/shard_map/ppermute | solution.py:578
  183.4 5.4 %collective-permute-start.17 = (f32[24,128]{1,0:T(8,128)}, f32[24,128]{1,0:T(8,128)S(1)}, u32[]{:S(2)}, u32[]{:S(2)}) collective-permute-start(f32[24,128]{1,0:T(8,128)} %dense_stats.1), channel_id=1, source_target_pairs={{0,2},{1,3},{2,0},{3,1},{4,6},{5,7},{6,4},{7,5},{8,10},{9,11},{10,... | collective-permute-start | bytes 36872 | tf_op jit(solution)/shard_map/ppermute | solution.py:578
  184.7 5.1 %collective-permute-start.16 = (f32[24,128]{1,0:T(8,128)}, f32[24,128]{1,0:T(8,128)S(1)}, u32[]{:S(2)}, u32[]{:S(2)}) collective-permute-start(f32[24,128]{1,0:T(8,128)} %dense_stats.1), channel_id=1, source_target_pairs={{0,1},{1,2},{2,3},{3,0},{4,5},{5,6},{6,7},{7,4},{8,9},{9,10},{10,1... | collective-permute-start | bytes 36872 | tf_op jit(solution)/shard_map/ppermute | solution.py:578
  191.3 6.6 %collective-permute-start.19 = (f32[24,128]{1,0:T(8,128)S(1)}, f32[24,128]{1,0:T(8,128)S(1)}, u32[]{:S(2)}, u32[]{:S(2)}) collective-permute-start(f32[24,128]{1,0:T(8,128)S(1)} %pad_maximum_fusion.s0), channel_id=1, source_target_pairs={{0,4},{1,5},{2,6},{3,7},{4,8},{5,9},{6,10},{7,11},{8,12},{9,13},{1... | collective-permute-start | bytes 36872 | tf_op jit(solution)/shard_map/ppermute | solution.py:578
  191.4 6.5 %collective-permute-start.20 = (f32[24,128]{1,0:T(8,128)S(1)}, f32[24,128]{1,0:T(8,128)S(1)}, u32[]{:S(2)}, u32[]{:S(2)}) collective-permute-start(f32[24,128]{1,0:T(8,128)S(1)} %pad_maximum_fusion.s0), channel_id=1, source_target_pairs={{0,8},{1,9},{2,10},{3,11},{4,12},{5,13},{6,14},{7,15},{8,0},{9,1},... | collective-permute-start | bytes 36872 | tf_op jit(solution)/shard_map/ppermute | solution.py:578
  195.3 3.9 %collective-permute-start.21 = (f32[24,128]{1,0:T(8,128)S(1)}, f32[24,128]{1,0:T(8,128)S(1)}, u32[]{:S(2)}, u32[]{:S(2)}) collective-permute-start(f32[24,128]{1,0:T(8,128)S(1)} %pad_maximum_fusion.s0), channel_id=1, source_target_pairs={{0,12},{1,13},{2,14},{3,15},{4,0},{5,1},{6,2},{7,3},{8,4},{9,5},{1... | collective-permute-start | bytes 36872 | tf_op jit(solution)/shard_map/ppermute | solution.py:578
  205.2 34.3 %collective-permute-start.24 = (bf16[128,1024]{1,0:T(8,128)(2,1)}, bf16[128,1024]{1,0:T(8,128)(2,1)S(1)}, u32[]{:S(2)}, u32[]{:S(2)}) collective-permute-start(bf16[128,1024]{1,0:T(8,128)(2,1)} %get-tuple-element.42), channel_id=1, source_target_pairs={{12,0},{13,1},{14,2},{15,3},{28,16},{29,17},{30,18},{31,19},{44,32... | collective-permute-start | bytes 786440 | tf_op jit(solution)/shard_map/ppermute | solution.py:578
  206.5 33.0 %collective-permute-start.23 = (bf16[128,1024]{1,0:T(8,128)(2,1)}, bf16[128,1024]{1,0:T(8,128)(2,1)S(1)}, u32[]{:S(2)}, u32[]{:S(2)}) collective-permute-start(bf16[128,1024]{1,0:T(8,128)(2,1)} %get-tuple-element.42), channel_id=1, source_target_pairs={{8,0},{9,1},{10,2},{11,3},{24,16},{25,17},{26,18},{27,19},{40,32},... | collective-permute-start | bytes 786440 | tf_op jit(solution)/shard_map/ppermute | solution.py:578
  207.8 31.7 %collective-permute-start.22 = (bf16[128,1024]{1,0:T(8,128)(2,1)}, bf16[128,1024]{1,0:T(8,128)(2,1)}, u32[]{:S(2)}, u32[]{:S(2)}) collective-permute-start(bf16[128,1024]{1,0:T(8,128)(2,1)} %get-tuple-element.42), channel_id=1, source_target_pairs={{4,0},{5,1},{6,2},{7,3},{20,16},{21,17},{22,18},{23,19},{36,32},{3... | collective-permute-start | bytes 786440 | tf_op jit(solution)/shard_map/ppermute | solution.py:578
  214.3 25.2 %copy-start.23 = (bf16[128,1024]{1,0:T(8,128)(2,1)S(1)}, bf16[128,1024]{1,0:T(8,128)(2,1)}, u32[]{:S(2)}) copy-start(bf16[128,1024]{1,0:T(8,128)(2,1)} %get-tuple-element.42) | copy-start | bytes 786436
  215.4 68.2 %all-to-all-start.3 = ((bf16[128,5,8,128]{3,2,1,0:T(8,128)(2,1)}), bf16[128,5,8,128]{3,2,1,0:T(8,128)(2,1)S(1)}, u32[]{:S(2)}, u32[]{:S(2)}) async-start(bf16[128,5,8,128]{3,2,1,0:T(8,128)(2,1)} %bitcast.17), calls=%async_computation.3 | async-start | bytes 2621440 | tf_op jit(solution)/shard_map/all_to_all | solution.py:575
  240.7 26.5 %collective-permute-start.27 = (bf16[128,1024]{1,0:T(8,128)(2,1)S(1)}, bf16[128,1024]{1,0:T(8,128)(2,1)S(1)}, u32[]{:S(2)}, u32[]{:S(2)}) collective-permute-start(bf16[128,1024]{1,0:T(8,128)(2,1)S(1)} %add_convert_fusion.1), channel_id=1, source_target_pairs={{3,0},{19,16},{35,32},{51,48},{67,64},{83,80},{99,96},{115,112}} | collective-permute-start | bytes 786440 | tf_op jit(solution)/shard_map/ppermute | solution.py:578
  242.0 25.2 %collective-permute-start.26 = (bf16[128,1024]{1,0:T(8,128)(2,1)S(1)}, bf16[128,1024]{1,0:T(8,128)(2,1)S(1)}, u32[]{:S(2)}, u32[]{:S(2)}) collective-permute-start(bf16[128,1024]{1,0:T(8,128)(2,1)S(1)} %add_convert_fusion.1), channel_id=1, source_target_pairs={{2,0},{18,16},{34,32},{50,48},{66,64},{82,80},{98,96},{114,112}} | collective-permute-start | bytes 786440 | tf_op jit(solution)/shard_map/ppermute | solution.py:578
  243.3 23.9 %collective-permute-start.25 = (bf16[128,1024]{1,0:T(8,128)(2,1)S(1)}, bf16[128,1024]{1,0:T(8,128)(2,1)S(1)}, u32[]{:S(2)}, u32[]{:S(2)}) collective-permute-start(bf16[128,1024]{1,0:T(8,128)(2,1)S(1)} %add_convert_fusion.1), channel_id=1, source_target_pairs={{1,0},{17,16},{33,32},{49,48},{65,64},{81,80},{97,96},{113,112}} | collective-permute-start | bytes 786440 | tf_op jit(solution)/shard_map/ppermute | solution.py:578
  244.7 27.9 %collective-permute-start.37 = (f32[1024,128]{1,0:T(8,128)S(1)}, f32[1024,128]{1,0:T(8,128)S(1)}, u32[]{:S(2)}, u32[]{:S(2)}) collective-permute-start(f32[1024,128]{1,0:T(8,128)S(1)} %slice_bitcast_fusion), channel_id=1, source_target_pairs={{0,16},{1,17},{2,18},{3,19},{4,20},{5,21},{6,22},{7,23},{8,24},{9,... | collective-permute-start | bytes 1572872 | tf_op jit(solution)/shard_map/ppermute | solution.py:578
  267.4 29.9 %copy-start.10 = (bf16[128,1024]{1,0:T(8,128)(2,1)}, bf16[128,1024]{1,0:T(8,128)(2,1)S(1)}, u32[]{:S(2)}) copy-start(bf16[128,1024]{1,0:T(8,128)(2,1)S(1)} %add_convert_fusion.rest_0_) | copy-start | bytes 786436
  267.4 8.3 %collective-permute-start.28 = (bf16[128,1024]{1,0:T(8,128)(2,1)S(1)}, bf16[128,1024]{1,0:T(8,128)(2,1)S(1)}, u32[]{:S(2)}, u32[]{:S(2)}) collective-permute-start(bf16[128,1024]{1,0:T(8,128)(2,1)S(1)} %add_convert_fusion.rest_0_), channel_id=1, source_target_pairs={{32,0}} | collective-permute-start | bytes 786440 | tf_op jit(solution)/shard_map/ppermute | solution.py:578
  268.7 25.9 %collective-permute-start.29 = (bf16[128,1024]{1,0:T(8,128)(2,1)S(1)}, bf16[128,1024]{1,0:T(8,128)(2,1)}, u32[]{:S(2)}, u32[]{:S(2)}) collective-permute-start(bf16[128,1024]{1,0:T(8,128)(2,1)S(1)} %add_convert_fusion.rest_0_), channel_id=1, source_target_pairs={{64,0}} | collective-permute-start | bytes 786440 | tf_op jit(solution)/shard_map/ppermute | solution.py:578
  270.0 25.9 %collective-permute-start.30 = (bf16[128,1024]{1,0:T(8,128)(2,1)S(1)}, bf16[128,1024]{1,0:T(8,128)(2,1)}, u32[]{:S(2)}, u32[]{:S(2)}) collective-permute-start(bf16[128,1024]{1,0:T(8,128)(2,1)S(1)} %add_convert_fusion.rest_0_), channel_id=1, source_target_pairs={{96,0}} | collective-permute-start | bytes 786440 | tf_op jit(solution)/shard_map/ppermute | solution.py:578
  271.3 25.9 %collective-permute-start.31 = (bf16[128,1024]{1,0:T(8,128)(2,1)S(1)}, bf16[128,1024]{1,0:T(8,128)(2,1)}, u32[]{:S(2)}, u32[]{:S(2)}) collective-permute-start(bf16[128,1024]{1,0:T(8,128)(2,1)S(1)} %add_convert_fusion.rest_0_), channel_id=1, source_target_pairs={{16,0}} | collective-permute-start | bytes 786440 | tf_op jit(solution)/shard_map/ppermute | solution.py:578
  272.6 40.9 %collective-permute-start.35 = (bf16[2,128,1024]{2,1,0:T(8,128)(2,1)}, bf16[2,128,1024]{2,1,0:T(8,128)(2,1)S(1)}, u32[]{:S(2)}, u32[]{:S(2)}) collective-permute-start(bf16[2,128,1024]{2,1,0:T(8,128)(2,1)} %get-tuple-element.44), channel_id=1, source_target_pairs={{0,1},{1,2},{2,3},{3,4},{4,5},{5,6},{6,7},{7,8},{8,9},{9,10},{10,1... | collective-permute-start | bytes 1572872 | tf_op jit(solution)/shard_map/ppermute | solution.py:578
  275.7 37.9 %collective-permute-start.36 = (bf16[2,128,1024]{2,1,0:T(8,128)(2,1)}, bf16[2,128,1024]{2,1,0:T(8,128)(2,1)S(1)}, u32[]{:S(2)}, u32[]{:S(2)}) collective-permute-start(bf16[2,128,1024]{2,1,0:T(8,128)(2,1)} %get-tuple-element.45), channel_id=1, source_target_pairs={{0,127},{1,0},{2,1},{3,2},{4,3},{5,4},{6,5},{7,6},{8,7},{9,8},{10,... | collective-permute-start | bytes 1572872 | tf_op jit(solution)/shard_map/ppermute | solution.py:578
  289.0 24.6 %all-to-all-start.5 = ((bf16[128,2,8,128]{3,2,1,0:T(8,128)(2,1)}), bf16[128,2,8,128]{3,2,1,0:T(8,128)(2,1)S(1)}, u32[]{:S(2)}, u32[]{:S(2)}) async-start(bf16[128,2,8,128]{3,2,1,0:T(8,128)(2,1)} %scatter_last.1), calls=%async_computation.5 | async-start | bytes 1048576 | tf_op jit(solution)/shard_map/all_to_all | solution.py:575
  294.6 10.4 %collective-permute-start.32 = (bf16[128,1024]{1,0:T(8,128)(2,1)S(1)}, bf16[128,1024]{1,0:T(8,128)(2,1)S(1)}, u32[]{:S(2)}, u32[]{:S(2)}) collective-permute-start(bf16[128,1024]{1,0:T(8,128)(2,1)S(1)} %add_convert_fusion.rest_0_), channel_id=1, source_target_pairs={{48,0}} | collective-permute-start | bytes 786440 | tf_op jit(solution)/shard_map/ppermute | solution.py:578
  296.0 11.1 %collective-permute-start.33 = (bf16[128,1024]{1,0:T(8,128)(2,1)S(1)}, bf16[128,1024]{1,0:T(8,128)(2,1)S(1)}, u32[]{:S(2)}, u32[]{:S(2)}) collective-permute-start(bf16[128,1024]{1,0:T(8,128)(2,1)S(1)} %add_convert_fusion.rest_0_), channel_id=1, source_target_pairs={{80,0}} | collective-permute-start | bytes 786440 | tf_op jit(solution)/shard_map/ppermute | solution.py:578
  297.3 12.5 %collective-permute-start.34 = (bf16[128,1024]{1,0:T(8,128)(2,1)S(1)}, bf16[128,1024]{1,0:T(8,128)(2,1)S(1)}, u32[]{:S(2)}, u32[]{:S(2)}) collective-permute-start(bf16[128,1024]{1,0:T(8,128)(2,1)S(1)} %add_convert_fusion.rest_0_), channel_id=1, source_target_pairs={{112,0}} | collective-permute-start | bytes 786440 | tf_op jit(solution)/shard_map/ppermute | solution.py:578
  (29 other events, 91.1 us)

commit v6 on v5

--- a/solution.py
+++ b/solution.py
@@ -86,18 +86,36 @@
     )(table, held)
 
 
-def give_body(meta_ref, held_ref, out_ref):
-    out_ref[...] = held_ref[:, 1 - meta_ref[1]]
-
-
-def give_pieces(meta, held):
-    return pl.pallas_call(
-        give_body,
-        out_shape=jax.ShapeDtypeStruct(held.shape[:1] + held.shape[2:], BF16),
-        in_specs=[pl.BlockSpec(memory_space=pltpu.SMEM), pl.BlockSpec(memory_space=VM)],
-        out_specs=pl.BlockSpec(memory_space=VM),
-        name="give_pieces",
-    )(meta, held)
+def gather_give_body(table_ref, meta_ref, held_ref, out_ref, give_ref, *, rows, chunk):
+    gather_body(table_ref, held_ref, out_ref, rows=rows, chunk=chunk)
+
+    @pl.when(pl.program_id(0) == 0)
+    def _():
+        give_ref[...] = held_ref[:, 1 - meta_ref[1]]
+
+
+def gather_give(table, meta, held, blocks, chunk):
+    steps = 2
+    rows = blocks // steps
+    return pl.pallas_call(
+        functools.partial(gather_give_body, rows=rows, chunk=chunk),
+        out_shape=(
+            jax.ShapeDtypeStruct((blocks, SENT, PIECE, HEAD_SIZE), BF16),
+            jax.ShapeDtypeStruct((blocks, PIECE, HEAD_SIZE), BF16),
+        ),
+        grid_spec=pltpu.PrefetchScalarGridSpec(
+            num_scalar_prefetch=2,
+            grid=(steps,),
+            in_specs=[
+                pl.BlockSpec((blocks, CHUNKS, PIECE, HEAD_SIZE), lambda i, t, m: (0, 0, 0, 0))
+            ],
+            out_specs=[
+                pl.BlockSpec((rows, SENT, PIECE, HEAD_SIZE), lambda i, t, m: (i, 0, 0, 0)),
+                pl.BlockSpec((blocks, PIECE, HEAD_SIZE), lambda i, t, m: (0, 0, 0)),
+            ],
+        ),
+        name="gather_give",
+    )(table, meta, held)
 
 
 def add_listed(table_ref, got_ref, accs, rows):
@@ -140,8 +158,8 @@
     def _():
         core = meta_ref[1]
         second = listed_total(accs)
-        mine = dense_ref[0].reshape(second.shape)
-        other = other_ref[...].reshape(second.shape)
+        mine = dense_ref[...].reshape(second.shape)
+        other = other_ref[...].astype(F32).reshape(second.shape)
         out_ref[:, core] = (jnp.where(core == 0, first_ref[...], second) + mine).astype(BF16)
         out_ref[:, 1 - core] = (jnp.where(core == 0, second, first_ref[...]) + other).astype(BF16)
 
@@ -181,7 +199,7 @@
             in_specs=[
                 pl.BlockSpec((rows, SENT, PIECE, HEAD_SIZE), lambda i, t, m: (i, 0, 0, 0)),
                 whole,
-                pl.BlockSpec((1, blocks * PIECE, HEAD_SIZE), lambda i, t, m: (0, 0, 0)),
+                pl.BlockSpec((blocks * PIECE, HEAD_SIZE), lambda i, t, m: (0, 0)),
                 pl.BlockSpec((blocks * PIECE, HEAD_SIZE), lambda i, t, m: (0, 0)),
             ],
             out_specs=pl.BlockSpec(
@@ -343,7 +361,18 @@
         vc[...] = mine
 
 
-def stats_body(meta_ref, q_ref, held_ref, other_ref, out_ref, kc, vc):
+def stats_body(
+    meta_ref, p0, p1, p2, p3, held_ref, other_ref, out_ref, q_ref, kc, vc, sem
+):
+    parts = (p0, p1, p2, p3)
+    for n, part in enumerate(parts):
+
+        @pl.when(meta_ref[3] == n)
+        def _():
+            copy = pltpu.make_async_copy(part, q_ref, sem)
+            copy.start()
+            copy.wait()
+
     load_held(meta_ref, held_ref, other_ref, kc, vc)
     for p in range(GROUP_SIZE // 2):
         scores = dot(kc[...], two_heads(q_ref.at[0], p), 1, 1)
@@ -356,16 +385,25 @@
                 out_ref[at : at + 1] = row[:, j * BLOCK : (j + 1) * BLOCK]
 
 
-def dense_stats(meta, qo, held, other):
+def dense_stats(meta, parts, held, other):
     keys = held.shape[0] * PIECE
     return pl.pallas_call(
         stats_body,
-        out_shape=jax.ShapeDtypeStruct((3 * GROUP_SIZE, BLOCK), F32),
-        in_specs=[pl.BlockSpec(memory_space=pltpu.SMEM)] + [pl.BlockSpec(memory_space=VM)] * 3,
-        out_specs=pl.BlockSpec(memory_space=VM),
-        scratch_shapes=[VM((keys, HEAD_SIZE), BF16), VM((keys, HEAD_SIZE), BF16)],
+        out_shape=(
+            jax.ShapeDtypeStruct((3 * GROUP_SIZE, BLOCK), F32),
+            jax.ShapeDtypeStruct(parts[0].shape, BF16),
+        ),
+        in_specs=[pl.BlockSpec(memory_space=pltpu.SMEM)]
+        + [pl.BlockSpec(memory_space=pl.ANY)] * 4
+        + [pl.BlockSpec(memory_space=VM)] * 2,
+        out_specs=[pl.BlockSpec(memory_space=VM)] * 2,
+        scratch_shapes=[
+            VM((keys, HEAD_SIZE), BF16),
+            VM((keys, HEAD_SIZE), BF16),
+            pltpu.SemaphoreType.DMA(()),
+        ],
         name="dense_stats",
-    )(meta, qo, held, other)
+    )(meta, *parts, held, other)
 
 
 def merge_stats(parts):
@@ -378,7 +416,8 @@
 
 
 def dense_body(
-    meta_ref, q_ref, held_ref, other_ref, s0, s1, s2, s3, dkv_ref, dq_ref, kc, vc, kt, stats
+    meta_ref, q_ref, held_ref, other_ref, s0, s1, s2, s3, keep_ref, give_ref, dq_ref,
+    kc, vc, kt, stats, dkv_ref,
 ):
     load_held(meta_ref, held_ref, other_ref, kc, vc)
     kt[...] = kc[...].T
@@ -409,6 +448,8 @@
             dq_ref[:, pl.ds((2 * p + j) * HEAD_SIZE, HEAD_SIZE)] = (
                 dqt[:, j * BLOCK : (j + 1) * BLOCK].T.astype(BF16)
             )
+    keep_ref[...] = dkv_ref[0]
+    give_ref[...] = dkv_ref[1].astype(BF16)
 
 
 def dense_grads(meta, qo, held, other, stats):
@@ -416,16 +457,18 @@
     return pl.pallas_call(
         dense_body,
         out_shape=(
-            jax.ShapeDtypeStruct((2, keys, HEAD_SIZE), F32),
+            jax.ShapeDtypeStruct((keys, HEAD_SIZE), F32),
+            jax.ShapeDtypeStruct((keys, HEAD_SIZE), BF16),
             jax.ShapeDtypeStruct((BLOCK, GROUP_SIZE * HEAD_SIZE), BF16),
         ),
         in_specs=[pl.BlockSpec(memory_space=pltpu.SMEM)] + [pl.BlockSpec(memory_space=VM)] * 7,
-        out_specs=[pl.BlockSpec(memory_space=VM)] * 2,
+        out_specs=[pl.BlockSpec(memory_space=VM)] * 3,
         scratch_shapes=[
             VM((keys, HEAD_SIZE), BF16),
             VM((keys, HEAD_SIZE), BF16),
             VM((HEAD_SIZE, keys), BF16),
             VM((3 * GROUP_SIZE, BLOCK), F32),
+            VM((2, keys, HEAD_SIZE), F32),
         ],
         name="dense_grads",
     )(meta, qo, held, other, *stats)
@@ -566,8 +609,8 @@
     meta = meta.astype(jnp.int32)
     table = key_blocks.reshape(-1)
     valid = slot_valid.reshape(-1)
-    up = [(i, (i + 1) % blocks) for i in range(blocks)]
-    down = [(i, (i - 1) % blocks) for i in range(blocks)]
+    up = [(i, i + 1) for i in range(1, blocks - 1)]
+    down = [(i + 1, i) for i in range(1, blocks - 1)]
     partner = [(i, (i // tp_size ^ 1) * tp_size + i % tp_size) for i in range(blocks)]
     four = range(4)
 
@@ -594,10 +637,9 @@
     for c in (4, 2, 6, 3, 5, 7, 1):
         moved[c] = send(slices[c // 2 + HALF * (c % 2)], [(0, c * tp_size)])
 
-    listed = []
-    for j in range(CHUNKS):
-        listed.append(gather_pieces(table, held, blocks, j))
-    given = give_pieces(meta, held)
+    listed = [gather_pieces(table, held, blocks, 0)]
+    more, given = gather_give(table, meta, held, blocks, 1)
+    listed.append(more)
     given = send(given, partner)
     shape = (HALF, 2, GROUPS, SENT, PIECE, HEAD_SIZE)
     got = []
@@ -608,7 +650,6 @@
     moved = [qo] + [send_tp(qo, [(0, n)]) for n in range(1, 4)]
     qo = pick(meta, 2, moved)
     moved = [qo] + [send_tp(qo, [(x, 4 * n + x) for x in four]) for n in range(1, 4)]
-    qo = pick(meta, 3, moved)
 
     grads, back = (), []
     calls = HALF // CALL_HEADS
@@ -623,12 +664,12 @@
     dq, own, to_prev, to_next = grads[:4]
     from_next, from_prev = send(to_prev, down), send(to_next, up)
 
-    stats = dense_stats(meta, qo, held, given)
+    stats, qo = dense_stats(meta, moved, held, given)
     others = [send_tp(stats, along_x(n)) for n in range(1, 4)]
     stats = merge_stats([stats] + others)
     others = [send_tp(stats, along_z(n)) for n in range(1, 4)]
-    dense, part = dense_grads(meta, qo, held, given, [stats] + others)
-    dense_other = send(dense[1], partner)
+    dense, to_partner, part = dense_grads(meta, qo, held, given, [stats] + others)
+    dense_other = send(to_partner, partner)
     others = [send_tp(part, [(4 * n + x, x) for x in four]) for n in range(1, 4)]
     total = add(part, *others)
     others = [send_tp(total, [(n, 0)]) for n in range(1, 4)]

time: 319 us -> 322 us (level)
  starting transfers between devices: 132 us -> 138 us
  Pallas kernels: 57.1 us -> 53.8 us
    all_to_all x6, starting transfers between devices: 71.4 us -> 80.1 us  [swap(): return lax.all_to_all(x, BOTH, split_axis=0, concat_axis=0, tiled=True)]
    pallas_call x2 -> x1, Pallas kernels: 7 us -> 3.49 us  [gather_pieces(): pl.pallas_call(functools.partial(gather_body, rows=rows, chunk=chunk), ou...]
    pallas_call x3 -> x2, Pallas kernels: 7.68 us -> 5.32 us  [pick(): pl.pallas_call(functools.partial(pick_body, at=at), out_shape=jax.ShapeDt...]
    unnamed x68 -> x70, local copies, waits for them, and re-layouts: 13.5 us -> 12.8 us
  transfers between devices with their start and end apart: 44 -> 44, of which waited for: 15 -> 16; matrix products, arithmetic and copies ran while one was open for 2% -> 2% of each run, Pallas kernels for 15% -> 14%
where the time goes in v6:
time: 322 us; the launch traced here: 320 us
  starting transfers between devices  138 us (43%)
  waiting for transfers between devices  110 us (34%)
  Pallas kernels  53.8 us (17%)
  local copies, waits for them, and re-layouts  14.8 us (5%)
    ppermute x38, waiting for transfers between devices, send(): return lax.ppermute(x, BOTH, pairs)  88.4 us
    all_to_all x6, starting transfers between devices, swap(): return lax.all_to_all(x, BOTH, split_axis=0, concat_axis=0, tiled=True)  80.1 us
    ppermute x38, starting transfers between devices, send(): return lax.ppermute(x, BOTH, pairs)  57.6 us
    all_to_all x6, waiting for transfers between devices, swap(): return lax.all_to_all(x, BOTH, split_axis=0, concat_axis=0, tiled=True)  21.5 us
    unnamed x70, local copies, waits for them, and re-layouts  12.8 us
    pallas_call x2, Pallas kernels, sparse_grads(): pl.pallas_call(sparse_body, out_shape=(jax.ShapeDtypeStruct(q.shape, BF16...  10.5 us
  transfers between devices with their start and end apart: 44, of which 16 were waited for; matrix products, arithmetic and copies ran while one was open for 2% of the time, Pallas kernels for 14%

profile of v6, /device:TPU:0, one launch (start us, length us, event | category | flops | bytes accessed | tf_op | source)
XLA Modules:
  0.0 320.3 jit_solution(1233219022028200343)
XLA Ops:
  0.6 2.1 pack_pieces.1
  2.8 11.2 %all-to-all-start = ((bf16[128,2,8,128]{3,2,1,0:T(8,128)(2,1)}), bf16[128,2,8,128]{3,2,1,0:T(8,128)(2,1)S(1)}, u32[]{:S(2)}, u32[]{:S(2)}) async-start(bf16[128,2,8,128]{3,2,1,0:T(8,128)(2,1)} %bitcast.16), calls=%async_computation | async-start | bytes 1048576 | tf_op jit(solution)/shard_map/all_to_all | solution.py:618
  14.7 12.8 %all-to-all-done.held_ref = bf16[128,2,8,128]{3,2,1,0:T(8,128)(2,1)S(1)} async-done(((bf16[128,2,8,128]{3,2,1,0:T(8,128)(2,1)}), bf16[128,2,8,128]{3,2,1,0:T(8,128)(2,1)S(1)}, u32[]{:S(2)}, u32[]{:S(2)}) %all-to-all-start) | async-done | bytes 524320 | tf_op jit(solution)/shard_map/all_to_all | solution.py:618
  28.3 3.5 %gather_pieces.1 = bf16[128,5,8,128]{3,2,1,0:T(8,128)(2,1)} custom-call(s32[1024]{0:T(1024)} %reshape.31.table_ref, bf16[128,2,8,128]{3,2,1,0:T(8,128)(2,1)} %copy-done), custom_call_target="tpu_custom_call" | custom-call | tf_op jit(solution)/shard_map/gather_pieces/pallas_call | solution.py:74
  31.8 4.6 %all-to-all-start.2 = ((bf16[128,5,8,128]{3,2,1,0:T(8,128)(2,1)}), bf16[128,5,8,128]{3,2,1,0:T(8,128)(2,1)S(1)}, u32[]{:S(2)}, u32[]{:S(2)}) async-start(bf16[128,5,8,128]{3,2,1,0:T(8,128)(2,1)} %gather_pieces.1), calls=%async_computation.2 | async-start | bytes 2621440 | tf_op jit(solution)/shard_map/all_to_all | solution.py:618
  37.2 4.5 %spread_heads.1 = (bf16[2,128,1024]{2,1,0:T(8,128)(2,1)}, bf16[2,128,1024]{2,1,0:T(8,128)(2,1)}, bf16[2,128,1024]{2,1,0:T(8,128)(2,1)}, bf16[2,128,1024]{2,1,0:T...) custom-call(s32[5]{0:T(128)} %stack.23.meta_ref, ...), custom_call_target="tpu_custom_call" | custom-call | tf_op jit(solution)/shard_map/spread_heads/pallas_call | solution.py:523
  41.7 2.1 collective-permute-start.2
  43.8 2.1 collective-permute-start.3
  45.9 3.6 %gather_give.1 = (bf16[128,5,8,128]{3,2,1,0:T(8,128)(2,1)}, bf16[128,8,128]{2,1,0:T(8,128)(2,1)}) custom-call(s32[1024]{0:T(1024)} %reshape.31.table_ref, s32[5]{0:T(128)} %stack.23.meta_ref, bf16[128,2,8,128]{3,2,1,0:T(8,128)(2,1)} %copy-done), custom_call_target="tpu_custom_call" | custom-call | tf_op jit(solution)/shard_map/gather_give/pallas_call | solution.py:100
  49.5 8.7 %all-to-all-done.2 = bf16[128,5,8,128]{3,2,1,0:T(8,128)(2,1)S(1)} async-done(((bf16[128,5,8,128]{3,2,1,0:T(8,128)(2,1)}), bf16[128,5,8,128]{3,2,1,0:T(8,128)(2,1)S(1)}, u32[]{:S(2)}, u32[]{:S(2)}) %all-to-all-start.2) | async-done | bytes 1310752 | tf_op jit(solution)/shard_map/all_to_all | solution.py:618
  59.2 4.6 %all-to-all-start.1 = ((bf16[128,5,8,128]{3,2,1,0:T(8,128)(2,1)}), bf16[128,5,8,128]{3,2,1,0:T(8,128)(2,1)S(1)}, u32[]{:S(2)}, u32[]{:S(2)}) async-start(bf16[128,5,8,128]{3,2,1,0:T(8,128)(2,1)} %get-tuple-element.34), calls=%async_computation.1 | async-start | bytes 2621440 | tf_op jit(solution)/shard_map/all_to_all | solution.py:618
  63.9 2.5 collective-permute-start.4
  66.4 3.3 %collective-permute-start.5 = (bf16[2,128,1024]{2,1,0:T(8,128)(2,1)}, bf16[2,128,1024]{2,1,0:T(8,128)(2,1)}, u32[]{:S(2)}, u32[]{:S(2)}) collective-permute-start(bf16[2,128,1024]{2,1,0:T(8,128)(2,1)} %get-tuple-element.44), channel_id=1, source_target_pairs={{0,64}} | collective-permute-start | bytes 1572872 | tf_op jit(solution)/shard_map/ppermute | solution.py:621
  72.4 1.3 collective-permute-start.8
  73.7 8.9 %collective-permute-done.4.rest_3_ = bf16[2,128,1024]{2,1,0:T(8,128)(2,1)S(1)} collective-permute-done((bf16[2,128,1024]{2,1,0:T(8,128)(2,1)}, bf16[2,128,1024]{2,1,0:T(8,128)(2,1)S(1)}, u32[]{:S(2)}, u32[]{:S(2)}) %collective-permute-start.4) | collective-permute-done | bytes 524320 | tf_op jit(solution)/shard_map/ppermute | solution.py:621
  83.4 4.9 %collective-permute-done.5.rest_4_ = bf16[2,128,1024]{2,1,0:T(8,128)(2,1)} collective-permute-done((bf16[2,128,1024]{2,1,0:T(8,128)(2,1)}, bf16[2,128,1024]{2,1,0:T(8,128)(2,1)}, u32[]{:S(2)}, u32[]{:S(2)}) %collective-permute-start.5) | collective-permute-done | bytes 524320 | tf_op jit(solution)/shard_map/ppermute | solution.py:621
  89.0 4.9 %collective-permute-done.6.rest_5_ = bf16[2,128,1024]{2,1,0:T(8,128)(2,1)S(1)} collective-permute-done((bf16[2,128,1024]{2,1,0:T(8,128)(2,1)}, bf16[2,128,1024]{2,1,0:T(8,128)(2,1)S(1)}, u32[]{:S(2)}, u32[]{:S(2)}) %collective-permute-start.6) | collective-permute-done | bytes 524320 | tf_op jit(solution)/shard_map/ppermute | solution.py:621
  96.4 2.7 pick.2.rest_0_
  99.1 2.1 collective-permute-start.9
  101.2 2.1 collective-permute-start.10
  103.3 2.1 collective-permute-start.11
  107.2 5.2 %sparse_grads.2 = (bf16[128,8192]{1,0:T(8,128)(2,1)}, f32[2,128,1024]{2,1,0:T(8,128)}, bf16[2,128,1024]{2,1,0:T(8,128)(2,1)}, bf16[2,128,1024]{2,1,0:T(8,128)(2,1)}, bf16[4,2,16,5,8,128]{5,4,3,2,1,0:T(8,128)(2,1)}) custom-call(s32[5]{0:T(128)} %stack.23.meta_ref, s32[1024]{0:T(1024)} %reshape.30.valid_ref, bf16[128,8192]{1,0:T(8,128)(2,1)} %q_ref.5, ...), custom_call_target="tpu_custom_call" | custom-call | tf_op jit(solution)/shard_map/sparse_grads/pallas_call | solution.py:316
  113.5 22.6 %all-to-all-start.4 = ((bf16[128,5,8,128]{3,2,1,0:T(8,128)(2,1)}), bf16[128,5,8,128]{3,2,1,0:T(8,128)(2,1)S(1)}, u32[]{:S(2)}, u32[]{:S(2)}) async-start(bf16[128,5,8,128]{3,2,1,0:T(8,128)(2,1)} %bitcast.14), calls=%async_computation.4 | async-start | bytes 2621440 | tf_op jit(solution)/shard_map/all_to_all | solution.py:618
  136.1 2.7 pick.3.p0
  138.8 3.0 collective-permute-start.12
  141.8 2.5 collective-permute-start.13
  145.7 1.5 collective-permute-done.15.other_ref
  147.2 14.9 %collective-permute-done.12.p1 = bf16[2,128,1024]{2,1,0:T(8,128)(2,1)S(1)} collective-permute-done((bf16[2,128,1024]{2,1,0:T(8,128)(2,1)}, bf16[2,128,1024]{2,1,0:T(8,128)(2,1)S(1)}, u32[]{:S(2)}, u32[]{:S(2)}) %collective-permute-start.12) | collective-permute-done | bytes 524320 | tf_op jit(solution)/shard_map/ppermute | solution.py:621
  162.1 11.2 %collective-permute-done.13.p2 = bf16[2,128,1024]{2,1,0:T(8,128)(2,1)S(1)} collective-permute-done((bf16[2,128,1024]{2,1,0:T(8,128)(2,1)}, bf16[2,128,1024]{2,1,0:T(8,128)(2,1)S(1)}, u32[]{:S(2)}, u32[]{:S(2)}) %collective-permute-start.13) | collective-permute-done | bytes 524320 | tf_op jit(solution)/shard_map/ppermute | solution.py:621
  174.9 5.3 %dense_stats.1 = (f32[24,128]{1,0:T(8,128)}, bf16[2,128,1024]{2,1,0:T(8,128)(2,1)}) custom-call(s32[5]{0:T(128)} %stack.23.meta_ref, bf16[2,128,1024]{2,1,0:T(8,128)(2,1)} %pick.3.p0, bf16[2,128,1024]{2,1,0:T(8,128)(2,1)} %copy-done.17, bf16[2,128,1024]{2,1,0:T(8,128)(2,1)} %copy-done.18, bf16[2,128,1024]{2,1,0:T(8,128)(2,1)} %copy-done.19, ...), custom_call_target="tpu_custom_call" | custom-call | tf_op jit(solution)/shard_map/dense_stats/pallas_call | solution.py:390
  180.3 2.3 collective-permute-start.18
  184.5 3.5 %collective-permute-done.17 = f32[24,128]{1,0:T(8,128)S(1)} collective-permute-done((f32[24,128]{1,0:T(8,128)}, f32[24,128]{1,0:T(8,128)S(1)}, u32[]{:S(2)}, u32[]{:S(2)}) %collective-permute-start.17) | collective-permute-done | bytes 12320 | tf_op jit(solution)/shard_map/ppermute | solution.py:621
  190.4 4.0 %collective-permute-start.20 = (f32[24,128]{1,0:T(8,128)S(1)}, f32[24,128]{1,0:T(8,128)S(1)}, u32[]{:S(2)}, u32[]{:S(2)}) collective-permute-start(f32[24,128]{1,0:T(8,128)S(1)} %pad_maximum_fusion.s0), channel_id=1, source_target_pairs={{0,8},{1,9},{2,10},{3,11},{4,12},{5,13},{6,14},{7,15},{8,0},{9,1},... | collective-permute-start | bytes 36872 | tf_op jit(solution)/shard_map/ppermute | solution.py:621
  194.4 2.5 collective-permute-start.21
  197.0 1.4 collective-permute-done.21.s3
  199.0 5.2 %dense_grads.1 = (f32[1024,128]{1,0:T(8,128)}, bf16[1024,128]{1,0:T(8,128)(2,1)}, bf16[128,1024]{1,0:T(8,128)(2,1)}) custom-call(s32[5]{0:T(128)} %stack.23.meta_ref, bf16[2,128,1024]{2,1,0:T(8,128)(2,1)} %get-tuple-element.49.q_ref, bf16[128,2,8,128]{3,2,1,0:T(8,128)(2,1)} %copy-done, bf16[128,8,128]{2,1,0:T(8,128)(2,1)} %copy-done.10, ...), custom_call_target="tpu_custom_call" | custom-call | tf_op jit(solution)/shard_map/dense_grads/pallas_call | solution.py:457
  208.1 5.2 %sparse_grads.3 = (bf16[128,8192]{1,0:T(8,128)(2,1)}, f32[2,128,1024]{2,1,0:T(8,128)}, bf16[2,128,1024]{2,1,0:T(8,128)(2,1)}, bf16[2,128,1024]{2,1,0:T(8,128)(2,1)}, bf16[4,2,16,5,8,128]{5,4,3,2,1,0:T(8,128)(2,1)}) custom-call(s32[5]{0:T(128)} %stack.23.meta_ref, ...), custom_call_target="tpu_custom_call", output_to_operand_aliasing={{0}: (8, {}), {1}: (9, {}), {2}: (10, {}), {3}: (11, {})} | custom-call | tf_op jit(solution)/shard_map/sparse_grads/pallas_call | solution.py:316
  214.4 24.1 %all-to-all-start.3 = ((bf16[128,5,8,128]{3,2,1,0:T(8,128)(2,1)}), bf16[128,5,8,128]{3,2,1,0:T(8,128)(2,1)S(1)}, u32[]{:S(2)}, u32[]{:S(2)}) async-start(bf16[128,5,8,128]{3,2,1,0:T(8,128)(2,1)} %bitcast.15), calls=%async_computation.3 | async-start | bytes 2621440 | tf_op jit(solution)/shard_map/all_to_all | solution.py:618
  243.7 22.5 %collective-permute-done.27 = bf16[128,1024]{1,0:T(8,128)(2,1)S(1)} collective-permute-done((bf16[128,1024]{1,0:T(8,128)(2,1)S(1)}, bf16[128,1024]{1,0:T(8,128)(2,1)S(1)}, u32[]{:S(2)}, u32[]{:S(2)}) %collective-permute-start.27) | collective-permute-done | bytes 262176 | tf_op jit(solution)/shard_map/ppermute | solution.py:621
  272.4 2.3 collective-permute-done.28.rest_1_
  275.4 3.7 %scatter_pieces.1.first_ref = f32[128,8,128]{2,1,0:T(8,128)} custom-call(s32[1024]{0:T(1024)} %reshape.31.table_ref, bf16[128,5,8,128]{3,2,1,0:T(8,128)(2,1)} %copy-done.2), custom_call_target="tpu_custom_call" | custom-call | tf_op jit(solution)/shard_map/scatter_pieces/pallas_call | solution.py:175
  280.2 4.3 %scatter_last.1 = bf16[128,2,8,128]{3,2,1,0:T(8,128)(2,1)} custom-call(s32[1024]{0:T(1024)} %reshape.31.table_ref, s32[5]{0:T(128)} %stack.23.meta_ref, bf16[128,5,8,128]{3,2,1,0:T(8,128)(2,1)} %copy-done.3, f32[128,8,128]{2,1,0:T(8,128)} %scatter_pieces.1.first_ref, f32[1024,128]{1,0:T(8,128)} %get-tuple-element.57.dense_ref, bf16[1024,128]{1,0:T(8,128)(2,1)} %copy-done.25), custom_call_target="tpu_custom_call" | custom-call | tf_op jit(solution)/shard_map/scatter_last/pallas_call | solution.py:193
  284.5 13.0 %all-to-all-start.5 = ((bf16[128,2,8,128]{3,2,1,0:T(8,128)(2,1)}), bf16[128,2,8,128]{3,2,1,0:T(8,128)(2,1)S(1)}, u32[]{:S(2)}, u32[]{:S(2)}) async-start(bf16[128,2,8,128]{3,2,1,0:T(8,128)(2,1)} %scatter_last.1), calls=%async_computation.5 | async-start | bytes 1048576 | tf_op jit(solution)/shard_map/all_to_all | solution.py:618
  301.4 6.5 %collective-permute-done.32.rest_5_ = bf16[128,1024]{1,0:T(8,128)(2,1)S(1)} collective-permute-done((bf16[128,1024]{1,0:T(8,128)(2,1)S(1)}, bf16[128,1024]{1,0:T(8,128)(2,1)S(1)}, u32[]{:S(2)}, u32[]{:S(2)}) %collective-permute-start.32) | collective-permute-done | bytes 262176 | tf_op jit(solution)/shard_map/ppermute | solution.py:621
  307.9 2.0 collective-permute-done.33.rest_6_
  309.9 2.8 collective-permute-done.34.rest_7_
  313.4 3.1 put_first.1
  317.6 2.6 combine.1
  (132 shorter events, 44.3 us)
Async XLA Ops:
  2.8 24.8 %all-to-all-start = ((bf16[128,2,8,128]{3,2,1,0:T(8,128)(2,1)}), bf16[128,2,8,128]{3,2,1,0:T(8,128)(2,1)S(1)}, u32[]{:S(2)}, u32[]{:S(2)}) async-start(bf16[128,2,8,128]{3,2,1,0:T(8,128)(2,1)} %bitcast.16), calls=%async_computation | async-start | bytes 1048576 | tf_op jit(solution)/shard_map/all_to_all | solution.py:618
  31.8 26.4 %all-to-all-start.2 = ((bf16[128,5,8,128]{3,2,1,0:T(8,128)(2,1)}), bf16[128,5,8,128]{3,2,1,0:T(8,128)(2,1)S(1)}, u32[]{:S(2)}, u32[]{:S(2)}) async-start(bf16[128,5,8,128]{3,2,1,0:T(8,128)(2,1)} %gather_pieces.1), calls=%async_computation.2 | async-start | bytes 2621440 | tf_op jit(solution)/shard_map/all_to_all | solution.py:618
  41.7 29.4 %collective-permute-start.2 = (bf16[2,128,1024]{2,1,0:T(8,128)(2,1)}, bf16[2,128,1024]{2,1,0:T(8,128)(2,1)}, u32[]{:S(2)}, u32[]{:S(2)}) collective-permute-start(bf16[2,128,1024]{2,1,0:T(8,128)(2,1)} %get-tuple-element.41), channel_id=1, source_target_pairs={{0,16}} | collective-permute-start | bytes 1572872 | tf_op jit(solution)/shard_map/ppermute | solution.py:621
  43.8 28.6 %collective-permute-start.3 = (bf16[2,128,1024]{2,1,0:T(8,128)(2,1)}, bf16[2,128,1024]{2,1,0:T(8,128)(2,1)}, u32[]{:S(2)}, u32[]{:S(2)}) collective-permute-start(bf16[2,128,1024]{2,1,0:T(8,128)(2,1)} %get-tuple-element.42), channel_id=1, source_target_pairs={{0,32}} | collective-permute-start | bytes 1572872 | tf_op jit(solution)/shard_map/ppermute | solution.py:621
  58.2 24.5 %copy-start.6 = (bf16[2,128,1024]{2,1,0:T(8,128)(2,1)S(1)}, bf16[2,128,1024]{2,1,0:T(8,128)(2,1)}, u32[]{:S(2)}) copy-start(bf16[2,128,1024]{2,1,0:T(8,128)(2,1)} %get-tuple-element.32.self_ref) | copy-start | bytes 1572868
  59.2 53.2 %all-to-all-start.1 = ((bf16[128,5,8,128]{3,2,1,0:T(8,128)(2,1)}), bf16[128,5,8,128]{3,2,1,0:T(8,128)(2,1)S(1)}, u32[]{:S(2)}, u32[]{:S(2)}) async-start(bf16[128,5,8,128]{3,2,1,0:T(8,128)(2,1)} %get-tuple-element.34), calls=%async_computation.1 | async-start | bytes 2621440 | tf_op jit(solution)/shard_map/all_to_all | solution.py:618
  63.9 18.8 %collective-permute-start.4 = (bf16[2,128,1024]{2,1,0:T(8,128)(2,1)}, bf16[2,128,1024]{2,1,0:T(8,128)(2,1)S(1)}, u32[]{:S(2)}, u32[]{:S(2)}) collective-permute-start(bf16[2,128,1024]{2,1,0:T(8,128)(2,1)} %get-tuple-element.43), channel_id=1, source_target_pairs={{0,48}} | collective-permute-start | bytes 1572872 | tf_op jit(solution)/shard_map/ppermute | solution.py:621
  66.4 21.9 %collective-permute-start.5 = (bf16[2,128,1024]{2,1,0:T(8,128)(2,1)}, bf16[2,128,1024]{2,1,0:T(8,128)(2,1)}, u32[]{:S(2)}, u32[]{:S(2)}) collective-permute-start(bf16[2,128,1024]{2,1,0:T(8,128)(2,1)} %get-tuple-element.44), channel_id=1, source_target_pairs={{0,64}} | collective-permute-start | bytes 1572872 | tf_op jit(solution)/shard_map/ppermute | solution.py:621
  69.7 24.2 %collective-permute-start.6 = (bf16[2,128,1024]{2,1,0:T(8,128)(2,1)}, bf16[2,128,1024]{2,1,0:T(8,128)(2,1)S(1)}, u32[]{:S(2)}, u32[]{:S(2)}) collective-permute-start(bf16[2,128,1024]{2,1,0:T(8,128)(2,1)} %get-tuple-element.45), channel_id=1, source_target_pairs={{0,80}} | collective-permute-start | bytes 1572872 | tf_op jit(solution)/shard_map/ppermute | solution.py:621
  71.1 23.7 %collective-permute-start.7 = (bf16[2,128,1024]{2,1,0:T(8,128)(2,1)}, bf16[2,128,1024]{2,1,0:T(8,128)(2,1)S(1)}, u32[]{:S(2)}, u32[]{:S(2)}) collective-permute-start(bf16[2,128,1024]{2,1,0:T(8,128)(2,1)} %get-tuple-element.46), channel_id=1, source_target_pairs={{0,96}} | collective-permute-start | bytes 1572872 | tf_op jit(solution)/shard_map/ppermute | solution.py:621
  72.4 23.2 %collective-permute-start.8 = (bf16[2,128,1024]{2,1,0:T(8,128)(2,1)}, bf16[2,128,1024]{2,1,0:T(8,128)(2,1)S(1)}, u32[]{:S(2)}, u32[]{:S(2)}) collective-permute-start(bf16[2,128,1024]{2,1,0:T(8,128)(2,1)} %get-tuple-element.47), channel_id=1, source_target_pairs={{0,112}} | collective-permute-start | bytes 1572872 | tf_op jit(solution)/shard_map/ppermute | solution.py:621
  82.7 23.5 %collective-permute-start = (bf16[2,128,1024]{2,1,0:T(8,128)(2,1)S(1)}, bf16[2,128,1024]{2,1,0:T(8,128)(2,1)S(1)}, u32[]{:S(2)}, u32[]{:S(2)}) collective-permute-start(bf16[2,128,1024]{2,1,0:T(8,128)(2,1)S(1)} %copy-done.6), channel_id=1, source_target_pairs={{1,2},{2,3},{3,4},{4,5},{5,6},{6,7},{7,8},{8,9},{9,10},{10,11},{11... | collective-permute-start | bytes 1572872 | tf_op jit(solution)/shard_map/ppermute | solution.py:621
  88.3 17.9 %collective-permute-start.1 = (bf16[2,128,1024]{2,1,0:T(8,128)(2,1)S(1)}, bf16[2,128,1024]{2,1,0:T(8,128)(2,1)S(1)}, u32[]{:S(2)}, u32[]{:S(2)}) collective-permute-start(bf16[2,128,1024]{2,1,0:T(8,128)(2,1)S(1)} %copy-done.6), channel_id=1, source_target_pairs={{2,1},{3,2},{4,3},{5,4},{6,5},{7,6},{8,7},{9,8},{10,9},{11,10},{12... | collective-permute-start | bytes 1572872 | tf_op jit(solution)/shard_map/ppermute | solution.py:621
  99.1 37.0 %collective-permute-start.9 = (bf16[2,128,1024]{2,1,0:T(8,128)(2,1)}, bf16[2,128,1024]{2,1,0:T(8,128)(2,1)}, u32[]{:S(2)}, u32[]{:S(2)}) collective-permute-start(bf16[2,128,1024]{2,1,0:T(8,128)(2,1)} %pick.2.rest_0_), channel_id=1, source_target_pairs={{0,1},{16,17},{32,33},{48,49},{64,65},{80,81},{96,97},{112,113}} | collective-permute-start | bytes 1572872 | tf_op jit(solution)/shard_map/ppermute | solution.py:621
  101.2 34.9 %collective-permute-start.10 = (bf16[2,128,1024]{2,1,0:T(8,128)(2,1)}, bf16[2,128,1024]{2,1,0:T(8,128)(2,1)}, u32[]{:S(2)}, u32[]{:S(2)}) collective-permute-start(bf16[2,128,1024]{2,1,0:T(8,128)(2,1)} %pick.2.rest_0_), channel_id=1, source_target_pairs={{0,2},{16,18},{32,34},{48,50},{64,66},{80,82},{96,98},{112,114}} | collective-permute-start | bytes 1572872 | tf_op jit(solution)/shard_map/ppermute | solution.py:621
  103.3 32.8 %collective-permute-start.11 = (bf16[2,128,1024]{2,1,0:T(8,128)(2,1)}, bf16[2,128,1024]{2,1,0:T(8,128)(2,1)}, u32[]{:S(2)}, u32[]{:S(2)}) collective-permute-start(bf16[2,128,1024]{2,1,0:T(8,128)(2,1)} %pick.2.rest_0_), channel_id=1, source_target_pairs={{0,3},{16,19},{32,35},{48,51},{64,67},{80,83},{96,99},{112,115}} | collective-permute-start | bytes 1572872 | tf_op jit(solution)/shard_map/ppermute | solution.py:621
  113.5 99.9 %all-to-all-start.4 = ((bf16[128,5,8,128]{3,2,1,0:T(8,128)(2,1)}), bf16[128,5,8,128]{3,2,1,0:T(8,128)(2,1)S(1)}, u32[]{:S(2)}, u32[]{:S(2)}) async-start(bf16[128,5,8,128]{3,2,1,0:T(8,128)(2,1)} %bitcast.14), calls=%async_computation.4 | async-start | bytes 2621440 | tf_op jit(solution)/shard_map/all_to_all | solution.py:618
  138.8 23.3 %collective-permute-start.12 = (bf16[2,128,1024]{2,1,0:T(8,128)(2,1)}, bf16[2,128,1024]{2,1,0:T(8,128)(2,1)S(1)}, u32[]{:S(2)}, u32[]{:S(2)}) collective-permute-start(bf16[2,128,1024]{2,1,0:T(8,128)(2,1)} %pick.3.p0), channel_id=1, source_target_pairs={{0,4},{1,5},{2,6},{3,7},{16,20},{17,21},{18,22},{19,23},{32,36},{3... | collective-permute-start | bytes 1572872 | tf_op jit(solution)/shard_map/ppermute | solution.py:621
  141.8 31.5 %collective-permute-start.13 = (bf16[2,128,1024]{2,1,0:T(8,128)(2,1)}, bf16[2,128,1024]{2,1,0:T(8,128)(2,1)S(1)}, u32[]{:S(2)}, u32[]{:S(2)}) collective-permute-start(bf16[2,128,1024]{2,1,0:T(8,128)(2,1)} %pick.3.p0), channel_id=1, source_target_pairs={{0,8},{1,9},{2,10},{3,11},{16,24},{17,25},{18,26},{19,27},{32,40},... | collective-permute-start | bytes 1572872 | tf_op jit(solution)/shard_map/ppermute | solution.py:621
  144.3 29.1 %collective-permute-start.14 = (bf16[2,128,1024]{2,1,0:T(8,128)(2,1)}, bf16[2,128,1024]{2,1,0:T(8,128)(2,1)S(1)}, u32[]{:S(2)}, u32[]{:S(2)}) collective-permute-start(bf16[2,128,1024]{2,1,0:T(8,128)(2,1)} %pick.3.p0), channel_id=1, source_target_pairs={{0,12},{1,13},{2,14},{3,15},{16,28},{17,29},{18,30},{19,31},{32,44... | collective-permute-start | bytes 1572872 | tf_op jit(solution)/shard_map/ppermute | solution.py:621
  145.6 1.6 collective-permute-start.15
  147.2 26.1 %copy-start.10 = (bf16[128,8,128]{2,1,0:T(8,128)(2,1)}, bf16[128,8,128]{2,1,0:T(8,128)(2,1)S(1)}, u32[]{:S(2)}) copy-start(bf16[128,8,128]{2,1,0:T(8,128)(2,1)S(1)} %collective-permute-done.15.other_ref) | copy-start | bytes 786436
  180.3 4.2 %collective-permute-start.18 = (f32[24,128]{1,0:T(8,128)}, f32[24,128]{1,0:T(8,128)S(1)}, u32[]{:S(2)}, u32[]{:S(2)}) collective-permute-start(f32[24,128]{1,0:T(8,128)} %get-tuple-element.50), channel_id=1, source_target_pairs={{0,3},{1,0},{2,1},{3,2},{4,7},{5,4},{6,5},{7,6},{8,11},{9,8},{10,9... | collective-permute-start | bytes 36872 | tf_op jit(solution)/shard_map/ppermute | solution.py:621
  182.5 5.4 %collective-permute-start.17 = (f32[24,128]{1,0:T(8,128)}, f32[24,128]{1,0:T(8,128)S(1)}, u32[]{:S(2)}, u32[]{:S(2)}) collective-permute-start(f32[24,128]{1,0:T(8,128)} %get-tuple-element.50), channel_id=1, source_target_pairs={{0,2},{1,3},{2,0},{3,1},{4,6},{5,7},{6,4},{7,5},{8,10},{9,11},{10,... | collective-permute-start | bytes 36872 | tf_op jit(solution)/shard_map/ppermute | solution.py:621
  183.8 5.1 %collective-permute-start.16 = (f32[24,128]{1,0:T(8,128)}, f32[24,128]{1,0:T(8,128)S(1)}, u32[]{:S(2)}, u32[]{:S(2)}) collective-permute-start(f32[24,128]{1,0:T(8,128)} %get-tuple-element.50), channel_id=1, source_target_pairs={{0,1},{1,2},{2,3},{3,0},{4,5},{5,6},{6,7},{7,4},{8,9},{9,10},{10,1... | collective-permute-start | bytes 36872 | tf_op jit(solution)/shard_map/ppermute | solution.py:621
  190.4 6.6 %collective-permute-start.19 = (f32[24,128]{1,0:T(8,128)S(1)}, f32[24,128]{1,0:T(8,128)S(1)}, u32[]{:S(2)}, u32[]{:S(2)}) collective-permute-start(f32[24,128]{1,0:T(8,128)S(1)} %pad_maximum_fusion.s0), channel_id=1, source_target_pairs={{0,4},{1,5},{2,6},{3,7},{4,8},{5,9},{6,10},{7,11},{8,12},{9,13},{1... | collective-permute-start | bytes 36872 | tf_op jit(solution)/shard_map/ppermute | solution.py:621
  190.4 6.5 %collective-permute-start.20 = (f32[24,128]{1,0:T(8,128)S(1)}, f32[24,128]{1,0:T(8,128)S(1)}, u32[]{:S(2)}, u32[]{:S(2)}) collective-permute-start(f32[24,128]{1,0:T(8,128)S(1)} %pad_maximum_fusion.s0), channel_id=1, source_target_pairs={{0,8},{1,9},{2,10},{3,11},{4,12},{5,13},{6,14},{7,15},{8,0},{9,1},... | collective-permute-start | bytes 36872 | tf_op jit(solution)/shard_map/ppermute | solution.py:621
  194.4 3.9 %collective-permute-start.21 = (f32[24,128]{1,0:T(8,128)S(1)}, f32[24,128]{1,0:T(8,128)S(1)}, u32[]{:S(2)}, u32[]{:S(2)}) collective-permute-start(f32[24,128]{1,0:T(8,128)S(1)} %pad_maximum_fusion.s0), channel_id=1, source_target_pairs={{0,12},{1,13},{2,14},{3,15},{4,0},{5,1},{6,2},{7,3},{8,4},{9,5},{1... | collective-permute-start | bytes 36872 | tf_op jit(solution)/shard_map/ppermute | solution.py:621
  204.2 34.3 %collective-permute-start.24 = (bf16[128,1024]{1,0:T(8,128)(2,1)}, bf16[128,1024]{1,0:T(8,128)(2,1)S(1)}, u32[]{:S(2)}, u32[]{:S(2)}) collective-permute-start(bf16[128,1024]{1,0:T(8,128)(2,1)} %get-tuple-element.51), channel_id=1, source_target_pairs={{12,0},{13,1},{14,2},{15,3},{28,16},{29,17},{30,18},{31,19},{44,32... | collective-permute-start | bytes 786440 | tf_op jit(solution)/shard_map/ppermute | solution.py:621
  205.5 33.1 %collective-permute-start.23 = (bf16[128,1024]{1,0:T(8,128)(2,1)}, bf16[128,1024]{1,0:T(8,128)(2,1)S(1)}, u32[]{:S(2)}, u32[]{:S(2)}) collective-permute-start(bf16[128,1024]{1,0:T(8,128)(2,1)} %get-tuple-element.51), channel_id=1, source_target_pairs={{8,0},{9,1},{10,2},{11,3},{24,16},{25,17},{26,18},{27,19},{40,32},... | collective-permute-start | bytes 786440 | tf_op jit(solution)/shard_map/ppermute | solution.py:621
  206.8 31.8 %collective-permute-start.22 = (bf16[128,1024]{1,0:T(8,128)(2,1)}, bf16[128,1024]{1,0:T(8,128)(2,1)}, u32[]{:S(2)}, u32[]{:S(2)}) collective-permute-start(bf16[128,1024]{1,0:T(8,128)(2,1)} %get-tuple-element.51), channel_id=1, source_target_pairs={{4,0},{5,1},{6,2},{7,3},{20,16},{21,17},{22,18},{23,19},{36,32},{3... | collective-permute-start | bytes 786440 | tf_op jit(solution)/shard_map/ppermute | solution.py:621
  213.3 25.2 %copy-start.21 = (bf16[128,1024]{1,0:T(8,128)(2,1)S(1)}, bf16[128,1024]{1,0:T(8,128)(2,1)}, u32[]{:S(2)}) copy-start(bf16[128,1024]{1,0:T(8,128)(2,1)} %get-tuple-element.51) | copy-start | bytes 786436
  214.4 64.7 %all-to-all-start.3 = ((bf16[128,5,8,128]{3,2,1,0:T(8,128)(2,1)}), bf16[128,5,8,128]{3,2,1,0:T(8,128)(2,1)S(1)}, u32[]{:S(2)}, u32[]{:S(2)}) async-start(bf16[128,5,8,128]{3,2,1,0:T(8,128)(2,1)} %bitcast.15), calls=%async_computation.3 | async-start | bytes 2621440 | tf_op jit(solution)/shard_map/all_to_all | solution.py:618
  239.7 26.5 %collective-permute-start.27 = (bf16[128,1024]{1,0:T(8,128)(2,1)S(1)}, bf16[128,1024]{1,0:T(8,128)(2,1)S(1)}, u32[]{:S(2)}, u32[]{:S(2)}) collective-permute-start(bf16[128,1024]{1,0:T(8,128)(2,1)S(1)} %add_convert_fusion.1), channel_id=1, source_target_pairs={{3,0},{19,16},{35,32},{51,48},{67,64},{83,80},{99,96},{115,112}} | collective-permute-start | bytes 786440 | tf_op jit(solution)/shard_map/ppermute | solution.py:621
  241.0 25.2 %collective-permute-start.26 = (bf16[128,1024]{1,0:T(8,128)(2,1)S(1)}, bf16[128,1024]{1,0:T(8,128)(2,1)S(1)}, u32[]{:S(2)}, u32[]{:S(2)}) collective-permute-start(bf16[128,1024]{1,0:T(8,128)(2,1)S(1)} %add_convert_fusion.1), channel_id=1, source_target_pairs={{2,0},{18,16},{34,32},{50,48},{66,64},{82,80},{98,96},{114,112}} | collective-permute-start | bytes 786440 | tf_op jit(solution)/shard_map/ppermute | solution.py:621
  242.3 23.9 %collective-permute-start.25 = (bf16[128,1024]{1,0:T(8,128)(2,1)S(1)}, bf16[128,1024]{1,0:T(8,128)(2,1)S(1)}, u32[]{:S(2)}, u32[]{:S(2)}) collective-permute-start(bf16[128,1024]{1,0:T(8,128)(2,1)S(1)} %add_convert_fusion.1), channel_id=1, source_target_pairs={{1,0},{17,16},{33,32},{49,48},{65,64},{81,80},{97,96},{113,112}} | collective-permute-start | bytes 786440 | tf_op jit(solution)/shard_map/ppermute | solution.py:621
  243.6 28.0 %collective-permute-start.37 = (bf16[1024,128]{1,0:T(8,128)(2,1)S(1)}, bf16[1024,128]{1,0:T(8,128)(2,1)S(1)}, u32[]{:S(2)}, u32[]{:S(2)}) collective-permute-start(bf16[1024,128]{1,0:T(8,128)(2,1)S(1)} %copy-done.33), channel_id=1, source_target_pairs={{0,16},{1,17},{2,18},{3,19},{4,20},{5,21},{6,22},{7,23},{8,24},{9,... | collective-permute-start | bytes 786440 | tf_op jit(solution)/shard_map/ppermute | solution.py:621
  266.4 33.7 %copy-start.9 = (bf16[128,1024]{1,0:T(8,128)(2,1)}, bf16[128,1024]{1,0:T(8,128)(2,1)S(1)}, u32[]{:S(2)}) copy-start(bf16[128,1024]{1,0:T(8,128)(2,1)S(1)} %add_convert_fusion.rest_0_) | copy-start | bytes 786436
  266.5 8.3 %collective-permute-start.28 = (bf16[128,1024]{1,0:T(8,128)(2,1)S(1)}, bf16[128,1024]{1,0:T(8,128)(2,1)S(1)}, u32[]{:S(2)}, u32[]{:S(2)}) collective-permute-start(bf16[128,1024]{1,0:T(8,128)(2,1)S(1)} %add_convert_fusion.rest_0_), channel_id=1, source_target_pairs={{32,0}} | collective-permute-start | bytes 786440 | tf_op jit(solution)/shard_map/ppermute | solution.py:621
  267.8 29.7 %collective-permute-start.29 = (bf16[128,1024]{1,0:T(8,128)(2,1)S(1)}, bf16[128,1024]{1,0:T(8,128)(2,1)}, u32[]{:S(2)}, u32[]{:S(2)}) collective-permute-start(bf16[128,1024]{1,0:T(8,128)(2,1)S(1)} %add_convert_fusion.rest_0_), channel_id=1, source_target_pairs={{64,0}} | collective-permute-start | bytes 786440 | tf_op jit(solution)/shard_map/ppermute | solution.py:621
  269.1 29.7 %collective-permute-start.30 = (bf16[128,1024]{1,0:T(8,128)(2,1)S(1)}, bf16[128,1024]{1,0:T(8,128)(2,1)}, u32[]{:S(2)}, u32[]{:S(2)}) collective-permute-start(bf16[128,1024]{1,0:T(8,128)(2,1)S(1)} %add_convert_fusion.rest_0_), channel_id=1, source_target_pairs={{96,0}} | collective-permute-start | bytes 786440 | tf_op jit(solution)/shard_map/ppermute | solution.py:621
  270.4 29.7 %collective-permute-start.31 = (bf16[128,1024]{1,0:T(8,128)(2,1)S(1)}, bf16[128,1024]{1,0:T(8,128)(2,1)}, u32[]{:S(2)}, u32[]{:S(2)}) collective-permute-start(bf16[128,1024]{1,0:T(8,128)(2,1)S(1)} %add_convert_fusion.rest_0_), channel_id=1, source_target_pairs={{16,0}} | collective-permute-start | bytes 786440 | tf_op jit(solution)/shard_map/ppermute | solution.py:621
  271.7 44.8 %collective-permute-start.35 = (bf16[2,128,1024]{2,1,0:T(8,128)(2,1)}, bf16[2,128,1024]{2,1,0:T(8,128)(2,1)S(1)}, u32[]{:S(2)}, u32[]{:S(2)}) collective-permute-start(bf16[2,128,1024]{2,1,0:T(8,128)(2,1)} %get-tuple-element.53), channel_id=1, source_target_pairs={{1,2},{2,3},{3,4},{4,5},{5,6},{6,7},{7,8},{8,9},{9,10},{10,11},{11... | collective-permute-start | bytes 1572872 | tf_op jit(solution)/shard_map/ppermute | solution.py:621
  274.7 41.7 %collective-permute-start.36 = (bf16[2,128,1024]{2,1,0:T(8,128)(2,1)}, bf16[2,128,1024]{2,1,0:T(8,128)(2,1)S(1)}, u32[]{:S(2)}, u32[]{:S(2)}) collective-permute-start(bf16[2,128,1024]{2,1,0:T(8,128)(2,1)} %get-tuple-element.54), channel_id=1, source_target_pairs={{2,1},{3,2},{4,3},{5,4},{6,5},{7,6},{8,7},{9,8},{10,9},{11,10},{12... | collective-permute-start | bytes 1572872 | tf_op jit(solution)/shard_map/ppermute | solution.py:621
  284.5 32.0 %all-to-all-start.5 = ((bf16[128,2,8,128]{3,2,1,0:T(8,128)(2,1)}), bf16[128,2,8,128]{3,2,1,0:T(8,128)(2,1)S(1)}, u32[]{:S(2)}, u32[]{:S(2)}) async-start(bf16[128,2,8,128]{3,2,1,0:T(8,128)(2,1)} %scatter_last.1), calls=%async_computation.5 | async-start | bytes 1048576 | tf_op jit(solution)/shard_map/all_to_all | solution.py:618
  297.5 10.4 %collective-permute-start.32 = (bf16[128,1024]{1,0:T(8,128)(2,1)S(1)}, bf16[128,1024]{1,0:T(8,128)(2,1)S(1)}, u32[]{:S(2)}, u32[]{:S(2)}) collective-permute-start(bf16[128,1024]{1,0:T(8,128)(2,1)S(1)} %add_convert_fusion.rest_0_), channel_id=1, source_target_pairs={{48,0}} | collective-permute-start | bytes 786440 | tf_op jit(solution)/shard_map/ppermute | solution.py:621
  298.8 11.1 %collective-permute-start.33 = (bf16[128,1024]{1,0:T(8,128)(2,1)S(1)}, bf16[128,1024]{1,0:T(8,128)(2,1)S(1)}, u32[]{:S(2)}, u32[]{:S(2)}) collective-permute-start(bf16[128,1024]{1,0:T(8,128)(2,1)S(1)} %add_convert_fusion.rest_0_), channel_id=1, source_target_pairs={{80,0}} | collective-permute-start | bytes 786440 | tf_op jit(solution)/shard_map/ppermute | solution.py:621
  300.1 12.5 %collective-permute-start.34 = (bf16[128,1024]{1,0:T(8,128)(2,1)S(1)}, bf16[128,1024]{1,0:T(8,128)(2,1)S(1)}, u32[]{:S(2)}, u32[]{:S(2)}) collective-permute-start(bf16[128,1024]{1,0:T(8,128)(2,1)S(1)} %add_convert_fusion.rest_0_), channel_id=1, source_target_pairs={{112,0}} | collective-permute-start | bytes 786440 | tf_op jit(solution)/shard_map/ppermute | solution.py:621
  (30 other events, 105.2 us)

commit v7 on v6

--- a/solution.py
+++ b/solution.py
@@ -53,10 +53,11 @@
         in_specs=[pl.BlockSpec(memory_space=VM)] * 2,
         out_specs=[pl.BlockSpec(memory_space=VM)] * 2,
         name="pack_pieces",
+        compiler_params=pltpu.CompilerParams(vmem_limit_bytes=12 << 20),
     )(k, v)
 
 
-def gather_body(table_ref, held_ref, out_ref, *, rows, chunk):
+def gather_body(table_ref, meta_ref, held_ref, out_ref, *give_ref, rows, chunk):
     base = pl.program_id(0) * rows
 
     def one(d, carry):
@@ -66,148 +67,90 @@
         return carry
 
     lax.fori_loop(0, rows, one, 0, unroll=8)
-
-
-def gather_pieces(table, held, blocks, chunk):
+    if give_ref:
+
+        @pl.when(pl.program_id(0) == 0)
+        def _():
+            give_ref[0][...] = held_ref[:, 1 - meta_ref[1]]
+
+
+def gather_pieces(table, meta, held, blocks, chunk, give):
     steps = 2
     rows = blocks // steps
+    shapes = [jax.ShapeDtypeStruct((blocks, SENT, PIECE, HEAD_SIZE), BF16)]
+    specs = [pl.BlockSpec((rows, SENT, PIECE, HEAD_SIZE), lambda i, t, m: (i, 0, 0, 0))]
+    if give:
+        shapes.append(jax.ShapeDtypeStruct((blocks, PIECE, HEAD_SIZE), BF16))
+        specs.append(pl.BlockSpec((blocks, PIECE, HEAD_SIZE), lambda i, t, m: (0, 0, 0)))
     return pl.pallas_call(
         functools.partial(gather_body, rows=rows, chunk=chunk),
-        out_shape=jax.ShapeDtypeStruct((blocks, SENT, PIECE, HEAD_SIZE), BF16),
-        grid_spec=pltpu.PrefetchScalarGridSpec(
-            num_scalar_prefetch=1,
-            grid=(steps,),
-            in_specs=[
-                pl.BlockSpec((blocks, CHUNKS, PIECE, HEAD_SIZE), lambda i, t: (0, 0, 0, 0))
-            ],
-            out_specs=pl.BlockSpec((rows, SENT, PIECE, HEAD_SIZE), lambda i, t: (i, 0, 0, 0)),
-        ),
-        name="gather_pieces",
-    )(table, held)
-
-
-def gather_give_body(table_ref, meta_ref, held_ref, out_ref, give_ref, *, rows, chunk):
-    gather_body(table_ref, held_ref, out_ref, rows=rows, chunk=chunk)
-
-    @pl.when(pl.program_id(0) == 0)
-    def _():
-        give_ref[...] = held_ref[:, 1 - meta_ref[1]]
-
-
-def gather_give(table, meta, held, blocks, chunk):
-    steps = 2
-    rows = blocks // steps
-    return pl.pallas_call(
-        functools.partial(gather_give_body, rows=rows, chunk=chunk),
-        out_shape=(
-            jax.ShapeDtypeStruct((blocks, SENT, PIECE, HEAD_SIZE), BF16),
-            jax.ShapeDtypeStruct((blocks, PIECE, HEAD_SIZE), BF16),
-        ),
+        out_shape=shapes,
         grid_spec=pltpu.PrefetchScalarGridSpec(
             num_scalar_prefetch=2,
             grid=(steps,),
-            in_specs=[
-                pl.BlockSpec((blocks, CHUNKS, PIECE, HEAD_SIZE), lambda i, t, m: (0, 0, 0, 0))
-            ],
-            out_specs=[
-                pl.BlockSpec((rows, SENT, PIECE, HEAD_SIZE), lambda i, t, m: (i, 0, 0, 0)),
-                pl.BlockSpec((blocks, PIECE, HEAD_SIZE), lambda i, t, m: (0, 0, 0)),
-            ],
+            in_specs=[pl.BlockSpec(memory_space=VM)],
+            out_specs=specs,
         ),
-        name="gather_give",
+        name="gather_pieces",
+        compiler_params=pltpu.CompilerParams(vmem_limit_bytes=12 << 20),
     )(table, meta, held)
 
 
-def add_listed(table_ref, got_ref, accs, rows):
-    base = pl.program_id(0) * rows
-
-    @pl.when(pl.program_id(0) == 0)
-    def _():
-        for acc in accs:
-            acc[...] = jnp.zeros_like(acc)
+def add_listed(table_ref, got_ref, accs, blocks):
+    for acc in accs:
+        acc[...] = jnp.zeros_like(acc)
 
     def one(d, total):
         for s in range(1, SENT):
-            block = table_ref[(base + d) * NB + FIRST_SENT + s]
-            accs[s][block] += got_ref[d, s].astype(F32)
+            block = table_ref[d * NB + FIRST_SENT + s]
+            accs[s - 1][block] += got_ref[d, s].astype(F32)
         return total + got_ref[d, 0].astype(F32)
 
     zero = jnp.zeros((PIECE, HEAD_SIZE), F32)
-    accs[0][...] += lax.fori_loop(0, rows, one, zero, unroll=8)
-
-
-def listed_total(accs):
-    accs[1][0] += accs[0][...]
-    return (accs[1][...] + accs[2][...]) + (accs[3][...] + accs[4][...])
-
-
-def scatter_body(table_ref, got_ref, out_ref, *accs, rows):
-    add_listed(table_ref, got_ref, accs, rows)
-
-    @pl.when(pl.program_id(0) == pl.num_programs(0) - 1)
-    def _():
-        out_ref[...] = listed_total(accs)
+    accs[0][0] += lax.fori_loop(0, blocks, one, zero, unroll=8)
+    return (accs[0][...] + accs[1][...]) + (accs[2][...] + accs[3][...])
+
+
+def scatter_body(table_ref, got_ref, out_ref, *accs, blocks):
+    out_ref[...] = add_listed(table_ref, got_ref, accs, blocks)
 
 
 def scatter_last_body(
-    table_ref, meta_ref, got_ref, first_ref, dense_ref, other_ref, out_ref, *accs, rows
+    table_ref, meta_ref, got_ref, first_ref, dense_ref, other_ref, out_ref, *accs, blocks
 ):
-    add_listed(table_ref, got_ref, accs, rows)
-
-    @pl.when(pl.program_id(0) == pl.num_programs(0) - 1)
-    def _():
-        core = meta_ref[1]
-        second = listed_total(accs)
-        mine = dense_ref[...].reshape(second.shape)
-        other = other_ref[...].astype(F32).reshape(second.shape)
-        out_ref[:, core] = (jnp.where(core == 0, first_ref[...], second) + mine).astype(BF16)
-        out_ref[:, 1 - core] = (jnp.where(core == 0, second, first_ref[...]) + other).astype(BF16)
+    core = meta_ref[1]
+    second = add_listed(table_ref, got_ref, accs, blocks)
+    mine = dense_ref[...].reshape(second.shape)
+    other = other_ref[...].astype(F32).reshape(second.shape)
+    out_ref[:, core] = (jnp.where(core == 0, first_ref[...], second) + mine).astype(BF16)
+    out_ref[:, 1 - core] = (jnp.where(core == 0, second, first_ref[...]) + other).astype(BF16)
 
 
 def slot_sums(blocks):
-    whole = VM((blocks, PIECE, HEAD_SIZE), F32)
-    return [VM((PIECE, HEAD_SIZE), F32)] + [whole] * (SENT - 1)
+    return [VM((blocks, PIECE, HEAD_SIZE), F32)] * (SENT - 1)
 
 
 def scatter_pieces(table, got, blocks):
-    steps = 2
-    rows = blocks // steps
-    return pl.pallas_call(
-        functools.partial(scatter_body, rows=rows),
+    return pl.pallas_call(
+        functools.partial(scatter_body, blocks=blocks),
         out_shape=jax.ShapeDtypeStruct((blocks, PIECE, HEAD_SIZE), F32),
-        grid_spec=pltpu.PrefetchScalarGridSpec(
-            num_scalar_prefetch=1,
-            grid=(steps,),
-            in_specs=[pl.BlockSpec((rows, SENT, PIECE, HEAD_SIZE), lambda i, t: (i, 0, 0, 0))],
-            out_specs=pl.BlockSpec((blocks, PIECE, HEAD_SIZE), lambda i, t: (0, 0, 0)),
-            scratch_shapes=slot_sums(blocks),
-        ),
+        in_specs=[pl.BlockSpec(memory_space=pltpu.SMEM), pl.BlockSpec(memory_space=VM)],
+        out_specs=pl.BlockSpec(memory_space=VM),
+        scratch_shapes=slot_sums(blocks),
         name="scatter_pieces",
+        compiler_params=pltpu.CompilerParams(vmem_limit_bytes=12 << 20),
     )(table, got)
 
 
 def scatter_last(table, meta, got, first, dense, other, blocks):
-    steps = 2
-    rows = blocks // steps
-    whole = pl.BlockSpec((blocks, PIECE, HEAD_SIZE), lambda i, t, m: (0, 0, 0))
-    return pl.pallas_call(
-        functools.partial(scatter_last_body, rows=rows),
+    return pl.pallas_call(
+        functools.partial(scatter_last_body, blocks=blocks),
         out_shape=jax.ShapeDtypeStruct((blocks, CHUNKS, PIECE, HEAD_SIZE), BF16),
-        grid_spec=pltpu.PrefetchScalarGridSpec(
-            num_scalar_prefetch=2,
-            grid=(steps,),
-            in_specs=[
-                pl.BlockSpec((rows, SENT, PIECE, HEAD_SIZE), lambda i, t, m: (i, 0, 0, 0)),
-                whole,
-                pl.BlockSpec((blocks * PIECE, HEAD_SIZE), lambda i, t, m: (0, 0)),
-                pl.BlockSpec((blocks * PIECE, HEAD_SIZE), lambda i, t, m: (0, 0)),
-            ],
-            out_specs=pl.BlockSpec(
-                (blocks, CHUNKS, PIECE, HEAD_SIZE), lambda i, t, m: (0, 0, 0, 0)
-            ),
-            scratch_shapes=slot_sums(blocks),
-        ),
+        in_specs=[pl.BlockSpec(memory_space=pltpu.SMEM)] * 2 + [pl.BlockSpec(memory_space=VM)] * 4,
+        out_specs=pl.BlockSpec(memory_space=VM),
+        scratch_shapes=slot_sums(blocks),
         name="scatter_last",
+        compiler_params=pltpu.CompilerParams(vmem_limit_bytes=12 << 20),
     )(table, meta, got, first, dense, other)
 
 
@@ -243,7 +186,7 @@
                 dst[s * BLOCK : (s + 1) * BLOCK] = part[kv]
             for s in range(SENT):
                 at = (FIRST_SENT + s) * BLOCK
-                dst[at : at + BLOCK] = g_ref[0, kv, :, s].reshape(BLOCK, HEAD_SIZE)
+                dst[at : at + BLOCK] = g_ref[pl.program_id(0), kv, :, s].reshape(BLOCK, HEAD_SIZE)
         kt[...] = kc[...].T
         live = [valid_ref[b * NB + s] > 0 for s in range(NB)]
 
@@ -325,7 +268,7 @@
         grid_spec=pltpu.PrefetchScalarGridSpec(
             num_scalar_prefetch=2,
             grid=(CALL_HEADS,),
-            in_specs=[wide, wide, pair, pair, pair, pieces]
+            in_specs=[wide, wide, pair, pair, pair, pl.BlockSpec(memory_space=VM)]
             + [pl.BlockSpec(memory_space=pl.ANY)] * len(earlier),
             out_specs=[wide, pair, pair, pair, pieces],
             scratch_shapes=[
@@ -342,6 +285,7 @@
         ),
         input_output_aliases={8 + n: n for n in range(len(earlier))},
         name="sparse_grads",
+        compiler_params=pltpu.CompilerParams(vmem_limit_bytes=24 << 20),
     )(meta, valid, q, o, own, before, after, got, *earlier)
 
 
@@ -403,6 +347,7 @@
             pltpu.SemaphoreType.DMA(()),
         ],
         name="dense_stats",
+        compiler_params=pltpu.CompilerParams(vmem_limit_bytes=20 << 20),
     )(meta, *parts, held, other)
 
 
@@ -471,6 +416,7 @@
             VM((2, keys, HEAD_SIZE), F32),
         ],
         name="dense_grads",
+        compiler_params=pltpu.CompilerParams(vmem_limit_bytes=24 << 20),
     )(meta, qo, held, other, *stats)
 
 
@@ -492,6 +438,7 @@
         in_specs=[pl.BlockSpec(memory_space=VM)] * 4,
         out_specs=[pl.BlockSpec(memory_space=VM)] * 2,
         name="combine",
+        compiler_params=pltpu.CompilerParams(vmem_limit_bytes=12 << 20),
     )(own, from_prev, from_next, got)
 
 
@@ -530,6 +477,7 @@
             pltpu.SemaphoreType.DMA((2, KEY_HEADS, 2)),
         ],
         name="spread_heads",
+        compiler_params=pltpu.CompilerParams(vmem_limit_bytes=12 << 20),
     )(meta, q, o)
 
 
@@ -565,6 +513,7 @@
             pltpu.SemaphoreType.DMA((2, KEY_HEADS)),
         ],
         name="put_first",
+        compiler_params=pltpu.CompilerParams(vmem_limit_bytes=12 << 20),
     )(meta, dq, *parts)
 
 
@@ -588,6 +537,7 @@
         out_specs=pl.BlockSpec(memory_space=VM),
         scratch_shapes=[pltpu.SemaphoreType.DMA(())],
         name="pick",
+        compiler_params=pltpu.CompilerParams(vmem_limit_bytes=12 << 20),
     )(meta, *parts)
 
 
@@ -637,8 +587,8 @@
     for c in (4, 2, 6, 3, 5, 7, 1):
         moved[c] = send(slices[c // 2 + HALF * (c % 2)], [(0, c * tp_size)])
 
-    listed = [gather_pieces(table, held, blocks, 0)]
-    more, given = gather_give(table, meta, held, blocks, 1)
+    listed = list(gather_pieces(table, meta, held, blocks, 0, False))
+    more, given = gather_pieces(table, meta, held, blocks, 1, True)
     listed.append(more)
     given = send(given, partner)
     shape = (HALF, 2, GROUPS, SENT, PIECE, HEAD_SIZE)

time: 322 us -> 313 us (0.972)
  Pallas kernels: 53.8 us -> 32.7 us
  starting transfers between devices: 138 us -> 147 us
  local copies, waits for them, and re-layouts: 14.8 us -> 22.9 us
    unnamed x70 -> x64, local copies, waits for them, and re-layouts: 12.8 us -> 22.7 us
    all_to_all x6, starting transfers between devices: 80.1 us -> 88.9 us  [swap(): return lax.all_to_all(x, BOTH, split_axis=0, concat_axis=0, tiled=True)]
    pallas_call x3 -> x2, Pallas kernels: 11.6 us -> 5 us  [the longest x1 2.69 us: scatter_last(): pl.pallas_call(functools.partial(scatter_last_body, blocks=blocks), out_s...]
    pallas_call x2, Pallas kernels: 5.32 us -> 1.26 us  [pick(): pl.pallas_call(functools.partial(pick_body, at=at), out_shape=jax.ShapeDt...]
  transfers between devices with their start and end apart: 44 -> 44, of which waited for: 16 -> 16; matrix products, arithmetic and copies ran while one was open for 2% -> 1% of each run, Pallas kernels for 14% -> 9%
where the time goes in v7:
time: 313 us; the launch traced here: 312 us
  starting transfers between devices  147 us (47%)
  waiting for transfers between devices  107 us (34%)
  Pallas kernels  32.7 us (10%)
  local copies, waits for them, and re-layouts  22.9 us (7%)
    all_to_all x6, starting transfers between devices, swap(): return lax.all_to_all(x, BOTH, split_axis=0, concat_axis=0, tiled=True)  88.9 us
    ppermute x38, waiting for transfers between devices, send(): return lax.ppermute(x, BOTH, pairs)  86.7 us
    ppermute x38, starting transfers between devices, send(): return lax.ppermute(x, BOTH, pairs)  57.7 us
    unnamed x64, local copies, waits for them, and re-layouts  22.7 us
    all_to_all x6, waiting for transfers between devices, swap(): return lax.all_to_all(x, BOTH, split_axis=0, concat_axis=0, tiled=True)  19.9 us
    pallas_call x2, Pallas kernels, sparse_grads(): pl.pallas_call(sparse_body, out_shape=(jax.ShapeDtypeStruct(q.shape, BF16...  9.48 us
  transfers between devices with their start and end apart: 44, of which 16 were waited for; matrix products, arithmetic and copies ran while one was open for 1% of the time, Pallas kernels for 9%

profile of v7, /device:TPU:0, one launch (start us, length us, event | category | flops | bytes accessed | tf_op | source)
XLA Modules:
  0.0 311.8 jit_solution(9217945941656621768)
XLA Ops:
  3.6 11.2 %all-to-all-start = ((bf16[128,2,8,128]{3,2,1,0:T(8,128)(2,1)}), bf16[128,2,8,128]{3,2,1,0:T(8,128)(2,1)S(1)}, u32[]{:S(2)}, u32[]{:S(2)}) async-start(bf16[128,2,8,128]{3,2,1,0:T(8,128)(2,1)} %bitcast.5), calls=%async_computation | async-start | bytes 1048576 | tf_op jit(solution)/shard_map/all_to_all | solution.py:568
  15.1 13.2 %all-to-all-done.held_ref = bf16[128,2,8,128]{3,2,1,0:T(8,128)(2,1)S(1)} async-done(((bf16[128,2,8,128]{3,2,1,0:T(8,128)(2,1)}), bf16[128,2,8,128]{3,2,1,0:T(8,128)(2,1)S(1)}, u32[]{:S(2)}, u32[]{:S(2)}) %all-to-all-start) | async-done | bytes 524320 | tf_op jit(solution)/shard_map/all_to_all | solution.py:568
  28.4 1.5 gather_pieces.3
  30.9 5.8 %all-to-all-start.2 = ((bf16[128,5,8,128]{3,2,1,0:T(8,128)(2,1)}), bf16[128,5,8,128]{3,2,1,0:T(8,128)(2,1)}, u32[]{:S(2)}, u32[]{:S(2)}) async-start(bf16[128,5,8,128]{3,2,1,0:T(8,128)(2,1)} %copy-done.4), calls=%async_computation.2 | async-start | bytes 2621440 | tf_op jit(solution)/shard_map/all_to_all | solution.py:568
  36.8 1.6 copy-done.1
  38.4 2.2 spread_heads.1
  46.8 2.1 collective-permute-start.3
  48.9 1.6 gather_pieces.2
  51.5 6.7 %all-to-all-done.2 = bf16[128,5,8,128]{3,2,1,0:T(8,128)(2,1)} async-done(((bf16[128,5,8,128]{3,2,1,0:T(8,128)(2,1)}), bf16[128,5,8,128]{3,2,1,0:T(8,128)(2,1)}, u32[]{:S(2)}, u32[]{:S(2)}) %all-to-all-start.2) | async-done | bytes 1310752 | tf_op jit(solution)/shard_map/all_to_all | solution.py:568
  58.2 5.7 %all-to-all-start.1 = ((bf16[128,5,8,128]{3,2,1,0:T(8,128)(2,1)}), bf16[128,5,8,128]{3,2,1,0:T(8,128)(2,1)}, u32[]{:S(2)}, u32[]{:S(2)}) async-start(bf16[128,5,8,128]{3,2,1,0:T(8,128)(2,1)} %copy-done.10), calls=%async_computation.1 | async-start | bytes 2621440 | tf_op jit(solution)/shard_map/all_to_all | solution.py:568
  63.9 2.5 collective-permute-start.4
  66.4 2.5 collective-permute-start.5
  68.9 1.3 collective-permute-start.6
  73.7 8.5 %collective-permute-done.4.rest_3_ = bf16[2,128,1024]{2,1,0:T(8,128)(2,1)S(1)} collective-permute-done((bf16[2,128,1024]{2,1,0:T(8,128)(2,1)}, bf16[2,128,1024]{2,1,0:T(8,128)(2,1)S(1)}, u32[]{:S(2)}, u32[]{:S(2)}) %collective-permute-start.4) | collective-permute-done | bytes 524320 | tf_op jit(solution)/shard_map/ppermute | solution.py:571
  82.2 1.5 collective-permute-start
  83.7 4.1 %collective-permute-done.5.rest_4_ = bf16[2,128,1024]{2,1,0:T(8,128)(2,1)S(1)} collective-permute-done((bf16[2,128,1024]{2,1,0:T(8,128)(2,1)}, bf16[2,128,1024]{2,1,0:T(8,128)(2,1)S(1)}, u32[]{:S(2)}, u32[]{:S(2)}) %collective-permute-start.5) | collective-permute-done | bytes 524320 | tf_op jit(solution)/shard_map/ppermute | solution.py:571
  87.8 1.5 collective-permute-start.1
  89.3 4.1 %collective-permute-done.6.rest_5_ = bf16[2,128,1024]{2,1,0:T(8,128)(2,1)S(1)} collective-permute-done((bf16[2,128,1024]{2,1,0:T(8,128)(2,1)}, bf16[2,128,1024]{2,1,0:T(8,128)(2,1)S(1)}, u32[]{:S(2)}, u32[]{:S(2)}) %collective-permute-start.6) | collective-permute-done | bytes 524320 | tf_op jit(solution)/shard_map/ppermute | solution.py:571
  96.2 2.1 collective-permute-start.9
  98.3 2.1 collective-permute-start.10
  100.4 2.1 collective-permute-start.11
  102.7 1.6 copy-done.2
  104.3 4.7 %sparse_grads.2 = (bf16[128,8192]{1,0:T(8,128)(2,1)}, f32[2,128,1024]{2,1,0:T(8,128)S(1)}, bf16[2,128,1024]{2,1,0:T(8,128)(2,1)}, bf16[2,128,1024]{2,1,0:T(8,128)(2,1)}, bf16[4,2,16,5,8,128]{5,4,3,2,1,0:T(8,128)(2,1)S(1)}) custom-call(s32[5]{0:T(128)S(1)} %stack.23.meta_ref, s32[1024]{0:T(1024)S(1)} %reshape.30.valid_ref, bf16[128,8192]{1,0:T(8,128)(2,1)S(1)} %copy-done, ...), custom_call_target="tpu_custom_call" | custom-call | tf_op jit(solution)/shard_map/sparse_grads/pallas_call | solution.py:259
  111.1 27.1 %all-to-all-start.4 = ((bf16[128,5,8,128]{3,2,1,0:T(8,128)(2,1)}), bf16[128,5,8,128]{3,2,1,0:T(8,128)(2,1)}, u32[]{:S(2)}, u32[]{:S(2)}) async-start(bf16[128,5,8,128]{3,2,1,0:T(8,128)(2,1)} %bitcast.12), calls=%async_computation.4 | async-start | bytes 2621440 | tf_op jit(solution)/shard_map/all_to_all | solution.py:568
  138.8 3.0 collective-permute-start.12
  141.8 2.5 collective-permute-start.13
  144.3 1.3 collective-permute-start.14
  145.7 1.5 collective-permute-done.15.other_ref
  147.2 16.4 %collective-permute-done.12.p1 = bf16[2,128,1024]{2,1,0:T(8,128)(2,1)S(1)} collective-permute-done((bf16[2,128,1024]{2,1,0:T(8,128)(2,1)S(1)}, bf16[2,128,1024]{2,1,0:T(8,128)(2,1)S(1)}, u32[]{:S(2)}, u32[]{:S(2)}) %collective-permute-start.12) | collective-permute-done | bytes 524320 | tf_op jit(solution)/shard_map/ppermute | solution.py:571
  163.7 11.1 %collective-permute-done.13.p2 = bf16[2,128,1024]{2,1,0:T(8,128)(2,1)S(1)} collective-permute-done((bf16[2,128,1024]{2,1,0:T(8,128)(2,1)S(1)}, bf16[2,128,1024]{2,1,0:T(8,128)(2,1)S(1)}, u32[]{:S(2)}, u32[]{:S(2)}) %collective-permute-start.13) | collective-permute-done | bytes 524320 | tf_op jit(solution)/shard_map/ppermute | solution.py:571
  174.8 3.1 dense_stats.1
  177.9 2.3 collective-permute-start.18
  182.2 3.2 %collective-permute-done.17 = f32[24,128]{1,0:T(8,128)S(1)} collective-permute-done((f32[24,128]{1,0:T(8,128)S(1)}, f32[24,128]{1,0:T(8,128)S(1)}, u32[]{:S(2)}, u32[]{:S(2)}) %collective-permute-start.17) | collective-permute-done | bytes 12320 | tf_op jit(solution)/shard_map/ppermute | solution.py:571
  186.4 4.1 %collective-permute-start.20 = (f32[24,128]{1,0:T(8,128)S(1)}, f32[24,128]{1,0:T(8,128)S(1)}, u32[]{:S(2)}, u32[]{:S(2)}) collective-permute-start(f32[24,128]{1,0:T(8,128)S(1)} %pad_maximum_fusion.s0), channel_id=1, source_target_pairs={{0,8},{1,9},{2,10},{3,11},{4,12},{5,13},{6,14},{7,15},{8,0},{9,1},... | collective-permute-start | bytes 36872 | tf_op jit(solution)/shard_map/ppermute | solution.py:571
  190.5 2.5 collective-permute-start.21
  193.0 1.4 collective-permute-done.21.s3
  194.4 3.6 %dense_grads.1 = (f32[1024,128]{1,0:T(8,128)S(1)}, bf16[1024,128]{1,0:T(8,128)(2,1)S(1)}, bf16[128,1024]{1,0:T(8,128)(2,1)S(1)}) custom-call(s32[5]{0:T(128)S(1)} %stack.23.meta_ref, bf16[2,128,1024]{2,1,0:T(8,128)(2,1)S(1)} %get-tuple-element.49.q_ref, bf16[128,2,8,128]{3,2,1,0:T(8,128)(2,1)S(1)} %all-to-all-done.held_ref, ...), custom_call_target="tpu_custom_call" | custom-call | tf_op jit(solution)/shard_map/dense_grads/pallas_call | solution.py:402
  202.7 4.8 %sparse_grads.3 = (bf16[128,8192]{1,0:T(8,128)(2,1)}, f32[2,128,1024]{2,1,0:T(8,128)S(1)}, bf16[2,128,1024]{2,1,0:T(8,128)(2,1)}, bf16[2,128,1024]{2,1,0:T(8,128)(2,1)}, bf16[4,2,16,5,8,128]{5,4,3,2,1,0:T(8,128)(2,1)S(1)}) custom-call(s32[5]{0:T(128)S(1)} %stack.23.meta_ref, ...), custom_call_target="tpu_custom_call", output_to_operand_aliasing={{0}: (8, {}), {1}: (9, {}), {2}: (10, {}), {3}: (11, {})} | custom-call | tf_op jit(solution)/shard_map/sparse_grads/pallas_call | solution.py:259
  209.5 25.5 %all-to-all-start.3 = ((bf16[128,5,8,128]{3,2,1,0:T(8,128)(2,1)}), bf16[128,5,8,128]{3,2,1,0:T(8,128)(2,1)S(1)}, u32[]{:S(2)}, u32[]{:S(2)}) async-start(bf16[128,5,8,128]{3,2,1,0:T(8,128)(2,1)} %bitcast.13), calls=%async_computation.3 | async-start | bytes 2621440 | tf_op jit(solution)/shard_map/all_to_all | solution.py:568
  240.3 22.4 %collective-permute-done.27 = bf16[128,1024]{1,0:T(8,128)(2,1)S(1)} collective-permute-done((bf16[128,1024]{1,0:T(8,128)(2,1)S(1)}, bf16[128,1024]{1,0:T(8,128)(2,1)S(1)}, u32[]{:S(2)}, u32[]{:S(2)}) %collective-permute-start.27) | collective-permute-done | bytes 262176 | tf_op jit(solution)/shard_map/ppermute | solution.py:571
  269.6 1.7 collective-permute-done.28.rest_1_
  271.9 2.3 scatter_pieces.1.first_ref
  276.2 2.7 scatter_last.1
  278.9 13.7 %all-to-all-start.5 = ((bf16[128,2,8,128]{3,2,1,0:T(8,128)(2,1)}), bf16[128,2,8,128]{3,2,1,0:T(8,128)(2,1)S(1)}, u32[]{:S(2)}, u32[]{:S(2)}) async-start(bf16[128,2,8,128]{3,2,1,0:T(8,128)(2,1)} %scatter_last.1), calls=%async_computation.5 | async-start | bytes 1048576 | tf_op jit(solution)/shard_map/all_to_all | solution.py:568
  296.5 6.5 %collective-permute-done.32.rest_5_ = bf16[128,1024]{1,0:T(8,128)(2,1)S(1)} collective-permute-done((bf16[128,1024]{1,0:T(8,128)(2,1)S(1)}, bf16[128,1024]{1,0:T(8,128)(2,1)S(1)}, u32[]{:S(2)}, u32[]{:S(2)}) %collective-permute-start.32) | collective-permute-done | bytes 262176 | tf_op jit(solution)/shard_map/ppermute | solution.py:571
  303.0 2.0 collective-permute-done.33.rest_6_
  305.0 2.8 collective-permute-done.34.rest_7_
  307.8 3.0 put_first.1
  (126 shorter events, 49.9 us)
Async XLA Ops:
  2.5 12.3 %copy-start.29 = (s32[128,8]{0,1:T(8,128)S(1)}, s32[128,8]{0,1:T(8,128)}, u32[]{:S(2)}) copy-start(s32[128,8]{0,1:T(8,128)} %param.10) | copy-start | bytes 12292
  3.6 24.8 %all-to-all-start = ((bf16[128,2,8,128]{3,2,1,0:T(8,128)(2,1)}), bf16[128,2,8,128]{3,2,1,0:T(8,128)(2,1)S(1)}, u32[]{:S(2)}, u32[]{:S(2)}) async-start(bf16[128,2,8,128]{3,2,1,0:T(8,128)(2,1)} %bitcast.5), calls=%async_computation | async-start | bytes 1048576 | tf_op jit(solution)/shard_map/all_to_all | solution.py:568
  30.9 27.2 %all-to-all-start.2 = ((bf16[128,5,8,128]{3,2,1,0:T(8,128)(2,1)}), bf16[128,5,8,128]{3,2,1,0:T(8,128)(2,1)}, u32[]{:S(2)}, u32[]{:S(2)}) async-start(bf16[128,5,8,128]{3,2,1,0:T(8,128)(2,1)} %copy-done.4), calls=%async_computation.2 | async-start | bytes 2621440 | tf_op jit(solution)/shard_map/all_to_all | solution.py:568
  45.5 24.8 %collective-permute-start.2 = (bf16[2,128,1024]{2,1,0:T(8,128)(2,1)}, bf16[2,128,1024]{2,1,0:T(8,128)(2,1)S(1)}, u32[]{:S(2)}, u32[]{:S(2)}) collective-permute-start(bf16[2,128,1024]{2,1,0:T(8,128)(2,1)} %get-tuple-element.41), channel_id=1, source_target_pairs={{0,16}} | collective-permute-start | bytes 1572872 | tf_op jit(solution)/shard_map/ppermute | solution.py:571
  46.8 25.6 %collective-permute-start.3 = (bf16[2,128,1024]{2,1,0:T(8,128)(2,1)}, bf16[2,128,1024]{2,1,0:T(8,128)(2,1)}, u32[]{:S(2)}, u32[]{:S(2)}) collective-permute-start(bf16[2,128,1024]{2,1,0:T(8,128)(2,1)} %get-tuple-element.42), channel_id=1, source_target_pairs={{0,32}} | collective-permute-start | bytes 1572872 | tf_op jit(solution)/shard_map/ppermute | solution.py:571
  58.2 52.9 %all-to-all-start.1 = ((bf16[128,5,8,128]{3,2,1,0:T(8,128)(2,1)}), bf16[128,5,8,128]{3,2,1,0:T(8,128)(2,1)}, u32[]{:S(2)}, u32[]{:S(2)}) async-start(bf16[128,5,8,128]{3,2,1,0:T(8,128)(2,1)} %copy-done.10), calls=%async_computation.1 | async-start | bytes 2621440 | tf_op jit(solution)/shard_map/all_to_all | solution.py:568
  63.9 18.3 %collective-permute-start.4 = (bf16[2,128,1024]{2,1,0:T(8,128)(2,1)}, bf16[2,128,1024]{2,1,0:T(8,128)(2,1)S(1)}, u32[]{:S(2)}, u32[]{:S(2)}) collective-permute-start(bf16[2,128,1024]{2,1,0:T(8,128)(2,1)} %copy-done.26), channel_id=1, source_target_pairs={{0,48}} | collective-permute-start | bytes 1572872 | tf_op jit(solution)/shard_map/ppermute | solution.py:571
  66.4 21.5 %collective-permute-start.5 = (bf16[2,128,1024]{2,1,0:T(8,128)(2,1)}, bf16[2,128,1024]{2,1,0:T(8,128)(2,1)S(1)}, u32[]{:S(2)}, u32[]{:S(2)}) collective-permute-start(bf16[2,128,1024]{2,1,0:T(8,128)(2,1)} %copy-done.25), channel_id=1, source_target_pairs={{0,64}} | collective-permute-start | bytes 1572872 | tf_op jit(solution)/shard_map/ppermute | solution.py:571
  68.9 24.5 %collective-permute-start.6 = (bf16[2,128,1024]{2,1,0:T(8,128)(2,1)}, bf16[2,128,1024]{2,1,0:T(8,128)(2,1)S(1)}, u32[]{:S(2)}, u32[]{:S(2)}) collective-permute-start(bf16[2,128,1024]{2,1,0:T(8,128)(2,1)} %copy-done.24), channel_id=1, source_target_pairs={{0,80}} | collective-permute-start | bytes 1572872 | tf_op jit(solution)/shard_map/ppermute | solution.py:571
  71.0 22.4 %collective-permute-start.7 = (bf16[2,128,1024]{2,1,0:T(8,128)(2,1)}, bf16[2,128,1024]{2,1,0:T(8,128)(2,1)S(1)}, u32[]{:S(2)}, u32[]{:S(2)}) collective-permute-start(bf16[2,128,1024]{2,1,0:T(8,128)(2,1)} %copy-done.23), channel_id=1, source_target_pairs={{0,96}} | collective-permute-start | bytes 1572872 | tf_op jit(solution)/shard_map/ppermute | solution.py:571
  72.4 21.1 %collective-permute-start.8 = (bf16[2,128,1024]{2,1,0:T(8,128)(2,1)}, bf16[2,128,1024]{2,1,0:T(8,128)(2,1)S(1)}, u32[]{:S(2)}, u32[]{:S(2)}) collective-permute-start(bf16[2,128,1024]{2,1,0:T(8,128)(2,1)} %copy-done.22), channel_id=1, source_target_pairs={{0,112}} | collective-permute-start | bytes 1572872 | tf_op jit(solution)/shard_map/ppermute | solution.py:571
  82.2 20.5 %collective-permute-start = (bf16[2,128,1024]{2,1,0:T(8,128)(2,1)}, bf16[2,128,1024]{2,1,0:T(8,128)(2,1)}, u32[]{:S(2)}, u32[]{:S(2)}) collective-permute-start(bf16[2,128,1024]{2,1,0:T(8,128)(2,1)} %get-tuple-element.32.self_ref), channel_id=1, source_target_pairs={{1,2},{2,3},{3,4},{4,5},{5,6},{6,7},{7,8},{8,9},{9,10},{10,11},{11... | collective-permute-start | bytes 1572872 | tf_op jit(solution)/shard_map/ppermute | solution.py:571
  87.8 14.9 %collective-permute-start.1 = (bf16[2,128,1024]{2,1,0:T(8,128)(2,1)}, bf16[2,128,1024]{2,1,0:T(8,128)(2,1)}, u32[]{:S(2)}, u32[]{:S(2)}) collective-permute-start(bf16[2,128,1024]{2,1,0:T(8,128)(2,1)} %get-tuple-element.32.self_ref), channel_id=1, source_target_pairs={{2,1},{3,2},{4,3},{5,4},{6,5},{7,6},{8,7},{9,8},{10,9},{11,10},{12... | collective-permute-start | bytes 1572872 | tf_op jit(solution)/shard_map/ppermute | solution.py:571
  96.2 42.0 %collective-permute-start.9 = (bf16[2,128,1024]{2,1,0:T(8,128)(2,1)S(1)}, bf16[2,128,1024]{2,1,0:T(8,128)(2,1)}, u32[]{:S(2)}, u32[]{:S(2)}) collective-permute-start(bf16[2,128,1024]{2,1,0:T(8,128)(2,1)S(1)} %pick.2.rest_0_), channel_id=1, source_target_pairs={{0,1},{16,17},{32,33},{48,49},{64,65},{80,81},{96,97},{112,113}} | collective-permute-start | bytes 1572872 | tf_op jit(solution)/shard_map/ppermute | solution.py:571
  98.3 39.9 %collective-permute-start.10 = (bf16[2,128,1024]{2,1,0:T(8,128)(2,1)S(1)}, bf16[2,128,1024]{2,1,0:T(8,128)(2,1)}, u32[]{:S(2)}, u32[]{:S(2)}) collective-permute-start(bf16[2,128,1024]{2,1,0:T(8,128)(2,1)S(1)} %pick.2.rest_0_), channel_id=1, source_target_pairs={{0,2},{16,18},{32,34},{48,50},{64,66},{80,82},{96,98},{112,114}} | collective-permute-start | bytes 1572872 | tf_op jit(solution)/shard_map/ppermute | solution.py:571
  100.4 37.8 %collective-permute-start.11 = (bf16[2,128,1024]{2,1,0:T(8,128)(2,1)S(1)}, bf16[2,128,1024]{2,1,0:T(8,128)(2,1)}, u32[]{:S(2)}, u32[]{:S(2)}) collective-permute-start(bf16[2,128,1024]{2,1,0:T(8,128)(2,1)S(1)} %pick.2.rest_0_), channel_id=1, source_target_pairs={{0,3},{16,19},{32,35},{48,51},{64,67},{80,83},{96,99},{112,115}} | collective-permute-start | bytes 1572872 | tf_op jit(solution)/shard_map/ppermute | solution.py:571
  111.1 98.4 %all-to-all-start.4 = ((bf16[128,5,8,128]{3,2,1,0:T(8,128)(2,1)}), bf16[128,5,8,128]{3,2,1,0:T(8,128)(2,1)}, u32[]{:S(2)}, u32[]{:S(2)}) async-start(bf16[128,5,8,128]{3,2,1,0:T(8,128)(2,1)} %bitcast.12), calls=%async_computation.4 | async-start | bytes 2621440 | tf_op jit(solution)/shard_map/all_to_all | solution.py:568
  138.2 7.4 %copy-start.28 = (bf16[128,8,128]{2,1,0:T(8,128)(2,1)S(1)}, bf16[128,8,128]{2,1,0:T(8,128)(2,1)}, u32[]{:S(2)}) copy-start(bf16[128,8,128]{2,1,0:T(8,128)(2,1)} %copy-done.27) | copy-start | bytes 786436
  138.8 24.8 %collective-permute-start.12 = (bf16[2,128,1024]{2,1,0:T(8,128)(2,1)S(1)}, bf16[2,128,1024]{2,1,0:T(8,128)(2,1)S(1)}, u32[]{:S(2)}, u32[]{:S(2)}) collective-permute-start(bf16[2,128,1024]{2,1,0:T(8,128)(2,1)S(1)} %pick.3.p0), channel_id=1, source_target_pairs={{0,4},{1,5},{2,6},{3,7},{16,20},{17,21},{18,22},{19,23},{32,36},{3... | collective-permute-start | bytes 1572872 | tf_op jit(solution)/shard_map/ppermute | solution.py:571
  141.8 33.0 %collective-permute-start.13 = (bf16[2,128,1024]{2,1,0:T(8,128)(2,1)S(1)}, bf16[2,128,1024]{2,1,0:T(8,128)(2,1)S(1)}, u32[]{:S(2)}, u32[]{:S(2)}) collective-permute-start(bf16[2,128,1024]{2,1,0:T(8,128)(2,1)S(1)} %pick.3.p0), channel_id=1, source_target_pairs={{0,8},{1,9},{2,10},{3,11},{16,24},{17,25},{18,26},{19,27},{32,40},... | collective-permute-start | bytes 1572872 | tf_op jit(solution)/shard_map/ppermute | solution.py:571
  144.3 30.5 %collective-permute-start.14 = (bf16[2,128,1024]{2,1,0:T(8,128)(2,1)S(1)}, bf16[2,128,1024]{2,1,0:T(8,128)(2,1)S(1)}, u32[]{:S(2)}, u32[]{:S(2)}) collective-permute-start(bf16[2,128,1024]{2,1,0:T(8,128)(2,1)S(1)} %pick.3.p0), channel_id=1, source_target_pairs={{0,12},{1,13},{2,14},{3,15},{16,28},{17,29},{18,30},{19,31},{32,44... | collective-permute-start | bytes 1572872 | tf_op jit(solution)/shard_map/ppermute | solution.py:571
  145.6 1.6 collective-permute-start.15
  174.8 27.9 %copy-start.3 = (bf16[128,8192]{1,0:T(8,128)(2,1)S(1)}, bf16[128,8192]{1,0:T(8,128)(2,1)}, u32[]{:S(2)}) copy-start(bf16[128,8192]{1,0:T(8,128)(2,1)} %o_ref.5) | copy-start | bytes 6291460
  177.9 24.8 %copy-start.6 = (f32[2,128,1024]{2,1,0:T(8,128)S(1)}, f32[2,128,1024]{2,1,0:T(8,128)}, u32[]{:S(2)}) copy-start(f32[2,128,1024]{2,1,0:T(8,128)} %copy-done.5) | copy-start | bytes 3145732
  177.9 4.3 %collective-permute-start.18 = (f32[24,128]{1,0:T(8,128)S(1)}, f32[24,128]{1,0:T(8,128)S(1)}, u32[]{:S(2)}, u32[]{:S(2)}) collective-permute-start(f32[24,128]{1,0:T(8,128)S(1)} %get-tuple-element.50), channel_id=1, source_target_pairs={{0,3},{1,0},{2,1},{3,2},{4,7},{5,4},{6,5},{7,6},{8,11},{9,8},{10,9... | collective-permute-start | bytes 36872 | tf_op jit(solution)/shard_map/ppermute | solution.py:571
  180.2 5.2 %collective-permute-start.17 = (f32[24,128]{1,0:T(8,128)S(1)}, f32[24,128]{1,0:T(8,128)S(1)}, u32[]{:S(2)}, u32[]{:S(2)}) collective-permute-start(f32[24,128]{1,0:T(8,128)S(1)} %get-tuple-element.50), channel_id=1, source_target_pairs={{0,2},{1,3},{2,0},{3,1},{4,6},{5,7},{6,4},{7,5},{8,10},{9,11},{10,... | collective-permute-start | bytes 36872 | tf_op jit(solution)/shard_map/ppermute | solution.py:571
  181.4 4.9 %collective-permute-start.16 = (f32[24,128]{1,0:T(8,128)S(1)}, f32[24,128]{1,0:T(8,128)S(1)}, u32[]{:S(2)}, u32[]{:S(2)}) collective-permute-start(f32[24,128]{1,0:T(8,128)S(1)} %get-tuple-element.50), channel_id=1, source_target_pairs={{0,1},{1,2},{2,3},{3,0},{4,5},{5,6},{6,7},{7,4},{8,9},{9,10},{10,1... | collective-permute-start | bytes 36872 | tf_op jit(solution)/shard_map/ppermute | solution.py:571
  186.3 6.7 %collective-permute-start.19 = (f32[24,128]{1,0:T(8,128)S(1)}, f32[24,128]{1,0:T(8,128)S(1)}, u32[]{:S(2)}, u32[]{:S(2)}) collective-permute-start(f32[24,128]{1,0:T(8,128)S(1)} %pad_maximum_fusion.s0), channel_id=1, source_target_pairs={{0,4},{1,5},{2,6},{3,7},{4,8},{5,9},{6,10},{7,11},{8,12},{9,13},{1... | collective-permute-start | bytes 36872 | tf_op jit(solution)/shard_map/ppermute | solution.py:571
  186.4 6.6 %collective-permute-start.20 = (f32[24,128]{1,0:T(8,128)S(1)}, f32[24,128]{1,0:T(8,128)S(1)}, u32[]{:S(2)}, u32[]{:S(2)}) collective-permute-start(f32[24,128]{1,0:T(8,128)S(1)} %pad_maximum_fusion.s0), channel_id=1, source_target_pairs={{0,8},{1,9},{2,10},{3,11},{4,12},{5,13},{6,14},{7,15},{8,0},{9,1},... | collective-permute-start | bytes 36872 | tf_op jit(solution)/shard_map/ppermute | solution.py:571
  190.5 3.9 %collective-permute-start.21 = (f32[24,128]{1,0:T(8,128)S(1)}, f32[24,128]{1,0:T(8,128)S(1)}, u32[]{:S(2)}, u32[]{:S(2)}) collective-permute-start(f32[24,128]{1,0:T(8,128)S(1)} %pad_maximum_fusion.s0), channel_id=1, source_target_pairs={{0,12},{1,13},{2,14},{3,15},{4,0},{5,1},{6,2},{7,3},{8,4},{9,5},{1... | collective-permute-start | bytes 36872 | tf_op jit(solution)/shard_map/ppermute | solution.py:571
  198.8 36.2 %collective-permute-start.24 = (bf16[128,1024]{1,0:T(8,128)(2,1)S(1)}, bf16[128,1024]{1,0:T(8,128)(2,1)}, u32[]{:S(2)}, u32[]{:S(2)}) collective-permute-start(bf16[128,1024]{1,0:T(8,128)(2,1)S(1)} %get-tuple-element.51), channel_id=1, source_target_pairs={{12,0},{13,1},{14,2},{15,3},{28,16},{29,17},{30,18},{31,19},{44,32... | collective-permute-start | bytes 786440 | tf_op jit(solution)/shard_map/ppermute | solution.py:571
  200.1 34.9 %collective-permute-start.23 = (bf16[128,1024]{1,0:T(8,128)(2,1)S(1)}, bf16[128,1024]{1,0:T(8,128)(2,1)}, u32[]{:S(2)}, u32[]{:S(2)}) collective-permute-start(bf16[128,1024]{1,0:T(8,128)(2,1)S(1)} %get-tuple-element.51), channel_id=1, source_target_pairs={{8,0},{9,1},{10,2},{11,3},{24,16},{25,17},{26,18},{27,19},{40,32},... | collective-permute-start | bytes 786440 | tf_op jit(solution)/shard_map/ppermute | solution.py:571
  201.4 33.6 %collective-permute-start.22 = (bf16[128,1024]{1,0:T(8,128)(2,1)S(1)}, bf16[128,1024]{1,0:T(8,128)(2,1)}, u32[]{:S(2)}, u32[]{:S(2)}) collective-permute-start(bf16[128,1024]{1,0:T(8,128)(2,1)S(1)} %get-tuple-element.51), channel_id=1, source_target_pairs={{4,0},{5,1},{6,2},{7,3},{20,16},{21,17},{22,18},{23,19},{36,32},{3... | collective-permute-start | bytes 786440 | tf_op jit(solution)/shard_map/ppermute | solution.py:571
  209.5 64.7 %all-to-all-start.3 = ((bf16[128,5,8,128]{3,2,1,0:T(8,128)(2,1)}), bf16[128,5,8,128]{3,2,1,0:T(8,128)(2,1)S(1)}, u32[]{:S(2)}, u32[]{:S(2)}) async-start(bf16[128,5,8,128]{3,2,1,0:T(8,128)(2,1)} %bitcast.13), calls=%async_computation.3 | async-start | bytes 2621440 | tf_op jit(solution)/shard_map/all_to_all | solution.py:568
  236.3 26.4 %collective-permute-start.27 = (bf16[128,1024]{1,0:T(8,128)(2,1)S(1)}, bf16[128,1024]{1,0:T(8,128)(2,1)S(1)}, u32[]{:S(2)}, u32[]{:S(2)}) collective-permute-start(bf16[128,1024]{1,0:T(8,128)(2,1)S(1)} %add_convert_fusion.1), channel_id=1, source_target_pairs={{3,0},{19,16},{35,32},{51,48},{67,64},{83,80},{99,96},{115,112}} | collective-permute-start | bytes 786440 | tf_op jit(solution)/shard_map/ppermute | solution.py:571
  237.6 25.1 %collective-permute-start.26 = (bf16[128,1024]{1,0:T(8,128)(2,1)S(1)}, bf16[128,1024]{1,0:T(8,128)(2,1)S(1)}, u32[]{:S(2)}, u32[]{:S(2)}) collective-permute-start(bf16[128,1024]{1,0:T(8,128)(2,1)S(1)} %add_convert_fusion.1), channel_id=1, source_target_pairs={{2,0},{18,16},{34,32},{50,48},{66,64},{82,80},{98,96},{114,112}} | collective-permute-start | bytes 786440 | tf_op jit(solution)/shard_map/ppermute | solution.py:571
  238.9 23.8 %collective-permute-start.25 = (bf16[128,1024]{1,0:T(8,128)(2,1)S(1)}, bf16[128,1024]{1,0:T(8,128)(2,1)S(1)}, u32[]{:S(2)}, u32[]{:S(2)}) collective-permute-start(bf16[128,1024]{1,0:T(8,128)(2,1)S(1)} %add_convert_fusion.1), channel_id=1, source_target_pairs={{1,0},{17,16},{33,32},{49,48},{65,64},{81,80},{97,96},{113,112}} | collective-permute-start | bytes 786440 | tf_op jit(solution)/shard_map/ppermute | solution.py:571
  240.2 27.9 %collective-permute-start.37 = (bf16[1024,128]{1,0:T(8,128)(2,1)S(1)}, bf16[1024,128]{1,0:T(8,128)(2,1)S(1)}, u32[]{:S(2)}, u32[]{:S(2)}) collective-permute-start(bf16[1024,128]{1,0:T(8,128)(2,1)S(1)} %get-tuple-element.58), channel_id=1, source_target_pairs={{0,16},{1,17},{2,18},{3,19},{4,20},{5,21},{6,22},{7,23},{8,24},{9,... | collective-permute-start | bytes 786440 | tf_op jit(solution)/shard_map/ppermute | solution.py:571
  262.9 8.3 %collective-permute-start.28 = (bf16[128,1024]{1,0:T(8,128)(2,1)S(1)}, bf16[128,1024]{1,0:T(8,128)(2,1)S(1)}, u32[]{:S(2)}, u32[]{:S(2)}) collective-permute-start(bf16[128,1024]{1,0:T(8,128)(2,1)S(1)} %add_convert_fusion.rest_0_), channel_id=1, source_target_pairs={{32,0}} | collective-permute-start | bytes 786440 | tf_op jit(solution)/shard_map/ppermute | solution.py:571
  264.2 28.3 %collective-permute-start.29 = (bf16[128,1024]{1,0:T(8,128)(2,1)S(1)}, bf16[128,1024]{1,0:T(8,128)(2,1)}, u32[]{:S(2)}, u32[]{:S(2)}) collective-permute-start(bf16[128,1024]{1,0:T(8,128)(2,1)S(1)} %add_convert_fusion.rest_0_), channel_id=1, source_target_pairs={{64,0}} | collective-permute-start | bytes 786440 | tf_op jit(solution)/shard_map/ppermute | solution.py:571
  265.5 28.3 %collective-permute-start.30 = (bf16[128,1024]{1,0:T(8,128)(2,1)S(1)}, bf16[128,1024]{1,0:T(8,128)(2,1)}, u32[]{:S(2)}, u32[]{:S(2)}) collective-permute-start(bf16[128,1024]{1,0:T(8,128)(2,1)S(1)} %add_convert_fusion.rest_0_), channel_id=1, source_target_pairs={{96,0}} | collective-permute-start | bytes 786440 | tf_op jit(solution)/shard_map/ppermute | solution.py:571
  266.8 28.4 %collective-permute-start.31 = (bf16[128,1024]{1,0:T(8,128)(2,1)S(1)}, bf16[128,1024]{1,0:T(8,128)(2,1)}, u32[]{:S(2)}, u32[]{:S(2)}) collective-permute-start(bf16[128,1024]{1,0:T(8,128)(2,1)S(1)} %add_convert_fusion.rest_0_), channel_id=1, source_target_pairs={{16,0}} | collective-permute-start | bytes 786440 | tf_op jit(solution)/shard_map/ppermute | solution.py:571
  268.9 41.9 %collective-permute-start.35 = (bf16[2,128,1024]{2,1,0:T(8,128)(2,1)}, bf16[2,128,1024]{2,1,0:T(8,128)(2,1)S(1)}, u32[]{:S(2)}, u32[]{:S(2)}) collective-permute-start(bf16[2,128,1024]{2,1,0:T(8,128)(2,1)} %get-tuple-element.53), channel_id=1, source_target_pairs={{1,2},{2,3},{3,4},{4,5},{5,6},{6,7},{7,8},{8,9},{9,10},{10,11},{11... | collective-permute-start | bytes 1572872 | tf_op jit(solution)/shard_map/ppermute | solution.py:571
  271.2 39.6 %collective-permute-start.36 = (bf16[2,128,1024]{2,1,0:T(8,128)(2,1)}, bf16[2,128,1024]{2,1,0:T(8,128)(2,1)S(1)}, u32[]{:S(2)}, u32[]{:S(2)}) collective-permute-start(bf16[2,128,1024]{2,1,0:T(8,128)(2,1)} %get-tuple-element.54), channel_id=1, source_target_pairs={{2,1},{3,2},{4,3},{5,4},{6,5},{7,6},{8,7},{9,8},{10,9},{11,10},{12... | collective-permute-start | bytes 1572872 | tf_op jit(solution)/shard_map/ppermute | solution.py:571
  278.9 31.9 %all-to-all-start.5 = ((bf16[128,2,8,128]{3,2,1,0:T(8,128)(2,1)}), bf16[128,2,8,128]{3,2,1,0:T(8,128)(2,1)S(1)}, u32[]{:S(2)}, u32[]{:S(2)}) async-start(bf16[128,2,8,128]{3,2,1,0:T(8,128)(2,1)} %scatter_last.1), calls=%async_computation.5 | async-start | bytes 1048576 | tf_op jit(solution)/shard_map/all_to_all | solution.py:568
  292.6 10.4 %collective-permute-start.32 = (bf16[128,1024]{1,0:T(8,128)(2,1)S(1)}, bf16[128,1024]{1,0:T(8,128)(2,1)S(1)}, u32[]{:S(2)}, u32[]{:S(2)}) collective-permute-start(bf16[128,1024]{1,0:T(8,128)(2,1)S(1)} %add_convert_fusion.rest_0_), channel_id=1, source_target_pairs={{48,0}} | collective-permute-start | bytes 786440 | tf_op jit(solution)/shard_map/ppermute | solution.py:571
  293.9 11.1 %collective-permute-start.33 = (bf16[128,1024]{1,0:T(8,128)(2,1)S(1)}, bf16[128,1024]{1,0:T(8,128)(2,1)S(1)}, u32[]{:S(2)}, u32[]{:S(2)}) collective-permute-start(bf16[128,1024]{1,0:T(8,128)(2,1)S(1)} %add_convert_fusion.rest_0_), channel_id=1, source_target_pairs={{80,0}} | collective-permute-start | bytes 786440 | tf_op jit(solution)/shard_map/ppermute | solution.py:571
  295.2 12.5 %collective-permute-start.34 = (bf16[128,1024]{1,0:T(8,128)(2,1)S(1)}, bf16[128,1024]{1,0:T(8,128)(2,1)S(1)}, u32[]{:S(2)}, u32[]{:S(2)}) collective-permute-start(bf16[128,1024]{1,0:T(8,128)(2,1)S(1)} %add_convert_fusion.rest_0_), channel_id=1, source_target_pairs={{112,0}} | collective-permute-start | bytes 786440 | tf_op jit(solution)/shard_map/ppermute | solution.py:571
  (27 other events, 45.0 us)

commit v8 on v7

--- a/solution.py
+++ b/solution.py
@@ -53,7 +53,6 @@
         in_specs=[pl.BlockSpec(memory_space=VM)] * 2,
         out_specs=[pl.BlockSpec(memory_space=VM)] * 2,
         name="pack_pieces",
-        compiler_params=pltpu.CompilerParams(vmem_limit_bytes=12 << 20),
     )(k, v)
 
 
@@ -186,7 +185,7 @@
                 dst[s * BLOCK : (s + 1) * BLOCK] = part[kv]
             for s in range(SENT):
                 at = (FIRST_SENT + s) * BLOCK
-                dst[at : at + BLOCK] = g_ref[pl.program_id(0), kv, :, s].reshape(BLOCK, HEAD_SIZE)
+                dst[at : at + BLOCK] = g_ref[0, kv, :, s].reshape(BLOCK, HEAD_SIZE)
         kt[...] = kc[...].T
         live = [valid_ref[b * NB + s] > 0 for s in range(NB)]
 
@@ -268,7 +267,7 @@
         grid_spec=pltpu.PrefetchScalarGridSpec(
             num_scalar_prefetch=2,
             grid=(CALL_HEADS,),
-            in_specs=[wide, wide, pair, pair, pair, pl.BlockSpec(memory_space=VM)]
+            in_specs=[wide, wide, pair, pair, pair, pieces]
             + [pl.BlockSpec(memory_space=pl.ANY)] * len(earlier),
             out_specs=[wide, pair, pair, pair, pieces],
             scratch_shapes=[
@@ -285,7 +284,6 @@
         ),
         input_output_aliases={8 + n: n for n in range(len(earlier))},
         name="sparse_grads",
-        compiler_params=pltpu.CompilerParams(vmem_limit_bytes=24 << 20),
     )(meta, valid, q, o, own, before, after, got, *earlier)
 
 
@@ -477,7 +475,6 @@
             pltpu.SemaphoreType.DMA((2, KEY_HEADS, 2)),
         ],
         name="spread_heads",
-        compiler_params=pltpu.CompilerParams(vmem_limit_bytes=12 << 20),
     )(meta, q, o)
 
 
@@ -513,7 +510,6 @@
             pltpu.SemaphoreType.DMA((2, KEY_HEADS)),
         ],
         name="put_first",
-        compiler_params=pltpu.CompilerParams(vmem_limit_bytes=12 << 20),
     )(meta, dq, *parts)
 
 
@@ -537,7 +533,6 @@
         out_specs=pl.BlockSpec(memory_space=VM),
         scratch_shapes=[pltpu.SemaphoreType.DMA(())],
         name="pick",
-        compiler_params=pltpu.CompilerParams(vmem_limit_bytes=12 << 20),
     )(meta, *parts)
 
 
@@ -625,7 +620,7 @@
     others = [send_tp(total, [(n, 0)]) for n in range(1, 4)]
     total = add(total, *others)
     parts = [total] * KEY_HEADS
-    for c in range(1, ctx_size):
+    for c in (4, 5, 2, 3, 6, 7, 1):
         parts[c // 2 + HALF * (c % 2)] = send(total, [(c * tp_size, 0)])
     d_q = put_first(meta, dq, parts)
 

time: 313 us -> 311 us (level)
  local copies, waits for them, and re-layouts: 22.9 us -> 10.1 us
  Pallas kernels: 32.7 us -> 43.6 us
    unnamed x64 -> x46, local copies, waits for them, and re-layouts: 22.7 us -> 9.19 us
    all_to_all x6, starting transfers between devices: 88.9 us -> 82.4 us  [swap(): return lax.all_to_all(x, BOTH, split_axis=0, concat_axis=0, tiled=True)]
    pallas_call x2, Pallas kernels: 1.26 us -> 5.27 us  [pick(): pl.pallas_call(functools.partial(pick_body, at=at), out_shape=jax.ShapeDt...]
    all_to_all x6, waiting for transfers between devices: 19.9 us -> 23.7 us  [swap(): return lax.all_to_all(x, BOTH, split_axis=0, concat_axis=0, tiled=True)]
    ppermute x38, starting transfers between devices: 57.7 us -> 61.5 us  [send(): return lax.ppermute(x, BOTH, pairs)]
  transfers between devices with their start and end apart: 44 -> 44, of which waited for: 16 -> 16; matrix products, arithmetic and copies ran while one was open for 1% -> 1% of each run, Pallas kernels for 9% -> 12%
where the time goes in v8:
time: 311 us; the launch traced here: 309 us
  starting transfers between devices  144 us (46%)
  waiting for transfers between devices  108 us (35%)
  Pallas kernels  43.6 us (14%)
  local copies, waits for them, and re-layouts  10.1 us (3%)
    ppermute x38, waiting for transfers between devices, send(): return lax.ppermute(x, BOTH, pairs)  84.6 us
    all_to_all x6, starting transfers between devices, swap(): return lax.all_to_all(x, BOTH, split_axis=0, concat_axis=0, tiled=True)  82.4 us
    ppermute x38, starting transfers between devices, send(): return lax.ppermute(x, BOTH, pairs)  61.5 us
    all_to_all x6, waiting for transfers between devices, swap(): return lax.all_to_all(x, BOTH, split_axis=0, concat_axis=0, tiled=True)  23.7 us
    pallas_call x2, Pallas kernels, sparse_grads(): pl.pallas_call(sparse_body, out_shape=(jax.ShapeDtypeStruct(q.shape, BF16...  10.5 us
    unnamed x46, local copies, waits for them, and re-layouts  9.19 us
  transfers between devices with their start and end apart: 44, of which 16 were waited for; matrix products, arithmetic and copies ran while one was open for 1% of the time, Pallas kernels for 12%

profile of v8, /device:TPU:0, one launch (start us, length us, event | category | flops | bytes accessed | tf_op | source)
XLA Modules:
  0.0 309.3 jit_solution(8003075488057164350)
XLA Ops:
  0.6 2.1 pack_pieces.1
  2.8 11.2 %all-to-all-start = ((bf16[128,2,8,128]{3,2,1,0:T(8,128)(2,1)}), bf16[128,2,8,128]{3,2,1,0:T(8,128)(2,1)S(1)}, u32[]{:S(2)}, u32[]{:S(2)}) async-start(bf16[128,2,8,128]{3,2,1,0:T(8,128)(2,1)} %bitcast.16), calls=%async_computation | async-start | bytes 1048576 | tf_op jit(solution)/shard_map/all_to_all | solution.py:563
  14.3 13.2 %all-to-all-done.held_ref = bf16[128,2,8,128]{3,2,1,0:T(8,128)(2,1)S(1)} async-done(((bf16[128,2,8,128]{3,2,1,0:T(8,128)(2,1)}), bf16[128,2,8,128]{3,2,1,0:T(8,128)(2,1)S(1)}, u32[]{:S(2)}, u32[]{:S(2)}) %all-to-all-start) | async-done | bytes 524320 | tf_op jit(solution)/shard_map/all_to_all | solution.py:563
  27.5 2.4 gather_pieces.3
  29.9 4.6 %all-to-all-start.2 = ((bf16[128,5,8,128]{3,2,1,0:T(8,128)(2,1)}), bf16[128,5,8,128]{3,2,1,0:T(8,128)(2,1)S(1)}, u32[]{:S(2)}, u32[]{:S(2)}) async-start(bf16[128,5,8,128]{3,2,1,0:T(8,128)(2,1)} %gather_pieces.3), calls=%async_computation.2 | async-start | bytes 2621440 | tf_op jit(solution)/shard_map/all_to_all | solution.py:563
  34.5 4.6 %spread_heads.1 = (bf16[2,128,1024]{2,1,0:T(8,128)(2,1)}, bf16[2,128,1024]{2,1,0:T(8,128)(2,1)}, bf16[2,128,1024]{2,1,0:T(8,128)(2,1)}, bf16[2,128,1024]{2,1,0:T...) custom-call(s32[5]{0:T(128)} %copy-done.4, ...), custom_call_target="tpu_custom_call" | custom-call | tf_op jit(solution)/shard_map/spread_heads/pallas_call | solution.py:468
  39.2 2.1 collective-permute-start.2
  41.2 2.1 collective-permute-start.3
  43.4 2.4 gather_pieces.2
  45.8 10.5 %all-to-all-done.2 = bf16[128,5,8,128]{3,2,1,0:T(8,128)(2,1)S(1)} async-done(((bf16[128,5,8,128]{3,2,1,0:T(8,128)(2,1)}), bf16[128,5,8,128]{3,2,1,0:T(8,128)(2,1)S(1)}, u32[]{:S(2)}, u32[]{:S(2)}) %all-to-all-start.2) | async-done | bytes 1310752 | tf_op jit(solution)/shard_map/all_to_all | solution.py:563
  57.3 4.6 %all-to-all-start.1 = ((bf16[128,5,8,128]{3,2,1,0:T(8,128)(2,1)}), bf16[128,5,8,128]{3,2,1,0:T(8,128)(2,1)S(1)}, u32[]{:S(2)}, u32[]{:S(2)}) async-start(bf16[128,5,8,128]{3,2,1,0:T(8,128)(2,1)} %get-tuple-element.34), calls=%async_computation.1 | async-start | bytes 2621440 | tf_op jit(solution)/shard_map/all_to_all | solution.py:563
  62.0 2.5 collective-permute-start.4
  64.5 3.3 %collective-permute-start.5 = (bf16[2,128,1024]{2,1,0:T(8,128)(2,1)}, bf16[2,128,1024]{2,1,0:T(8,128)(2,1)}, u32[]{:S(2)}, u32[]{:S(2)}) collective-permute-start(bf16[2,128,1024]{2,1,0:T(8,128)(2,1)} %get-tuple-element.44), channel_id=1, source_target_pairs={{0,64}} | collective-permute-start | bytes 1572872 | tf_op jit(solution)/shard_map/ppermute | solution.py:566
  67.9 2.1 collective-permute-start.6
  69.9 2.1 collective-permute-start.7
  72.0 2.1 collective-permute-start.8
  74.1 6.6 %collective-permute-done.4.rest_3_ = bf16[2,128,1024]{2,1,0:T(8,128)(2,1)S(1)} collective-permute-done((bf16[2,128,1024]{2,1,0:T(8,128)(2,1)}, bf16[2,128,1024]{2,1,0:T(8,128)(2,1)S(1)}, u32[]{:S(2)}, u32[]{:S(2)}) %collective-permute-start.4) | collective-permute-done | bytes 524320 | tf_op jit(solution)/shard_map/ppermute | solution.py:566
  81.6 4.8 %collective-permute-done.5.rest_4_ = bf16[2,128,1024]{2,1,0:T(8,128)(2,1)} collective-permute-done((bf16[2,128,1024]{2,1,0:T(8,128)(2,1)}, bf16[2,128,1024]{2,1,0:T(8,128)(2,1)}, u32[]{:S(2)}, u32[]{:S(2)}) %collective-permute-start.5) | collective-permute-done | bytes 524320 | tf_op jit(solution)/shard_map/ppermute | solution.py:566
  87.1 4.9 %collective-permute-done.6.rest_5_ = bf16[2,128,1024]{2,1,0:T(8,128)(2,1)} collective-permute-done((bf16[2,128,1024]{2,1,0:T(8,128)(2,1)}, bf16[2,128,1024]{2,1,0:T(8,128)(2,1)}, u32[]{:S(2)}, u32[]{:S(2)}) %collective-permute-start.6) | collective-permute-done | bytes 524320 | tf_op jit(solution)/shard_map/ppermute | solution.py:566
  92.0 2.7 pick.2.rest_0_
  94.8 2.1 collective-permute-start.9
  96.9 2.1 collective-permute-start.10
  98.9 2.1 collective-permute-start.11
  102.8 5.3 %sparse_grads.2 = (bf16[128,8192]{1,0:T(8,128)(2,1)}, f32[2,128,1024]{2,1,0:T(8,128)}, bf16[2,128,1024]{2,1,0:T(8,128)(2,1)}, bf16[2,128,1024]{2,1,0:T(8,128)(2,1)}, bf16[4,2,16,5,8,128]{5,4,3,2,1,0:T(8,128)(2,1)}) custom-call(s32[5]{0:T(128)} %copy-done.4, s32[1024]{0:T(1024)} %reshape.30.valid_ref, bf16[128,8192]{1,0:T(8,128)(2,1)} %q_ref.5, ...), custom_call_target="tpu_custom_call" | custom-call | tf_op jit(solution)/shard_map/sparse_grads/pallas_call | solution.py:258
  109.2 25.2 %all-to-all-start.4 = ((bf16[128,5,8,128]{3,2,1,0:T(8,128)(2,1)}), bf16[128,5,8,128]{3,2,1,0:T(8,128)(2,1)S(1)}, u32[]{:S(2)}, u32[]{:S(2)}) async-start(bf16[128,5,8,128]{3,2,1,0:T(8,128)(2,1)} %bitcast.14), calls=%async_computation.4 | async-start | bytes 2621440 | tf_op jit(solution)/shard_map/all_to_all | solution.py:563
  134.4 2.6 pick.3.p0
  137.0 3.0 collective-permute-start.12
  140.0 2.5 collective-permute-start.13
  145.4 15.0 %collective-permute-done.12.p1 = bf16[2,128,1024]{2,1,0:T(8,128)(2,1)S(1)} collective-permute-done((bf16[2,128,1024]{2,1,0:T(8,128)(2,1)}, bf16[2,128,1024]{2,1,0:T(8,128)(2,1)S(1)}, u32[]{:S(2)}, u32[]{:S(2)}) %collective-permute-start.12) | collective-permute-done | bytes 524320 | tf_op jit(solution)/shard_map/ppermute | solution.py:566
  160.4 11.2 %collective-permute-done.13.p2 = bf16[2,128,1024]{2,1,0:T(8,128)(2,1)S(1)} collective-permute-done((bf16[2,128,1024]{2,1,0:T(8,128)(2,1)}, bf16[2,128,1024]{2,1,0:T(8,128)(2,1)S(1)}, u32[]{:S(2)}, u32[]{:S(2)}) %collective-permute-start.13) | collective-permute-done | bytes 524320 | tf_op jit(solution)/shard_map/ppermute | solution.py:566
  172.7 3.1 dense_stats.1
  175.8 2.3 collective-permute-start.18
  180.0 3.2 %collective-permute-done.17 = f32[24,128]{1,0:T(8,128)S(1)} collective-permute-done((f32[24,128]{1,0:T(8,128)S(1)}, f32[24,128]{1,0:T(8,128)S(1)}, u32[]{:S(2)}, u32[]{:S(2)}) %collective-permute-start.17) | collective-permute-done | bytes 12320 | tf_op jit(solution)/shard_map/ppermute | solution.py:566
  184.3 4.0 %collective-permute-start.20 = (f32[24,128]{1,0:T(8,128)S(1)}, f32[24,128]{1,0:T(8,128)S(1)}, u32[]{:S(2)}, u32[]{:S(2)}) collective-permute-start(f32[24,128]{1,0:T(8,128)S(1)} %pad_maximum_fusion.s0), channel_id=1, source_target_pairs={{0,8},{1,9},{2,10},{3,11},{4,12},{5,13},{6,14},{7,15},{8,0},{9,1},... | collective-permute-start | bytes 36872 | tf_op jit(solution)/shard_map/ppermute | solution.py:566
  188.3 2.5 collective-permute-start.21
  192.2 3.6 %dense_grads.1 = (f32[1024,128]{1,0:T(8,128)S(1)}, bf16[1024,128]{1,0:T(8,128)(2,1)S(1)}, bf16[128,1024]{1,0:T(8,128)(2,1)S(1)}) custom-call(s32[5]{0:T(128)S(1)} %copy-done.6, bf16[2,128,1024]{2,1,0:T(8,128)(2,1)S(1)} %get-tuple-element.49.q_ref, bf16[128,2,8,128]{3,2,1,0:T(8,128)(2,1)S(1)} %all-to-all-done.held_ref, ...), custom_call_target="tpu_custom_call" | custom-call | tf_op jit(solution)/shard_map/dense_grads/pallas_call | solution.py:400
  201.2 5.2 %sparse_grads.3 = (bf16[128,8192]{1,0:T(8,128)(2,1)}, f32[2,128,1024]{2,1,0:T(8,128)}, bf16[2,128,1024]{2,1,0:T(8,128)(2,1)}, bf16[2,128,1024]{2,1,0:T(8,128)(2,1)}, bf16[4,2,16,5,8,128]{5,4,3,2,1,0:T(8,128)(2,1)}) custom-call(s32[5]{0:T(128)} %copy-done.4, ...), custom_call_target="tpu_custom_call", output_to_operand_aliasing={{0}: (8, {}), {1}: (9, {}), {2}: (10, {}), {3}: (11, {})} | custom-call | tf_op jit(solution)/shard_map/sparse_grads/pallas_call | solution.py:258
  206.5 24.8 %all-to-all-start.3 = ((bf16[128,5,8,128]{3,2,1,0:T(8,128)(2,1)}), bf16[128,5,8,128]{3,2,1,0:T(8,128)(2,1)S(1)}, u32[]{:S(2)}, u32[]{:S(2)}) async-start(bf16[128,5,8,128]{3,2,1,0:T(8,128)(2,1)} %bitcast.15), calls=%async_computation.3 | async-start | bytes 2621440 | tf_op jit(solution)/shard_map/all_to_all | solution.py:563
  237.3 21.7 %collective-permute-done.27 = bf16[128,1024]{1,0:T(8,128)(2,1)S(1)} collective-permute-done((bf16[128,1024]{1,0:T(8,128)(2,1)S(1)}, bf16[128,1024]{1,0:T(8,128)(2,1)S(1)}, u32[]{:S(2)}, u32[]{:S(2)}) %collective-permute-start.27) | collective-permute-done | bytes 262176 | tf_op jit(solution)/shard_map/ppermute | solution.py:566
  266.6 1.8 collective-permute-done.28.rest_1_
  270.6 1.6 scatter_pieces.1.first_ref
  273.3 2.7 scatter_last.1
  275.9 12.0 %all-to-all-start.5 = ((bf16[128,2,8,128]{3,2,1,0:T(8,128)(2,1)}), bf16[128,2,8,128]{3,2,1,0:T(8,128)(2,1)S(1)}, u32[]{:S(2)}, u32[]{:S(2)}) async-start(bf16[128,2,8,128]{3,2,1,0:T(8,128)(2,1)} %scatter_last.1), calls=%async_computation.5 | async-start | bytes 1048576 | tf_op jit(solution)/shard_map/all_to_all | solution.py:563
  291.9 6.5 %collective-permute-done.32.rest_5_ = bf16[128,1024]{1,0:T(8,128)(2,1)S(1)} collective-permute-done((bf16[128,1024]{1,0:T(8,128)(2,1)}, bf16[128,1024]{1,0:T(8,128)(2,1)S(1)}, u32[]{:S(2)}, u32[]{:S(2)}) %collective-permute-start.32) | collective-permute-done | bytes 262176 | tf_op jit(solution)/shard_map/ppermute | solution.py:566
  298.4 1.9 collective-permute-done.33.rest_6_
  300.3 2.8 collective-permute-done.34.rest_7_
  303.9 3.2 %put_first.1 = bf16[128,8192]{1,0:T(8,128)(2,1)} custom-call(s32[5]{0:T(128)} %copy-done.4, bf16[128,8192]{1,0:T(8,128)(2,1)} %get-tuple-element.39.dq_ref, bf16[128,1024]{1,0:T(8,128)(2,1)} %add_convert_fusion.rest_0_, bf16[128,1024]{1,0:T(8,128)(2,1)} %copy-done.15, ...), custom_call_target="tpu_custom_call", output_to_operand_aliasing={{}: (1, {})} | custom-call | tf_op jit(solution)/shard_map/put_first/pallas_call | solution.py:502
  307.1 2.2 combine.1
  (108 shorter events, 40.8 us)
Async XLA Ops:
  0.6 13.3 %copy-start.20 = (s32[128,8]{0,1:T(8,128)S(1)}, s32[128,8]{0,1:T(8,128)}, u32[]{:S(2)}) copy-start(s32[128,8]{0,1:T(8,128)} %param.10) | copy-start | bytes 12292
  2.8 24.8 %all-to-all-start = ((bf16[128,2,8,128]{3,2,1,0:T(8,128)(2,1)}), bf16[128,2,8,128]{3,2,1,0:T(8,128)(2,1)S(1)}, u32[]{:S(2)}, u32[]{:S(2)}) async-start(bf16[128,2,8,128]{3,2,1,0:T(8,128)(2,1)} %bitcast.16), calls=%async_computation | async-start | bytes 1048576 | tf_op jit(solution)/shard_map/all_to_all | solution.py:563
  14.3 15.6 %copy-start.4 = (s32[5]{0:T(128)}, s32[5]{0:T(128)S(1)}, u32[]{:S(2)}) copy-start(s32[5]{0:T(128)S(1)} %stack.23.meta_ref) | copy-start | bytes 64
  29.9 26.4 %all-to-all-start.2 = ((bf16[128,5,8,128]{3,2,1,0:T(8,128)(2,1)}), bf16[128,5,8,128]{3,2,1,0:T(8,128)(2,1)S(1)}, u32[]{:S(2)}, u32[]{:S(2)}) async-start(bf16[128,5,8,128]{3,2,1,0:T(8,128)(2,1)} %gather_pieces.3), calls=%async_computation.2 | async-start | bytes 2621440 | tf_op jit(solution)/shard_map/all_to_all | solution.py:563
  39.2 30.8 %collective-permute-start.2 = (bf16[2,128,1024]{2,1,0:T(8,128)(2,1)}, bf16[2,128,1024]{2,1,0:T(8,128)(2,1)}, u32[]{:S(2)}, u32[]{:S(2)}) collective-permute-start(bf16[2,128,1024]{2,1,0:T(8,128)(2,1)} %get-tuple-element.41), channel_id=1, source_target_pairs={{0,16}} | collective-permute-start | bytes 1572872 | tf_op jit(solution)/shard_map/ppermute | solution.py:566
  41.2 30.8 %collective-permute-start.3 = (bf16[2,128,1024]{2,1,0:T(8,128)(2,1)}, bf16[2,128,1024]{2,1,0:T(8,128)(2,1)}, u32[]{:S(2)}, u32[]{:S(2)}) collective-permute-start(bf16[2,128,1024]{2,1,0:T(8,128)(2,1)} %get-tuple-element.42), channel_id=1, source_target_pairs={{0,32}} | collective-permute-start | bytes 1572872 | tf_op jit(solution)/shard_map/ppermute | solution.py:566
  57.3 50.7 %all-to-all-start.1 = ((bf16[128,5,8,128]{3,2,1,0:T(8,128)(2,1)}), bf16[128,5,8,128]{3,2,1,0:T(8,128)(2,1)S(1)}, u32[]{:S(2)}, u32[]{:S(2)}) async-start(bf16[128,5,8,128]{3,2,1,0:T(8,128)(2,1)} %get-tuple-element.34), calls=%async_computation.1 | async-start | bytes 2621440 | tf_op jit(solution)/shard_map/all_to_all | solution.py:563
  62.0 18.8 %collective-permute-start.4 = (bf16[2,128,1024]{2,1,0:T(8,128)(2,1)}, bf16[2,128,1024]{2,1,0:T(8,128)(2,1)S(1)}, u32[]{:S(2)}, u32[]{:S(2)}) collective-permute-start(bf16[2,128,1024]{2,1,0:T(8,128)(2,1)} %get-tuple-element.43), channel_id=1, source_target_pairs={{0,48}} | collective-permute-start | bytes 1572872 | tf_op jit(solution)/shard_map/ppermute | solution.py:566
  64.5 21.9 %collective-permute-start.5 = (bf16[2,128,1024]{2,1,0:T(8,128)(2,1)}, bf16[2,128,1024]{2,1,0:T(8,128)(2,1)}, u32[]{:S(2)}, u32[]{:S(2)}) collective-permute-start(bf16[2,128,1024]{2,1,0:T(8,128)(2,1)} %get-tuple-element.44), channel_id=1, source_target_pairs={{0,64}} | collective-permute-start | bytes 1572872 | tf_op jit(solution)/shard_map/ppermute | solution.py:566
  67.9 24.2 %collective-permute-start.6 = (bf16[2,128,1024]{2,1,0:T(8,128)(2,1)}, bf16[2,128,1024]{2,1,0:T(8,128)(2,1)}, u32[]{:S(2)}, u32[]{:S(2)}) collective-permute-start(bf16[2,128,1024]{2,1,0:T(8,128)(2,1)} %get-tuple-element.45), channel_id=1, source_target_pairs={{0,80}} | collective-permute-start | bytes 1572872 | tf_op jit(solution)/shard_map/ppermute | solution.py:566
  69.9 22.1 %collective-permute-start.7 = (bf16[2,128,1024]{2,1,0:T(8,128)(2,1)}, bf16[2,128,1024]{2,1,0:T(8,128)(2,1)}, u32[]{:S(2)}, u32[]{:S(2)}) collective-permute-start(bf16[2,128,1024]{2,1,0:T(8,128)(2,1)} %get-tuple-element.46), channel_id=1, source_target_pairs={{0,96}} | collective-permute-start | bytes 1572872 | tf_op jit(solution)/shard_map/ppermute | solution.py:566
  72.0 20.0 %collective-permute-start.8 = (bf16[2,128,1024]{2,1,0:T(8,128)(2,1)}, bf16[2,128,1024]{2,1,0:T(8,128)(2,1)}, u32[]{:S(2)}, u32[]{:S(2)}) collective-permute-start(bf16[2,128,1024]{2,1,0:T(8,128)(2,1)} %get-tuple-element.47), channel_id=1, source_target_pairs={{0,112}} | collective-permute-start | bytes 1572872 | tf_op jit(solution)/shard_map/ppermute | solution.py:566
  80.8 21.0 %collective-permute-start = (bf16[2,128,1024]{2,1,0:T(8,128)(2,1)}, bf16[2,128,1024]{2,1,0:T(8,128)(2,1)S(1)}, u32[]{:S(2)}, u32[]{:S(2)}) collective-permute-start(bf16[2,128,1024]{2,1,0:T(8,128)(2,1)} %get-tuple-element.32.self_ref), channel_id=1, source_target_pairs={{1,2},{2,3},{3,4},{4,5},{5,6},{6,7},{7,8},{8,9},{9,10},{10,11},{11... | collective-permute-start | bytes 1572872 | tf_op jit(solution)/shard_map/ppermute | solution.py:566
  86.4 15.4 %collective-permute-start.1 = (bf16[2,128,1024]{2,1,0:T(8,128)(2,1)}, bf16[2,128,1024]{2,1,0:T(8,128)(2,1)S(1)}, u32[]{:S(2)}, u32[]{:S(2)}) collective-permute-start(bf16[2,128,1024]{2,1,0:T(8,128)(2,1)} %get-tuple-element.32.self_ref), channel_id=1, source_target_pairs={{2,1},{3,2},{4,3},{5,4},{6,5},{7,6},{8,7},{9,8},{10,9},{11,10},{12... | collective-permute-start | bytes 1572872 | tf_op jit(solution)/shard_map/ppermute | solution.py:566
  94.8 39.6 %collective-permute-start.9 = (bf16[2,128,1024]{2,1,0:T(8,128)(2,1)}, bf16[2,128,1024]{2,1,0:T(8,128)(2,1)}, u32[]{:S(2)}, u32[]{:S(2)}) collective-permute-start(bf16[2,128,1024]{2,1,0:T(8,128)(2,1)} %pick.2.rest_0_), channel_id=1, source_target_pairs={{0,1},{16,17},{32,33},{48,49},{64,65},{80,81},{96,97},{112,113}} | collective-permute-start | bytes 1572872 | tf_op jit(solution)/shard_map/ppermute | solution.py:566
  96.9 37.5 %collective-permute-start.10 = (bf16[2,128,1024]{2,1,0:T(8,128)(2,1)}, bf16[2,128,1024]{2,1,0:T(8,128)(2,1)}, u32[]{:S(2)}, u32[]{:S(2)}) collective-permute-start(bf16[2,128,1024]{2,1,0:T(8,128)(2,1)} %pick.2.rest_0_), channel_id=1, source_target_pairs={{0,2},{16,18},{32,34},{48,50},{64,66},{80,82},{96,98},{112,114}} | collective-permute-start | bytes 1572872 | tf_op jit(solution)/shard_map/ppermute | solution.py:566
  98.9 35.5 %collective-permute-start.11 = (bf16[2,128,1024]{2,1,0:T(8,128)(2,1)}, bf16[2,128,1024]{2,1,0:T(8,128)(2,1)}, u32[]{:S(2)}, u32[]{:S(2)}) collective-permute-start(bf16[2,128,1024]{2,1,0:T(8,128)(2,1)} %pick.2.rest_0_), channel_id=1, source_target_pairs={{0,3},{16,19},{32,35},{48,51},{64,67},{80,83},{96,99},{112,115}} | collective-permute-start | bytes 1572872 | tf_op jit(solution)/shard_map/ppermute | solution.py:566
  109.2 97.3 %all-to-all-start.4 = ((bf16[128,5,8,128]{3,2,1,0:T(8,128)(2,1)}), bf16[128,5,8,128]{3,2,1,0:T(8,128)(2,1)S(1)}, u32[]{:S(2)}, u32[]{:S(2)}) async-start(bf16[128,5,8,128]{3,2,1,0:T(8,128)(2,1)} %bitcast.14), calls=%async_computation.4 | async-start | bytes 2621440 | tf_op jit(solution)/shard_map/all_to_all | solution.py:563
  134.4 37.3 %copy-start.6 = (s32[5]{0:T(128)S(1)}, s32[5]{0:T(128)}, u32[]{:S(2)}) copy-start(s32[5]{0:T(128)} %copy-done.4) | copy-start | bytes 64
  137.0 23.4 %collective-permute-start.12 = (bf16[2,128,1024]{2,1,0:T(8,128)(2,1)}, bf16[2,128,1024]{2,1,0:T(8,128)(2,1)S(1)}, u32[]{:S(2)}, u32[]{:S(2)}) collective-permute-start(bf16[2,128,1024]{2,1,0:T(8,128)(2,1)} %pick.3.p0), channel_id=1, source_target_pairs={{0,4},{1,5},{2,6},{3,7},{16,20},{17,21},{18,22},{19,23},{32,36},{3... | collective-permute-start | bytes 1572872 | tf_op jit(solution)/shard_map/ppermute | solution.py:566
  140.0 31.6 %collective-permute-start.13 = (bf16[2,128,1024]{2,1,0:T(8,128)(2,1)}, bf16[2,128,1024]{2,1,0:T(8,128)(2,1)S(1)}, u32[]{:S(2)}, u32[]{:S(2)}) collective-permute-start(bf16[2,128,1024]{2,1,0:T(8,128)(2,1)} %pick.3.p0), channel_id=1, source_target_pairs={{0,8},{1,9},{2,10},{3,11},{16,24},{17,25},{18,26},{19,27},{32,40},... | collective-permute-start | bytes 1572872 | tf_op jit(solution)/shard_map/ppermute | solution.py:566
  142.5 29.2 %collective-permute-start.14 = (bf16[2,128,1024]{2,1,0:T(8,128)(2,1)}, bf16[2,128,1024]{2,1,0:T(8,128)(2,1)S(1)}, u32[]{:S(2)}, u32[]{:S(2)}) collective-permute-start(bf16[2,128,1024]{2,1,0:T(8,128)(2,1)} %pick.3.p0), channel_id=1, source_target_pairs={{0,12},{1,13},{2,14},{3,15},{16,28},{17,29},{18,30},{19,31},{32,44... | collective-permute-start | bytes 1572872 | tf_op jit(solution)/shard_map/ppermute | solution.py:566
  143.8 1.6 collective-permute-start.15
  175.8 4.2 %collective-permute-start.18 = (f32[24,128]{1,0:T(8,128)S(1)}, f32[24,128]{1,0:T(8,128)S(1)}, u32[]{:S(2)}, u32[]{:S(2)}) collective-permute-start(f32[24,128]{1,0:T(8,128)S(1)} %get-tuple-element.50), channel_id=1, source_target_pairs={{0,3},{1,0},{2,1},{3,2},{4,7},{5,4},{6,5},{7,6},{8,11},{9,8},{10,9... | collective-permute-start | bytes 36872 | tf_op jit(solution)/shard_map/ppermute | solution.py:566
  178.0 5.2 %collective-permute-start.17 = (f32[24,128]{1,0:T(8,128)S(1)}, f32[24,128]{1,0:T(8,128)S(1)}, u32[]{:S(2)}, u32[]{:S(2)}) collective-permute-start(f32[24,128]{1,0:T(8,128)S(1)} %get-tuple-element.50), channel_id=1, source_target_pairs={{0,2},{1,3},{2,0},{3,1},{4,6},{5,7},{6,4},{7,5},{8,10},{9,11},{10,... | collective-permute-start | bytes 36872 | tf_op jit(solution)/shard_map/ppermute | solution.py:566
  179.3 4.9 %collective-permute-start.16 = (f32[24,128]{1,0:T(8,128)S(1)}, f32[24,128]{1,0:T(8,128)S(1)}, u32[]{:S(2)}, u32[]{:S(2)}) collective-permute-start(f32[24,128]{1,0:T(8,128)S(1)} %get-tuple-element.50), channel_id=1, source_target_pairs={{0,1},{1,2},{2,3},{3,0},{4,5},{5,6},{6,7},{7,4},{8,9},{9,10},{10,1... | collective-permute-start | bytes 36872 | tf_op jit(solution)/shard_map/ppermute | solution.py:566
  184.2 6.6 %collective-permute-start.19 = (f32[24,128]{1,0:T(8,128)S(1)}, f32[24,128]{1,0:T(8,128)S(1)}, u32[]{:S(2)}, u32[]{:S(2)}) collective-permute-start(f32[24,128]{1,0:T(8,128)S(1)} %pad_maximum_fusion.s0), channel_id=1, source_target_pairs={{0,4},{1,5},{2,6},{3,7},{4,8},{5,9},{6,10},{7,11},{8,12},{9,13},{1... | collective-permute-start | bytes 36872 | tf_op jit(solution)/shard_map/ppermute | solution.py:566
  184.3 6.5 %collective-permute-start.20 = (f32[24,128]{1,0:T(8,128)S(1)}, f32[24,128]{1,0:T(8,128)S(1)}, u32[]{:S(2)}, u32[]{:S(2)}) collective-permute-start(f32[24,128]{1,0:T(8,128)S(1)} %pad_maximum_fusion.s0), channel_id=1, source_target_pairs={{0,8},{1,9},{2,10},{3,11},{4,12},{5,13},{6,14},{7,15},{8,0},{9,1},... | collective-permute-start | bytes 36872 | tf_op jit(solution)/shard_map/ppermute | solution.py:566
  188.3 3.9 %collective-permute-start.21 = (f32[24,128]{1,0:T(8,128)S(1)}, f32[24,128]{1,0:T(8,128)S(1)}, u32[]{:S(2)}, u32[]{:S(2)}) collective-permute-start(f32[24,128]{1,0:T(8,128)S(1)} %pad_maximum_fusion.s0), channel_id=1, source_target_pairs={{0,12},{1,13},{2,14},{3,15},{4,0},{5,1},{6,2},{7,3},{8,4},{9,5},{1... | collective-permute-start | bytes 36872 | tf_op jit(solution)/shard_map/ppermute | solution.py:566
  197.4 34.0 %collective-permute-start.24 = (bf16[128,1024]{1,0:T(8,128)(2,1)S(1)}, bf16[128,1024]{1,0:T(8,128)(2,1)S(1)}, u32[]{:S(2)}, u32[]{:S(2)}) collective-permute-start(bf16[128,1024]{1,0:T(8,128)(2,1)S(1)} %get-tuple-element.51), channel_id=1, source_target_pairs={{12,0},{13,1},{14,2},{15,3},{28,16},{29,17},{30,18},{31,19},{44,32... | collective-permute-start | bytes 786440 | tf_op jit(solution)/shard_map/ppermute | solution.py:566
  198.6 32.7 %collective-permute-start.23 = (bf16[128,1024]{1,0:T(8,128)(2,1)S(1)}, bf16[128,1024]{1,0:T(8,128)(2,1)}, u32[]{:S(2)}, u32[]{:S(2)}) collective-permute-start(bf16[128,1024]{1,0:T(8,128)(2,1)S(1)} %get-tuple-element.51), channel_id=1, source_target_pairs={{8,0},{9,1},{10,2},{11,3},{24,16},{25,17},{26,18},{27,19},{40,32},... | collective-permute-start | bytes 786440 | tf_op jit(solution)/shard_map/ppermute | solution.py:566
  199.9 32.1 %collective-permute-start.22 = (bf16[128,1024]{1,0:T(8,128)(2,1)S(1)}, bf16[128,1024]{1,0:T(8,128)(2,1)}, u32[]{:S(2)}, u32[]{:S(2)}) collective-permute-start(bf16[128,1024]{1,0:T(8,128)(2,1)S(1)} %get-tuple-element.51), channel_id=1, source_target_pairs={{4,0},{5,1},{6,2},{7,3},{20,16},{21,17},{22,18},{23,19},{36,32},{3... | collective-permute-start | bytes 786440 | tf_op jit(solution)/shard_map/ppermute | solution.py:566
  206.5 65.7 %all-to-all-start.3 = ((bf16[128,5,8,128]{3,2,1,0:T(8,128)(2,1)}), bf16[128,5,8,128]{3,2,1,0:T(8,128)(2,1)S(1)}, u32[]{:S(2)}, u32[]{:S(2)}) async-start(bf16[128,5,8,128]{3,2,1,0:T(8,128)(2,1)} %bitcast.15), calls=%async_computation.3 | async-start | bytes 2621440 | tf_op jit(solution)/shard_map/all_to_all | solution.py:563
  233.3 25.7 %collective-permute-start.27 = (bf16[128,1024]{1,0:T(8,128)(2,1)S(1)}, bf16[128,1024]{1,0:T(8,128)(2,1)S(1)}, u32[]{:S(2)}, u32[]{:S(2)}) collective-permute-start(bf16[128,1024]{1,0:T(8,128)(2,1)S(1)} %add_convert_fusion.1), channel_id=1, source_target_pairs={{3,0},{19,16},{35,32},{51,48},{67,64},{83,80},{99,96},{115,112}} | collective-permute-start | bytes 786440 | tf_op jit(solution)/shard_map/ppermute | solution.py:566
  234.6 24.4 %collective-permute-start.26 = (bf16[128,1024]{1,0:T(8,128)(2,1)S(1)}, bf16[128,1024]{1,0:T(8,128)(2,1)S(1)}, u32[]{:S(2)}, u32[]{:S(2)}) collective-permute-start(bf16[128,1024]{1,0:T(8,128)(2,1)S(1)} %add_convert_fusion.1), channel_id=1, source_target_pairs={{2,0},{18,16},{34,32},{50,48},{66,64},{82,80},{98,96},{114,112}} | collective-permute-start | bytes 786440 | tf_op jit(solution)/shard_map/ppermute | solution.py:566
  235.9 23.1 %collective-permute-start.25 = (bf16[128,1024]{1,0:T(8,128)(2,1)S(1)}, bf16[128,1024]{1,0:T(8,128)(2,1)S(1)}, u32[]{:S(2)}, u32[]{:S(2)}) collective-permute-start(bf16[128,1024]{1,0:T(8,128)(2,1)S(1)} %add_convert_fusion.1), channel_id=1, source_target_pairs={{1,0},{17,16},{33,32},{49,48},{65,64},{81,80},{97,96},{113,112}} | collective-permute-start | bytes 786440 | tf_op jit(solution)/shard_map/ppermute | solution.py:566
  237.2 35.0 %copy-start.7 = (s32[5]{0:T(128)S(1)}, s32[5]{0:T(128)}, u32[]{:S(2)}) copy-start(s32[5]{0:T(128)} %copy-done.4) | copy-start | bytes 64
  237.3 27.9 %collective-permute-start.37 = (bf16[1024,128]{1,0:T(8,128)(2,1)S(1)}, bf16[1024,128]{1,0:T(8,128)(2,1)S(1)}, u32[]{:S(2)}, u32[]{:S(2)}) collective-permute-start(bf16[1024,128]{1,0:T(8,128)(2,1)S(1)} %copy-done.9), channel_id=1, source_target_pairs={{0,16},{1,17},{2,18},{3,19},{4,20},{5,21},{6,22},{7,23},{8,24},{9,... | collective-permute-start | bytes 786440 | tf_op jit(solution)/shard_map/ppermute | solution.py:566
  260.0 8.5 %collective-permute-start.28 = (bf16[128,1024]{1,0:T(8,128)(2,1)}, bf16[128,1024]{1,0:T(8,128)(2,1)S(1)}, u32[]{:S(2)}, u32[]{:S(2)}) collective-permute-start(bf16[128,1024]{1,0:T(8,128)(2,1)} %add_convert_fusion.rest_0_), channel_id=1, source_target_pairs={{32,0}} | collective-permute-start | bytes 786440 | tf_op jit(solution)/shard_map/ppermute | solution.py:566
  261.2 26.7 %collective-permute-start.29 = (bf16[128,1024]{1,0:T(8,128)(2,1)}, bf16[128,1024]{1,0:T(8,128)(2,1)}, u32[]{:S(2)}, u32[]{:S(2)}) collective-permute-start(bf16[128,1024]{1,0:T(8,128)(2,1)} %add_convert_fusion.rest_0_), channel_id=1, source_target_pairs={{64,0}} | collective-permute-start | bytes 786440 | tf_op jit(solution)/shard_map/ppermute | solution.py:566
  262.5 26.7 %collective-permute-start.30 = (bf16[128,1024]{1,0:T(8,128)(2,1)}, bf16[128,1024]{1,0:T(8,128)(2,1)}, u32[]{:S(2)}, u32[]{:S(2)}) collective-permute-start(bf16[128,1024]{1,0:T(8,128)(2,1)} %add_convert_fusion.rest_0_), channel_id=1, source_target_pairs={{96,0}} | collective-permute-start | bytes 786440 | tf_op jit(solution)/shard_map/ppermute | solution.py:566
  263.8 26.7 %collective-permute-start.31 = (bf16[128,1024]{1,0:T(8,128)(2,1)}, bf16[128,1024]{1,0:T(8,128)(2,1)}, u32[]{:S(2)}, u32[]{:S(2)}) collective-permute-start(bf16[128,1024]{1,0:T(8,128)(2,1)} %add_convert_fusion.rest_0_), channel_id=1, source_target_pairs={{16,0}} | collective-permute-start | bytes 786440 | tf_op jit(solution)/shard_map/ppermute | solution.py:566
  265.2 41.9 %collective-permute-start.35 = (bf16[2,128,1024]{2,1,0:T(8,128)(2,1)}, bf16[2,128,1024]{2,1,0:T(8,128)(2,1)}, u32[]{:S(2)}, u32[]{:S(2)}) collective-permute-start(bf16[2,128,1024]{2,1,0:T(8,128)(2,1)} %get-tuple-element.53), channel_id=1, source_target_pairs={{1,2},{2,3},{3,4},{4,5},{5,6},{6,7},{7,8},{8,9},{9,10},{10,11},{11... | collective-permute-start | bytes 1572872 | tf_op jit(solution)/shard_map/ppermute | solution.py:566
  269.1 37.9 %collective-permute-start.36 = (bf16[2,128,1024]{2,1,0:T(8,128)(2,1)}, bf16[2,128,1024]{2,1,0:T(8,128)(2,1)}, u32[]{:S(2)}, u32[]{:S(2)}) collective-permute-start(bf16[2,128,1024]{2,1,0:T(8,128)(2,1)} %get-tuple-element.54), channel_id=1, source_target_pairs={{2,1},{3,2},{4,3},{5,4},{6,5},{7,6},{8,7},{9,8},{10,9},{11,10},{12... | collective-permute-start | bytes 1572872 | tf_op jit(solution)/shard_map/ppermute | solution.py:566
  275.9 31.1 %all-to-all-start.5 = ((bf16[128,2,8,128]{3,2,1,0:T(8,128)(2,1)}), bf16[128,2,8,128]{3,2,1,0:T(8,128)(2,1)S(1)}, u32[]{:S(2)}, u32[]{:S(2)}) async-start(bf16[128,2,8,128]{3,2,1,0:T(8,128)(2,1)} %scatter_last.1), calls=%async_computation.5 | async-start | bytes 1048576 | tf_op jit(solution)/shard_map/all_to_all | solution.py:563
  288.0 10.5 %collective-permute-start.32 = (bf16[128,1024]{1,0:T(8,128)(2,1)}, bf16[128,1024]{1,0:T(8,128)(2,1)S(1)}, u32[]{:S(2)}, u32[]{:S(2)}) collective-permute-start(bf16[128,1024]{1,0:T(8,128)(2,1)} %add_convert_fusion.rest_0_), channel_id=1, source_target_pairs={{48,0}} | collective-permute-start | bytes 786440 | tf_op jit(solution)/shard_map/ppermute | solution.py:566
  289.3 11.1 %collective-permute-start.33 = (bf16[128,1024]{1,0:T(8,128)(2,1)}, bf16[128,1024]{1,0:T(8,128)(2,1)S(1)}, u32[]{:S(2)}, u32[]{:S(2)}) collective-permute-start(bf16[128,1024]{1,0:T(8,128)(2,1)} %add_convert_fusion.rest_0_), channel_id=1, source_target_pairs={{80,0}} | collective-permute-start | bytes 786440 | tf_op jit(solution)/shard_map/ppermute | solution.py:566
  290.6 12.6 %collective-permute-start.34 = (bf16[128,1024]{1,0:T(8,128)(2,1)}, bf16[128,1024]{1,0:T(8,128)(2,1)S(1)}, u32[]{:S(2)}, u32[]{:S(2)}) collective-permute-start(bf16[128,1024]{1,0:T(8,128)(2,1)} %add_convert_fusion.rest_0_), channel_id=1, source_target_pairs={{112,0}} | collective-permute-start | bytes 786440 | tf_op jit(solution)/shard_map/ppermute | solution.py:566
  (18 other events, 45.0 us)
